TPU v7x, 512 devices: a whole 4x4x16 slice. The times are simulated.
512 devices in a mesh: expert: 64 (over z, y), replica: 8 (over x, core).
Axes of the slice: x: 4, y: 4, z: 16, core: 2. Of those that a mesh axis runs over, the one named last changes fastest.
Arguments:
- grad_out: bfloat16 [16384, 2048], P(('expert', 'replica')), may hold values from -12 to 12
- routes: int32 [16384, 6], P(('expert', 'replica')), may hold values from 0 to 63, all different within a row; in each aligned block of 32 rows (0 to 31, 32 to 63, ...) at most 3 rows name the same one
- gates: float32 [16384, 6], P(('expert', 'replica')), may hold values from 0.03 to 0.6
- w_gate: bfloat16 [64, 1408, 2048], P('expert', 'replica'), may hold values from -0.125 to 0.125
- w_up: bfloat16 [64, 1408, 2048], P('expert', 'replica'), may hold values from -0.125 to 0.125
- w_down: bfloat16 [64, 1408, 2048], P('expert', 'replica'), may hold values from -0.15625 to 0.15625
- saved_gate: bfloat16 [64, 8, 64, 3, 1408], P('expert', 'replica'), may hold values from -8 to 8
- saved_up: bfloat16 [64, 8, 64, 3, 1408], P('expert', 'replica'), may hold values from -6 to 6
Outputs:
- grad_in: bfloat16 [16384, 2048], P(('expert', 'replica'))
Inputs may be any that keep to these rules, and one draw needn't show every extreme that they name: `routes`: among the 32 tokens of one device, at most 3 entries name one expert; some expert is named 3 times; the 6 entries of a token differ.
All inputs are finite; a program needn't handle non-finite values.
Results may differ from a plain program's by a relative error of at most 0.01.
Values may be sent and summed in bfloat16 or wider, within the bound.
No kernel may reach another device: no remote copies, remote signals or barrier semaphores. Data moves between devices by JAX's collectives and lax.ppermute only.
A program may use at most 128 MiB of HBM per device.

v0:
```python
import jax
import jax.numpy as jnp
from jax import lax
from jax.experimental import pallas as pl
from jax.experimental.pallas import tpu as pltpu
from jax.sharding import PartitionSpec as P

F32 = jnp.float32
BF16 = jnp.bfloat16
VM = pl.BlockSpec(memory_space=pltpu.VMEM)
SM = pl.BlockSpec(memory_space=pltpu.SMEM)
LINKS = 4


def call(kernel, ins, outs, flops=0, smem=0, scratch=()):
    moved = sum(a.size * a.dtype.itemsize for a in ins) + sum(o.size * o.dtype.itemsize for o in outs)
    single = len(outs) == 1
    return pl.pallas_call(
        kernel,
        out_shape=outs[0] if single else tuple(outs),
        in_specs=[SM] * smem + [VM] * (len(ins) - smem),
        out_specs=VM if single else tuple([VM] * len(outs)),
        scratch_shapes=list(scratch),
        cost_estimate=pl.CostEstimate(flops=flops, bytes_accessed=moved, transcendentals=0),
    )(*ins)


def pack(value, out_ref):
    experts, deep, lanes = out_ref.shape
    slots = value.shape[0] // experts
    chunks = deep // slots
    for s in range(slots):
        block = value[s * experts : (s + 1) * experts].astype(BF16)
        parts = jnp.stack([block[:, c * lanes : (c + 1) * lanes] for c in range(chunks)])
        out_ref[:, s * chunks : (s + 1) * chunks, :] = jnp.swapaxes(parts, 0, 1)


def unpack(packed_ref, s, slots):
    _, deep, _ = packed_ref.shape
    chunks = deep // slots
    parts = jnp.swapaxes(packed_ref[:, s * chunks : (s + 1) * chunks, :], 0, 1)
    return jnp.concatenate([parts[c] for c in range(chunks)], axis=1)


def place_kernel(routes_ref, gates_ref, grad_ref, out_ref, hot_ref):
    top, tokens = routes_ref.shape
    experts, _, _ = out_ref.shape
    rows = hot_ref.shape[0]
    row = lax.broadcasted_iota(jnp.int32, (rows, tokens), 0)
    number = row // experts
    named = row - number * experts
    slot = number.astype(F32)
    hits = jnp.zeros((rows, tokens), F32)
    gate = jnp.zeros((rows, tokens), F32)
    for k in range(top):
        hit = routes_ref[k : k + 1, :] == named
        hits = jnp.where(hit, 1.0, hits)
        gate = jnp.where(hit, gates_ref[k : k + 1, :], gate)
    before = (
        lax.broadcasted_iota(jnp.int32, (tokens, tokens), 0)
        < lax.broadcasted_iota(jnp.int32, (tokens, tokens), 1)
    ).astype(BF16)
    earlier = jnp.dot(hits.astype(BF16), before, preferred_element_type=F32)
    chosen = (hits > 0.5) & (jnp.abs(earlier - slot) < 0.5)
    weight = jnp.sum(jnp.where(chosen, gate, 0.0), axis=1, keepdims=True)
    hot = jnp.where(chosen, 1.0, 0.0).astype(BF16)
    hot_ref[...] = hot
    pack(weight * jnp.dot(hot, grad_ref[...], preferred_element_type=F32), out_ref)


def select_kernel(index_ref, gate_ref, up_ref, keep_ref, send_ref):
    slice_width = keep_ref.shape[3]
    for j in range(2 * LINKS):
        place = index_ref[j]
        low = j * slice_width
        parts = (gate_ref[:, low : low + slice_width], up_ref[:, low : low + slice_width])

        @pl.when(index_ref[2 * LINKS + j] == 1)
        def _():
            keep_ref[0, place] = parts[0]
            keep_ref[1, place] = parts[1]

        @pl.when(index_ref[2 * LINKS + j] == 0)
        def _():
            send_ref[0, place] = parts[0]
            send_ref[1, place] = parts[1]


def factor_kernel(saved_ref, gate_ref, up_ref):
    for p in range(LINKS):
        g = saved_ref[0, p].astype(F32)
        u = saved_ref[1, p].astype(F32)
        sig = jax.nn.sigmoid(g)
        up_ref[p] = g * sig
        gate_ref[p] = u * sig * (1.0 + g * (1.0 - sig))


def hidden_kernel(
    packed_ref, own_ref, left_ref, right_ref, far1_ref, far2_ref, gf_ref, uf_ref, gate_ref, up_ref, rows_ref
):
    slots = rows_ref.shape[0] // packed_ref.shape[0]
    for s in range(slots):
        rows_ref[s * packed_ref.shape[0] : (s + 1) * packed_ref.shape[0], :] = unpack(packed_ref, s, slots)

    def nt(a, b):
        return lax.dot_general(a, b, (((1,), (1,)), ((), ())), preferred_element_type=F32)

    half = far1_ref.shape[1]
    for p in range(LINKS):
        if p < 3:
            grad = nt(rows_ref[...], (own_ref, left_ref, right_ref)[p][...])
        else:
            grad = nt(rows_ref[:, :half], far1_ref[...]) + nt(rows_ref[:, half:], far2_ref[...])
        gate_ref[p] = (grad * gf_ref[p]).astype(BF16)
        up_ref[p] = (grad * uf_ref[p]).astype(BF16)


def output_kernel(gate_ref, up_ref, own_ref, left_ref, right_ref, farg_ref, faru_ref, *rest):
    out_ref = rest[-1]
    width = farg_ref.shape[0]

    def mm(a, b):
        return jnp.dot(a, b, preferred_element_type=F32)

    total = mm(gate_ref[3], farg_ref[...]) + mm(up_ref[3], faru_ref[...])
    for p, ref in enumerate((own_ref, left_ref, right_ref)):
        total += mm(gate_ref[p], ref[:width]) + mm(up_ref[p], ref[width:])
    if len(rest) == 2:
        total += rest[0][...].astype(F32)
    if len(out_ref.shape) == 3:
        pack(total, out_ref)
    else:
        out_ref[...] = total.astype(out_ref.dtype)


def turn_kernel(hot_ref, out_ref):
    out_ref[...] = hot_ref[...].T


def combine_kernel(hot_ref, *refs):
    out_ref = refs[-1]
    tokens, width = out_ref.shape
    half = width // 2
    for n, ref in enumerate(refs[:-1]):
        experts = ref.shape[0]
        slots = hot_ref.shape[1] // experts
        total = jnp.zeros((tokens, half), F32)
        for s in range(slots):
            total += jnp.dot(
                hot_ref[:, s * experts : (s + 1) * experts],
                unpack(ref, s, slots),
                preferred_element_type=F32,
            )
        out_ref[:, n * half : (n + 1) * half] = total.astype(BF16)


def body(grad_out, routes, gates, w_gate, w_up, w_down, saved_gate, saved_up):
    experts = lax.axis_size("expert")
    copies = lax.axis_size("replica")
    tokens, width = grad_out.shape
    slots = saved_gate.shape[3]
    slice_width = w_gate.shape[1]
    rows = experts * slots
    half = width // 2
    chunks = half // 128
    deep = slots * chunks
    replica = lax.axis_index("replica")
    link, core = replica // 2, replica % 2

    def along(a, by):
        pairs = [(2 * i + k, 2 * ((i + by) % LINKS) + k) for i in range(LINKS) for k in range(2)]
        return lax.ppermute(a, "replica", pairs)

    def across(a):
        return lax.ppermute(a, "replica", [(i, i ^ 1) for i in range(copies)])

    def exchange(a):
        return lax.all_to_all(a, "expert", split_axis=0, concat_axis=0, tiled=True)

    down = w_down[0]
    down_left, down_right = along(down, 1), along(down, -1)

    packed, hot = call(
        place_kernel,
        (routes.T, gates.T, grad_out),
        (
            jax.ShapeDtypeStruct((experts, 2 * deep, 128), BF16),
            jax.ShapeDtypeStruct((rows, tokens), BF16),
        ),
        2 * rows * tokens * width,
    )
    arrived = exchange(packed)

    first = jnp.concatenate([w_gate[0, :, :half], w_up[0, :, :half]], axis=0)
    second = jnp.concatenate([w_gate[0, :, half:], w_up[0, :, half:]], axis=0)
    first_left, first_right = along(first, 1), along(first, -1)
    down_far1 = along(down_left[:, :half], 1)
    down_far2 = along(down_right[:, half:], -1)
    second_left, second_right = along(second, 1), along(second, -1)
    first_farg = along(first_left[:slice_width], 1)
    first_faru = along(first_right[slice_width:], -1)
    second_farg = along(second_left[:slice_width], 1)
    second_faru = along(second_right[slice_width:], -1)

    order = jnp.arange(2 * LINKS, dtype=jnp.int32)
    offset = (order // 2 - link) & (LINKS - 1)
    where = jnp.where(offset == 0, 0, jnp.where(offset == 1, 2, jnp.where(offset == 2, 3, 1)))
    mine = (order % 2 == core).astype(jnp.int32)
    saved = tuple(a[0, 0].transpose(1, 0, 2).reshape(rows, -1) for a in (saved_gate, saved_up))
    piece = jax.ShapeDtypeStruct((2, LINKS, rows, slice_width), BF16)
    keep, send = call(select_kernel, (jnp.concatenate([where, mine]),) + saved, (piece, piece), smem=1)
    factor = jax.ShapeDtypeStruct((LINKS, rows, slice_width), F32)
    own_factors = call(factor_kernel, (keep,), (factor, factor))
    sent = across(send)
    other_factors = call(factor_kernel, (sent,), (factor, factor))

    downs = (down, down_left, down_right, down_far1, down_far2)
    hidden = jax.ShapeDtypeStruct((LINKS, rows, slice_width), BF16)
    cost = 2 * rows * LINKS * slice_width * width
    room = (pltpu.VMEM((rows, width), BF16),)
    other_rows = across(arrived)
    own_hidden = call(hidden_kernel, (arrived,) + downs + tuple(own_factors), (hidden, hidden), cost, scratch=room)
    other_hidden = call(
        hidden_kernel, (other_rows,) + downs + tuple(other_factors), (hidden, hidden), cost, scratch=room
    )

    results = []
    for pieces in (
        (first, first_left, first_right, first_farg, first_faru),
        (second, second_left, second_right, second_farg, second_faru),
    ):
        theirs = call(output_kernel, tuple(other_hidden) + pieces, (jax.ShapeDtypeStruct((rows, half), BF16),), cost)
        back = across(theirs)
        outgoing = call(
            output_kernel,
            tuple(own_hidden) + pieces + (back,),
            (jax.ShapeDtypeStruct((experts, deep, 128), BF16),),
            cost,
        )
        results.append(exchange(outgoing))
    turned = call(turn_kernel, (hot,), (jax.ShapeDtypeStruct((tokens, rows), BF16),))
    return call(combine_kernel, (turned,) + tuple(results), (jax.ShapeDtypeStruct((tokens, width), BF16),))


def solution(mesh):
    in_specs = (
        P(("expert", "replica"), None),
        P(("expert", "replica"), None),
        P(("expert", "replica"), None),
        P("expert", "replica", None),
        P("expert", "replica", None),
        P("expert", "replica", None),
        P("expert", "replica", None, None, None),
        P("expert", "replica", None, None, None),
    )
    out_specs = P(("expert", "replica"), None)

    return jax.shard_map(body, mesh=mesh, in_specs=in_specs, out_specs=out_specs, check_vma=False)
```

profile of v0, /device:TPU:6, one launch (start us, length us, event | category | flops | bytes accessed | tf_op | source)
XLA Modules:
  0.0 199.0 jit_solution(11144303408940351355)
XLA Ops:
  0.0 2.5 %shard_map.82 = (bf16[64,48,128]{2,1,0:T(8,128)(2,1)}, bf16[192,32]{1,0:T(8,128)(2,1)}) custom-call(s32[6,32]{1,0:T(8,128)} %bitcast.23, f32[6,32]{1,0:T(8,128)} %bitcast.24, bf16[32,2048]{1,0:T(8,128)(2,1)} %grad_ref.1), custom_call_target="tpu_custom_call" | custom-call | flops 25165824 | bytes 931328 | tf_op jit(solution)/shard_map/pallas_call | solution.py:18
  2.5 19.1 %all-to-all-start = ((bf16[64,48,128]{2,1,0:T(8,128)(2,1)}), bf16[64,48,128]{2,1,0:T(8,128)(2,1)}, u32[]{:S(2)}, u32[]{:S(2)}) async-start(bf16[64,48,128]{2,1,0:T(8,128)(2,1)} %get-tuple-element.18), calls=%async_computation | async-start | bytes 1572864 | tf_op jit(solution)/shard_map/all_to_all | solution.py:178
  21.6 2.4 %collective-permute-start = (bf16[176,2048]{1,0:T(8,128)(2,1)}, bf16[176,2048]{1,0:T(8,128)(2,1)S(1)}, u32[]{:S(2)}, u32[]{:S(2)}) collective-permute-start(bf16[176,2048]{1,0:T(8,128)(2,1)} %bitcast.2.own_ref), channel_id=1, source_target_pairs={{0,2},{1,3},{2,4},{3,5},{4,6},{5,7},{6,0},{7,1},{8,10},{9,11},{10,... | collective-permute-start | bytes 2162696 | tf_op jit(solution)/shard_map/ppermute | solution.py:172
  24.0 3.5 %collective-permute-start.1 = (bf16[176,2048]{1,0:T(8,128)(2,1)}, bf16[176,2048]{1,0:T(8,128)(2,1)S(1)}, u32[]{:S(2)}, u32[]{:S(2)}) collective-permute-start(bf16[176,2048]{1,0:T(8,128)(2,1)} %bitcast.2.own_ref), channel_id=1, source_target_pairs={{0,6},{1,7},{2,0},{3,1},{4,2},{5,3},{6,4},{7,5},{8,14},{9,15},{10,... | collective-permute-start | bytes 2162696 | tf_op jit(solution)/shard_map/ppermute | solution.py:172
  27.5 2.0 %slice_bitcast_fusion = (bf16[176,1024]{1,0:T(8,128)(2,1)S(1)}, bf16[176,1024]{1,0:T(8,128)(2,1)S(1)}, bf16[176,1024]{1,0:T(8,128)(2,1)S(1)}, bf16[176,1024]{1,0:T(8,128)(2,1)}) fusion(bf16[1,176,2048]{2,1,0:T(8,128)(2,1)S(1)} %copy-done.14, bf16[1,176,2048]{2,1,0:T(8,128)(2,1)} %param.11), kind=kLoop, calls=%fused_computation.2 | loop fusion | bytes 2883584 | tf_op jit(solution)/shard_map/squeeze | solution.py:195
  29.6 3.6 %collective-permute-start.4 = (bf16[352,1024]{1,0:T(8,128)(2,1)S(1)}, bf16[352,1024]{1,0:T(8,128)(2,1)S(1)}, u32[]{:S(2)}, u32[]{:S(2)}) collective-permute-start(bf16[352,1024]{1,0:T(8,128)(2,1)S(1)} %pad_maximum_fusion.own_ref), channel_id=1, source_target_pairs={{0,2},{1,3},{2,4},{3,5},{4,6},{5,7},{6,0},{7,1},{8,10},{9,11},{10,... | collective-permute-start | bytes 2162696 | tf_op jit(solution)/shard_map/ppermute | solution.py:172
  33.2 2.2 %collective-permute-start.5 = (bf16[352,1024]{1,0:T(8,128)(2,1)S(1)}, bf16[352,1024]{1,0:T(8,128)(2,1)}, u32[]{:S(2)}, u32[]{:S(2)}) collective-permute-start(bf16[352,1024]{1,0:T(8,128)(2,1)S(1)} %pad_maximum_fusion.own_ref), channel_id=1, source_target_pairs={{0,6},{1,7},{2,0},{3,1},{4,2},{5,3},{6,4},{7,5},{8,14},{9,15},{10,... | collective-permute-start | bytes 2162696 | tf_op jit(solution)/shard_map/ppermute | solution.py:172
  36.2 3.4 %shard_map.84 = (bf16[2,4,192,176]{3,2,1,0:T(8,128)(2,1)}, bf16[2,4,192,176]{3,2,1,0:T(8,128)(2,1)}) custom-call(s32[16]{0:T(128)} %pad_add_fusion.index_ref, bf16[192,1408]{1,0:T(8,128)(2,1)} %bitcast.21, bf16[192,1408]{1,0:T(8,128)(2,1)} %bitcast.22), custom_call_target="tpu_custom_call" | custom-call | bytes 2162752 | tf_op jit(solution)/shard_map/pallas_call | solution.py:18
  39.6 2.3 %copy.9 = bf16[2,4,192,176]{2,3,1,0:T(8,128)(2,1)} copy(bf16[2,4,192,176]{3,2,1,0:T(8,128)(2,1)} %get-tuple-element.24) | data formatting | bytes 1081344 | tf_op jit(solution)/shard_map/pallas_call | solution.py:18
  41.9 1.9 collective-permute-start.9
  43.8 21.7 %all-to-all-done.packed_ref = bf16[64,48,128]{2,1,0:T(8,128)(2,1)} async-done(((bf16[64,48,128]{2,1,0:T(8,128)(2,1)}), bf16[64,48,128]{2,1,0:T(8,128)(2,1)}, u32[]{:S(2)}, u32[]{:S(2)}) %all-to-all-start) | async-done | bytes 786464 | tf_op jit(solution)/shard_map/all_to_all | solution.py:178
  65.6 1.9 collective-permute-start.8
  67.5 0.8 slice.40
  68.3 2.4 %collective-permute-start.2 = (bf16[176,1024]{1,0:T(8,128)(2,1)}, bf16[176,1024]{1,0:T(8,128)(2,1)}, u32[]{:S(2)}, u32[]{:S(2)}) collective-permute-start(bf16[176,1024]{1,0:T(8,128)(2,1)} %slice.40), channel_id=1, source_target_pairs={{0,2},{1,3},{2,4},{3,5},{4,6},{5,7},{6,0},{7,1},{8,10},{9,11},{10,... | collective-permute-start | bytes 1081352 | tf_op jit(solution)/shard_map/ppermute | solution.py:172
  70.7 0.8 slice.41
  71.4 3.4 %collective-permute-start.3 = (bf16[176,1024]{1,0:T(8,128)(2,1)}, bf16[176,1024]{1,0:T(8,128)(2,1)}, u32[]{:S(2)}, u32[]{:S(2)}) collective-permute-start(bf16[176,1024]{1,0:T(8,128)(2,1)} %slice.41), channel_id=1, source_target_pairs={{0,6},{1,7},{2,0},{3,1},{4,2},{5,3},{6,4},{7,5},{8,14},{9,15},{10,... | collective-permute-start | bytes 1081352 | tf_op jit(solution)/shard_map/ppermute | solution.py:172
  74.9 0.8 slice.42
  75.7 3.6 %collective-permute-start.6 = (bf16[176,1024]{1,0:T(8,128)(2,1)}, bf16[176,1024]{1,0:T(8,128)(2,1)S(1)}, u32[]{:S(2)}, u32[]{:S(2)}) collective-permute-start(bf16[176,1024]{1,0:T(8,128)(2,1)} %slice.42), channel_id=1, source_target_pairs={{0,2},{1,3},{2,4},{3,5},{4,6},{5,7},{6,0},{7,1},{8,10},{9,11},{10,... | collective-permute-start | bytes 1081352 | tf_op jit(solution)/shard_map/ppermute | solution.py:172
  79.2 1.0 slice.43
  80.3 2.2 %collective-permute-start.7 = (bf16[176,1024]{1,0:T(8,128)(2,1)S(1)}, bf16[176,1024]{1,0:T(8,128)(2,1)S(1)}, u32[]{:S(2)}, u32[]{:S(2)}) collective-permute-start(bf16[176,1024]{1,0:T(8,128)(2,1)S(1)} %slice.43), channel_id=1, source_target_pairs={{0,6},{1,7},{2,0},{3,1},{4,2},{5,3},{6,4},{7,5},{8,14},{9,15},{10,... | collective-permute-start | bytes 1081352 | tf_op jit(solution)/shard_map/ppermute | solution.py:172
  82.5 2.3 %copy.10.saved_ref = bf16[2,4,192,176]{3,2,1,0:T(8,128)(2,1)} copy(bf16[2,4,192,176]{2,3,1,0:T(8,128)(2,1)} %collective-permute-done.9) | data formatting | bytes 1081344 | tf_op jit(solution)/shard_map/ppermute | solution.py:175
  84.9 2.6 %shard_map.87 = (f32[4,192,176]{2,1,0:T(8,128)}, f32[4,192,176]{2,1,0:T(8,128)}) custom-call(bf16[2,4,192,176]{3,2,1,0:T(8,128)(2,1)} %copy.10.saved_ref), custom_call_target="tpu_custom_call" | custom-call | bytes 1622016 | tf_op jit(solution)/shard_map/pallas_call | solution.py:18
  87.4 4.4 %shard_map.88 = (bf16[4,192,176]{2,1,0:T(8,128)(2,1)}, bf16[4,192,176]{2,1,0:T(8,128)(2,1)}) custom-call(bf16[64,48,128]{2,1,0:T(8,128)(2,1)} %collective-permute-done.8.packed_ref, bf16[176,2048]{1,0:T(8,128)(2,1)} %bitcast.2.own_ref, bf16[176,2048]{1,0:T(8,128)(2,1)} %copy-done.2, bf16[176,2048]{1,0:T(8,128)(2,1)} %copy-done.3, ...), custom_call_target="tpu_custom_call" | custom-call | flops 553648128 | bytes 5292032 | tf_op jit(solution)/shard_map/pallas_call | solution.py:18
  91.8 1.5 collective-permute-done.7.faru_ref
  94.1 3.8 %shard_map.89 = bf16[192,1024]{1,0:T(8,128)(2,1)} custom-call(bf16[4,192,176]{2,1,0:T(8,128)(2,1)} %get-tuple-element.27.gate_ref, bf16[4,192,176]{2,1,0:T(8,128)(2,1)} %get-tuple-element.28.up_ref, bf16[352,1024]{1,0:T(8,128)(2,1)} %copy-done, bf16[352,1024]{1,0:T(8,128)(2,1)} %copy-done.4, bf16[352,1024]{1,0:T(8,128)(2,1)} %collective-permute-done.5.right_ref, ...), custom_call_target="tpu_custom_call" | custom-call | flops 553648128 | bytes 3817472 | tf_op jit(solution)/shard_map/pallas_call | solution.py:18
  97.9 1.9 collective-permute-start.10
  99.9 3.4 %collective-permute-start.11 = (bf16[352,1024]{1,0:T(8,128)(2,1)S(1)}, bf16[352,1024]{1,0:T(8,128)(2,1)S(1)}, u32[]{:S(2)}, u32[]{:S(2)}) collective-permute-start(bf16[352,1024]{1,0:T(8,128)(2,1)S(1)} %pad_maximum_fusion.1.own_ref), channel_id=1, source_target_pairs={{0,2},{1,3},{2,4},{3,5},{4,6},{5,7},{6,0},{7,1},{8,10},{9,11},{10,... | collective-permute-start | bytes 2162696 | tf_op jit(solution)/shard_map/ppermute | solution.py:172
  103.3 2.4 %collective-permute-start.12 = (bf16[352,1024]{1,0:T(8,128)(2,1)S(1)}, bf16[352,1024]{1,0:T(8,128)(2,1)S(1)}, u32[]{:S(2)}, u32[]{:S(2)}) collective-permute-start(bf16[352,1024]{1,0:T(8,128)(2,1)S(1)} %pad_maximum_fusion.1.own_ref), channel_id=1, source_target_pairs={{0,6},{1,7},{2,0},{3,1},{4,2},{5,3},{6,4},{7,5},{8,14},{9,15},{10,... | collective-permute-start | bytes 2162696 | tf_op jit(solution)/shard_map/ppermute | solution.py:172
  105.7 2.6 %shard_map.85 = (f32[4,192,176]{2,1,0:T(8,128)}, f32[4,192,176]{2,1,0:T(8,128)}) custom-call(bf16[2,4,192,176]{3,2,1,0:T(8,128)(2,1)} %get-tuple-element.19.saved_ref), custom_call_target="tpu_custom_call" | custom-call | bytes 1622016 | tf_op jit(solution)/shard_map/pallas_call | solution.py:18
  108.3 4.4 %shard_map.86 = (bf16[4,192,176]{2,1,0:T(8,128)(2,1)}, bf16[4,192,176]{2,1,0:T(8,128)(2,1)}) custom-call(bf16[64,48,128]{2,1,0:T(8,128)(2,1)} %all-to-all-done.packed_ref, bf16[176,2048]{1,0:T(8,128)(2,1)} %bitcast.2.own_ref, bf16[176,2048]{1,0:T(8,128)(2,1)} %copy-done.2, bf16[176,2048]{1,0:T(8,128)(2,1)} %copy-done.3, ...), custom_call_target="tpu_custom_call" | custom-call | flops 553648128 | bytes 5292032 | tf_op jit(solution)/shard_map/pallas_call | solution.py:18
  112.7 0.8 copy-done.15
  113.5 3.9 %shard_map.90 = bf16[64,24,128]{2,1,0:T(8,128)(2,1)} custom-call(bf16[4,192,176]{2,1,0:T(8,128)(2,1)} %get-tuple-element.22.gate_ref, bf16[4,192,176]{2,1,0:T(8,128)(2,1)} %get-tuple-element.23.up_ref, bf16[352,1024]{1,0:T(8,128)(2,1)} %copy-done, bf16[352,1024]{1,0:T(8,128)(2,1)} %copy-done.4, bf16[352,1024]{1,0:T(8,128)(2,1)} %collective-permute-done.5.right_ref, ...), custom_call_target="tpu_custom_call" | custom-call | flops 553648128 | bytes 4210688 | tf_op jit(solution)/shard_map/pallas_call | solution.py:18
  117.4 5.8 %all-to-all-start.1 = ((bf16[64,24,128]{2,1,0:T(8,128)(2,1)}), bf16[64,24,128]{2,1,0:T(8,128)(2,1)S(1)}, u32[]{:S(2)}, u32[]{:S(2)}) async-start(bf16[64,24,128]{2,1,0:T(8,128)(2,1)} %shard_map.90), calls=%async_computation.1 | async-start | bytes 786432 | tf_op jit(solution)/shard_map/all_to_all | solution.py:178
  123.3 4.6 %collective-permute-start.13 = (bf16[176,1024]{1,0:T(8,128)(2,1)S(1)}, bf16[176,1024]{1,0:T(8,128)(2,1)S(1)}, u32[]{:S(2)}, u32[]{:S(2)}) collective-permute-start(bf16[176,1024]{1,0:T(8,128)(2,1)S(1)} %slice.44), channel_id=1, source_target_pairs={{0,2},{1,3},{2,4},{3,5},{4,6},{5,7},{6,0},{7,1},{8,10},{9,11},{10,... | collective-permute-start | bytes 1081352 | tf_op jit(solution)/shard_map/ppermute | solution.py:172
  128.0 1.9 collective-permute-start.14
  129.9 5.5 %collective-permute-done.13.farg_ref = bf16[176,1024]{1,0:T(8,128)(2,1)S(1)} collective-permute-done((bf16[176,1024]{1,0:T(8,128)(2,1)S(1)}, bf16[176,1024]{1,0:T(8,128)(2,1)S(1)}, u32[]{:S(2)}, u32[]{:S(2)}) %collective-permute-start.13) | collective-permute-done | bytes 360480 | tf_op jit(solution)/shard_map/ppermute | solution.py:172
  135.4 5.4 %collective-permute-done.14.faru_ref = bf16[176,1024]{1,0:T(8,128)(2,1)S(1)} collective-permute-done((bf16[176,1024]{1,0:T(8,128)(2,1)S(1)}, bf16[176,1024]{1,0:T(8,128)(2,1)S(1)}, u32[]{:S(2)}, u32[]{:S(2)}) %collective-permute-start.14) | collective-permute-done | bytes 360480 | tf_op jit(solution)/shard_map/ppermute | solution.py:172
  140.8 0.7 copy-done.13
  141.5 3.7 %shard_map.91 = bf16[192,1024]{1,0:T(8,128)(2,1)} custom-call(bf16[4,192,176]{2,1,0:T(8,128)(2,1)} %get-tuple-element.27.gate_ref, bf16[4,192,176]{2,1,0:T(8,128)(2,1)} %get-tuple-element.28.up_ref, bf16[352,1024]{1,0:T(8,128)(2,1)} %copy-done.1, bf16[352,1024]{1,0:T(8,128)(2,1)} %copy-done.5, bf16[352,1024]{1,0:T(8,128)(2,1)} %copy-done.6, ...), custom_call_target="tpu_custom_call" | custom-call | flops 553648128 | bytes 3817472 | tf_op jit(solution)/shard_map/pallas_call | solution.py:18
  145.2 1.9 collective-permute-start.15
  147.1 1.9 collective-permute-done.15.rest_0_
  149.0 0.8 copy-done.16
  149.8 3.9 %shard_map.92 = bf16[64,24,128]{2,1,0:T(8,128)(2,1)} custom-call(bf16[4,192,176]{2,1,0:T(8,128)(2,1)} %get-tuple-element.22.gate_ref, bf16[4,192,176]{2,1,0:T(8,128)(2,1)} %get-tuple-element.23.up_ref, bf16[352,1024]{1,0:T(8,128)(2,1)} %copy-done.1, bf16[352,1024]{1,0:T(8,128)(2,1)} %copy-done.5, bf16[352,1024]{1,0:T(8,128)(2,1)} %copy-done.6, ...), custom_call_target="tpu_custom_call" | custom-call | flops 553648128 | bytes 4210688 | tf_op jit(solution)/shard_map/pallas_call | solution.py:18
  153.7 14.8 %all-to-all-start.2 = ((bf16[64,24,128]{2,1,0:T(8,128)(2,1)}), bf16[64,24,128]{2,1,0:T(8,128)(2,1)S(1)}, u32[]{:S(2)}, u32[]{:S(2)}) async-start(bf16[64,24,128]{2,1,0:T(8,128)(2,1)} %shard_map.92), calls=%async_computation.2 | async-start | bytes 786432 | tf_op jit(solution)/shard_map/all_to_all | solution.py:178
  168.6 1.5 shard_map.83.hot_ref
  170.0 26.0 %all-to-all-done.2.refs_1_ = bf16[64,24,128]{2,1,0:T(8,128)(2,1)S(1)} async-done(((bf16[64,24,128]{2,1,0:T(8,128)(2,1)}), bf16[64,24,128]{2,1,0:T(8,128)(2,1)S(1)}, u32[]{:S(2)}, u32[]{:S(2)}) %all-to-all-start.2) | async-done | bytes 393248 | tf_op jit(solution)/shard_map/all_to_all | solution.py:178
  196.1 0.8 copy-done.8
  196.9 2.2 %shard_map.93 = bf16[32,2048]{1,0:T(8,128)(2,1)} custom-call(bf16[32,192]{1,0:T(8,128)(2,1)} %shard_map.83.hot_ref, bf16[64,24,128]{2,1,0:T(8,128)(2,1)} %copy-done.7, bf16[64,24,128]{2,1,0:T(8,128)(2,1)} %copy-done.8), custom_call_target="tpu_custom_call" | custom-call | bytes 929792 | tf_op jit(solution)/shard_map/pallas_call | solution.py:18
  (50 shorter events, 1.6 us)
Async XLA Ops:
  2.5 25.0 %copy-start.14 = (bf16[1,176,2048]{2,1,0:T(8,128)(2,1)S(1)}, bf16[1,176,2048]{2,1,0:T(8,128)(2,1)}, u32[]{:S(2)}) copy-start(bf16[1,176,2048]{2,1,0:T(8,128)(2,1)} %param.12) | copy-start | bytes 2162692
  2.5 63.0 %all-to-all-start = ((bf16[64,48,128]{2,1,0:T(8,128)(2,1)}), bf16[64,48,128]{2,1,0:T(8,128)(2,1)}, u32[]{:S(2)}, u32[]{:S(2)}) async-start(bf16[64,48,128]{2,1,0:T(8,128)(2,1)} %get-tuple-element.18), calls=%async_computation | async-start | bytes 1572864 | tf_op jit(solution)/shard_map/all_to_all | solution.py:178
  21.6 22.2 %collective-permute-start = (bf16[176,2048]{1,0:T(8,128)(2,1)}, bf16[176,2048]{1,0:T(8,128)(2,1)S(1)}, u32[]{:S(2)}, u32[]{:S(2)}) collective-permute-start(bf16[176,2048]{1,0:T(8,128)(2,1)} %bitcast.2.own_ref), channel_id=1, source_target_pairs={{0,2},{1,3},{2,4},{3,5},{4,6},{5,7},{6,0},{7,1},{8,10},{9,11},{10,... | collective-permute-start | bytes 2162696 | tf_op jit(solution)/shard_map/ppermute | solution.py:172
  24.0 44.2 %collective-permute-start.1 = (bf16[176,2048]{1,0:T(8,128)(2,1)}, bf16[176,2048]{1,0:T(8,128)(2,1)S(1)}, u32[]{:S(2)}, u32[]{:S(2)}) collective-permute-start(bf16[176,2048]{1,0:T(8,128)(2,1)} %bitcast.2.own_ref), channel_id=1, source_target_pairs={{0,6},{1,7},{2,0},{3,1},{4,2},{5,3},{6,4},{7,5},{8,14},{9,15},{10,... | collective-permute-start | bytes 2162696 | tf_op jit(solution)/shard_map/ppermute | solution.py:172
  29.6 12.3 %copy-start = (bf16[352,1024]{1,0:T(8,128)(2,1)}, bf16[352,1024]{1,0:T(8,128)(2,1)S(1)}, u32[]{:S(2)}) copy-start(bf16[352,1024]{1,0:T(8,128)(2,1)S(1)} %pad_maximum_fusion.own_ref) | copy-start | bytes 2162692
  29.6 41.8 %collective-permute-start.4 = (bf16[352,1024]{1,0:T(8,128)(2,1)S(1)}, bf16[352,1024]{1,0:T(8,128)(2,1)S(1)}, u32[]{:S(2)}, u32[]{:S(2)}) collective-permute-start(bf16[352,1024]{1,0:T(8,128)(2,1)S(1)} %pad_maximum_fusion.own_ref), channel_id=1, source_target_pairs={{0,2},{1,3},{2,4},{3,5},{4,6},{5,7},{6,0},{7,1},{8,10},{9,11},{10,... | collective-permute-start | bytes 2162696 | tf_op jit(solution)/shard_map/ppermute | solution.py:172
  33.2 42.5 %collective-permute-start.5 = (bf16[352,1024]{1,0:T(8,128)(2,1)S(1)}, bf16[352,1024]{1,0:T(8,128)(2,1)}, u32[]{:S(2)}, u32[]{:S(2)}) collective-permute-start(bf16[352,1024]{1,0:T(8,128)(2,1)S(1)} %pad_maximum_fusion.own_ref), channel_id=1, source_target_pairs={{0,6},{1,7},{2,0},{3,1},{4,2},{5,3},{6,4},{7,5},{8,14},{9,15},{10,... | collective-permute-start | bytes 2162696 | tf_op jit(solution)/shard_map/ppermute | solution.py:172
  41.9 38.4 %collective-permute-start.9 = (bf16[2,4,192,176]{2,3,1,0:T(8,128)(2,1)}, bf16[2,4,192,176]{2,3,1,0:T(8,128)(2,1)}, u32[]{:S(2)}, u32[]{:S(2)}) collective-permute-start(bf16[2,4,192,176]{2,3,1,0:T(8,128)(2,1)} %copy.9), channel_id=1, source_target_pairs={{0,1},{1,0},{2,3},{3,2},{4,5},{5,4},{6,7},{7,6},{8,9},{9,8},{10,11... | collective-permute-start | bytes 1622024 | tf_op jit(solution)/shard_map/ppermute | solution.py:175
  43.8 31.8 %copy-start.2 = (bf16[176,2048]{1,0:T(8,128)(2,1)}, bf16[176,2048]{1,0:T(8,128)(2,1)S(1)}, u32[]{:S(2)}) copy-start(bf16[176,2048]{1,0:T(8,128)(2,1)S(1)} %collective-permute-done.left_ref) | copy-start | bytes 2162692
  65.6 21.9 %collective-permute-start.8 = (bf16[64,48,128]{2,1,0:T(8,128)(2,1)}, bf16[64,48,128]{2,1,0:T(8,128)(2,1)}, u32[]{:S(2)}, u32[]{:S(2)}) collective-permute-start(bf16[64,48,128]{2,1,0:T(8,128)(2,1)} %all-to-all-done.packed_ref), channel_id=1, source_target_pairs={{0,1},{1,0},{2,3},{3,2},{4,5},{5,4},{6,7},{7,6},{8,9},{9,8},{10,11... | collective-permute-start | bytes 2359304 | tf_op jit(solution)/shard_map/ppermute | solution.py:175
  68.3 12.0 %copy-start.3 = (bf16[176,2048]{1,0:T(8,128)(2,1)}, bf16[176,2048]{1,0:T(8,128)(2,1)S(1)}, u32[]{:S(2)}) copy-start(bf16[176,2048]{1,0:T(8,128)(2,1)S(1)} %collective-permute-done.1.right_ref) | copy-start | bytes 2162692
  68.3 19.2 %collective-permute-start.2 = (bf16[176,1024]{1,0:T(8,128)(2,1)}, bf16[176,1024]{1,0:T(8,128)(2,1)}, u32[]{:S(2)}, u32[]{:S(2)}) collective-permute-start(bf16[176,1024]{1,0:T(8,128)(2,1)} %slice.40), channel_id=1, source_target_pairs={{0,2},{1,3},{2,4},{3,5},{4,6},{5,7},{6,0},{7,1},{8,10},{9,11},{10,... | collective-permute-start | bytes 1081352 | tf_op jit(solution)/shard_map/ppermute | solution.py:172
  71.4 13.4 %copy-start.4 = (bf16[352,1024]{1,0:T(8,128)(2,1)}, bf16[352,1024]{1,0:T(8,128)(2,1)S(1)}, u32[]{:S(2)}) copy-start(bf16[352,1024]{1,0:T(8,128)(2,1)S(1)} %collective-permute-done.4.left_ref) | copy-start | bytes 2162692
  71.4 16.0 %collective-permute-start.3 = (bf16[176,1024]{1,0:T(8,128)(2,1)}, bf16[176,1024]{1,0:T(8,128)(2,1)}, u32[]{:S(2)}, u32[]{:S(2)}) collective-permute-start(bf16[176,1024]{1,0:T(8,128)(2,1)} %slice.41), channel_id=1, source_target_pairs={{0,6},{1,7},{2,0},{3,1},{4,2},{5,3},{6,4},{7,5},{8,14},{9,15},{10,... | collective-permute-start | bytes 1081352 | tf_op jit(solution)/shard_map/ppermute | solution.py:172
  75.7 16.2 %collective-permute-start.6 = (bf16[176,1024]{1,0:T(8,128)(2,1)}, bf16[176,1024]{1,0:T(8,128)(2,1)S(1)}, u32[]{:S(2)}, u32[]{:S(2)}) collective-permute-start(bf16[176,1024]{1,0:T(8,128)(2,1)} %slice.42), channel_id=1, source_target_pairs={{0,2},{1,3},{2,4},{3,5},{4,6},{5,7},{6,0},{7,1},{8,10},{9,11},{10,... | collective-permute-start | bytes 1081352 | tf_op jit(solution)/shard_map/ppermute | solution.py:172
  80.3 13.1 %collective-permute-start.7 = (bf16[176,1024]{1,0:T(8,128)(2,1)S(1)}, bf16[176,1024]{1,0:T(8,128)(2,1)S(1)}, u32[]{:S(2)}, u32[]{:S(2)}) collective-permute-start(bf16[176,1024]{1,0:T(8,128)(2,1)S(1)} %slice.43), channel_id=1, source_target_pairs={{0,6},{1,7},{2,0},{3,1},{4,2},{5,3},{6,4},{7,5},{8,14},{9,15},{10,... | collective-permute-start | bytes 1081352 | tf_op jit(solution)/shard_map/ppermute | solution.py:172
  91.8 1.5 copy-start.10
  93.4 0.7 copy-start.11
  94.1 5.7 %copy-start.9 = (bf16[176,1024]{1,0:T(8,128)(2,1)S(1)}, bf16[176,1024]{1,0:T(8,128)(2,1)}, u32[]{:S(2)}) copy-start(bf16[176,1024]{1,0:T(8,128)(2,1)} %get-tuple-element.34) | copy-start | bytes 1081348
  97.9 14.9 %collective-permute-start.10 = (bf16[192,1024]{1,0:T(8,128)(2,1)}, bf16[192,1024]{1,0:T(8,128)(2,1)S(1)}, u32[]{:S(2)}, u32[]{:S(2)}) collective-permute-start(bf16[192,1024]{1,0:T(8,128)(2,1)} %shard_map.89), channel_id=1, source_target_pairs={{0,1},{1,0},{2,3},{3,2},{4,5},{5,4},{6,7},{7,6},{8,9},{9,8},{10,11... | collective-permute-start | bytes 1179656 | tf_op jit(solution)/shard_map/ppermute | solution.py:175
  99.8 12.9 %copy-start.1 = (bf16[352,1024]{1,0:T(8,128)(2,1)}, bf16[352,1024]{1,0:T(8,128)(2,1)S(1)}, u32[]{:S(2)}) copy-start(bf16[352,1024]{1,0:T(8,128)(2,1)S(1)} %pad_maximum_fusion.1.own_ref) | copy-start | bytes 2162692
  99.9 23.4 %collective-permute-start.11 = (bf16[352,1024]{1,0:T(8,128)(2,1)S(1)}, bf16[352,1024]{1,0:T(8,128)(2,1)S(1)}, u32[]{:S(2)}, u32[]{:S(2)}) collective-permute-start(bf16[352,1024]{1,0:T(8,128)(2,1)S(1)} %pad_maximum_fusion.1.own_ref), channel_id=1, source_target_pairs={{0,2},{1,3},{2,4},{3,5},{4,6},{5,7},{6,0},{7,1},{8,10},{9,11},{10,... | collective-permute-start | bytes 2162696 | tf_op jit(solution)/shard_map/ppermute | solution.py:172
  103.3 24.6 %collective-permute-start.12 = (bf16[352,1024]{1,0:T(8,128)(2,1)S(1)}, bf16[352,1024]{1,0:T(8,128)(2,1)S(1)}, u32[]{:S(2)}, u32[]{:S(2)}) collective-permute-start(bf16[352,1024]{1,0:T(8,128)(2,1)S(1)} %pad_maximum_fusion.1.own_ref), channel_id=1, source_target_pairs={{0,6},{1,7},{2,0},{3,1},{4,2},{5,3},{6,4},{7,5},{8,14},{9,15},{10,... | collective-permute-start | bytes 2162696 | tf_op jit(solution)/shard_map/ppermute | solution.py:172
  112.7 0.8 copy-start.15
  117.4 36.4 %all-to-all-start.1 = ((bf16[64,24,128]{2,1,0:T(8,128)(2,1)}), bf16[64,24,128]{2,1,0:T(8,128)(2,1)S(1)}, u32[]{:S(2)}, u32[]{:S(2)}) async-start(bf16[64,24,128]{2,1,0:T(8,128)(2,1)} %shard_map.90), calls=%async_computation.1 | async-start | bytes 786432 | tf_op jit(solution)/shard_map/all_to_all | solution.py:178
  123.2 17.5 %copy-start.5 = (bf16[352,1024]{1,0:T(8,128)(2,1)}, bf16[352,1024]{1,0:T(8,128)(2,1)S(1)}, u32[]{:S(2)}) copy-start(bf16[352,1024]{1,0:T(8,128)(2,1)S(1)} %collective-permute-done.11.left_ref) | copy-start | bytes 2162692
  123.3 12.1 %collective-permute-start.13 = (bf16[176,1024]{1,0:T(8,128)(2,1)S(1)}, bf16[176,1024]{1,0:T(8,128)(2,1)S(1)}, u32[]{:S(2)}, u32[]{:S(2)}) collective-permute-start(bf16[176,1024]{1,0:T(8,128)(2,1)S(1)} %slice.44), channel_id=1, source_target_pairs={{0,2},{1,3},{2,4},{3,5},{4,6},{5,7},{6,0},{7,1},{8,10},{9,11},{10,... | collective-permute-start | bytes 1081352 | tf_op jit(solution)/shard_map/ppermute | solution.py:172
  127.9 12.8 %copy-start.6 = (bf16[352,1024]{1,0:T(8,128)(2,1)}, bf16[352,1024]{1,0:T(8,128)(2,1)S(1)}, u32[]{:S(2)}) copy-start(bf16[352,1024]{1,0:T(8,128)(2,1)S(1)} %collective-permute-done.12.right_ref) | copy-start | bytes 2162692
  128.0 12.8 %collective-permute-start.14 = (bf16[176,1024]{1,0:T(8,128)(2,1)S(1)}, bf16[176,1024]{1,0:T(8,128)(2,1)S(1)}, u32[]{:S(2)}, u32[]{:S(2)}) collective-permute-start(bf16[176,1024]{1,0:T(8,128)(2,1)S(1)} %slice.45), channel_id=1, source_target_pairs={{0,6},{1,7},{2,0},{3,1},{4,2},{5,3},{6,4},{7,5},{8,14},{9,15},{10,... | collective-permute-start | bytes 1081352 | tf_op jit(solution)/shard_map/ppermute | solution.py:172
  135.4 5.4 %copy-start.12 = (bf16[176,1024]{1,0:T(8,128)(2,1)}, bf16[176,1024]{1,0:T(8,128)(2,1)S(1)}, u32[]{:S(2)}) copy-start(bf16[176,1024]{1,0:T(8,128)(2,1)S(1)} %collective-permute-done.13.farg_ref) | copy-start | bytes 1081348
  140.8 0.7 copy-start.13
  145.2 3.8 %collective-permute-start.15 = (bf16[192,1024]{1,0:T(8,128)(2,1)}, bf16[192,1024]{1,0:T(8,128)(2,1)S(1)}, u32[]{:S(2)}, u32[]{:S(2)}) collective-permute-start(bf16[192,1024]{1,0:T(8,128)(2,1)} %shard_map.91), channel_id=1, source_target_pairs={{0,1},{1,0},{2,3},{3,2},{4,5},{5,4},{6,7},{7,6},{8,9},{9,8},{10,11... | collective-permute-start | bytes 1179656 | tf_op jit(solution)/shard_map/ppermute | solution.py:175
  149.0 0.8 copy-start.16
  153.7 42.3 %copy-start.7 = (bf16[64,24,128]{2,1,0:T(8,128)(2,1)}, bf16[64,24,128]{2,1,0:T(8,128)(2,1)S(1)}, u32[]{:S(2)}) copy-start(bf16[64,24,128]{2,1,0:T(8,128)(2,1)S(1)} %all-to-all-done.1.refs_0_) | copy-start | bytes 1179652
  153.7 42.3 %all-to-all-start.2 = ((bf16[64,24,128]{2,1,0:T(8,128)(2,1)}), bf16[64,24,128]{2,1,0:T(8,128)(2,1)S(1)}, u32[]{:S(2)}, u32[]{:S(2)}) async-start(bf16[64,24,128]{2,1,0:T(8,128)(2,1)} %shard_map.92), calls=%async_computation.2 | async-start | bytes 786432 | tf_op jit(solution)/shard_map/all_to_all | solution.py:178
  196.1 0.8 copy-start.8
where the time goes:
time: 200 us; the launch traced here: 199 us
  starting transfers between devices  83.1 us (42%)
  waiting for transfers between devices  62.1 us (31%)
  Pallas kernels  38.8 us (19%)
  local copies, waits for them, and re-layouts  13.9 us (7%)
    all_to_all x3, waiting for transfers between devices, exchange(): return lax.all_to_all(a, 'expert', split_axis=0, concat_axis=0, tiled=True)  47.8 us
    all_to_all x3, starting transfers between devices, exchange(): return lax.all_to_all(a, 'expert', split_axis=0, concat_axis=0, tiled=True)  39.7 us
    pallas_call x12, Pallas kernels, call(): pl.pallas_call(kernel, out_shape=outs[0] if single else tuple(outs), in_s...  38.8 us
    ppermute x12, starting transfers between devices, along(): return lax.ppermute(a, 'replica', pairs)  35.7 us
    ppermute x12, waiting for transfers between devices, along(): return lax.ppermute(a, 'replica', pairs)  12.4 us
    ppermute x4, starting transfers between devices, across(): return lax.ppermute(a, 'replica', [(i, i ^ 1) for i in range(copies)])  7.64 us
  transfers between devices with their start and end apart: 19, of which 6 were waited for; matrix products, arithmetic and copies ran while one was open for 5% of the time, Pallas kernels for 15%

commit v1 on v0

v1 whole, which is shorter than its diff:
```python
import jax
import jax.numpy as jnp
from jax import lax
from jax.experimental import pallas as pl
from jax.experimental.pallas import tpu as pltpu
from jax.sharding import PartitionSpec as P

F32 = jnp.float32
BF16 = jnp.bfloat16
VM = pl.BlockSpec(memory_space=pltpu.VMEM)
SM = pl.BlockSpec(memory_space=pltpu.SMEM)
LINKS = 4


def call(kernel, ins, outs, flops=0, smem=0, scratch=(), spec=VM):
    moved = sum(a.size * a.dtype.itemsize for a in ins) + sum(o.size * o.dtype.itemsize for o in outs)
    single = len(outs) == 1
    return pl.pallas_call(
        kernel,
        out_shape=outs[0] if single else tuple(outs),
        in_specs=[SM] * smem + [spec] * (len(ins) - smem),
        out_specs=VM if single else tuple([VM] * len(outs)),
        scratch_shapes=list(scratch),
        cost_estimate=pl.CostEstimate(flops=flops, bytes_accessed=moved, transcendentals=0),
    )(*ins)


def fetch(copies, sems):
    made = [pltpu.make_async_copy(src, dst, sems.at[n]) for n, (src, dst) in enumerate(copies)]
    for copy in made:
        copy.start()
    return made


def pack(value, out_ref, part=0, parts=1):
    experts, deep, lanes = out_ref.shape
    slots = value.shape[0] // experts
    chunks = deep // slots
    span = chunks // parts
    for s in range(slots):
        block = value[s * experts : (s + 1) * experts].astype(BF16)
        stack = jnp.stack([block[:, c * lanes : (c + 1) * lanes] for c in range(span)])
        low = s * chunks + part * span
        out_ref[:, low : low + span, :] = jnp.swapaxes(stack, 0, 1)


def unpack(packed_ref, s, slots):
    _, deep, _ = packed_ref.shape
    chunks = deep // slots
    parts = jnp.swapaxes(packed_ref[:, s * chunks : (s + 1) * chunks, :], 0, 1)
    return jnp.concatenate([parts[c] for c in range(chunks)], axis=1)


def place_kernel(routes_ref, gates_ref, grad_ref, out_ref, hot_ref):
    top, tokens = routes_ref.shape
    experts, _, _ = out_ref.shape
    rows = hot_ref.shape[0]
    row = lax.broadcasted_iota(jnp.int32, (rows, tokens), 0)
    number = row // experts
    named = row - number * experts
    slot = number.astype(F32)
    hits = jnp.zeros((rows, tokens), F32)
    gate = jnp.zeros((rows, tokens), F32)
    for k in range(top):
        hit = routes_ref[k : k + 1, :] == named
        hits = jnp.where(hit, 1.0, hits)
        gate = jnp.where(hit, gates_ref[k : k + 1, :], gate)
    before = (
        lax.broadcasted_iota(jnp.int32, (tokens, tokens), 0)
        < lax.broadcasted_iota(jnp.int32, (tokens, tokens), 1)
    ).astype(BF16)
    earlier = jnp.dot(hits.astype(BF16), before, preferred_element_type=F32)
    chosen = (hits > 0.5) & (jnp.abs(earlier - slot) < 0.5)
    weight = jnp.sum(jnp.where(chosen, gate, 0.0), axis=1, keepdims=True)
    hot = jnp.where(chosen, 1.0, 0.0).astype(BF16)
    hot_ref[...] = hot
    pack(weight * jnp.dot(hot, grad_ref[...], preferred_element_type=F32), out_ref)


def factor_kernel(core_ref, gate_ref, up_ref, gf_ref, uf_ref):
    slice_width = gf_ref.shape[1] // LINKS
    first = core_ref[0] == 0
    for q in range(LINKS):
        low = 2 * q * slice_width
        mid, high = low + slice_width, low + 2 * slice_width
        g = jnp.where(first, gate_ref[:, low:mid].astype(F32), gate_ref[:, mid:high].astype(F32))
        u = jnp.where(first, up_ref[:, low:mid].astype(F32), up_ref[:, mid:high].astype(F32))
        sig = jax.nn.sigmoid(g)
        place = slice(q * slice_width, (q + 1) * slice_width)
        uf_ref[:, place] = g * sig
        gf_ref[:, place] = u * sig * (1.0 + g * (1.0 - sig))


def spots(link_ref, width):
    link = link_ref[0]
    steps = (0, LINKS - 1, 1, 2)
    return [pl.ds(pl.multiple_of(((link + by) & (LINKS - 1)) * width, 16), width) for by in steps]


def hidden_kernel(
    link_ref, packed_in, own_in, left_in, right_in, far1_in, far2_in, gf_in, uf_in,
    gate_ref, up_ref, packed_ref, down_ref, gf_ref, uf_ref, rows_ref, sems,
):
    width = own_in.shape[0]
    half = far1_in.shape[1]
    own, left, right, far = spots(link_ref, width)
    copies = fetch(
        [
            (packed_in, packed_ref),
            (own_in, down_ref.at[own, :]),
            (left_in, down_ref.at[left, :]),
            (right_in, down_ref.at[right, :]),
            (far1_in, down_ref.at[far, pl.ds(0, half)]),
            (far2_in, down_ref.at[far, pl.ds(half, half)]),
            (gf_in, gf_ref),
            (uf_in, uf_ref),
        ],
        sems,
    )
    copies[0].wait()
    experts = packed_ref.shape[0]
    slots = rows_ref.shape[0] // experts
    for s in range(slots):
        rows_ref[s * experts : (s + 1) * experts, :] = unpack(packed_ref, s, slots)
    for copy in copies[1:]:
        copy.wait()
    grad = lax.dot_general(
        rows_ref[...], down_ref[...], (((1,), (1,)), ((), ())), preferred_element_type=F32
    )
    gate_ref[...] = (grad * gf_ref[...]).astype(BF16)
    up_ref[...] = (grad * uf_ref[...]).astype(BF16)


def output_kernel(link_ref, gate_in, up_in, own_in, left_in, right_in, farg_in, faru_in, *rest):
    back_in = rest[0] if len(rest) == 7 else None
    out_ref, gate_ref, up_ref, weight_ref, back_ref, sems = rest[-6:]
    width = farg_in.shape[0]
    hidden = gate_in.shape[1]
    full = weight_ref.shape[1]
    span = full // 2
    own, left, right, far = spots(link_ref, width)
    small = [(gate_in, gate_ref), (up_in, up_ref)]
    if back_in is not None:
        small.append((back_in, back_ref))
    begun = fetch(small, sems.at[0])
    halves = []
    for n in range(2):
        columns = pl.ds(n * span, span)
        copies = []
        for piece, place in ((own_in, own), (left_in, left), (right_in, right)):
            copies.append((piece.at[pl.ds(0, width), columns], weight_ref.at[place, columns]))
            lower = pl.ds(pl.multiple_of(place.start + hidden, 16), width)
            copies.append((piece.at[pl.ds(width, width), columns], weight_ref.at[lower, columns]))
        copies.append((farg_in.at[:, columns], weight_ref.at[far, columns]))
        lower = pl.ds(pl.multiple_of(far.start + hidden, 16), width)
        copies.append((faru_in.at[:, columns], weight_ref.at[lower, columns]))
        halves.append(fetch(copies, sems.at[n + 1]))
    for copy in begun:
        copy.wait()
    for n in range(2):
        for copy in halves[n]:
            copy.wait()
        columns = slice(n * span, (n + 1) * span)
        total = jnp.dot(gate_ref[...], weight_ref[:hidden, columns], preferred_element_type=F32)
        total += jnp.dot(up_ref[...], weight_ref[hidden:, columns], preferred_element_type=F32)
        if back_in is None:
            out_ref[:, columns] = total.astype(out_ref.dtype)
        else:
            pack(total + back_ref[:, columns].astype(F32), out_ref, n, 2)


def turn_kernel(hot_ref, out_ref):
    out_ref[...] = hot_ref[...].T


def combine_kernel(hot_ref, back_ref, out_ref):
    tokens, width = out_ref.shape
    experts = back_ref.shape[0]
    slots = hot_ref.shape[1] // experts
    total = jnp.zeros((tokens, width), F32)
    for s in range(slots):
        total += jnp.dot(
            hot_ref[:, s * experts : (s + 1) * experts], unpack(back_ref, s, slots), preferred_element_type=F32
        )
    out_ref[...] = total.astype(BF16)


def body(grad_out, routes, gates, w_gate, w_up, w_down, saved_gate, saved_up):
    experts = lax.axis_size("expert")
    copies = lax.axis_size("replica")
    tokens, width = grad_out.shape
    slots = saved_gate.shape[3]
    slice_width = w_gate.shape[1]
    rows = experts * slots
    half = width // 2
    chunks = half // 128
    deep = slots * chunks
    replica = lax.axis_index("replica")

    def along(a, by):
        pairs = [(2 * i + k, 2 * ((i + by) % LINKS) + k) for i in range(LINKS) for k in range(2)]
        return lax.ppermute(a, "replica", pairs)

    def across(a):
        return lax.ppermute(a, "replica", [(i, i ^ 1) for i in range(copies)])

    def exchange(a):
        return lax.all_to_all(a, "expert", split_axis=0, concat_axis=0, tiled=True)

    down = w_down[0]
    down_left, down_right = along(down, 1), along(down, -1)

    packed, hot = call(
        place_kernel,
        (routes.T, gates.T, grad_out),
        (
            jax.ShapeDtypeStruct((experts, 2 * deep, 128), BF16),
            jax.ShapeDtypeStruct((rows, tokens), BF16),
        ),
        2 * rows * tokens * width,
    )
    arrived = exchange(packed)

    pair = jnp.concatenate([w_gate[0], w_up[0]], axis=0)
    pair_left, pair_right = along(pair, 1), along(pair, -1)
    down_far1 = along(down_left[:, :half], 1)
    down_far2 = along(down_right[:, half:], -1)
    for_right, for_left = pair_left[:slice_width], pair_right[slice_width:]
    pair_farg, pair_faru = along(for_right, 1), along(for_left, -1)

    link_at = (replica >> 1).reshape(1)
    core_at = (replica & 1).reshape(1)
    saved = tuple(a[0, 0].transpose(1, 0, 2).reshape(rows, -1) for a in (saved_gate, saved_up))
    hidden_units = LINKS * slice_width
    factor = jax.ShapeDtypeStruct((rows, hidden_units), F32)
    own_factors = call(factor_kernel, (core_at,) + saved, (factor, factor), smem=1)
    sent = (across(saved[0]), across(saved[1]))
    other_factors = call(factor_kernel, (core_at,) + sent, (factor, factor), smem=1)

    downs = (down, down_left, down_right, down_far1, down_far2)
    hidden = jax.ShapeDtypeStruct((rows, hidden_units), BF16)
    cost = 2 * rows * hidden_units * width
    scratch = (
        pltpu.VMEM((experts, 2 * deep, 128), BF16),
        pltpu.VMEM((hidden_units, width), BF16),
        pltpu.VMEM((rows, hidden_units), F32),
        pltpu.VMEM((rows, hidden_units), F32),
        pltpu.VMEM((rows, width), BF16),
        pltpu.SemaphoreType.DMA((8,)),
    )
    other_rows = across(arrived)

    def hide(packed_rows, factors):
        ins = (link_at, packed_rows) + downs + tuple(factors)
        return call(hidden_kernel, ins, (hidden, hidden), cost, 1, scratch, pl.BlockSpec(memory_space=pl.ANY))

    own_hidden = hide(arrived, own_factors)
    other_hidden = hide(other_rows, other_factors)

    pieces = (pair, pair_left, pair_right, pair_farg, pair_faru)
    scratch2 = (
        pltpu.VMEM((rows, hidden_units), BF16),
        pltpu.VMEM((rows, hidden_units), BF16),
        pltpu.VMEM((2 * hidden_units, width), BF16),
        pltpu.VMEM((rows, width), BF16),
        pltpu.SemaphoreType.DMA((3, 8)),
    )

    def give(grads, extra, out):
        ins = (link_at,) + tuple(grads) + pieces + extra
        return call(output_kernel, ins, (out,), 2 * cost, 1, scratch2, pl.BlockSpec(memory_space=pl.ANY))

    theirs = give(other_hidden, (), jax.ShapeDtypeStruct((rows, width), BF16))
    back = across(theirs)
    outgoing = give(own_hidden, (back,), jax.ShapeDtypeStruct((experts, 2 * deep, 128), BF16))
    returned = exchange(outgoing)
    turned = call(turn_kernel, (hot,), (jax.ShapeDtypeStruct((tokens, rows), BF16),))
    return call(combine_kernel, (turned, returned), (jax.ShapeDtypeStruct((tokens, width), BF16),))


def solution(mesh):
    in_specs = (
        P(("expert", "replica"), None),
        P(("expert", "replica"), None),
        P(("expert", "replica"), None),
        P("expert", "replica", None),
        P("expert", "replica", None),
        P("expert", "replica", None),
        P("expert", "replica", None, None, None),
        P("expert", "replica", None, None, None),
    )
    out_specs = P(("expert", "replica"), None)

    return jax.shard_map(body, mesh=mesh, in_specs=in_specs, out_specs=out_specs, check_vma=False)
```

time: 200 us -> 195 us (0.975)
  the two profiles are of different devices: /device:TPU:6 before, /device:TPU:8 now
where the time goes in v1:
time: 195 us; the launch traced here: 194 us
  waiting for transfers between devices  84.3 us (43%)
  starting transfers between devices  69.9 us (36%)
  Pallas kernels  30.6 us (16%)
  local copies, waits for them, and re-layouts  8.8 us (5%)
    all_to_all x2, waiting for transfers between devices, exchange(): return lax.all_to_all(a, 'expert', split_axis=0, concat_axis=0, tiled=True)  44.5 us
    ppermute x8, waiting for transfers between devices, along(): return lax.ppermute(a, 'replica', pairs)  39.8 us
    all_to_all x2, starting transfers between devices, exchange(): return lax.all_to_all(a, 'expert', split_axis=0, concat_axis=0, tiled=True)  34 us
    pallas_call x9, Pallas kernels, call(): pl.pallas_call(kernel, out_shape=outs[0] if single else tuple(outs), in_s...  30.6 us
    ppermute x8, starting transfers between devices, along(): return lax.ppermute(a, 'replica', pairs)  28.2 us
    ppermute x4, starting transfers between devices, across(): return lax.ppermute(a, 'replica', [(i, i ^ 1) for i in range(copies)])  7.66 us
  transfers between devices with their start and end apart: 14, of which 7 were waited for; matrix products, arithmetic and copies ran while one was open for 3% of the time, Pallas kernels for 8%

profile of v1, /device:TPU:8, one launch (start us, length us, event | category | flops | bytes accessed | tf_op | source)
XLA Modules:
  0.0 193.9 jit_solution(4696626604924349941)
XLA Ops:
  0.0 2.6 %shard_map.82 = (bf16[64,48,128]{2,1,0:T(8,128)(2,1)}, bf16[192,32]{1,0:T(8,128)(2,1)}) custom-call(s32[6,32]{1,0:T(8,128)} %bitcast.21, f32[6,32]{1,0:T(8,128)} %bitcast.22, bf16[32,2048]{1,0:T(8,128)(2,1)} %grad_ref.1), custom_call_target="tpu_custom_call" | custom-call | flops 25165824 | bytes 931328 | tf_op jit(solution)/shard_map/pallas_call | solution.py:18
  2.7 18.9 %all-to-all-start = ((bf16[64,48,128]{2,1,0:T(8,128)(2,1)}), bf16[64,48,128]{2,1,0:T(8,128)(2,1)}, u32[]{:S(2)}, u32[]{:S(2)}) async-start(bf16[64,48,128]{2,1,0:T(8,128)(2,1)} %get-tuple-element.16), calls=%async_computation | async-start | bytes 1572864 | tf_op jit(solution)/shard_map/all_to_all | solution.py:208
  21.6 0.0 copy-start.10
  21.6 0.2 pad_maximum_fusion.own_in
  21.8 4.7 %collective-permute-start.5 = (bf16[352,2048]{1,0:T(8,128)(2,1)S(1)}, bf16[352,2048]{1,0:T(8,128)(2,1)S(1)}, u32[]{:S(2)}, u32[]{:S(2)}) collective-permute-start(bf16[352,2048]{1,0:T(8,128)(2,1)S(1)} %pad_maximum_fusion.own_in), channel_id=1, source_target_pairs={{0,6},{1,7},{2,0},{3,1},{4,2},{5,3},{6,4},{7,5},{8,14},{9,15},{10,... | collective-permute-start | bytes 4325384 | tf_op jit(solution)/shard_map/ppermute | solution.py:202
  26.4 1.9 collective-permute-start.4
  28.4 5.1 %collective-permute-start.1 = (bf16[176,2048]{1,0:T(8,128)(2,1)}, bf16[176,2048]{1,0:T(8,128)(2,1)}, u32[]{:S(2)}, u32[]{:S(2)}) collective-permute-start(bf16[176,2048]{1,0:T(8,128)(2,1)} %bitcast.3.own_in), channel_id=1, source_target_pairs={{0,6},{1,7},{2,0},{3,1},{4,2},{5,3},{6,4},{7,5},{8,14},{9,15},{10,... | collective-permute-start | bytes 2162696 | tf_op jit(solution)/shard_map/ppermute | solution.py:202
  33.5 1.9 collective-permute-start
  35.4 1.9 collective-permute-start.9
  37.4 21.0 %collective-permute-done.5.right_in = bf16[352,2048]{1,0:T(8,128)(2,1)S(1)} collective-permute-done((bf16[352,2048]{1,0:T(8,128)(2,1)S(1)}, bf16[352,2048]{1,0:T(8,128)(2,1)S(1)}, u32[]{:S(2)}, u32[]{:S(2)}) %collective-permute-start.5) | collective-permute-done | bytes 1441824 | tf_op jit(solution)/shard_map/ppermute | solution.py:202
  58.4 1.9 collective-permute-start.10
  60.3 3.8 %collective-permute-done.4.left_in = bf16[352,2048]{1,0:T(8,128)(2,1)} collective-permute-done((bf16[352,2048]{1,0:T(8,128)(2,1)S(1)}, bf16[352,2048]{1,0:T(8,128)(2,1)}, u32[]{:S(2)}, u32[]{:S(2)}) %collective-permute-start.4) | collective-permute-done | bytes 1441824 | tf_op jit(solution)/shard_map/ppermute | solution.py:202
  64.1 1.3 all-to-all-done.packed_in
  65.4 1.9 collective-permute-start.8
  67.3 1.0 slice.19
  68.3 2.1 %slice.18 = bf16[176,2048]{1,0:T(8,128)(2,1)} slice(bf16[352,2048]{1,0:T(8,128)(2,1)} %collective-permute-done.4.left_in), slice={[0:176], [0:2048]} | slice | bytes 1441792 | tf_op jit(solution)/shard_map/slice | solution.py:228
  70.4 1.8 collective-permute-done.1.right_in
  72.2 5.6 %collective-permute-start.7 = (bf16[176,2048]{1,0:T(8,128)(2,1)}, bf16[176,2048]{1,0:T(8,128)(2,1)S(1)}, u32[]{:S(2)}, u32[]{:S(2)}) collective-permute-start(bf16[176,2048]{1,0:T(8,128)(2,1)} %slice.19), channel_id=1, source_target_pairs={{0,6},{1,7},{2,0},{3,1},{4,2},{5,3},{6,4},{7,5},{8,14},{9,15},{10,... | collective-permute-start | bytes 2162696 | tf_op jit(solution)/shard_map/ppermute | solution.py:202
  77.8 0.0 collective-permute-done.left_in
  77.9 1.9 collective-permute-start.6
  79.8 1.0 slice.17
  80.8 1.0 slice.16
  81.8 0.0 collective-permute-done.9.gate_ref
  81.8 5.1 %collective-permute-start.3 = (bf16[176,1024]{1,0:T(8,128)(2,1)S(1)}, bf16[176,1024]{1,0:T(8,128)(2,1)S(1)}, u32[]{:S(2)}, u32[]{:S(2)}) collective-permute-start(bf16[176,1024]{1,0:T(8,128)(2,1)S(1)} %slice.17), channel_id=1, source_target_pairs={{0,6},{1,7},{2,0},{3,1},{4,2},{5,3},{6,4},{7,5},{8,14},{9,15},{10,... | collective-permute-start | bytes 1081352 | tf_op jit(solution)/shard_map/ppermute | solution.py:202
  87.0 0.0 collective-permute-done.10.up_ref
  87.0 1.9 collective-permute-start.2
  88.9 3.0 %shard_map.86 = (f32[192,704]{1,0:T(8,128)}, f32[192,704]{1,0:T(8,128)}) custom-call(s32[1]{0:T(128)} %bitcast.4.core_ref, bf16[192,1408]{1,0:T(8,128)(2,1)} %collective-permute-done.9.gate_ref, bf16[192,1408]{1,0:T(8,128)(2,1)} %collective-permute-done.10.up_ref), custom_call_target="tpu_custom_call" | custom-call | bytes 2162692 | tf_op jit(solution)/shard_map/pallas_call | solution.py:18
  91.9 7.8 %collective-permute-done.3.far2_in = bf16[176,1024]{1,0:T(8,128)(2,1)S(1)} collective-permute-done((bf16[176,1024]{1,0:T(8,128)(2,1)S(1)}, bf16[176,1024]{1,0:T(8,128)(2,1)S(1)}, u32[]{:S(2)}, u32[]{:S(2)}) %collective-permute-start.3) | collective-permute-done | bytes 360480 | tf_op jit(solution)/shard_map/ppermute | solution.py:202
  99.7 5.3 %collective-permute-done.2.far1_in = bf16[176,1024]{1,0:T(8,128)(2,1)S(1)} collective-permute-done((bf16[176,1024]{1,0:T(8,128)(2,1)S(1)}, bf16[176,1024]{1,0:T(8,128)(2,1)S(1)}, u32[]{:S(2)}, u32[]{:S(2)}) %collective-permute-start.2) | collective-permute-done | bytes 360480 | tf_op jit(solution)/shard_map/ppermute | solution.py:202
  105.1 0.0 collective-permute-done.8.packed_in
  105.1 0.7 copy-done.6
  105.8 4.2 %shard_map.87 = (bf16[192,704]{1,0:T(8,128)(2,1)}, bf16[192,704]{1,0:T(8,128)(2,1)}) custom-call(s32[1]{0:T(128)} %bitcast.2.link_ref, bf16[64,48,128]{2,1,0:T(8,128)(2,1)} %collective-permute-done.8.packed_in, bf16[176,2048]{1,0:T(8,128)(2,1)} %bitcast.3.own_in, bf16[176,2048]{1,0:T(8,128)(2,1)} %collective-permute-done.left_in, ...), custom_call_target="tpu_custom_call" | custom-call | flops 553648128 | bytes 5292036 | tf_op jit(solution)/shard_map/pallas_call | solution.py:18
  110.1 0.0 collective-permute-done.7.faru_in
  110.1 0.0 collective-permute-done.6.farg_in
  110.1 0.9 copy-done.3
  111.0 0.3 copy-done.4
  111.3 4.7 %shard_map.88 = bf16[192,2048]{1,0:T(8,128)(2,1)} custom-call(s32[1]{0:T(128)} %bitcast.2.link_ref, bf16[192,704]{1,0:T(8,128)(2,1)} %get-tuple-element.23.gate_in, bf16[192,704]{1,0:T(8,128)(2,1)} %get-tuple-element.24.up_in, bf16[352,2048]{1,0:T(8,128)(2,1)} %copy-done, bf16[352,2048]{1,0:T(8,128)(2,1)} %collective-permute-done.4.left_in, ...), custom_call_target="tpu_custom_call" | custom-call | flops 1107296256 | bytes 7094276 | tf_op jit(solution)/shard_map/pallas_call | solution.py:18
  116.0 1.9 collective-permute-start.11
  117.9 3.0 %shard_map.84 = (f32[192,704]{1,0:T(8,128)}, f32[192,704]{1,0:T(8,128)}) custom-call(s32[1]{0:T(128)} %bitcast.4.core_ref, bf16[192,1408]{1,0:T(8,128)(2,1)} %bitcast.19, bf16[192,1408]{1,0:T(8,128)(2,1)} %bitcast.10.up_ref), custom_call_target="tpu_custom_call" | custom-call | bytes 2162692 | tf_op jit(solution)/shard_map/pallas_call | solution.py:18
  120.9 4.2 %shard_map.85 = (bf16[192,704]{1,0:T(8,128)(2,1)}, bf16[192,704]{1,0:T(8,128)(2,1)}) custom-call(s32[1]{0:T(128)} %bitcast.2.link_ref, bf16[64,48,128]{2,1,0:T(8,128)(2,1)} %all-to-all-done.packed_in, bf16[176,2048]{1,0:T(8,128)(2,1)} %bitcast.3.own_in, bf16[176,2048]{1,0:T(8,128)(2,1)} %collective-permute-done.left_in, ...), custom_call_target="tpu_custom_call" | custom-call | flops 553648128 | bytes 5292036 | tf_op jit(solution)/shard_map/pallas_call | solution.py:18
  125.2 0.0 collective-permute-done.11.rest_0_
  125.2 0.9 copy-done.7
  126.1 5.0 %shard_map.89 = bf16[64,48,128]{2,1,0:T(8,128)(2,1)} custom-call(s32[1]{0:T(128)} %bitcast.2.link_ref, bf16[192,704]{1,0:T(8,128)(2,1)} %get-tuple-element.19.gate_in, bf16[192,704]{1,0:T(8,128)(2,1)} %get-tuple-element.20.up_in, bf16[352,2048]{1,0:T(8,128)(2,1)} %copy-done, bf16[352,2048]{1,0:T(8,128)(2,1)} %collective-permute-done.4.left_in, ...), custom_call_target="tpu_custom_call" | custom-call | flops 1107296256 | bytes 7880708 | tf_op jit(solution)/shard_map/pallas_call | solution.py:18
  131.1 15.1 %all-to-all-start.1 = ((bf16[64,48,128]{2,1,0:T(8,128)(2,1)}), bf16[64,48,128]{2,1,0:T(8,128)(2,1)S(1)}, u32[]{:S(2)}, u32[]{:S(2)}) async-start(bf16[64,48,128]{2,1,0:T(8,128)(2,1)} %shard_map.89), calls=%async_computation.1 | async-start | bytes 1572864 | tf_op jit(solution)/shard_map/all_to_all | solution.py:208
  146.2 1.5 shard_map.83.hot_ref
  147.7 43.1 %all-to-all-done.1.back_ref = bf16[64,48,128]{2,1,0:T(8,128)(2,1)S(1)} async-done(((bf16[64,48,128]{2,1,0:T(8,128)(2,1)}), bf16[64,48,128]{2,1,0:T(8,128)(2,1)S(1)}, u32[]{:S(2)}, u32[]{:S(2)}) %all-to-all-start.1) | async-done | bytes 786464 | tf_op jit(solution)/shard_map/all_to_all | solution.py:208
  190.8 0.9 copy-done.2
  191.7 2.2 %shard_map.90 = bf16[32,2048]{1,0:T(8,128)(2,1)} custom-call(bf16[32,192]{1,0:T(8,128)(2,1)} %shard_map.83.hot_ref, bf16[64,48,128]{2,1,0:T(8,128)(2,1)} %copy-done.2), custom_call_target="tpu_custom_call" | custom-call | bytes 929792 | tf_op jit(solution)/shard_map/pallas_call | solution.py:18
  (16 shorter events, 0.0 us)
Async XLA Ops:
  0.0 21.6 %copy-start.8 = (bf16[1,176,2048]{2,1,0:T(8,128)(2,1)S(1)}, bf16[1,176,2048]{2,1,0:T(8,128)(2,1)}, u32[]{:S(2)}) copy-start(bf16[1,176,2048]{2,1,0:T(8,128)(2,1)} %param.12) | copy-start | bytes 2162692
  0.0 21.6 %copy-start.9 = (bf16[1,176,2048]{2,1,0:T(8,128)(2,1)S(1)}, bf16[1,176,2048]{2,1,0:T(8,128)(2,1)}, u32[]{:S(2)}) copy-start(bf16[1,176,2048]{2,1,0:T(8,128)(2,1)} %param.11) | copy-start | bytes 2162692
  2.7 62.8 %all-to-all-start = ((bf16[64,48,128]{2,1,0:T(8,128)(2,1)}), bf16[64,48,128]{2,1,0:T(8,128)(2,1)}, u32[]{:S(2)}, u32[]{:S(2)}) async-start(bf16[64,48,128]{2,1,0:T(8,128)(2,1)} %get-tuple-element.16), calls=%async_computation | async-start | bytes 1572864 | tf_op jit(solution)/shard_map/all_to_all | solution.py:208
  21.6 13.9 %copy-start.10 = (bf16[1,1,64,3,1408]{4,2,3,1,0:T(8,128)(2,1)S(1)}, bf16[1,1,64,3,1408]{4,2,3,1,0:T(8,128)(2,1)}, u32[]{:S(2)}) copy-start(bf16[1,1,64,3,1408]{4,2,3,1,0:T(8,128)(2,1)} %param.14) | copy-start | bytes 1622020
  21.7 48.7 %copy-start = (bf16[352,2048]{1,0:T(8,128)(2,1)}, bf16[352,2048]{1,0:T(8,128)(2,1)S(1)}, u32[]{:S(2)}) copy-start(bf16[352,2048]{1,0:T(8,128)(2,1)S(1)} %pad_maximum_fusion.own_in) | copy-start | bytes 4325380
  21.8 36.6 %collective-permute-start.5 = (bf16[352,2048]{1,0:T(8,128)(2,1)S(1)}, bf16[352,2048]{1,0:T(8,128)(2,1)S(1)}, u32[]{:S(2)}, u32[]{:S(2)}) collective-permute-start(bf16[352,2048]{1,0:T(8,128)(2,1)S(1)} %pad_maximum_fusion.own_in), channel_id=1, source_target_pairs={{0,6},{1,7},{2,0},{3,1},{4,2},{5,3},{6,4},{7,5},{8,14},{9,15},{10,... | collective-permute-start | bytes 4325384 | tf_op jit(solution)/shard_map/ppermute | solution.py:202
  26.4 37.7 %collective-permute-start.4 = (bf16[352,2048]{1,0:T(8,128)(2,1)S(1)}, bf16[352,2048]{1,0:T(8,128)(2,1)}, u32[]{:S(2)}, u32[]{:S(2)}) collective-permute-start(bf16[352,2048]{1,0:T(8,128)(2,1)S(1)} %pad_maximum_fusion.own_in), channel_id=1, source_target_pairs={{0,2},{1,3},{2,4},{3,5},{4,6},{5,7},{6,0},{7,1},{8,10},{9,11},{10,... | collective-permute-start | bytes 4325384 | tf_op jit(solution)/shard_map/ppermute | solution.py:202
  28.4 43.9 %collective-permute-start.1 = (bf16[176,2048]{1,0:T(8,128)(2,1)}, bf16[176,2048]{1,0:T(8,128)(2,1)}, u32[]{:S(2)}, u32[]{:S(2)}) collective-permute-start(bf16[176,2048]{1,0:T(8,128)(2,1)} %bitcast.3.own_in), channel_id=1, source_target_pairs={{0,6},{1,7},{2,0},{3,1},{4,2},{5,3},{6,4},{7,5},{8,14},{9,15},{10,... | collective-permute-start | bytes 2162696 | tf_op jit(solution)/shard_map/ppermute | solution.py:202
  33.5 44.3 %collective-permute-start = (bf16[176,2048]{1,0:T(8,128)(2,1)}, bf16[176,2048]{1,0:T(8,128)(2,1)}, u32[]{:S(2)}, u32[]{:S(2)}) collective-permute-start(bf16[176,2048]{1,0:T(8,128)(2,1)} %bitcast.3.own_in), channel_id=1, source_target_pairs={{0,2},{1,3},{2,4},{3,5},{4,6},{5,7},{6,0},{7,1},{8,10},{9,11},{10,... | collective-permute-start | bytes 2162696 | tf_op jit(solution)/shard_map/ppermute | solution.py:202
  35.4 46.4 %collective-permute-start.9 = (bf16[192,1408]{1,0:T(8,128)(2,1)S(1)}, bf16[192,1408]{1,0:T(8,128)(2,1)}, u32[]{:S(2)}, u32[]{:S(2)}) collective-permute-start(bf16[192,1408]{1,0:T(8,128)(2,1)S(1)} %bitcast.20), channel_id=1, source_target_pairs={{0,1},{1,0},{2,3},{3,2},{4,5},{5,4},{6,7},{7,6},{8,9},{9,8},{10,11... | collective-permute-start | bytes 1622024 | tf_op jit(solution)/shard_map/ppermute | solution.py:205
  58.4 12.0 %copy-start.1 = (bf16[352,2048]{1,0:T(8,128)(2,1)}, bf16[352,2048]{1,0:T(8,128)(2,1)S(1)}, u32[]{:S(2)}) copy-start(bf16[352,2048]{1,0:T(8,128)(2,1)S(1)} %collective-permute-done.5.right_in) | copy-start | bytes 4325380
  58.4 28.6 %collective-permute-start.10 = (bf16[192,1408]{1,0:T(8,128)(2,1)}, bf16[192,1408]{1,0:T(8,128)(2,1)}, u32[]{:S(2)}, u32[]{:S(2)}) collective-permute-start(bf16[192,1408]{1,0:T(8,128)(2,1)} %bitcast.10.up_ref), channel_id=1, source_target_pairs={{0,1},{1,0},{2,3},{3,2},{4,5},{5,4},{6,7},{7,6},{8,9},{9,8},{10,11... | collective-permute-start | bytes 1622024 | tf_op jit(solution)/shard_map/ppermute | solution.py:205
  65.4 39.6 %collective-permute-start.8 = (bf16[64,48,128]{2,1,0:T(8,128)(2,1)}, bf16[64,48,128]{2,1,0:T(8,128)(2,1)}, u32[]{:S(2)}, u32[]{:S(2)}) collective-permute-start(bf16[64,48,128]{2,1,0:T(8,128)(2,1)} %all-to-all-done.packed_in), channel_id=1, source_target_pairs={{0,1},{1,0},{2,3},{3,2},{4,5},{5,4},{6,7},{7,6},{8,9},{9,8},{10,11... | collective-permute-start | bytes 2359304 | tf_op jit(solution)/shard_map/ppermute | solution.py:205
  72.2 37.8 %collective-permute-start.7 = (bf16[176,2048]{1,0:T(8,128)(2,1)}, bf16[176,2048]{1,0:T(8,128)(2,1)S(1)}, u32[]{:S(2)}, u32[]{:S(2)}) collective-permute-start(bf16[176,2048]{1,0:T(8,128)(2,1)} %slice.19), channel_id=1, source_target_pairs={{0,6},{1,7},{2,0},{3,1},{4,2},{5,3},{6,4},{7,5},{8,14},{9,15},{10,... | collective-permute-start | bytes 2162696 | tf_op jit(solution)/shard_map/ppermute | solution.py:202
  77.9 32.3 %collective-permute-start.6 = (bf16[176,2048]{1,0:T(8,128)(2,1)}, bf16[176,2048]{1,0:T(8,128)(2,1)S(1)}, u32[]{:S(2)}, u32[]{:S(2)}) collective-permute-start(bf16[176,2048]{1,0:T(8,128)(2,1)} %slice.18), channel_id=1, source_target_pairs={{0,2},{1,3},{2,4},{3,5},{4,6},{5,7},{6,0},{7,1},{8,10},{9,11},{10,... | collective-permute-start | bytes 2162696 | tf_op jit(solution)/shard_map/ppermute | solution.py:202
  81.8 17.9 %collective-permute-start.3 = (bf16[176,1024]{1,0:T(8,128)(2,1)S(1)}, bf16[176,1024]{1,0:T(8,128)(2,1)S(1)}, u32[]{:S(2)}, u32[]{:S(2)}) collective-permute-start(bf16[176,1024]{1,0:T(8,128)(2,1)S(1)} %slice.17), channel_id=1, source_target_pairs={{0,6},{1,7},{2,0},{3,1},{4,2},{5,3},{6,4},{7,5},{8,14},{9,15},{10,... | collective-permute-start | bytes 1081352 | tf_op jit(solution)/shard_map/ppermute | solution.py:202
  87.0 18.1 %collective-permute-start.2 = (bf16[176,1024]{1,0:T(8,128)(2,1)S(1)}, bf16[176,1024]{1,0:T(8,128)(2,1)S(1)}, u32[]{:S(2)}, u32[]{:S(2)}) collective-permute-start(bf16[176,1024]{1,0:T(8,128)(2,1)S(1)} %slice.16), channel_id=1, source_target_pairs={{0,2},{1,3},{2,4},{3,5},{4,6},{5,7},{6,0},{7,1},{8,10},{9,11},{10,... | collective-permute-start | bytes 1081352 | tf_op jit(solution)/shard_map/ppermute | solution.py:202
  99.7 5.3 %copy-start.5 = (bf16[176,1024]{1,0:T(8,128)(2,1)}, bf16[176,1024]{1,0:T(8,128)(2,1)S(1)}, u32[]{:S(2)}) copy-start(bf16[176,1024]{1,0:T(8,128)(2,1)S(1)} %collective-permute-done.3.far2_in) | copy-start | bytes 1081348
  105.1 0.8 copy-start.6
  110.1 0.9 copy-start.3
  110.1 1.2 copy-start.4
  116.0 9.2 %collective-permute-start.11 = (bf16[192,2048]{1,0:T(8,128)(2,1)}, bf16[192,2048]{1,0:T(8,128)(2,1)S(1)}, u32[]{:S(2)}, u32[]{:S(2)}) collective-permute-start(bf16[192,2048]{1,0:T(8,128)(2,1)} %shard_map.88), channel_id=1, source_target_pairs={{0,1},{1,0},{2,3},{3,2},{4,5},{5,4},{6,7},{7,6},{8,9},{9,8},{10,11... | collective-permute-start | bytes 2359304 | tf_op jit(solution)/shard_map/ppermute | solution.py:205
  125.2 0.9 copy-start.7
  131.1 59.7 %all-to-all-start.1 = ((bf16[64,48,128]{2,1,0:T(8,128)(2,1)}), bf16[64,48,128]{2,1,0:T(8,128)(2,1)S(1)}, u32[]{:S(2)}, u32[]{:S(2)}) async-start(bf16[64,48,128]{2,1,0:T(8,128)(2,1)} %shard_map.89), calls=%async_computation.1 | async-start | bytes 1572864 | tf_op jit(solution)/shard_map/all_to_all | solution.py:208
  190.8 0.9 copy-start.2

commit v2 on v1

--- a/solution.py
+++ b/solution.py
@@ -12,7 +12,7 @@
 LINKS = 4
 
 
-def call(kernel, ins, outs, flops=0, smem=0, scratch=(), spec=VM):
+def call(kernel, ins, outs, flops=0, smem=0, scratch=(), spec=VM, limit=24 << 20):
     moved = sum(a.size * a.dtype.itemsize for a in ins) + sum(o.size * o.dtype.itemsize for o in outs)
     single = len(outs) == 1
     return pl.pallas_call(
@@ -21,6 +21,7 @@
         in_specs=[SM] * smem + [spec] * (len(ins) - smem),
         out_specs=VM if single else tuple([VM] * len(outs)),
         scratch_shapes=list(scratch),
+        compiler_params=pltpu.CompilerParams(vmem_limit_bytes=limit),
         cost_estimate=pl.CostEstimate(flops=flops, bytes_accessed=moved, transcendentals=0),
     )(*ins)
 
@@ -98,25 +99,14 @@
 
 
 def hidden_kernel(
-    link_ref, packed_in, own_in, left_in, right_in, far1_in, far2_in, gf_in, uf_in,
+    link_ref, packed_in, own_in, left_in, right_in, far_in, gf_in, uf_in,
     gate_ref, up_ref, packed_ref, down_ref, gf_ref, uf_ref, rows_ref, sems,
 ):
     width = own_in.shape[0]
-    half = far1_in.shape[1]
-    own, left, right, far = spots(link_ref, width)
-    copies = fetch(
-        [
-            (packed_in, packed_ref),
-            (own_in, down_ref.at[own, :]),
-            (left_in, down_ref.at[left, :]),
-            (right_in, down_ref.at[right, :]),
-            (far1_in, down_ref.at[far, pl.ds(0, half)]),
-            (far2_in, down_ref.at[far, pl.ds(half, half)]),
-            (gf_in, gf_ref),
-            (uf_in, uf_ref),
-        ],
-        sems,
-    )
+    copies = [(packed_in, packed_ref)]
+    for piece, place in zip((own_in, left_in, right_in, far_in), spots(link_ref, width)):
+        copies.append((piece, down_ref.at[place, :]))
+    copies = fetch(copies + [(gf_in, gf_ref), (uf_in, uf_ref)], sems)
     copies[0].wait()
     experts = packed_ref.shape[0]
     slots = rows_ref.shape[0] // experts
@@ -131,20 +121,26 @@
     up_ref[...] = (grad * uf_ref[...]).astype(BF16)
 
 
-def output_kernel(link_ref, gate_in, up_in, own_in, left_in, right_in, farg_in, faru_in, *rest):
-    back_in = rest[0] if len(rest) == 7 else None
-    out_ref, gate_ref, up_ref, weight_ref, back_ref, sems = rest[-6:]
+def output_kernel(
+    link_ref, own_gate_in, own_up_in, other_gate_in, other_up_in, own_in, left_in, right_in, farg_in, faru_in,
+    own_ref, theirs_ref, gate_ref, up_ref, weight_ref, sems,
+):
     width = farg_in.shape[0]
-    hidden = gate_in.shape[1]
-    full = weight_ref.shape[1]
-    span = full // 2
+    rows, hidden = own_gate_in.shape
+    parts = sems.shape[0] - 1
+    span = weight_ref.shape[1] // parts
     own, left, right, far = spots(link_ref, width)
-    small = [(gate_in, gate_ref), (up_in, up_ref)]
-    if back_in is not None:
-        small.append((back_in, back_ref))
-    begun = fetch(small, sems.at[0])
-    halves = []
-    for n in range(2):
+    begun = fetch(
+        [
+            (own_gate_in, gate_ref.at[pl.ds(0, rows), :]),
+            (own_up_in, up_ref.at[pl.ds(0, rows), :]),
+            (other_gate_in, gate_ref.at[pl.ds(rows, rows), :]),
+            (other_up_in, up_ref.at[pl.ds(rows, rows), :]),
+        ],
+        sems.at[0],
+    )
+    blocks = []
+    for n in range(parts):
         columns = pl.ds(n * span, span)
         copies = []
         for piece, place in ((own_in, own), (left_in, left), (right_in, right)):
@@ -154,19 +150,21 @@
         copies.append((farg_in.at[:, columns], weight_ref.at[far, columns]))
         lower = pl.ds(pl.multiple_of(far.start + hidden, 16), width)
         copies.append((faru_in.at[:, columns], weight_ref.at[lower, columns]))
-        halves.append(fetch(copies, sems.at[n + 1]))
+        blocks.append(fetch(copies, sems.at[n + 1]))
     for copy in begun:
         copy.wait()
-    for n in range(2):
-        for copy in halves[n]:
+    for n in range(parts):
+        for copy in blocks[n]:
             copy.wait()
         columns = slice(n * span, (n + 1) * span)
         total = jnp.dot(gate_ref[...], weight_ref[:hidden, columns], preferred_element_type=F32)
         total += jnp.dot(up_ref[...], weight_ref[hidden:, columns], preferred_element_type=F32)
-        if back_in is None:
-            out_ref[:, columns] = total.astype(out_ref.dtype)
-        else:
-            pack(total + back_ref[:, columns].astype(F32), out_ref, n, 2)
+        own_ref[:, columns] = total[:rows].astype(BF16)
+        theirs_ref[:, columns] = total[rows:].astype(BF16)
+
+
+def join_kernel(own_ref, back_ref, out_ref):
+    pack(own_ref[...].astype(F32) + back_ref[...].astype(F32), out_ref)
 
 
 def turn_kernel(hot_ref, out_ref):
@@ -223,8 +221,7 @@
 
     pair = jnp.concatenate([w_gate[0], w_up[0]], axis=0)
     pair_left, pair_right = along(pair, 1), along(pair, -1)
-    down_far1 = along(down_left[:, :half], 1)
-    down_far2 = along(down_right[:, half:], -1)
+    down_far = along(down_left, 1)
     for_right, for_left = pair_left[:slice_width], pair_right[slice_width:]
     pair_farg, pair_faru = along(for_right, 1), along(for_left, -1)
 
@@ -237,7 +234,7 @@
     sent = (across(saved[0]), across(saved[1]))
     other_factors = call(factor_kernel, (core_at,) + sent, (factor, factor), smem=1)
 
-    downs = (down, down_left, down_right, down_far1, down_far2)
+    downs = (down, down_left, down_right, down_far)
     hidden = jax.ShapeDtypeStruct((rows, hidden_units), BF16)
     cost = 2 * rows * hidden_units * width
     scratch = (
@@ -259,20 +256,23 @@
 
     pieces = (pair, pair_left, pair_right, pair_farg, pair_faru)
     scratch2 = (
-        pltpu.VMEM((rows, hidden_units), BF16),
-        pltpu.VMEM((rows, hidden_units), BF16),
+        pltpu.VMEM((2 * rows, hidden_units), BF16),
+        pltpu.VMEM((2 * rows, hidden_units), BF16),
         pltpu.VMEM((2 * hidden_units, width), BF16),
-        pltpu.VMEM((rows, width), BF16),
-        pltpu.SemaphoreType.DMA((3, 8)),
-    )
-
-    def give(grads, extra, out):
-        ins = (link_at,) + tuple(grads) + pieces + extra
-        return call(output_kernel, ins, (out,), 2 * cost, 1, scratch2, pl.BlockSpec(memory_space=pl.ANY))
-
-    theirs = give(other_hidden, (), jax.ShapeDtypeStruct((rows, width), BF16))
+        pltpu.SemaphoreType.DMA((5, 8)),
+    )
+    part = jax.ShapeDtypeStruct((rows, width), BF16)
+    ours, theirs = call(
+        output_kernel,
+        (link_at,) + tuple(own_hidden) + tuple(other_hidden) + pieces,
+        (part, part),
+        4 * cost,
+        1,
+        scratch2,
+        pl.BlockSpec(memory_space=pl.ANY),
+    )
     back = across(theirs)
-    outgoing = give(own_hidden, (back,), jax.ShapeDtypeStruct((experts, 2 * deep, 128), BF16))
+    outgoing = call(join_kernel, (ours, back), (jax.ShapeDtypeStruct((experts, 2 * deep, 128), BF16),))
     returned = exchange(outgoing)
     turned = call(turn_kernel, (hot,), (jax.ShapeDtypeStruct((tokens, rows), BF16),))
     return call(combine_kernel, (turned, returned), (jax.ShapeDtypeStruct((tokens, width), BF16),))

time: 195 us -> 193 us (0.990)
  waiting for transfers between devices: 84.3 us -> 102 us
  Pallas kernels: 30.6 us -> 19.4 us
  starting transfers between devices: 69.9 us -> 62.9 us
  local copies, waits for them, and re-layouts: 8.8 us -> 6.47 us
    ppermute x8 -> x7, waiting for transfers between devices: 39.8 us -> 55.3 us  [along(): return lax.ppermute(a, 'replica', pairs)]
    pallas_call x9, Pallas kernels: 30.6 us -> 19.4 us  [call(): pl.pallas_call(kernel, out_shape=outs[0] if single else tuple(outs), in_s...]
    ppermute x8 -> x7, starting transfers between devices: 28.2 us -> 20.9 us  [along(): return lax.ppermute(a, 'replica', pairs)]
    ppermute x4, waiting for transfers between devices: 0.01 us -> 2.26 us  [across(): return lax.ppermute(a, 'replica', [(i, i ^ 1) for i in range(copies)])]
    slice x2 -> x0, local copies, waits for them, and re-layouts: 2.02 us -> none  [the longest x1 1.01 us: body(): down_far1 = along(down_left[:, :half], 1)]
  transfers between devices with their start and end apart: 14 -> 13, of which waited for: 7 -> 7; matrix products, arithmetic and copies ran while one was open for 3% -> 3% of each run, Pallas kernels for 8% -> 5%
where the time goes in v2:
time: 193 us; the launch traced here: 192 us
  waiting for transfers between devices  102 us (53%)
  starting transfers between devices  62.9 us (33%)
  Pallas kernels  19.4 us (10%)
  local copies, waits for them, and re-layouts  6.47 us (3%)
    ppermute x7, waiting for transfers between devices, along(): return lax.ppermute(a, 'replica', pairs)  55.3 us
    all_to_all x2, waiting for transfers between devices, exchange(): return lax.all_to_all(a, 'expert', split_axis=0, concat_axis=0, tiled=True)  44.2 us
    all_to_all x2, starting transfers between devices, exchange(): return lax.all_to_all(a, 'expert', split_axis=0, concat_axis=0, tiled=True)  33.8 us
    ppermute x7, starting transfers between devices, along(): return lax.ppermute(a, 'replica', pairs)  20.9 us
    pallas_call x9, Pallas kernels, call(): pl.pallas_call(kernel, out_shape=outs[0] if single else tuple(outs), in_s...  19.4 us
    ppermute x4, starting transfers between devices, across(): return lax.ppermute(a, 'replica', [(i, i ^ 1) for i in range(copies)])  8.16 us
    slice x2, local copies, waits for them, and re-layouts, body(): for_right, for_left = (pair_left[:slice_width], pair_right[slice_width:])  4.17 us
  transfers between devices with their start and end apart: 13, of which 7 were waited for; matrix products, arithmetic and copies ran while one was open for 3% of the time, Pallas kernels for 5%

profile of v2, /device:TPU:8, one launch (start us, length us, event | category | flops | bytes accessed | tf_op | source)
XLA Modules:
  0.0 191.9 jit_solution(15450292209008312319)
XLA Ops:
  0.0 0.0 copy-start.2
  0.0 0.9 copy-done.2
  0.9 0.7 copy-done.3
  1.6 0.7 copy-done.4
  2.3 1.6 shard_map.82
  3.9 18.7 %all-to-all-start = ((bf16[64,48,128]{2,1,0:T(8,128)(2,1)}), bf16[64,48,128]{2,1,0:T(8,128)(2,1)S(1)}, u32[]{:S(2)}, u32[]{:S(2)}) async-start(bf16[64,48,128]{2,1,0:T(8,128)(2,1)} %get-tuple-element.18), calls=%async_computation | async-start | bytes 1572864 | tf_op jit(solution)/shard_map/all_to_all | solution.py:206
  22.6 0.0 copy-done.5
  22.6 0.0 copy-done.6
  22.6 0.0 copy-start
  22.7 0.0 copy-start.1
  22.7 1.2 pad_maximum_fusion.own_in
  23.9 4.7 %collective-permute-start.7 = (bf16[352,2048]{1,0:T(8,128)(2,1)}, bf16[352,2048]{1,0:T(8,128)(2,1)}, u32[]{:S(2)}, u32[]{:S(2)}) collective-permute-start(bf16[352,2048]{1,0:T(8,128)(2,1)} %pad_maximum_fusion.own_in), channel_id=1, source_target_pairs={{0,6},{1,7},{2,0},{3,1},{4,2},{5,3},{6,4},{7,5},{8,14},{9,15},{10,... | collective-permute-start | bytes 4325384 | tf_op jit(solution)/shard_map/ppermute | solution.py:200
  28.6 1.9 %collective-permute-start.6 = (bf16[352,2048]{1,0:T(8,128)(2,1)}, bf16[352,2048]{1,0:T(8,128)(2,1)}, u32[]{:S(2)}, u32[]{:S(2)}) collective-permute-start(bf16[352,2048]{1,0:T(8,128)(2,1)} %pad_maximum_fusion.own_in), channel_id=1, source_target_pairs={{0,2},{1,3},{2,4},{3,5},{4,6},{5,7},{6,0},{7,1},{8,10},{9,11},{10,... | collective-permute-start | bytes 4325384 | tf_op jit(solution)/shard_map/ppermute | solution.py:200
  30.5 0.0 copy-done
  30.5 2.7 %collective-permute-start = (bf16[176,2048]{1,0:T(8,128)(2,1)S(1)}, bf16[176,2048]{1,0:T(8,128)(2,1)S(1)}, u32[]{:S(2)}, u32[]{:S(2)}) collective-permute-start(bf16[176,2048]{1,0:T(8,128)(2,1)S(1)} %bitcast.17), channel_id=1, source_target_pairs={{0,2},{1,3},{2,4},{3,5},{4,6},{5,7},{6,0},{7,1},{8,10},{9,11},{10,... | collective-permute-start | bytes 2162696 | tf_op jit(solution)/shard_map/ppermute | solution.py:200
  33.2 0.0 copy-done.1
  33.2 1.9 %collective-permute-start.4 = (bf16[192,1408]{1,0:T(8,128)(2,1)S(1)}, bf16[192,1408]{1,0:T(8,128)(2,1)}, u32[]{:S(2)}, u32[]{:S(2)}) collective-permute-start(bf16[192,1408]{1,0:T(8,128)(2,1)S(1)} %bitcast.21), channel_id=1, source_target_pairs={{0,1},{1,0},{2,3},{3,2},{4,5},{5,4},{6,7},{7,6},{8,9},{9,8},{10,11... | collective-permute-start | bytes 1622024 | tf_op jit(solution)/shard_map/ppermute | solution.py:203
  35.1 2.4 %collective-permute-start.5 = (bf16[192,1408]{1,0:T(8,128)(2,1)}, bf16[192,1408]{1,0:T(8,128)(2,1)}, u32[]{:S(2)}, u32[]{:S(2)}) collective-permute-start(bf16[192,1408]{1,0:T(8,128)(2,1)} %bitcast.10.up_ref), channel_id=1, source_target_pairs={{0,1},{1,0},{2,3},{3,2},{4,5},{5,4},{6,7},{7,6},{8,9},{9,8},{10,11... | collective-permute-start | bytes 1622024 | tf_op jit(solution)/shard_map/ppermute | solution.py:203
  37.5 42.3 %collective-permute-done.left_in = bf16[176,2048]{1,0:T(8,128)(2,1)S(1)} collective-permute-done((bf16[176,2048]{1,0:T(8,128)(2,1)S(1)}, bf16[176,2048]{1,0:T(8,128)(2,1)S(1)}, u32[]{:S(2)}, u32[]{:S(2)}) %collective-permute-start) | collective-permute-done | bytes 720928 | tf_op jit(solution)/shard_map/ppermute | solution.py:200
  79.8 0.0 all-to-all-done.packed_in
  79.8 1.9 collective-permute-start.3
  81.7 0.0 collective-permute-done.7.right_in
  81.7 1.9 %collective-permute-start.1 = (bf16[176,2048]{1,0:T(8,128)(2,1)S(1)}, bf16[176,2048]{1,0:T(8,128)(2,1)S(1)}, u32[]{:S(2)}, u32[]{:S(2)}) collective-permute-start(bf16[176,2048]{1,0:T(8,128)(2,1)S(1)} %bitcast.18), channel_id=1, source_target_pairs={{0,6},{1,7},{2,0},{3,1},{4,2},{5,3},{6,4},{7,5},{8,14},{9,15},{10,... | collective-permute-start | bytes 2162696 | tf_op jit(solution)/shard_map/ppermute | solution.py:200
  83.7 0.0 collective-permute-done.6.left_in
  83.7 3.9 %collective-permute-start.2 = (bf16[176,2048]{1,0:T(8,128)(2,1)S(1)}, bf16[176,2048]{1,0:T(8,128)(2,1)}, u32[]{:S(2)}, u32[]{:S(2)}) collective-permute-start(bf16[176,2048]{1,0:T(8,128)(2,1)S(1)} %collective-permute-done.left_in), channel_id=1, source_target_pairs={{0,2},{1,3},{2,4},{3,5},{4,6},{5,7},{6,0},{7,1},{8,10},{9,11},{10,... | collective-permute-start | bytes 2162696 | tf_op jit(solution)/shard_map/ppermute | solution.py:200
  87.6 2.1 %slice.9 = bf16[176,2048]{1,0:T(8,128)(2,1)} slice(bf16[352,2048]{1,0:T(8,128)(2,1)} %collective-permute-done.7.right_in), slice={[176:352], [0:2048]} | slice | bytes 1441792 | tf_op jit(solution)/shard_map/slice | solution.py:225
  89.7 2.1 %slice.8 = bf16[176,2048]{1,0:T(8,128)(2,1)} slice(bf16[352,2048]{1,0:T(8,128)(2,1)} %collective-permute-done.6.left_in), slice={[0:176], [0:2048]} | slice | bytes 1441792 | tf_op jit(solution)/shard_map/slice | solution.py:225
  91.8 0.0 collective-permute-done.4.gate_ref
  91.8 3.1 %collective-permute-start.9 = (bf16[176,2048]{1,0:T(8,128)(2,1)}, bf16[176,2048]{1,0:T(8,128)(2,1)}, u32[]{:S(2)}, u32[]{:S(2)}) collective-permute-start(bf16[176,2048]{1,0:T(8,128)(2,1)} %slice.9), channel_id=1, source_target_pairs={{0,6},{1,7},{2,0},{3,1},{4,2},{5,3},{6,4},{7,5},{8,14},{9,15},{10,... | collective-permute-start | bytes 2162696 | tf_op jit(solution)/shard_map/ppermute | solution.py:200
  94.9 0.0 collective-permute-done.5.up_ref
  94.9 2.7 %collective-permute-start.8 = (bf16[176,2048]{1,0:T(8,128)(2,1)}, bf16[176,2048]{1,0:T(8,128)(2,1)}, u32[]{:S(2)}, u32[]{:S(2)}) collective-permute-start(bf16[176,2048]{1,0:T(8,128)(2,1)} %slice.8), channel_id=1, source_target_pairs={{0,2},{1,3},{2,4},{3,5},{4,6},{5,7},{6,0},{7,1},{8,10},{9,11},{10,... | collective-permute-start | bytes 2162696 | tf_op jit(solution)/shard_map/ppermute | solution.py:200
  97.7 1.9 shard_map.84
  99.6 2.1 %shard_map.86 = (f32[192,704]{1,0:T(8,128)S(1)}, f32[192,704]{1,0:T(8,128)S(1)}) custom-call(s32[1]{0:T(128)} %bitcast.4.core_ref, bf16[192,1408]{1,0:T(8,128)(2,1)} %collective-permute-done.4.gate_ref, bf16[192,1408]{1,0:T(8,128)(2,1)} %collective-permute-done.5.up_ref), custom_call_target="tpu_custom_call" | custom-call | bytes 2162692 | tf_op jit(solution)/shard_map/pallas_call | solution.py:18
  101.6 1.0 collective-permute-done.1.right_in
  102.7 3.3 %collective-permute-done.2.far_in = bf16[176,2048]{1,0:T(8,128)(2,1)} collective-permute-done((bf16[176,2048]{1,0:T(8,128)(2,1)S(1)}, bf16[176,2048]{1,0:T(8,128)(2,1)}, u32[]{:S(2)}, u32[]{:S(2)}) %collective-permute-start.2) | collective-permute-done | bytes 720928 | tf_op jit(solution)/shard_map/ppermute | solution.py:200
  105.9 3.1 %shard_map.85 = (bf16[192,704]{1,0:T(8,128)(2,1)S(1)}, bf16[192,704]{1,0:T(8,128)(2,1)S(1)}) custom-call(s32[1]{0:T(128)} %bitcast.2.link_ref, bf16[64,48,128]{2,1,0:T(8,128)(2,1)S(1)} %all-to-all-done.packed_in, bf16[176,2048]{1,0:T(8,128)(2,1)S(1)} %bitcast.19, bf16[176,2048]{1,0:T(8,128)(2,1)S(1)} %collective-permute-done.left_in, ...), custom_call_target="tpu_custom_call" | custom-call | flops 553648128 | bytes 5292036 | tf_op jit(solution)/shard_map/pallas_call | solution.py:18
  109.0 0.0 collective-permute-done.3.packed_in
  109.0 3.1 %shard_map.87 = (bf16[192,704]{1,0:T(8,128)(2,1)S(1)}, bf16[192,704]{1,0:T(8,128)(2,1)S(1)}) custom-call(s32[1]{0:T(128)} %bitcast.2.link_ref, bf16[64,48,128]{2,1,0:T(8,128)(2,1)} %collective-permute-done.3.packed_in, bf16[176,2048]{1,0:T(8,128)(2,1)S(1)} %bitcast.20, bf16[176,2048]{1,0:T(8,128)(2,1)S(1)} %collective-permute-done.left_in, ...), custom_call_target="tpu_custom_call" | custom-call | flops 553648128 | bytes 5292036 | tf_op jit(solution)/shard_map/pallas_call | solution.py:18
  112.2 5.5 %collective-permute-done.9.faru_in = bf16[176,2048]{1,0:T(8,128)(2,1)} collective-permute-done((bf16[176,2048]{1,0:T(8,128)(2,1)}, bf16[176,2048]{1,0:T(8,128)(2,1)}, u32[]{:S(2)}, u32[]{:S(2)}) %collective-permute-start.9) | collective-permute-done | bytes 720928 | tf_op jit(solution)/shard_map/ppermute | solution.py:200
  117.7 3.1 %collective-permute-done.8.farg_in = bf16[176,2048]{1,0:T(8,128)(2,1)} collective-permute-done((bf16[176,2048]{1,0:T(8,128)(2,1)}, bf16[176,2048]{1,0:T(8,128)(2,1)}, u32[]{:S(2)}, u32[]{:S(2)}) %collective-permute-start.8) | collective-permute-done | bytes 720928 | tf_op jit(solution)/shard_map/ppermute | solution.py:200
  120.9 5.1 %shard_map.88 = (bf16[192,2048]{1,0:T(8,128)(2,1)S(1)}, bf16[192,2048]{1,0:T(8,128)(2,1)S(1)}) custom-call(s32[1]{0:T(128)} %bitcast.2.link_ref, bf16[192,704]{1,0:T(8,128)(2,1)S(1)} %get-tuple-element.21.own_gate_in, bf16[192,704]{1,0:T(8,128)(2,1)S(1)} %get-tuple-element.22.own_up_in, bf16[192,704]{1,0:T(8,128)(2,1)S(1)} %get-tuple-element.25.other_gate_in, ...), custom_call_target="tpu_custom_call" | custom-call | flops 2214592512 | bytes 8421380 | tf_op jit(solution)/shard_map/pallas_call | solution.py:18
  126.0 1.9 %collective-permute-start.10 = (bf16[192,2048]{1,0:T(8,128)(2,1)S(1)}, bf16[192,2048]{1,0:T(8,128)(2,1)S(1)}, u32[]{:S(2)}, u32[]{:S(2)}) collective-permute-start(bf16[192,2048]{1,0:T(8,128)(2,1)S(1)} %get-tuple-element.28), channel_id=1, source_target_pairs={{0,1},{1,0},{2,3},{3,2},{4,5},{5,4},{6,7},{7,6},{8,9},{9,8},{10,11... | collective-permute-start | bytes 2359304 | tf_op jit(solution)/shard_map/ppermute | solution.py:203
  128.0 2.3 %collective-permute-done.10.back_ref = bf16[192,2048]{1,0:T(8,128)(2,1)S(1)} collective-permute-done((bf16[192,2048]{1,0:T(8,128)(2,1)S(1)}, bf16[192,2048]{1,0:T(8,128)(2,1)S(1)}, u32[]{:S(2)}, u32[]{:S(2)}) %collective-permute-start.10) | collective-permute-done | bytes 786464 | tf_op jit(solution)/shard_map/ppermute | solution.py:203
  130.2 1.3 shard_map.89
  131.5 15.1 %all-to-all-start.1 = ((bf16[64,48,128]{2,1,0:T(8,128)(2,1)}), bf16[64,48,128]{2,1,0:T(8,128)(2,1)S(1)}, u32[]{:S(2)}, u32[]{:S(2)}) async-start(bf16[64,48,128]{2,1,0:T(8,128)(2,1)} %shard_map.89), calls=%async_computation.1 | async-start | bytes 1572864 | tf_op jit(solution)/shard_map/all_to_all | solution.py:206
  146.6 0.1 shard_map.83.hot_ref
  146.6 44.2 %all-to-all-done.1.back_ref = bf16[64,48,128]{2,1,0:T(8,128)(2,1)S(1)} async-done(((bf16[64,48,128]{2,1,0:T(8,128)(2,1)}), bf16[64,48,128]{2,1,0:T(8,128)(2,1)S(1)}, u32[]{:S(2)}, u32[]{:S(2)}) %all-to-all-start.1) | async-done | bytes 786464 | tf_op jit(solution)/shard_map/all_to_all | solution.py:206
  190.8 1.1 shard_map.90
  (4 shorter events, 0.0 us)
Async XLA Ops:
  0.0 0.9 copy-start.2
  0.9 0.7 copy-start.3
  1.6 0.7 copy-start.4
  2.3 20.3 %copy-start.5 = (bf16[1,176,2048]{2,1,0:T(8,128)(2,1)S(1)}, bf16[1,176,2048]{2,1,0:T(8,128)(2,1)}, u32[]{:S(2)}) copy-start(bf16[1,176,2048]{2,1,0:T(8,128)(2,1)} %param.12) | copy-start | bytes 2162692
  2.3 20.3 %copy-start.6 = (bf16[1,176,2048]{2,1,0:T(8,128)(2,1)S(1)}, bf16[1,176,2048]{2,1,0:T(8,128)(2,1)}, u32[]{:S(2)}) copy-start(bf16[1,176,2048]{2,1,0:T(8,128)(2,1)} %param.11) | copy-start | bytes 2162692
  3.9 75.9 %all-to-all-start = ((bf16[64,48,128]{2,1,0:T(8,128)(2,1)}), bf16[64,48,128]{2,1,0:T(8,128)(2,1)S(1)}, u32[]{:S(2)}, u32[]{:S(2)}) async-start(bf16[64,48,128]{2,1,0:T(8,128)(2,1)} %get-tuple-element.18), calls=%async_computation | async-start | bytes 1572864 | tf_op jit(solution)/shard_map/all_to_all | solution.py:206
  22.6 7.9 %copy-start = (bf16[1,176,2048]{2,1,0:T(8,128)(2,1)S(1)}, bf16[1,176,2048]{2,1,0:T(8,128)(2,1)}, u32[]{:S(2)}) copy-start(bf16[1,176,2048]{2,1,0:T(8,128)(2,1)} %param.13) | copy-start | bytes 2162692
  22.7 10.5 %copy-start.1 = (bf16[1,1,64,3,1408]{4,2,3,1,0:T(8,128)(2,1)S(1)}, bf16[1,1,64,3,1408]{4,2,3,1,0:T(8,128)(2,1)}, u32[]{:S(2)}) copy-start(bf16[1,1,64,3,1408]{4,2,3,1,0:T(8,128)(2,1)} %param.14) | copy-start | bytes 1622020
  23.9 57.8 %collective-permute-start.7 = (bf16[352,2048]{1,0:T(8,128)(2,1)}, bf16[352,2048]{1,0:T(8,128)(2,1)}, u32[]{:S(2)}, u32[]{:S(2)}) collective-permute-start(bf16[352,2048]{1,0:T(8,128)(2,1)} %pad_maximum_fusion.own_in), channel_id=1, source_target_pairs={{0,6},{1,7},{2,0},{3,1},{4,2},{5,3},{6,4},{7,5},{8,14},{9,15},{10,... | collective-permute-start | bytes 4325384 | tf_op jit(solution)/shard_map/ppermute | solution.py:200
  28.6 55.1 %collective-permute-start.6 = (bf16[352,2048]{1,0:T(8,128)(2,1)}, bf16[352,2048]{1,0:T(8,128)(2,1)}, u32[]{:S(2)}, u32[]{:S(2)}) collective-permute-start(bf16[352,2048]{1,0:T(8,128)(2,1)} %pad_maximum_fusion.own_in), channel_id=1, source_target_pairs={{0,2},{1,3},{2,4},{3,5},{4,6},{5,7},{6,0},{7,1},{8,10},{9,11},{10,... | collective-permute-start | bytes 4325384 | tf_op jit(solution)/shard_map/ppermute | solution.py:200
  30.5 49.3 %collective-permute-start = (bf16[176,2048]{1,0:T(8,128)(2,1)S(1)}, bf16[176,2048]{1,0:T(8,128)(2,1)S(1)}, u32[]{:S(2)}, u32[]{:S(2)}) collective-permute-start(bf16[176,2048]{1,0:T(8,128)(2,1)S(1)} %bitcast.17), channel_id=1, source_target_pairs={{0,2},{1,3},{2,4},{3,5},{4,6},{5,7},{6,0},{7,1},{8,10},{9,11},{10,... | collective-permute-start | bytes 2162696 | tf_op jit(solution)/shard_map/ppermute | solution.py:200
  33.2 58.6 %collective-permute-start.4 = (bf16[192,1408]{1,0:T(8,128)(2,1)S(1)}, bf16[192,1408]{1,0:T(8,128)(2,1)}, u32[]{:S(2)}, u32[]{:S(2)}) collective-permute-start(bf16[192,1408]{1,0:T(8,128)(2,1)S(1)} %bitcast.21), channel_id=1, source_target_pairs={{0,1},{1,0},{2,3},{3,2},{4,5},{5,4},{6,7},{7,6},{8,9},{9,8},{10,11... | collective-permute-start | bytes 1622024 | tf_op jit(solution)/shard_map/ppermute | solution.py:203
  35.1 59.8 %collective-permute-start.5 = (bf16[192,1408]{1,0:T(8,128)(2,1)}, bf16[192,1408]{1,0:T(8,128)(2,1)}, u32[]{:S(2)}, u32[]{:S(2)}) collective-permute-start(bf16[192,1408]{1,0:T(8,128)(2,1)} %bitcast.10.up_ref), channel_id=1, source_target_pairs={{0,1},{1,0},{2,3},{3,2},{4,5},{5,4},{6,7},{7,6},{8,9},{9,8},{10,11... | collective-permute-start | bytes 1622024 | tf_op jit(solution)/shard_map/ppermute | solution.py:203
  79.8 29.2 %collective-permute-start.3 = (bf16[64,48,128]{2,1,0:T(8,128)(2,1)S(1)}, bf16[64,48,128]{2,1,0:T(8,128)(2,1)}, u32[]{:S(2)}, u32[]{:S(2)}) collective-permute-start(bf16[64,48,128]{2,1,0:T(8,128)(2,1)S(1)} %all-to-all-done.packed_in), channel_id=1, source_target_pairs={{0,1},{1,0},{2,3},{3,2},{4,5},{5,4},{6,7},{7,6},{8,9},{9,8},{10,11... | collective-permute-start | bytes 2359304 | tf_op jit(solution)/shard_map/ppermute | solution.py:203
  81.7 20.9 %collective-permute-start.1 = (bf16[176,2048]{1,0:T(8,128)(2,1)S(1)}, bf16[176,2048]{1,0:T(8,128)(2,1)S(1)}, u32[]{:S(2)}, u32[]{:S(2)}) collective-permute-start(bf16[176,2048]{1,0:T(8,128)(2,1)S(1)} %bitcast.18), channel_id=1, source_target_pairs={{0,6},{1,7},{2,0},{3,1},{4,2},{5,3},{6,4},{7,5},{8,14},{9,15},{10,... | collective-permute-start | bytes 2162696 | tf_op jit(solution)/shard_map/ppermute | solution.py:200
  83.7 22.2 %collective-permute-start.2 = (bf16[176,2048]{1,0:T(8,128)(2,1)S(1)}, bf16[176,2048]{1,0:T(8,128)(2,1)}, u32[]{:S(2)}, u32[]{:S(2)}) collective-permute-start(bf16[176,2048]{1,0:T(8,128)(2,1)S(1)} %collective-permute-done.left_in), channel_id=1, source_target_pairs={{0,2},{1,3},{2,4},{3,5},{4,6},{5,7},{6,0},{7,1},{8,10},{9,11},{10,... | collective-permute-start | bytes 2162696 | tf_op jit(solution)/shard_map/ppermute | solution.py:200
  91.8 25.9 %collective-permute-start.9 = (bf16[176,2048]{1,0:T(8,128)(2,1)}, bf16[176,2048]{1,0:T(8,128)(2,1)}, u32[]{:S(2)}, u32[]{:S(2)}) collective-permute-start(bf16[176,2048]{1,0:T(8,128)(2,1)} %slice.9), channel_id=1, source_target_pairs={{0,6},{1,7},{2,0},{3,1},{4,2},{5,3},{6,4},{7,5},{8,14},{9,15},{10,... | collective-permute-start | bytes 2162696 | tf_op jit(solution)/shard_map/ppermute | solution.py:200
  94.9 26.0 %collective-permute-start.8 = (bf16[176,2048]{1,0:T(8,128)(2,1)}, bf16[176,2048]{1,0:T(8,128)(2,1)}, u32[]{:S(2)}, u32[]{:S(2)}) collective-permute-start(bf16[176,2048]{1,0:T(8,128)(2,1)} %slice.8), channel_id=1, source_target_pairs={{0,2},{1,3},{2,4},{3,5},{4,6},{5,7},{6,0},{7,1},{8,10},{9,11},{10,... | collective-permute-start | bytes 2162696 | tf_op jit(solution)/shard_map/ppermute | solution.py:200
  126.0 4.2 %collective-permute-start.10 = (bf16[192,2048]{1,0:T(8,128)(2,1)S(1)}, bf16[192,2048]{1,0:T(8,128)(2,1)S(1)}, u32[]{:S(2)}, u32[]{:S(2)}) collective-permute-start(bf16[192,2048]{1,0:T(8,128)(2,1)S(1)} %get-tuple-element.28), channel_id=1, source_target_pairs={{0,1},{1,0},{2,3},{3,2},{4,5},{5,4},{6,7},{7,6},{8,9},{9,8},{10,11... | collective-permute-start | bytes 2359304 | tf_op jit(solution)/shard_map/ppermute | solution.py:203
  131.5 59.3 %all-to-all-start.1 = ((bf16[64,48,128]{2,1,0:T(8,128)(2,1)}), bf16[64,48,128]{2,1,0:T(8,128)(2,1)S(1)}, u32[]{:S(2)}, u32[]{:S(2)}) async-start(bf16[64,48,128]{2,1,0:T(8,128)(2,1)} %shard_map.89), calls=%async_computation.1 | async-start | bytes 1572864 | tf_op jit(solution)/shard_map/all_to_all | solution.py:206

commit v3 on v2

--- a/solution.py
+++ b/solution.py
@@ -10,6 +10,7 @@
 VM = pl.BlockSpec(memory_space=pltpu.VMEM)
 SM = pl.BlockSpec(memory_space=pltpu.SMEM)
 LINKS = 4
+SLOTS = 3
 
 
 def call(kernel, ins, outs, flops=0, smem=0, scratch=(), spec=VM, limit=24 << 20):
@@ -52,10 +53,10 @@
     return jnp.concatenate([parts[c] for c in range(chunks)], axis=1)
 
 
-def place_kernel(routes_ref, gates_ref, grad_ref, out_ref, hot_ref):
+def place_kernel(routes_ref, gates_ref, grad_ref, out_ref):
     top, tokens = routes_ref.shape
     experts, _, _ = out_ref.shape
-    rows = hot_ref.shape[0]
+    rows = experts * SLOTS
     row = lax.broadcasted_iota(jnp.int32, (rows, tokens), 0)
     number = row // experts
     named = row - number * experts
@@ -74,13 +75,11 @@
     chosen = (hits > 0.5) & (jnp.abs(earlier - slot) < 0.5)
     weight = jnp.sum(jnp.where(chosen, gate, 0.0), axis=1, keepdims=True)
     hot = jnp.where(chosen, 1.0, 0.0).astype(BF16)
-    hot_ref[...] = hot
     pack(weight * jnp.dot(hot, grad_ref[...], preferred_element_type=F32), out_ref)
 
 
-def factor_kernel(core_ref, gate_ref, up_ref, gf_ref, uf_ref):
+def factors(first, gate_ref, up_ref, gf_ref, uf_ref):
     slice_width = gf_ref.shape[1] // LINKS
-    first = core_ref[0] == 0
     for q in range(LINKS):
         low = 2 * q * slice_width
         mid, high = low + slice_width, low + 2 * slice_width
@@ -99,20 +98,23 @@
 
 
 def hidden_kernel(
-    link_ref, packed_in, own_in, left_in, right_in, far_in, gf_in, uf_in,
-    gate_ref, up_ref, packed_ref, down_ref, gf_ref, uf_ref, rows_ref, sems,
+    link_ref, core_ref, packed_in, own_in, left_in, right_in, far_in, saved_gate_in, saved_up_in,
+    gate_ref, up_ref, packed_ref, down_ref, saved_gate_ref, saved_up_ref, gf_ref, uf_ref, rows_ref, sems,
 ):
     width = own_in.shape[0]
-    copies = [(packed_in, packed_ref)]
+    copies = [(saved_gate_in, saved_gate_ref), (saved_up_in, saved_up_ref), (packed_in, packed_ref)]
     for piece, place in zip((own_in, left_in, right_in, far_in), spots(link_ref, width)):
         copies.append((piece, down_ref.at[place, :]))
-    copies = fetch(copies + [(gf_in, gf_ref), (uf_in, uf_ref)], sems)
+    copies = fetch(copies, sems)
     copies[0].wait()
+    copies[1].wait()
+    factors(core_ref[0] == 0, saved_gate_ref, saved_up_ref, gf_ref, uf_ref)
+    copies[2].wait()
     experts = packed_ref.shape[0]
     slots = rows_ref.shape[0] // experts
     for s in range(slots):
         rows_ref[s * experts : (s + 1) * experts, :] = unpack(packed_ref, s, slots)
-    for copy in copies[1:]:
+    for copy in copies[3:]:
         copy.wait()
     grad = lax.dot_general(
         rows_ref[...], down_ref[...], (((1,), (1,)), ((), ())), preferred_element_type=F32
@@ -122,10 +124,10 @@
 
 
 def output_kernel(
-    link_ref, own_gate_in, own_up_in, other_gate_in, other_up_in, own_in, left_in, right_in, farg_in, faru_in,
+    link_ref, own_gate_in, own_up_in, other_gate_in, other_up_in, own_in, left_in, right_in, far_in,
     own_ref, theirs_ref, gate_ref, up_ref, weight_ref, sems,
 ):
-    width = farg_in.shape[0]
+    width = own_in.shape[0] // 2
     rows, hidden = own_gate_in.shape
     parts = sems.shape[0] - 1
     span = weight_ref.shape[1] // parts
@@ -143,13 +145,10 @@
     for n in range(parts):
         columns = pl.ds(n * span, span)
         copies = []
-        for piece, place in ((own_in, own), (left_in, left), (right_in, right)):
+        for piece, place in ((own_in, own), (left_in, left), (right_in, right), (far_in, far)):
             copies.append((piece.at[pl.ds(0, width), columns], weight_ref.at[place, columns]))
             lower = pl.ds(pl.multiple_of(place.start + hidden, 16), width)
             copies.append((piece.at[pl.ds(width, width), columns], weight_ref.at[lower, columns]))
-        copies.append((farg_in.at[:, columns], weight_ref.at[far, columns]))
-        lower = pl.ds(pl.multiple_of(far.start + hidden, 16), width)
-        copies.append((faru_in.at[:, columns], weight_ref.at[lower, columns]))
         blocks.append(fetch(copies, sems.at[n + 1]))
     for copy in begun:
         copy.wait()
@@ -167,8 +166,24 @@
     pack(own_ref[...].astype(F32) + back_ref[...].astype(F32), out_ref)
 
 
-def turn_kernel(hot_ref, out_ref):
-    out_ref[...] = hot_ref[...].T
+def turn_kernel(routes_ref, hot_ref):
+    tokens, top = routes_ref.shape
+    rows = hot_ref.shape[1]
+    experts = rows // SLOTS
+    row = lax.broadcasted_iota(jnp.int32, (tokens, rows), 1)
+    number = row // experts
+    named = row - number * experts
+    slot = number.astype(F32)
+    hits = jnp.zeros((tokens, rows), F32)
+    for k in range(top):
+        hits = jnp.where(routes_ref[:, k : k + 1] == named, 1.0, hits)
+    before = (
+        lax.broadcasted_iota(jnp.int32, (tokens, tokens), 1)
+        < lax.broadcasted_iota(jnp.int32, (tokens, tokens), 0)
+    ).astype(BF16)
+    earlier = jnp.dot(before, hits.astype(BF16), preferred_element_type=F32)
+    chosen = (hits > 0.5) & (jnp.abs(earlier - slot) < 0.5)
+    hot_ref[...] = jnp.where(chosen, 1.0, 0.0).astype(BF16)
 
 
 def combine_kernel(hot_ref, back_ref, out_ref):
@@ -208,31 +223,24 @@
     down = w_down[0]
     down_left, down_right = along(down, 1), along(down, -1)
 
-    packed, hot = call(
+    packed = call(
         place_kernel,
         (routes.T, gates.T, grad_out),
-        (
-            jax.ShapeDtypeStruct((experts, 2 * deep, 128), BF16),
-            jax.ShapeDtypeStruct((rows, tokens), BF16),
-        ),
+        (jax.ShapeDtypeStruct((experts, 2 * deep, 128), BF16),),
         2 * rows * tokens * width,
     )
     arrived = exchange(packed)
 
     pair = jnp.concatenate([w_gate[0], w_up[0]], axis=0)
     pair_left, pair_right = along(pair, 1), along(pair, -1)
-    down_far = along(down_left, 1)
-    for_right, for_left = pair_left[:slice_width], pair_right[slice_width:]
-    pair_farg, pair_faru = along(for_right, 1), along(for_left, -1)
+    down_far = along(down_right, -1)
+    pair_far = along(pair_left, 1)
 
     link_at = (replica >> 1).reshape(1)
     core_at = (replica & 1).reshape(1)
     saved = tuple(a[0, 0].transpose(1, 0, 2).reshape(rows, -1) for a in (saved_gate, saved_up))
     hidden_units = LINKS * slice_width
-    factor = jax.ShapeDtypeStruct((rows, hidden_units), F32)
-    own_factors = call(factor_kernel, (core_at,) + saved, (factor, factor), smem=1)
     sent = (across(saved[0]), across(saved[1]))
-    other_factors = call(factor_kernel, (core_at,) + sent, (factor, factor), smem=1)
 
     downs = (down, down_left, down_right, down_far)
     hidden = jax.ShapeDtypeStruct((rows, hidden_units), BF16)
@@ -240,6 +248,8 @@
     scratch = (
         pltpu.VMEM((experts, 2 * deep, 128), BF16),
         pltpu.VMEM((hidden_units, width), BF16),
+        pltpu.VMEM(saved[0].shape, BF16),
+        pltpu.VMEM(saved[0].shape, BF16),
         pltpu.VMEM((rows, hidden_units), F32),
         pltpu.VMEM((rows, hidden_units), F32),
         pltpu.VMEM((rows, width), BF16),
@@ -247,14 +257,14 @@
     )
     other_rows = across(arrived)
 
-    def hide(packed_rows, factors):
-        ins = (link_at, packed_rows) + downs + tuple(factors)
-        return call(hidden_kernel, ins, (hidden, hidden), cost, 1, scratch, pl.BlockSpec(memory_space=pl.ANY))
-
-    own_hidden = hide(arrived, own_factors)
-    other_hidden = hide(other_rows, other_factors)
-
-    pieces = (pair, pair_left, pair_right, pair_farg, pair_faru)
+    def hide(packed_rows, kept):
+        ins = (link_at, core_at, packed_rows) + downs + tuple(kept)
+        return call(hidden_kernel, ins, (hidden, hidden), cost, 2, scratch, pl.BlockSpec(memory_space=pl.ANY))
+
+    own_hidden = hide(arrived, saved)
+    other_hidden = hide(other_rows, sent)
+
+    pieces = (pair, pair_left, pair_right, pair_far)
     scratch2 = (
         pltpu.VMEM((2 * rows, hidden_units), BF16),
         pltpu.VMEM((2 * rows, hidden_units), BF16),
@@ -274,7 +284,7 @@
     back = across(theirs)
     outgoing = call(join_kernel, (ours, back), (jax.ShapeDtypeStruct((experts, 2 * deep, 128), BF16),))
     returned = exchange(outgoing)
-    turned = call(turn_kernel, (hot,), (jax.ShapeDtypeStruct((tokens, rows), BF16),))
+    turned = call(turn_kernel, (routes,), (jax.ShapeDtypeStruct((tokens, rows), BF16),))
     return call(combine_kernel, (turned, returned), (jax.ShapeDtypeStruct((tokens, width), BF16),))
 
 

time: 193 us -> 195 us (1.010)
  waiting for transfers between devices: 102 us -> 111 us
  Pallas kernels: 19.4 us -> 16 us
  local copies, waits for them, and re-layouts: 6.47 us -> 3.43 us
    ppermute x7 -> x6, waiting for transfers between devices: 55.3 us -> 65.1 us  [along(): return lax.ppermute(a, 'replica', pairs)]
    slice x2 -> x0, local copies, waits for them, and re-layouts: 4.17 us -> none  [body(): for_right, for_left = (pair_left[:slice_width], pair_right[slice_width:])]
    pallas_call x9 -> x7, Pallas kernels: 19.4 us -> 16 us  [call(): pl.pallas_call(kernel, out_shape=outs[0] if single else tuple(outs), in_s...]
    ppermute x7 -> x6, starting transfers between devices: 20.9 us -> 19.7 us  [along(): return lax.ppermute(a, 'replica', pairs)]
  transfers between devices with their start and end apart: 13 -> 12, of which waited for: 7 -> 4; matrix products, arithmetic and copies ran while one was open for 3% -> 1% of each run, Pallas kernels for 5% -> 4%
where the time goes in v3:
time: 195 us; the launch traced here: 194 us
  waiting for transfers between devices  111 us (57%)
  starting transfers between devices  61.7 us (32%)
  Pallas kernels  16 us (8%)
  local copies, waits for them, and re-layouts  3.43 us (2%)
    ppermute x6, waiting for transfers between devices, along(): return lax.ppermute(a, 'replica', pairs)  65.1 us
    all_to_all x2, waiting for transfers between devices, exchange(): return lax.all_to_all(a, 'expert', split_axis=0, concat_axis=0, tiled=True)  43.9 us
    all_to_all x2, starting transfers between devices, exchange(): return lax.all_to_all(a, 'expert', split_axis=0, concat_axis=0, tiled=True)  33.8 us
    ppermute x6, starting transfers between devices, along(): return lax.ppermute(a, 'replica', pairs)  19.7 us
    pallas_call x7, Pallas kernels, call(): pl.pallas_call(kernel, out_shape=outs[0] if single else tuple(outs), in_s...  16 us
    ppermute x4, starting transfers between devices, across(): return lax.ppermute(a, 'replica', [(i, i ^ 1) for i in range(copies)])  8.16 us
  transfers between devices with their start and end apart: 12, of which 4 were waited for; matrix products, arithmetic and copies ran while one was open for 1% of the time, Pallas kernels for 4%

profile of v3, /device:TPU:8, one launch (start us, length us, event | category | flops | bytes accessed | tf_op | source)
XLA Modules:
  0.0 193.9 jit_solution(13928485990134615833)
XLA Ops:
  0.0 0.0 copy-start.3
  0.0 0.9 copy-done.3
  0.9 0.0 copy-start.4
  0.9 0.7 copy-done.4
  1.6 0.0 copy-start.6
  1.6 0.7 copy-done.6
  2.3 1.6 shard_map.83
  3.9 18.7 %all-to-all-start = ((bf16[64,48,128]{2,1,0:T(8,128)(2,1)}), bf16[64,48,128]{2,1,0:T(8,128)(2,1)S(1)}, u32[]{:S(2)}, u32[]{:S(2)}) async-start(bf16[64,48,128]{2,1,0:T(8,128)(2,1)} %shard_map.83), calls=%async_computation | async-start | bytes 1572864 | tf_op jit(solution)/shard_map/all_to_all | solution.py:221
  22.6 0.0 copy-done.7
  22.6 0.0 copy-done.8
  22.6 0.0 copy-start
  22.7 0.0 copy-start.1
  22.7 1.3 pad_maximum_fusion.own_in
  23.9 3.4 %collective-permute-start.6 = (bf16[352,2048]{1,0:T(8,128)(2,1)}, bf16[352,2048]{1,0:T(8,128)(2,1)}, u32[]{:S(2)}, u32[]{:S(2)}) collective-permute-start(bf16[352,2048]{1,0:T(8,128)(2,1)} %pad_maximum_fusion.own_in), channel_id=1, source_target_pairs={{0,2},{1,3},{2,4},{3,5},{4,6},{5,7},{6,0},{7,1},{8,10},{9,11},{10,... | collective-permute-start | bytes 4325384 | tf_op jit(solution)/shard_map/ppermute | solution.py:215
  27.3 0.0 copy-done
  27.3 3.7 %collective-permute-start.1 = (bf16[176,2048]{1,0:T(8,128)(2,1)S(1)}, bf16[176,2048]{1,0:T(8,128)(2,1)S(1)}, u32[]{:S(2)}, u32[]{:S(2)}) collective-permute-start(bf16[176,2048]{1,0:T(8,128)(2,1)S(1)} %bitcast.17), channel_id=1, source_target_pairs={{0,6},{1,7},{2,0},{3,1},{4,2},{5,3},{6,4},{7,5},{8,14},{9,15},{10,... | collective-permute-start | bytes 2162696 | tf_op jit(solution)/shard_map/ppermute | solution.py:215
  31.0 3.5 %collective-permute-start.7 = (bf16[352,2048]{1,0:T(8,128)(2,1)}, bf16[352,2048]{1,0:T(8,128)(2,1)}, u32[]{:S(2)}, u32[]{:S(2)}) collective-permute-start(bf16[352,2048]{1,0:T(8,128)(2,1)} %pad_maximum_fusion.own_in), channel_id=1, source_target_pairs={{0,6},{1,7},{2,0},{3,1},{4,2},{5,3},{6,4},{7,5},{8,14},{9,15},{10,... | collective-permute-start | bytes 4325384 | tf_op jit(solution)/shard_map/ppermute | solution.py:215
  34.4 25.6 %collective-permute-done.6.left_in = bf16[352,2048]{1,0:T(8,128)(2,1)} collective-permute-done((bf16[352,2048]{1,0:T(8,128)(2,1)}, bf16[352,2048]{1,0:T(8,128)(2,1)}, u32[]{:S(2)}, u32[]{:S(2)}) %collective-permute-start.6) | collective-permute-done | bytes 1441824 | tf_op jit(solution)/shard_map/ppermute | solution.py:215
  60.1 2.2 %collective-permute-start.8 = (bf16[352,2048]{1,0:T(8,128)(2,1)}, bf16[352,2048]{1,0:T(8,128)(2,1)}, u32[]{:S(2)}, u32[]{:S(2)}) collective-permute-start(bf16[352,2048]{1,0:T(8,128)(2,1)} %collective-permute-done.6.left_in), channel_id=1, source_target_pairs={{0,2},{1,3},{2,4},{3,5},{4,6},{5,7},{6,0},{7,1},{8,10},{9,11},{10,... | collective-permute-start | bytes 4325384 | tf_op jit(solution)/shard_map/ppermute | solution.py:215
  62.3 3.4 %collective-permute-start = (bf16[176,2048]{1,0:T(8,128)(2,1)S(1)}, bf16[176,2048]{1,0:T(8,128)(2,1)S(1)}, u32[]{:S(2)}, u32[]{:S(2)}) collective-permute-start(bf16[176,2048]{1,0:T(8,128)(2,1)S(1)} %bitcast.18), channel_id=1, source_target_pairs={{0,2},{1,3},{2,4},{3,5},{4,6},{5,7},{6,0},{7,1},{8,10},{9,11},{10,... | collective-permute-start | bytes 2162696 | tf_op jit(solution)/shard_map/ppermute | solution.py:215
  65.7 0.0 collective-permute-done.1.right_in
  65.7 3.7 %collective-permute-start.2 = (bf16[176,2048]{1,0:T(8,128)(2,1)S(1)}, bf16[176,2048]{1,0:T(8,128)(2,1)}, u32[]{:S(2)}, u32[]{:S(2)}) collective-permute-start(bf16[176,2048]{1,0:T(8,128)(2,1)S(1)} %collective-permute-done.1.right_in), channel_id=1, source_target_pairs={{0,6},{1,7},{2,0},{3,1},{4,2},{5,3},{6,4},{7,5},{8,14},{9,15},{10,... | collective-permute-start | bytes 2162696 | tf_op jit(solution)/shard_map/ppermute | solution.py:215
  69.4 0.0 all-to-all-done.packed_in
  69.4 1.9 collective-permute-start.3
  71.3 39.4 %collective-permute-done.left_in = bf16[176,2048]{1,0:T(8,128)(2,1)S(1)} collective-permute-done((bf16[176,2048]{1,0:T(8,128)(2,1)S(1)}, bf16[176,2048]{1,0:T(8,128)(2,1)S(1)}, u32[]{:S(2)}, u32[]{:S(2)}) %collective-permute-start) | collective-permute-done | bytes 720928 | tf_op jit(solution)/shard_map/ppermute | solution.py:215
  110.8 0.0 copy-done.1
  110.8 1.9 collective-permute-start.4
  112.7 0.0 collective-permute-done.2.far_in
  112.7 2.4 %collective-permute-start.5 = (bf16[192,1408]{1,0:T(8,128)(2,1)}, bf16[192,1408]{1,0:T(8,128)(2,1)}, u32[]{:S(2)}, u32[]{:S(2)}) collective-permute-start(bf16[192,1408]{1,0:T(8,128)(2,1)} %bitcast.23), channel_id=1, source_target_pairs={{0,1},{1,0},{2,3},{3,2},{4,5},{5,4},{6,7},{7,6},{8,9},{9,8},{10,11... | collective-permute-start | bytes 1622024 | tf_op jit(solution)/shard_map/ppermute | solution.py:218
  115.1 0.0 copy-start.2
  115.1 1.0 copy-done.2
  116.2 3.2 %shard_map.84 = (bf16[192,704]{1,0:T(8,128)(2,1)S(1)}, bf16[192,704]{1,0:T(8,128)(2,1)S(1)}) custom-call(s32[1]{0:T(128)} %bitcast.link_ref, s32[1]{0:T(128)} %bitcast.1.core_ref, bf16[64,48,128]{2,1,0:T(8,128)(2,1)S(1)} %all-to-all-done.packed_in, bf16[176,2048]{1,0:T(8,128)(2,1)S(1)} %bitcast.19, bf16[176,2048]{1,0:T(8,128)(2,1)S(1)} %collective-permute-done.left_in, ...), custom_call_target="tpu_custom_call" | custom-call | flops 553648128 | bytes 5292040 | tf_op jit(solution)/shard_map/pallas_call | solution.py:19
  119.4 0.0 collective-permute-done.4.saved_gate_in
  119.4 0.0 collective-permute-done.5.saved_up_in
  119.4 0.0 collective-permute-done.3.packed_in
  119.4 3.4 %shard_map.85 = (bf16[192,704]{1,0:T(8,128)(2,1)S(1)}, bf16[192,704]{1,0:T(8,128)(2,1)S(1)}) custom-call(s32[1]{0:T(128)} %bitcast.link_ref, s32[1]{0:T(128)} %bitcast.1.core_ref, bf16[64,48,128]{2,1,0:T(8,128)(2,1)} %collective-permute-done.3.packed_in, bf16[176,2048]{1,0:T(8,128)(2,1)S(1)} %bitcast.20, bf16[176,2048]{1,0:T(8,128)(2,1)S(1)} %collective-permute-done.left_in, ...), custom_call_target="tpu_custom_call" | custom-call | flops 553648128 | bytes 5292040 | tf_op jit(solution)/shard_map/pallas_call | solution.py:19
  122.8 0.0 collective-permute-done.7.right_in
  122.8 0.0 collective-permute-done.8.far_in
  122.9 5.2 %shard_map.86 = (bf16[192,2048]{1,0:T(8,128)(2,1)S(1)}, bf16[192,2048]{1,0:T(8,128)(2,1)S(1)}) custom-call(s32[1]{0:T(128)} %bitcast.link_ref, bf16[192,704]{1,0:T(8,128)(2,1)S(1)} %get-tuple-element.11.own_gate_in, bf16[192,704]{1,0:T(8,128)(2,1)S(1)} %get-tuple-element.12.own_up_in, bf16[192,704]{1,0:T(8,128)(2,1)S(1)} %get-tuple-element.13.other_gate_in, ...), custom_call_target="tpu_custom_call" | custom-call | flops 2214592512 | bytes 8421380 | tf_op jit(solution)/shard_map/pallas_call | solution.py:19
  128.0 1.9 collective-permute-start.9
  130.0 2.2 %collective-permute-done.9.back_ref = bf16[192,2048]{1,0:T(8,128)(2,1)S(1)} collective-permute-done((bf16[192,2048]{1,0:T(8,128)(2,1)S(1)}, bf16[192,2048]{1,0:T(8,128)(2,1)S(1)}, u32[]{:S(2)}, u32[]{:S(2)}) %collective-permute-start.9) | collective-permute-done | bytes 786464 | tf_op jit(solution)/shard_map/ppermute | solution.py:218
  132.2 1.3 shard_map.87
  133.5 15.1 %all-to-all-start.1 = ((bf16[64,48,128]{2,1,0:T(8,128)(2,1)}), bf16[64,48,128]{2,1,0:T(8,128)(2,1)S(1)}, u32[]{:S(2)}, u32[]{:S(2)}) async-start(bf16[64,48,128]{2,1,0:T(8,128)(2,1)} %shard_map.87), calls=%async_computation.1 | async-start | bytes 1572864 | tf_op jit(solution)/shard_map/all_to_all | solution.py:221
  148.6 0.0 copy-done.5
  148.6 0.1 copy.9.routes_ref
  148.7 0.2 shard_map.82.hot_ref
  148.9 43.9 %all-to-all-done.1.back_ref = bf16[64,48,128]{2,1,0:T(8,128)(2,1)S(1)} async-done(((bf16[64,48,128]{2,1,0:T(8,128)(2,1)}), bf16[64,48,128]{2,1,0:T(8,128)(2,1)S(1)}, u32[]{:S(2)}, u32[]{:S(2)}) %all-to-all-start.1) | async-done | bytes 786464 | tf_op jit(solution)/shard_map/all_to_all | solution.py:221
  192.8 1.1 shard_map.88
  (3 shorter events, 0.0 us)
Async XLA Ops:
  0.0 0.9 copy-start.3
  0.9 0.7 copy-start.4
  1.6 0.7 copy-start.6
  2.3 20.3 %copy-start.7 = (bf16[1,176,2048]{2,1,0:T(8,128)(2,1)S(1)}, bf16[1,176,2048]{2,1,0:T(8,128)(2,1)}, u32[]{:S(2)}) copy-start(bf16[1,176,2048]{2,1,0:T(8,128)(2,1)} %param.12) | copy-start | bytes 2162692
  2.3 20.4 %copy-start.8 = (bf16[1,176,2048]{2,1,0:T(8,128)(2,1)S(1)}, bf16[1,176,2048]{2,1,0:T(8,128)(2,1)}, u32[]{:S(2)}) copy-start(bf16[1,176,2048]{2,1,0:T(8,128)(2,1)} %param.11) | copy-start | bytes 2162692
  3.9 65.5 %all-to-all-start = ((bf16[64,48,128]{2,1,0:T(8,128)(2,1)}), bf16[64,48,128]{2,1,0:T(8,128)(2,1)S(1)}, u32[]{:S(2)}, u32[]{:S(2)}) async-start(bf16[64,48,128]{2,1,0:T(8,128)(2,1)} %shard_map.83), calls=%async_computation | async-start | bytes 1572864 | tf_op jit(solution)/shard_map/all_to_all | solution.py:221
  22.6 4.7 %copy-start = (bf16[1,176,2048]{2,1,0:T(8,128)(2,1)S(1)}, bf16[1,176,2048]{2,1,0:T(8,128)(2,1)}, u32[]{:S(2)}) copy-start(bf16[1,176,2048]{2,1,0:T(8,128)(2,1)} %param.13) | copy-start | bytes 2162692
  22.7 88.1 %copy-start.1 = (bf16[1,1,64,3,1408]{4,2,3,1,0:T(8,128)(2,1)S(1)}, bf16[1,1,64,3,1408]{4,2,3,1,0:T(8,128)(2,1)}, u32[]{:S(2)}) copy-start(bf16[1,1,64,3,1408]{4,2,3,1,0:T(8,128)(2,1)} %param.14) | copy-start | bytes 1622020
  23.9 36.2 %collective-permute-start.6 = (bf16[352,2048]{1,0:T(8,128)(2,1)}, bf16[352,2048]{1,0:T(8,128)(2,1)}, u32[]{:S(2)}, u32[]{:S(2)}) collective-permute-start(bf16[352,2048]{1,0:T(8,128)(2,1)} %pad_maximum_fusion.own_in), channel_id=1, source_target_pairs={{0,2},{1,3},{2,4},{3,5},{4,6},{5,7},{6,0},{7,1},{8,10},{9,11},{10,... | collective-permute-start | bytes 4325384 | tf_op jit(solution)/shard_map/ppermute | solution.py:215
  27.3 38.4 %collective-permute-start.1 = (bf16[176,2048]{1,0:T(8,128)(2,1)S(1)}, bf16[176,2048]{1,0:T(8,128)(2,1)S(1)}, u32[]{:S(2)}, u32[]{:S(2)}) collective-permute-start(bf16[176,2048]{1,0:T(8,128)(2,1)S(1)} %bitcast.17), channel_id=1, source_target_pairs={{0,6},{1,7},{2,0},{3,1},{4,2},{5,3},{6,4},{7,5},{8,14},{9,15},{10,... | collective-permute-start | bytes 2162696 | tf_op jit(solution)/shard_map/ppermute | solution.py:215
  31.0 91.8 %collective-permute-start.7 = (bf16[352,2048]{1,0:T(8,128)(2,1)}, bf16[352,2048]{1,0:T(8,128)(2,1)}, u32[]{:S(2)}, u32[]{:S(2)}) collective-permute-start(bf16[352,2048]{1,0:T(8,128)(2,1)} %pad_maximum_fusion.own_in), channel_id=1, source_target_pairs={{0,6},{1,7},{2,0},{3,1},{4,2},{5,3},{6,4},{7,5},{8,14},{9,15},{10,... | collective-permute-start | bytes 4325384 | tf_op jit(solution)/shard_map/ppermute | solution.py:215
  60.1 62.8 %collective-permute-start.8 = (bf16[352,2048]{1,0:T(8,128)(2,1)}, bf16[352,2048]{1,0:T(8,128)(2,1)}, u32[]{:S(2)}, u32[]{:S(2)}) collective-permute-start(bf16[352,2048]{1,0:T(8,128)(2,1)} %collective-permute-done.6.left_in), channel_id=1, source_target_pairs={{0,2},{1,3},{2,4},{3,5},{4,6},{5,7},{6,0},{7,1},{8,10},{9,11},{10,... | collective-permute-start | bytes 4325384 | tf_op jit(solution)/shard_map/ppermute | solution.py:215
  62.3 48.5 %collective-permute-start = (bf16[176,2048]{1,0:T(8,128)(2,1)S(1)}, bf16[176,2048]{1,0:T(8,128)(2,1)S(1)}, u32[]{:S(2)}, u32[]{:S(2)}) collective-permute-start(bf16[176,2048]{1,0:T(8,128)(2,1)S(1)} %bitcast.18), channel_id=1, source_target_pairs={{0,2},{1,3},{2,4},{3,5},{4,6},{5,7},{6,0},{7,1},{8,10},{9,11},{10,... | collective-permute-start | bytes 2162696 | tf_op jit(solution)/shard_map/ppermute | solution.py:215
  65.7 47.0 %collective-permute-start.2 = (bf16[176,2048]{1,0:T(8,128)(2,1)S(1)}, bf16[176,2048]{1,0:T(8,128)(2,1)}, u32[]{:S(2)}, u32[]{:S(2)}) collective-permute-start(bf16[176,2048]{1,0:T(8,128)(2,1)S(1)} %collective-permute-done.1.right_in), channel_id=1, source_target_pairs={{0,6},{1,7},{2,0},{3,1},{4,2},{5,3},{6,4},{7,5},{8,14},{9,15},{10,... | collective-permute-start | bytes 2162696 | tf_op jit(solution)/shard_map/ppermute | solution.py:215
  69.4 50.1 %collective-permute-start.3 = (bf16[64,48,128]{2,1,0:T(8,128)(2,1)S(1)}, bf16[64,48,128]{2,1,0:T(8,128)(2,1)}, u32[]{:S(2)}, u32[]{:S(2)}) collective-permute-start(bf16[64,48,128]{2,1,0:T(8,128)(2,1)S(1)} %all-to-all-done.packed_in), channel_id=1, source_target_pairs={{0,1},{1,0},{2,3},{3,2},{4,5},{5,4},{6,7},{7,6},{8,9},{9,8},{10,11... | collective-permute-start | bytes 2359304 | tf_op jit(solution)/shard_map/ppermute | solution.py:218
  110.8 8.7 %collective-permute-start.4 = (bf16[192,1408]{1,0:T(8,128)(2,1)S(1)}, bf16[192,1408]{1,0:T(8,128)(2,1)}, u32[]{:S(2)}, u32[]{:S(2)}) collective-permute-start(bf16[192,1408]{1,0:T(8,128)(2,1)S(1)} %bitcast.21), channel_id=1, source_target_pairs={{0,1},{1,0},{2,3},{3,2},{4,5},{5,4},{6,7},{7,6},{8,9},{9,8},{10,11... | collective-permute-start | bytes 1622024 | tf_op jit(solution)/shard_map/ppermute | solution.py:218
  112.7 6.7 %collective-permute-start.5 = (bf16[192,1408]{1,0:T(8,128)(2,1)}, bf16[192,1408]{1,0:T(8,128)(2,1)}, u32[]{:S(2)}, u32[]{:S(2)}) collective-permute-start(bf16[192,1408]{1,0:T(8,128)(2,1)} %bitcast.23), channel_id=1, source_target_pairs={{0,1},{1,0},{2,3},{3,2},{4,5},{5,4},{6,7},{7,6},{8,9},{9,8},{10,11... | collective-permute-start | bytes 1622024 | tf_op jit(solution)/shard_map/ppermute | solution.py:218
  115.1 1.1 copy-start.2
  128.0 4.2 %collective-permute-start.9 = (bf16[192,2048]{1,0:T(8,128)(2,1)S(1)}, bf16[192,2048]{1,0:T(8,128)(2,1)S(1)}, u32[]{:S(2)}, u32[]{:S(2)}) collective-permute-start(bf16[192,2048]{1,0:T(8,128)(2,1)S(1)} %get-tuple-element.16), channel_id=1, source_target_pairs={{0,1},{1,0},{2,3},{3,2},{4,5},{5,4},{6,7},{7,6},{8,9},{9,8},{10,11... | collective-permute-start | bytes 2359304 | tf_op jit(solution)/shard_map/ppermute | solution.py:218
  132.2 16.4 %copy-start.5 = (s32[32,6]{0,1:T(8,128)S(1)}, s32[32,6]{0,1:T(8,128)}, u32[]{:S(2)}) copy-start(s32[32,6]{0,1:T(8,128)} %param.9) | copy-start | bytes 2308
  133.5 59.3 %all-to-all-start.1 = ((bf16[64,48,128]{2,1,0:T(8,128)(2,1)}), bf16[64,48,128]{2,1,0:T(8,128)(2,1)S(1)}, u32[]{:S(2)}, u32[]{:S(2)}) async-start(bf16[64,48,128]{2,1,0:T(8,128)(2,1)} %shard_map.87), calls=%async_computation.1 | async-start | bytes 1572864 | tf_op jit(solution)/shard_map/all_to_all | solution.py:221

commit v4 on v3

--- a/solution.py
+++ b/solution.py
@@ -98,13 +98,17 @@
 
 
 def hidden_kernel(
-    link_ref, core_ref, packed_in, own_in, left_in, right_in, far_in, saved_gate_in, saved_up_in,
+    link_ref, core_ref, packed_in, own_in, left_in, right_in, far1_in, far2_in, saved_gate_in, saved_up_in,
     gate_ref, up_ref, packed_ref, down_ref, saved_gate_ref, saved_up_ref, gf_ref, uf_ref, rows_ref, sems,
 ):
     width = own_in.shape[0]
     copies = [(saved_gate_in, saved_gate_ref), (saved_up_in, saved_up_ref), (packed_in, packed_ref)]
-    for piece, place in zip((own_in, left_in, right_in, far_in), spots(link_ref, width)):
+    own, left, right, far = spots(link_ref, width)
+    for piece, place in ((own_in, own), (left_in, left), (right_in, right)):
         copies.append((piece, down_ref.at[place, :]))
+    cut = far1_in.shape[1]
+    copies.append((far1_in, down_ref.at[far, pl.ds(0, cut)]))
+    copies.append((far2_in, down_ref.at[far, pl.ds(cut, far2_in.shape[1])]))
     copies = fetch(copies, sems)
     copies[0].wait()
     copies[1].wait()
@@ -124,14 +128,16 @@
 
 
 def output_kernel(
-    link_ref, own_gate_in, own_up_in, other_gate_in, other_up_in, own_in, left_in, right_in, far_in,
+    link_ref, own_gate_in, own_up_in, other_gate_in, other_up_in,
+    gate0_in, gate1_in, gate2_in, gate3_in, up0_in, up1_in, up2_in, up3_in,
     own_ref, theirs_ref, gate_ref, up_ref, weight_ref, sems,
 ):
-    width = own_in.shape[0] // 2
+    width = gate0_in.shape[0]
     rows, hidden = own_gate_in.shape
     parts = sems.shape[0] - 1
     span = weight_ref.shape[1] // parts
-    own, left, right, far = spots(link_ref, width)
+    places = spots(link_ref, width)
+    gates, ups = (gate0_in, gate1_in, gate2_in, gate3_in), (up0_in, up1_in, up2_in, up3_in)
     begun = fetch(
         [
             (own_gate_in, gate_ref.at[pl.ds(0, rows), :]),
@@ -145,10 +151,10 @@
     for n in range(parts):
         columns = pl.ds(n * span, span)
         copies = []
-        for piece, place in ((own_in, own), (left_in, left), (right_in, right), (far_in, far)):
-            copies.append((piece.at[pl.ds(0, width), columns], weight_ref.at[place, columns]))
+        for gate_in, up_in, place in zip(gates, ups, places):
+            copies.append((gate_in.at[:, columns], weight_ref.at[place, columns]))
             lower = pl.ds(pl.multiple_of(place.start + hidden, 16), width)
-            copies.append((piece.at[pl.ds(width, width), columns], weight_ref.at[lower, columns]))
+            copies.append((up_in.at[:, columns], weight_ref.at[lower, columns]))
         blocks.append(fetch(copies, sems.at[n + 1]))
     for copy in begun:
         copy.wait()
@@ -231,10 +237,13 @@
     )
     arrived = exchange(packed)
 
-    pair = jnp.concatenate([w_gate[0], w_up[0]], axis=0)
-    pair_left, pair_right = along(pair, 1), along(pair, -1)
-    down_far = along(down_right, -1)
-    pair_far = along(pair_left, 1)
+    gate, up = w_gate[0], w_up[0]
+    gate_left, gate_right = along(gate, 1), along(gate, -1)
+    up_left, up_right = along(up, 1), along(up, -1)
+    cut = 3 * width // 4
+    down_far1 = along(down_left[:, :cut], 1)
+    down_far2 = along(down_right[:, cut:], -1)
+    gate_far, up_far = along(gate_left, 1), along(up_right, -1)
 
     link_at = (replica >> 1).reshape(1)
     core_at = (replica & 1).reshape(1)
@@ -242,7 +251,7 @@
     hidden_units = LINKS * slice_width
     sent = (across(saved[0]), across(saved[1]))
 
-    downs = (down, down_left, down_right, down_far)
+    downs = (down, down_left, down_right, down_far1, down_far2)
     hidden = jax.ShapeDtypeStruct((rows, hidden_units), BF16)
     cost = 2 * rows * hidden_units * width
     scratch = (
@@ -264,7 +273,7 @@
     own_hidden = hide(arrived, saved)
     other_hidden = hide(other_rows, sent)
 
-    pieces = (pair, pair_left, pair_right, pair_far)
+    pieces = (gate, gate_left, gate_right, gate_far, up, up_left, up_right, up_far)
     scratch2 = (
         pltpu.VMEM((2 * rows, hidden_units), BF16),
         pltpu.VMEM((2 * rows, hidden_units), BF16),

time: 195 us -> 173 us (0.89)
  waiting for transfers between devices: 111 us -> 82.7 us
  starting transfers between devices: 61.7 us -> 67.8 us
  local copies, waits for them, and re-layouts: 3.43 us -> 5.53 us
    ppermute x6 -> x10, waiting for transfers between devices: 65.1 us -> 26.9 us  [along(): return lax.ppermute(a, 'replica', pairs)]
    ppermute x6 -> x10, starting transfers between devices: 19.7 us -> 32.8 us  [along(): return lax.ppermute(a, 'replica', pairs)]
    all_to_all x2, waiting for transfers between devices: 43.9 us -> 53.6 us  [exchange(): return lax.all_to_all(a, 'expert', split_axis=0, concat_axis=0, tiled=True)]
    all_to_all x2, starting transfers between devices: 33.8 us -> 27.3 us  [exchange(): return lax.all_to_all(a, 'expert', split_axis=0, concat_axis=0, tiled=True)]
    unnamed x19 -> x23, local copies, waits for them, and re-layouts: 3.43 us -> 4.01 us
  transfers between devices with their start and end apart: 12 -> 16, of which waited for: 4 -> 7; matrix products, arithmetic and copies ran while one was open for 1% -> 1% of each run, Pallas kernels for 4% -> 4%
where the time goes in v4:
time: 173 us; the launch traced here: 172 us
  waiting for transfers between devices  82.7 us (48%)
  starting transfers between devices  67.8 us (39%)
  Pallas kernels  16 us (9%)
  local copies, waits for them, and re-layouts  5.53 us (3%)
    all_to_all x2, waiting for transfers between devices, exchange(): return lax.all_to_all(a, 'expert', split_axis=0, concat_axis=0, tiled=True)  53.6 us
    ppermute x10, starting transfers between devices, along(): return lax.ppermute(a, 'replica', pairs)  32.8 us
    all_to_all x2, starting transfers between devices, exchange(): return lax.all_to_all(a, 'expert', split_axis=0, concat_axis=0, tiled=True)  27.3 us
    ppermute x10, waiting for transfers between devices, along(): return lax.ppermute(a, 'replica', pairs)  26.9 us
    pallas_call x7, Pallas kernels, call(): pl.pallas_call(kernel, out_shape=outs[0] if single else tuple(outs), in_s...  16 us
    ppermute x4, starting transfers between devices, across(): return lax.ppermute(a, 'replica', [(i, i ^ 1) for i in range(copies)])  7.66 us
    unnamed x23, local copies, waits for them, and re-layouts  4.01 us
  transfers between devices with their start and end apart: 16, of which 7 were waited for; matrix products, arithmetic and copies ran while one was open for 1% of the time, Pallas kernels for 4%

profile of v4, /device:TPU:8, one launch (start us, length us, event | category | flops | bytes accessed | tf_op | source)
XLA Modules:
  0.0 172.4 jit_solution(9023545797089112602)
XLA Ops:
  0.0 0.9 copy-done.5
  0.9 0.7 copy-done.6
  1.6 0.7 copy-done.8
  2.3 1.6 shard_map.83
  3.9 18.9 %all-to-all-start = ((bf16[64,48,128]{2,1,0:T(8,128)(2,1)}), bf16[64,48,128]{2,1,0:T(8,128)(2,1)S(1)}, u32[]{:S(2)}, u32[]{:S(2)}) async-start(bf16[64,48,128]{2,1,0:T(8,128)(2,1)} %shard_map.83), calls=%async_computation | async-start | bytes 1572864 | tf_op jit(solution)/shard_map/all_to_all | solution.py:227
  22.8 3.4 %collective-permute-start = (bf16[176,2048]{1,0:T(8,128)(2,1)S(1)}, bf16[176,2048]{1,0:T(8,128)(2,1)S(1)}, u32[]{:S(2)}, u32[]{:S(2)}) collective-permute-start(bf16[176,2048]{1,0:T(8,128)(2,1)S(1)} %bitcast.17), channel_id=1, source_target_pairs={{0,2},{1,3},{2,4},{3,5},{4,6},{5,7},{6,0},{7,1},{8,10},{9,11},{10,... | collective-permute-start | bytes 2162696 | tf_op jit(solution)/shard_map/ppermute | solution.py:221
  26.2 3.7 %collective-permute-start.1 = (bf16[176,2048]{1,0:T(8,128)(2,1)S(1)}, bf16[176,2048]{1,0:T(8,128)(2,1)S(1)}, u32[]{:S(2)}, u32[]{:S(2)}) collective-permute-start(bf16[176,2048]{1,0:T(8,128)(2,1)S(1)} %bitcast.18), channel_id=1, source_target_pairs={{0,6},{1,7},{2,0},{3,1},{4,2},{5,3},{6,4},{7,5},{8,14},{9,15},{10,... | collective-permute-start | bytes 2162696 | tf_op jit(solution)/shard_map/ppermute | solution.py:221
  29.8 3.5 %collective-permute-start.11 = (bf16[176,2048]{1,0:T(8,128)(2,1)}, bf16[176,2048]{1,0:T(8,128)(2,1)}, u32[]{:S(2)}, u32[]{:S(2)}) collective-permute-start(bf16[176,2048]{1,0:T(8,128)(2,1)} %bitcast.26), channel_id=1, source_target_pairs={{0,6},{1,7},{2,0},{3,1},{4,2},{5,3},{6,4},{7,5},{8,14},{9,15},{10,... | collective-permute-start | bytes 2162696 | tf_op jit(solution)/shard_map/ppermute | solution.py:221
  33.3 2.4 %collective-permute-start.7 = (bf16[176,2048]{1,0:T(8,128)(2,1)}, bf16[176,2048]{1,0:T(8,128)(2,1)}, u32[]{:S(2)}, u32[]{:S(2)}) collective-permute-start(bf16[176,2048]{1,0:T(8,128)(2,1)} %bitcast.23), channel_id=1, source_target_pairs={{0,2},{1,3},{2,4},{3,5},{4,6},{5,7},{6,0},{7,1},{8,10},{9,11},{10,... | collective-permute-start | bytes 2162696 | tf_op jit(solution)/shard_map/ppermute | solution.py:221
  35.7 1.9 %collective-permute-start.5 = (bf16[192,1408]{1,0:T(8,128)(2,1)}, bf16[192,1408]{1,0:T(8,128)(2,1)S(1)}, u32[]{:S(2)}, u32[]{:S(2)}) collective-permute-start(bf16[192,1408]{1,0:T(8,128)(2,1)} %bitcast.7.saved_gate_in), channel_id=1, source_target_pairs={{0,1},{1,0},{2,3},{3,2},{4,5},{5,4},{6,7},{7,6},{8,9},{9,8},{10,11... | collective-permute-start | bytes 1622024 | tf_op jit(solution)/shard_map/ppermute | solution.py:224
  37.6 7.3 %collective-permute-done.left_in = bf16[176,2048]{1,0:T(8,128)(2,1)S(1)} collective-permute-done((bf16[176,2048]{1,0:T(8,128)(2,1)S(1)}, bf16[176,2048]{1,0:T(8,128)(2,1)S(1)}, u32[]{:S(2)}, u32[]{:S(2)}) %collective-permute-start) | collective-permute-done | bytes 720928 | tf_op jit(solution)/shard_map/ppermute | solution.py:221
  44.9 1.9 %collective-permute-start.6 = (bf16[192,1408]{1,0:T(8,128)(2,1)}, bf16[192,1408]{1,0:T(8,128)(2,1)S(1)}, u32[]{:S(2)}, u32[]{:S(2)}) collective-permute-start(bf16[192,1408]{1,0:T(8,128)(2,1)} %bitcast.10.saved_up_in), channel_id=1, source_target_pairs={{0,1},{1,0},{2,3},{3,2},{4,5},{5,4},{6,7},{7,6},{8,9},{9,8},{10,11... | collective-permute-start | bytes 1622024 | tf_op jit(solution)/shard_map/ppermute | solution.py:224
  46.8 0.8 slice.8
  47.6 0.0 collective-permute-done.1.right_in
  47.6 2.8 %collective-permute-start.2 = (bf16[176,1536]{1,0:T(8,128)(2,1)}, bf16[176,1536]{1,0:T(8,128)(2,1)S(1)}, u32[]{:S(2)}, u32[]{:S(2)}) collective-permute-start(bf16[176,1536]{1,0:T(8,128)(2,1)} %slice.8), channel_id=1, source_target_pairs={{0,2},{1,3},{2,4},{3,5},{4,6},{5,7},{6,0},{7,1},{8,10},{9,11},{10,... | collective-permute-start | bytes 1622024 | tf_op jit(solution)/shard_map/ppermute | solution.py:221
  50.5 0.7 slice.9
  51.2 0.0 collective-permute-done.5.saved_gate_in
  51.2 0.8 copy-done.1
  52.0 4.2 %collective-permute-start.3 = (bf16[176,512]{1,0:T(8,128)(2,1)}, bf16[176,512]{1,0:T(8,128)(2,1)}, u32[]{:S(2)}, u32[]{:S(2)}) collective-permute-start(bf16[176,512]{1,0:T(8,128)(2,1)} %slice.9), channel_id=1, source_target_pairs={{0,6},{1,7},{2,0},{3,1},{4,2},{5,3},{6,4},{7,5},{8,14},{9,15},{10,... | collective-permute-start | bytes 540680 | tf_op jit(solution)/shard_map/ppermute | solution.py:221
  56.2 0.0 collective-permute-done.6.saved_up_in
  56.2 0.8 copy-done.3
  57.0 9.7 %all-to-all-done.packed_in = bf16[64,48,128]{2,1,0:T(8,128)(2,1)S(1)} async-done(((bf16[64,48,128]{2,1,0:T(8,128)(2,1)}), bf16[64,48,128]{2,1,0:T(8,128)(2,1)S(1)}, u32[]{:S(2)}, u32[]{:S(2)}) %all-to-all-start) | async-done | bytes 786464 | tf_op jit(solution)/shard_map/all_to_all | solution.py:227
  66.7 1.9 %collective-permute-start.4 = (bf16[64,48,128]{2,1,0:T(8,128)(2,1)S(1)}, bf16[64,48,128]{2,1,0:T(8,128)(2,1)}, u32[]{:S(2)}, u32[]{:S(2)}) collective-permute-start(bf16[64,48,128]{2,1,0:T(8,128)(2,1)S(1)} %all-to-all-done.packed_in), channel_id=1, source_target_pairs={{0,1},{1,0},{2,3},{3,2},{4,5},{5,4},{6,7},{7,6},{8,9},{9,8},{10,11... | collective-permute-start | bytes 2359304 | tf_op jit(solution)/shard_map/ppermute | solution.py:224
  68.6 0.0 collective-permute-done.11.up2_in
  68.6 3.4 %collective-permute-start.10 = (bf16[176,2048]{1,0:T(8,128)(2,1)}, bf16[176,2048]{1,0:T(8,128)(2,1)}, u32[]{:S(2)}, u32[]{:S(2)}) collective-permute-start(bf16[176,2048]{1,0:T(8,128)(2,1)} %bitcast.27), channel_id=1, source_target_pairs={{0,2},{1,3},{2,4},{3,5},{4,6},{5,7},{6,0},{7,1},{8,10},{9,11},{10,... | collective-permute-start | bytes 2162696 | tf_op jit(solution)/shard_map/ppermute | solution.py:221
  72.0 0.0 collective-permute-done.7.gate1_in
  72.0 3.7 %collective-permute-start.8 = (bf16[176,2048]{1,0:T(8,128)(2,1)}, bf16[176,2048]{1,0:T(8,128)(2,1)}, u32[]{:S(2)}, u32[]{:S(2)}) collective-permute-start(bf16[176,2048]{1,0:T(8,128)(2,1)} %bitcast.24), channel_id=1, source_target_pairs={{0,6},{1,7},{2,0},{3,1},{4,2},{5,3},{6,4},{7,5},{8,14},{9,15},{10,... | collective-permute-start | bytes 2162696 | tf_op jit(solution)/shard_map/ppermute | solution.py:221
  75.7 0.0 collective-permute-done.3.far2_in
  75.7 3.5 %collective-permute-start.12 = (bf16[176,2048]{1,0:T(8,128)(2,1)}, bf16[176,2048]{1,0:T(8,128)(2,1)}, u32[]{:S(2)}, u32[]{:S(2)}) collective-permute-start(bf16[176,2048]{1,0:T(8,128)(2,1)} %collective-permute-done.11.up2_in), channel_id=1, source_target_pairs={{0,6},{1,7},{2,0},{3,1},{4,2},{5,3},{6,4},{7,5},{8,14},{9,15},{10,... | collective-permute-start | bytes 2162696 | tf_op jit(solution)/shard_map/ppermute | solution.py:221
  79.2 0.0 collective-permute-done.2.far1_in
  79.2 2.4 %collective-permute-start.9 = (bf16[176,2048]{1,0:T(8,128)(2,1)}, bf16[176,2048]{1,0:T(8,128)(2,1)}, u32[]{:S(2)}, u32[]{:S(2)}) collective-permute-start(bf16[176,2048]{1,0:T(8,128)(2,1)} %collective-permute-done.7.gate1_in), channel_id=1, source_target_pairs={{0,2},{1,3},{2,4},{3,5},{4,6},{5,7},{6,0},{7,1},{8,10},{9,11},{10,... | collective-permute-start | bytes 2162696 | tf_op jit(solution)/shard_map/ppermute | solution.py:221
  81.6 3.5 %shard_map.84 = (bf16[192,704]{1,0:T(8,128)(2,1)S(1)}, bf16[192,704]{1,0:T(8,128)(2,1)S(1)}) custom-call(s32[1]{0:T(128)} %bitcast.link_ref, s32[1]{0:T(128)} %bitcast.1.core_ref, bf16[64,48,128]{2,1,0:T(8,128)(2,1)S(1)} %all-to-all-done.packed_in, bf16[176,2048]{1,0:T(8,128)(2,1)S(1)} %bitcast.19, bf16[176,2048]{1,0:T(8,128)(2,1)S(1)} %collective-permute-done.left_in, ...), custom_call_target="tpu_custom_call" | custom-call | flops 553648128 | bytes 5292040 | tf_op jit(solution)/shard_map/pallas_call | solution.py:19
  85.1 0.0 copy-start.9
  85.1 0.0 copy-start.10
  85.1 3.2 %shard_map.85 = (bf16[192,704]{1,0:T(8,128)(2,1)S(1)}, bf16[192,704]{1,0:T(8,128)(2,1)S(1)}) custom-call(s32[1]{0:T(128)} %bitcast.link_ref, s32[1]{0:T(128)} %bitcast.1.core_ref, bf16[64,48,128]{2,1,0:T(8,128)(2,1)} %collective-permute-done.4.packed_in, bf16[176,2048]{1,0:T(8,128)(2,1)S(1)} %bitcast.20, bf16[176,2048]{1,0:T(8,128)(2,1)S(1)} %collective-permute-done.left_in, ...), custom_call_target="tpu_custom_call" | custom-call | flops 553648128 | bytes 5292040 | tf_op jit(solution)/shard_map/pallas_call | solution.py:19
  88.4 2.7 %collective-permute-done.10.up1_in = bf16[176,2048]{1,0:T(8,128)(2,1)} collective-permute-done((bf16[176,2048]{1,0:T(8,128)(2,1)}, bf16[176,2048]{1,0:T(8,128)(2,1)}, u32[]{:S(2)}, u32[]{:S(2)}) %collective-permute-start.10) | collective-permute-done | bytes 720928 | tf_op jit(solution)/shard_map/ppermute | solution.py:221
  91.1 2.2 %collective-permute-done.8.gate2_in = bf16[176,2048]{1,0:T(8,128)(2,1)} collective-permute-done((bf16[176,2048]{1,0:T(8,128)(2,1)}, bf16[176,2048]{1,0:T(8,128)(2,1)}, u32[]{:S(2)}, u32[]{:S(2)}) %collective-permute-start.8) | collective-permute-done | bytes 720928 | tf_op jit(solution)/shard_map/ppermute | solution.py:221
  93.3 14.7 %collective-permute-done.12.up3_in = bf16[176,2048]{1,0:T(8,128)(2,1)} collective-permute-done((bf16[176,2048]{1,0:T(8,128)(2,1)}, bf16[176,2048]{1,0:T(8,128)(2,1)}, u32[]{:S(2)}, u32[]{:S(2)}) %collective-permute-start.12) | collective-permute-done | bytes 720928 | tf_op jit(solution)/shard_map/ppermute | solution.py:221
  108.0 0.0 collective-permute-done.9.gate3_in
  108.0 5.1 %shard_map.86 = (bf16[192,2048]{1,0:T(8,128)(2,1)S(1)}, bf16[192,2048]{1,0:T(8,128)(2,1)S(1)}) custom-call(s32[1]{0:T(128)} %bitcast.link_ref, bf16[192,704]{1,0:T(8,128)(2,1)S(1)} %get-tuple-element.11.own_gate_in, bf16[192,704]{1,0:T(8,128)(2,1)S(1)} %get-tuple-element.12.own_up_in, bf16[192,704]{1,0:T(8,128)(2,1)S(1)} %get-tuple-element.13.other_gate_in, ...), custom_call_target="tpu_custom_call" | custom-call | flops 2214592512 | bytes 8421380 | tf_op jit(solution)/shard_map/pallas_call | solution.py:19
  113.1 1.9 %collective-permute-start.13 = (bf16[192,2048]{1,0:T(8,128)(2,1)S(1)}, bf16[192,2048]{1,0:T(8,128)(2,1)S(1)}, u32[]{:S(2)}, u32[]{:S(2)}) collective-permute-start(bf16[192,2048]{1,0:T(8,128)(2,1)S(1)} %get-tuple-element.16), channel_id=1, source_target_pairs={{0,1},{1,0},{2,3},{3,2},{4,5},{5,4},{6,7},{7,6},{8,9},{9,8},{10,11... | collective-permute-start | bytes 2359304 | tf_op jit(solution)/shard_map/ppermute | solution.py:224
  115.0 2.3 %collective-permute-done.13.back_ref = bf16[192,2048]{1,0:T(8,128)(2,1)S(1)} collective-permute-done((bf16[192,2048]{1,0:T(8,128)(2,1)S(1)}, bf16[192,2048]{1,0:T(8,128)(2,1)S(1)}, u32[]{:S(2)}, u32[]{:S(2)}) %collective-permute-start.13) | collective-permute-done | bytes 786464 | tf_op jit(solution)/shard_map/ppermute | solution.py:224
  117.3 1.3 shard_map.87
  118.6 8.5 %all-to-all-start.1 = ((bf16[64,48,128]{2,1,0:T(8,128)(2,1)}), bf16[64,48,128]{2,1,0:T(8,128)(2,1)S(1)}, u32[]{:S(2)}, u32[]{:S(2)}) async-start(bf16[64,48,128]{2,1,0:T(8,128)(2,1)} %shard_map.87), calls=%async_computation.1 | async-start | bytes 1572864 | tf_op jit(solution)/shard_map/all_to_all | solution.py:227
  127.0 0.1 copy.9.routes_ref
  127.1 0.2 shard_map.82.hot_ref
  127.4 43.9 %all-to-all-done.1.back_ref = bf16[64,48,128]{2,1,0:T(8,128)(2,1)S(1)} async-done(((bf16[64,48,128]{2,1,0:T(8,128)(2,1)}), bf16[64,48,128]{2,1,0:T(8,128)(2,1)S(1)}, u32[]{:S(2)}, u32[]{:S(2)}) %all-to-all-start.1) | async-done | bytes 786464 | tf_op jit(solution)/shard_map/all_to_all | solution.py:227
  171.3 1.1 shard_map.88
  (16 shorter events, 0.0 us)
Async XLA Ops:
  0.0 0.9 copy-start.5
  0.9 0.7 copy-start.6
  1.6 0.7 copy-start.8
  3.9 18.9 %copy-start = (bf16[1,176,2048]{2,1,0:T(8,128)(2,1)S(1)}, bf16[1,176,2048]{2,1,0:T(8,128)(2,1)}, u32[]{:S(2)}) copy-start(bf16[1,176,2048]{2,1,0:T(8,128)(2,1)} %param.13) | copy-start | bytes 2162692
  3.9 62.8 %all-to-all-start = ((bf16[64,48,128]{2,1,0:T(8,128)(2,1)}), bf16[64,48,128]{2,1,0:T(8,128)(2,1)S(1)}, u32[]{:S(2)}, u32[]{:S(2)}) async-start(bf16[64,48,128]{2,1,0:T(8,128)(2,1)} %shard_map.83), calls=%async_computation | async-start | bytes 1572864 | tf_op jit(solution)/shard_map/all_to_all | solution.py:227
  22.8 22.1 %collective-permute-start = (bf16[176,2048]{1,0:T(8,128)(2,1)S(1)}, bf16[176,2048]{1,0:T(8,128)(2,1)S(1)}, u32[]{:S(2)}, u32[]{:S(2)}) collective-permute-start(bf16[176,2048]{1,0:T(8,128)(2,1)S(1)} %bitcast.17), channel_id=1, source_target_pairs={{0,2},{1,3},{2,4},{3,5},{4,6},{5,7},{6,0},{7,1},{8,10},{9,11},{10,... | collective-permute-start | bytes 2162696 | tf_op jit(solution)/shard_map/ppermute | solution.py:221
  26.2 21.5 %collective-permute-start.1 = (bf16[176,2048]{1,0:T(8,128)(2,1)S(1)}, bf16[176,2048]{1,0:T(8,128)(2,1)S(1)}, u32[]{:S(2)}, u32[]{:S(2)}) collective-permute-start(bf16[176,2048]{1,0:T(8,128)(2,1)S(1)} %bitcast.18), channel_id=1, source_target_pairs={{0,6},{1,7},{2,0},{3,1},{4,2},{5,3},{6,4},{7,5},{8,14},{9,15},{10,... | collective-permute-start | bytes 2162696 | tf_op jit(solution)/shard_map/ppermute | solution.py:221
  29.8 38.8 %collective-permute-start.11 = (bf16[176,2048]{1,0:T(8,128)(2,1)}, bf16[176,2048]{1,0:T(8,128)(2,1)}, u32[]{:S(2)}, u32[]{:S(2)}) collective-permute-start(bf16[176,2048]{1,0:T(8,128)(2,1)} %bitcast.26), channel_id=1, source_target_pairs={{0,6},{1,7},{2,0},{3,1},{4,2},{5,3},{6,4},{7,5},{8,14},{9,15},{10,... | collective-permute-start | bytes 2162696 | tf_op jit(solution)/shard_map/ppermute | solution.py:221
  33.3 38.7 %collective-permute-start.7 = (bf16[176,2048]{1,0:T(8,128)(2,1)}, bf16[176,2048]{1,0:T(8,128)(2,1)}, u32[]{:S(2)}, u32[]{:S(2)}) collective-permute-start(bf16[176,2048]{1,0:T(8,128)(2,1)} %bitcast.23), channel_id=1, source_target_pairs={{0,2},{1,3},{2,4},{3,5},{4,6},{5,7},{6,0},{7,1},{8,10},{9,11},{10,... | collective-permute-start | bytes 2162696 | tf_op jit(solution)/shard_map/ppermute | solution.py:221
  35.7 15.5 %collective-permute-start.5 = (bf16[192,1408]{1,0:T(8,128)(2,1)}, bf16[192,1408]{1,0:T(8,128)(2,1)S(1)}, u32[]{:S(2)}, u32[]{:S(2)}) collective-permute-start(bf16[192,1408]{1,0:T(8,128)(2,1)} %bitcast.7.saved_gate_in), channel_id=1, source_target_pairs={{0,1},{1,0},{2,3},{3,2},{4,5},{5,4},{6,7},{7,6},{8,9},{9,8},{10,11... | collective-permute-start | bytes 1622024 | tf_op jit(solution)/shard_map/ppermute | solution.py:224
  44.9 11.3 %collective-permute-start.6 = (bf16[192,1408]{1,0:T(8,128)(2,1)}, bf16[192,1408]{1,0:T(8,128)(2,1)S(1)}, u32[]{:S(2)}, u32[]{:S(2)}) collective-permute-start(bf16[192,1408]{1,0:T(8,128)(2,1)} %bitcast.10.saved_up_in), channel_id=1, source_target_pairs={{0,1},{1,0},{2,3},{3,2},{4,5},{5,4},{6,7},{7,6},{8,9},{9,8},{10,11... | collective-permute-start | bytes 1622024 | tf_op jit(solution)/shard_map/ppermute | solution.py:224
  47.6 31.5 %collective-permute-start.2 = (bf16[176,1536]{1,0:T(8,128)(2,1)}, bf16[176,1536]{1,0:T(8,128)(2,1)S(1)}, u32[]{:S(2)}, u32[]{:S(2)}) collective-permute-start(bf16[176,1536]{1,0:T(8,128)(2,1)} %slice.8), channel_id=1, source_target_pairs={{0,2},{1,3},{2,4},{3,5},{4,6},{5,7},{6,0},{7,1},{8,10},{9,11},{10,... | collective-permute-start | bytes 1622024 | tf_op jit(solution)/shard_map/ppermute | solution.py:221
  51.2 0.8 copy-start.1
  52.0 23.7 %collective-permute-start.3 = (bf16[176,512]{1,0:T(8,128)(2,1)}, bf16[176,512]{1,0:T(8,128)(2,1)}, u32[]{:S(2)}, u32[]{:S(2)}) collective-permute-start(bf16[176,512]{1,0:T(8,128)(2,1)} %slice.9), channel_id=1, source_target_pairs={{0,6},{1,7},{2,0},{3,1},{4,2},{5,3},{6,4},{7,5},{8,14},{9,15},{10,... | collective-permute-start | bytes 540680 | tf_op jit(solution)/shard_map/ppermute | solution.py:221
  56.2 0.8 copy-start.3
  66.7 18.4 %collective-permute-start.4 = (bf16[64,48,128]{2,1,0:T(8,128)(2,1)S(1)}, bf16[64,48,128]{2,1,0:T(8,128)(2,1)}, u32[]{:S(2)}, u32[]{:S(2)}) collective-permute-start(bf16[64,48,128]{2,1,0:T(8,128)(2,1)S(1)} %all-to-all-done.packed_in), channel_id=1, source_target_pairs={{0,1},{1,0},{2,3},{3,2},{4,5},{5,4},{6,7},{7,6},{8,9},{9,8},{10,11... | collective-permute-start | bytes 2359304 | tf_op jit(solution)/shard_map/ppermute | solution.py:224
  68.6 22.4 %collective-permute-start.10 = (bf16[176,2048]{1,0:T(8,128)(2,1)}, bf16[176,2048]{1,0:T(8,128)(2,1)}, u32[]{:S(2)}, u32[]{:S(2)}) collective-permute-start(bf16[176,2048]{1,0:T(8,128)(2,1)} %bitcast.27), channel_id=1, source_target_pairs={{0,2},{1,3},{2,4},{3,5},{4,6},{5,7},{6,0},{7,1},{8,10},{9,11},{10,... | collective-permute-start | bytes 2162696 | tf_op jit(solution)/shard_map/ppermute | solution.py:221
  72.0 21.2 %collective-permute-start.8 = (bf16[176,2048]{1,0:T(8,128)(2,1)}, bf16[176,2048]{1,0:T(8,128)(2,1)}, u32[]{:S(2)}, u32[]{:S(2)}) collective-permute-start(bf16[176,2048]{1,0:T(8,128)(2,1)} %bitcast.24), channel_id=1, source_target_pairs={{0,6},{1,7},{2,0},{3,1},{4,2},{5,3},{6,4},{7,5},{8,14},{9,15},{10,... | collective-permute-start | bytes 2162696 | tf_op jit(solution)/shard_map/ppermute | solution.py:221
  75.7 32.2 %collective-permute-start.12 = (bf16[176,2048]{1,0:T(8,128)(2,1)}, bf16[176,2048]{1,0:T(8,128)(2,1)}, u32[]{:S(2)}, u32[]{:S(2)}) collective-permute-start(bf16[176,2048]{1,0:T(8,128)(2,1)} %collective-permute-done.11.up2_in), channel_id=1, source_target_pairs={{0,6},{1,7},{2,0},{3,1},{4,2},{5,3},{6,4},{7,5},{8,14},{9,15},{10,... | collective-permute-start | bytes 2162696 | tf_op jit(solution)/shard_map/ppermute | solution.py:221
  79.2 28.8 %collective-permute-start.9 = (bf16[176,2048]{1,0:T(8,128)(2,1)}, bf16[176,2048]{1,0:T(8,128)(2,1)}, u32[]{:S(2)}, u32[]{:S(2)}) collective-permute-start(bf16[176,2048]{1,0:T(8,128)(2,1)} %collective-permute-done.7.gate1_in), channel_id=1, source_target_pairs={{0,2},{1,3},{2,4},{3,5},{4,6},{5,7},{6,0},{7,1},{8,10},{9,11},{10,... | collective-permute-start | bytes 2162696 | tf_op jit(solution)/shard_map/ppermute | solution.py:221
  81.6 3.5 %copy-start.2 = (bf16[192,1408]{1,0:T(8,128)(2,1)S(1)}, bf16[192,1408]{1,0:T(8,128)(2,1)}, u32[]{:S(2)}) copy-start(bf16[192,1408]{1,0:T(8,128)(2,1)} %copy-done.1) | copy-start | bytes 1622020
  81.6 3.5 %copy-start.4 = (bf16[192,1408]{1,0:T(8,128)(2,1)S(1)}, bf16[192,1408]{1,0:T(8,128)(2,1)}, u32[]{:S(2)}) copy-start(bf16[192,1408]{1,0:T(8,128)(2,1)} %copy-done.3) | copy-start | bytes 1622020
  85.1 22.9 %copy-start.9 = (bf16[1,176,2048]{2,1,0:T(8,128)(2,1)S(1)}, bf16[1,176,2048]{2,1,0:T(8,128)(2,1)}, u32[]{:S(2)}) copy-start(bf16[1,176,2048]{2,1,0:T(8,128)(2,1)} %param.11) | copy-start | bytes 2162692
  85.1 22.9 %copy-start.10 = (bf16[1,176,2048]{2,1,0:T(8,128)(2,1)S(1)}, bf16[1,176,2048]{2,1,0:T(8,128)(2,1)}, u32[]{:S(2)}) copy-start(bf16[1,176,2048]{2,1,0:T(8,128)(2,1)} %param.12) | copy-start | bytes 2162692
  113.1 4.2 %collective-permute-start.13 = (bf16[192,2048]{1,0:T(8,128)(2,1)S(1)}, bf16[192,2048]{1,0:T(8,128)(2,1)S(1)}, u32[]{:S(2)}, u32[]{:S(2)}) collective-permute-start(bf16[192,2048]{1,0:T(8,128)(2,1)S(1)} %get-tuple-element.16), channel_id=1, source_target_pairs={{0,1},{1,0},{2,3},{3,2},{4,5},{5,4},{6,7},{7,6},{8,9},{9,8},{10,11... | collective-permute-start | bytes 2359304 | tf_op jit(solution)/shard_map/ppermute | solution.py:224
  118.6 8.5 %copy-start.7 = (s32[32,6]{0,1:T(8,128)S(1)}, s32[32,6]{0,1:T(8,128)}, u32[]{:S(2)}) copy-start(s32[32,6]{0,1:T(8,128)} %param.9) | copy-start | bytes 2308
  118.6 52.7 %all-to-all-start.1 = ((bf16[64,48,128]{2,1,0:T(8,128)(2,1)}), bf16[64,48,128]{2,1,0:T(8,128)(2,1)S(1)}, u32[]{:S(2)}, u32[]{:S(2)}) async-start(bf16[64,48,128]{2,1,0:T(8,128)(2,1)} %shard_map.87), calls=%async_computation.1 | async-start | bytes 1572864 | tf_op jit(solution)/shard_map/all_to_all | solution.py:227

commit v5 on v4

--- a/solution.py
+++ b/solution.py
@@ -91,24 +91,21 @@
         gf_ref[:, place] = u * sig * (1.0 + g * (1.0 - sig))
 
 
-def spots(link_ref, width):
-    link = link_ref[0]
-    steps = (0, LINKS - 1, 1, 2)
-    return [pl.ds(pl.multiple_of(((link + by) & (LINKS - 1)) * width, 16), width) for by in steps]
+def spots(link_ref, core_ref, width):
+    link, turn = link_ref[0], 2 * core_ref[0] - 1
+    steps = [(link + step * turn + LINKS) & (LINKS - 1) for step in range(LINKS)]
+    return [pl.ds(pl.multiple_of(step * width, 16), width) for step in steps]
 
 
 def hidden_kernel(
-    link_ref, core_ref, packed_in, own_in, left_in, right_in, far1_in, far2_in, saved_gate_in, saved_up_in,
+    link_ref, core_ref, packed_in, down0_in, down1_in, down2_in, down3_in, saved_gate_in, saved_up_in,
     gate_ref, up_ref, packed_ref, down_ref, saved_gate_ref, saved_up_ref, gf_ref, uf_ref, rows_ref, sems,
 ):
-    width = own_in.shape[0]
+    width = down0_in.shape[0]
     copies = [(saved_gate_in, saved_gate_ref), (saved_up_in, saved_up_ref), (packed_in, packed_ref)]
-    own, left, right, far = spots(link_ref, width)
-    for piece, place in ((own_in, own), (left_in, left), (right_in, right)):
+    downs = (down0_in, down1_in, down2_in, down3_in)
+    for piece, place in zip(downs, spots(link_ref, core_ref, width)):
         copies.append((piece, down_ref.at[place, :]))
-    cut = far1_in.shape[1]
-    copies.append((far1_in, down_ref.at[far, pl.ds(0, cut)]))
-    copies.append((far2_in, down_ref.at[far, pl.ds(cut, far2_in.shape[1])]))
     copies = fetch(copies, sems)
     copies[0].wait()
     copies[1].wait()
@@ -128,7 +125,7 @@
 
 
 def output_kernel(
-    link_ref, own_gate_in, own_up_in, other_gate_in, other_up_in,
+    link_ref, core_ref, own_gate_in, own_up_in, other_gate_in, other_up_in,
     gate0_in, gate1_in, gate2_in, gate3_in, up0_in, up1_in, up2_in, up3_in,
     own_ref, theirs_ref, gate_ref, up_ref, weight_ref, sems,
 ):
@@ -136,7 +133,7 @@
     rows, hidden = own_gate_in.shape
     parts = sems.shape[0] - 1
     span = weight_ref.shape[1] // parts
-    places = spots(link_ref, width)
+    places = spots(link_ref, core_ref, width)
     gates, ups = (gate0_in, gate1_in, gate2_in, gate3_in), (up0_in, up1_in, up2_in, up3_in)
     begun = fetch(
         [
@@ -216,8 +213,8 @@
     deep = slots * chunks
     replica = lax.axis_index("replica")
 
-    def along(a, by):
-        pairs = [(2 * i + k, 2 * ((i + by) % LINKS) + k) for i in range(LINKS) for k in range(2)]
+    def along(a):
+        pairs = [(2 * i + k, 2 * ((i + 1 - 2 * k) % LINKS) + k) for i in range(LINKS) for k in range(2)]
         return lax.ppermute(a, "replica", pairs)
 
     def across(a):
@@ -226,24 +223,19 @@
     def exchange(a):
         return lax.all_to_all(a, "expert", split_axis=0, concat_axis=0, tiled=True)
 
-    down = w_down[0]
-    down_left, down_right = along(down, 1), along(down, -1)
+    downs, gate_pieces, up_pieces = [w_down[0]], [w_gate[0]], [w_up[0]]
+    for _ in range(1, LINKS):
+        for pieces in (downs, gate_pieces, up_pieces):
+            pieces.append(along(pieces[-1]))
 
     packed = call(
         place_kernel,
         (routes.T, gates.T, grad_out),
         (jax.ShapeDtypeStruct((experts, 2 * deep, 128), BF16),),
         2 * rows * tokens * width,
+        limit=60 << 20,
     )
     arrived = exchange(packed)
-
-    gate, up = w_gate[0], w_up[0]
-    gate_left, gate_right = along(gate, 1), along(gate, -1)
-    up_left, up_right = along(up, 1), along(up, -1)
-    cut = 3 * width // 4
-    down_far1 = along(down_left[:, :cut], 1)
-    down_far2 = along(down_right[:, cut:], -1)
-    gate_far, up_far = along(gate_left, 1), along(up_right, -1)
 
     link_at = (replica >> 1).reshape(1)
     core_at = (replica & 1).reshape(1)
@@ -251,7 +243,6 @@
     hidden_units = LINKS * slice_width
     sent = (across(saved[0]), across(saved[1]))
 
-    downs = (down, down_left, down_right, down_far1, down_far2)
     hidden = jax.ShapeDtypeStruct((rows, hidden_units), BF16)
     cost = 2 * rows * hidden_units * width
     scratch = (
@@ -267,13 +258,13 @@
     other_rows = across(arrived)
 
     def hide(packed_rows, kept):
-        ins = (link_at, core_at, packed_rows) + downs + tuple(kept)
+        ins = (link_at, core_at, packed_rows) + tuple(downs) + tuple(kept)
         return call(hidden_kernel, ins, (hidden, hidden), cost, 2, scratch, pl.BlockSpec(memory_space=pl.ANY))
 
     own_hidden = hide(arrived, saved)
     other_hidden = hide(other_rows, sent)
 
-    pieces = (gate, gate_left, gate_right, gate_far, up, up_left, up_right, up_far)
+    pieces = tuple(gate_pieces + up_pieces)
     scratch2 = (
         pltpu.VMEM((2 * rows, hidden_units), BF16),
         pltpu.VMEM((2 * rows, hidden_units), BF16),
@@ -283,10 +274,10 @@
     part = jax.ShapeDtypeStruct((rows, width), BF16)
     ours, theirs = call(
         output_kernel,
-        (link_at,) + tuple(own_hidden) + tuple(other_hidden) + pieces,
+        (link_at, core_at) + tuple(own_hidden) + tuple(other_hidden) + pieces,
         (part, part),
         4 * cost,
-        1,
+        2,
         scratch2,
         pl.BlockSpec(memory_space=pl.ANY),
     )

time: 173 us -> 170 us (0.983)
  local copies, waits for them, and re-layouts: 5.53 us -> 1.14 us
    ppermute x10 -> x9, starting transfers between devices: 32.8 us -> 24.2 us  [along(): return lax.ppermute(a, 'replica', pairs)]
    ppermute x10 -> x9, waiting for transfers between devices: 26.9 us -> 34 us  [along(): return lax.ppermute(a, 'replica', pairs)]
    all_to_all x2, starting transfers between devices: 27.3 us -> 34.1 us  [exchange(): return lax.all_to_all(a, 'expert', split_axis=0, concat_axis=0, tiled=True)]
    all_to_all x2, waiting for transfers between devices: 53.6 us -> 48.1 us  [exchange(): return lax.all_to_all(a, 'expert', split_axis=0, concat_axis=0, tiled=True)]
    unnamed x23 -> x9, local copies, waits for them, and re-layouts: 4.01 us -> 1.14 us
  transfers between devices with their start and end apart: 16 -> 15, of which waited for: 7 -> 10; matrix products, arithmetic and copies ran while one was open for 1% -> 0% of each run, Pallas kernels for 4% -> 4%
where the time goes in v5:
time: 170 us; the launch traced here: 169 us
  waiting for transfers between devices  84.4 us (50%)
  starting transfers between devices  66.2 us (39%)
  Pallas kernels  16.9 us (10%)
    all_to_all x2, waiting for transfers between devices, exchange(): return lax.all_to_all(a, 'expert', split_axis=0, concat_axis=0, tiled=True)  48.1 us
    all_to_all x2, starting transfers between devices, exchange(): return lax.all_to_all(a, 'expert', split_axis=0, concat_axis=0, tiled=True)  34.1 us
    ppermute x9, waiting for transfers between devices, along(): return lax.ppermute(a, 'replica', pairs)  34 us
    ppermute x9, starting transfers between devices, along(): return lax.ppermute(a, 'replica', pairs)  24.2 us
    pallas_call x7, Pallas kernels, call(): pl.pallas_call(kernel, out_shape=outs[0] if single else tuple(outs), in_s...  16.9 us
    ppermute x4, starting transfers between devices, across(): return lax.ppermute(a, 'replica', [(i, i ^ 1) for i in range(copies)])  7.98 us
  transfers between devices with their start and end apart: 15, of which 10 were waited for; matrix products, arithmetic and copies ran while one was open for 0% of the time, Pallas kernels for 4%

profile of v5, /device:TPU:8, one launch (start us, length us, event | category | flops | bytes accessed | tf_op | source)
XLA Modules:
  0.0 168.9 jit_solution(4828696408632393838)
XLA Ops:
  0.0 2.5 %shard_map.83 = bf16[64,48,128]{2,1,0:T(8,128)(2,1)} custom-call(s32[6,32]{1,0:T(8,128)} %bitcast.24, f32[6,32]{1,0:T(8,128)} %bitcast.25, bf16[32,2048]{1,0:T(8,128)(2,1)} %grad_ref.1), custom_call_target="tpu_custom_call" | custom-call | flops 25165824 | bytes 919040 | tf_op jit(solution)/shard_map/pallas_call | solution.py:19
  2.5 0.0 copy-start
  2.5 0.0 copy-start.1
  2.5 18.9 %all-to-all-start = ((bf16[64,48,128]{2,1,0:T(8,128)(2,1)}), bf16[64,48,128]{2,1,0:T(8,128)(2,1)S(1)}, u32[]{:S(2)}, u32[]{:S(2)}) async-start(bf16[64,48,128]{2,1,0:T(8,128)(2,1)} %shard_map.83), calls=%async_computation | async-start | bytes 1572864 | tf_op jit(solution)/shard_map/all_to_all | solution.py:224
  21.4 0.0 copy-done
  21.4 3.4 %collective-permute-start = (bf16[176,2048]{1,0:T(8,128)(2,1)S(1)}, bf16[176,2048]{1,0:T(8,128)(2,1)S(1)}, u32[]{:S(2)}, u32[]{:S(2)}) collective-permute-start(bf16[176,2048]{1,0:T(8,128)(2,1)S(1)} %bitcast.17), channel_id=1, source_target_pairs={{0,2},{1,7},{2,4},{3,1},{4,6},{5,3},{6,0},{7,5},{8,10},{9,15},{10,... | collective-permute-start | bytes 2162696 | tf_op jit(solution)/shard_map/ppermute | solution.py:218
  24.8 3.4 %collective-permute-start.9 = (bf16[176,2048]{1,0:T(8,128)(2,1)}, bf16[176,2048]{1,0:T(8,128)(2,1)}, u32[]{:S(2)}, u32[]{:S(2)}) collective-permute-start(bf16[176,2048]{1,0:T(8,128)(2,1)} %bitcast.16.up0_in), channel_id=1, source_target_pairs={{0,2},{1,7},{2,4},{3,1},{4,6},{5,3},{6,0},{7,5},{8,10},{9,15},{10,... | collective-permute-start | bytes 2162696 | tf_op jit(solution)/shard_map/ppermute | solution.py:218
  28.2 3.1 %collective-permute-start.6 = (bf16[176,2048]{1,0:T(8,128)(2,1)}, bf16[176,2048]{1,0:T(8,128)(2,1)}, u32[]{:S(2)}, u32[]{:S(2)}) collective-permute-start(bf16[176,2048]{1,0:T(8,128)(2,1)} %bitcast.15.gate0_in), channel_id=1, source_target_pairs={{0,2},{1,7},{2,4},{3,1},{4,6},{5,3},{6,0},{7,5},{8,10},{9,15},{10,... | collective-permute-start | bytes 2162696 | tf_op jit(solution)/shard_map/ppermute | solution.py:218
  31.3 4.5 %collective-permute-done.down1_in = bf16[176,2048]{1,0:T(8,128)(2,1)S(1)} collective-permute-done((bf16[176,2048]{1,0:T(8,128)(2,1)S(1)}, bf16[176,2048]{1,0:T(8,128)(2,1)S(1)}, u32[]{:S(2)}, u32[]{:S(2)}) %collective-permute-start) | collective-permute-done | bytes 720928 | tf_op jit(solution)/shard_map/ppermute | solution.py:218
  35.8 2.2 %collective-permute-start.1 = (bf16[176,2048]{1,0:T(8,128)(2,1)S(1)}, bf16[176,2048]{1,0:T(8,128)(2,1)S(1)}, u32[]{:S(2)}, u32[]{:S(2)}) collective-permute-start(bf16[176,2048]{1,0:T(8,128)(2,1)S(1)} %collective-permute-done.down1_in), channel_id=1, source_target_pairs={{0,2},{1,7},{2,4},{3,1},{4,6},{5,3},{6,0},{7,5},{8,10},{9,15},{10,... | collective-permute-start | bytes 2162696 | tf_op jit(solution)/shard_map/ppermute | solution.py:218
  38.0 5.6 %collective-permute-done.9.up1_in = bf16[176,2048]{1,0:T(8,128)(2,1)} collective-permute-done((bf16[176,2048]{1,0:T(8,128)(2,1)}, bf16[176,2048]{1,0:T(8,128)(2,1)}, u32[]{:S(2)}, u32[]{:S(2)}) %collective-permute-start.9) | collective-permute-done | bytes 720928 | tf_op jit(solution)/shard_map/ppermute | solution.py:218
  43.6 2.2 %collective-permute-start.10 = (bf16[176,2048]{1,0:T(8,128)(2,1)}, bf16[176,2048]{1,0:T(8,128)(2,1)}, u32[]{:S(2)}, u32[]{:S(2)}) collective-permute-start(bf16[176,2048]{1,0:T(8,128)(2,1)} %collective-permute-done.9.up1_in), channel_id=1, source_target_pairs={{0,2},{1,7},{2,4},{3,1},{4,6},{5,3},{6,0},{7,5},{8,10},{9,15},{10,... | collective-permute-start | bytes 2162696 | tf_op jit(solution)/shard_map/ppermute | solution.py:218
  45.8 5.5 %collective-permute-done.6.gate1_in = bf16[176,2048]{1,0:T(8,128)(2,1)} collective-permute-done((bf16[176,2048]{1,0:T(8,128)(2,1)}, bf16[176,2048]{1,0:T(8,128)(2,1)}, u32[]{:S(2)}, u32[]{:S(2)}) %collective-permute-start.6) | collective-permute-done | bytes 720928 | tf_op jit(solution)/shard_map/ppermute | solution.py:218
  51.3 2.2 %collective-permute-start.7 = (bf16[176,2048]{1,0:T(8,128)(2,1)}, bf16[176,2048]{1,0:T(8,128)(2,1)}, u32[]{:S(2)}, u32[]{:S(2)}) collective-permute-start(bf16[176,2048]{1,0:T(8,128)(2,1)} %collective-permute-done.6.gate1_in), channel_id=1, source_target_pairs={{0,2},{1,7},{2,4},{3,1},{4,6},{5,3},{6,0},{7,5},{8,10},{9,15},{10,... | collective-permute-start | bytes 2162696 | tf_op jit(solution)/shard_map/ppermute | solution.py:218
  53.5 5.4 %collective-permute-done.1.down2_in = bf16[176,2048]{1,0:T(8,128)(2,1)S(1)} collective-permute-done((bf16[176,2048]{1,0:T(8,128)(2,1)S(1)}, bf16[176,2048]{1,0:T(8,128)(2,1)S(1)}, u32[]{:S(2)}, u32[]{:S(2)}) %collective-permute-start.1) | collective-permute-done | bytes 720928 | tf_op jit(solution)/shard_map/ppermute | solution.py:218
  59.0 2.2 %collective-permute-start.2 = (bf16[176,2048]{1,0:T(8,128)(2,1)S(1)}, bf16[176,2048]{1,0:T(8,128)(2,1)}, u32[]{:S(2)}, u32[]{:S(2)}) collective-permute-start(bf16[176,2048]{1,0:T(8,128)(2,1)S(1)} %collective-permute-done.1.down2_in), channel_id=1, source_target_pairs={{0,2},{1,7},{2,4},{3,1},{4,6},{5,3},{6,0},{7,5},{8,10},{9,15},{10,... | collective-permute-start | bytes 2162696 | tf_op jit(solution)/shard_map/ppermute | solution.py:218
  61.2 4.2 %all-to-all-done.packed_in = bf16[64,48,128]{2,1,0:T(8,128)(2,1)S(1)} async-done(((bf16[64,48,128]{2,1,0:T(8,128)(2,1)}), bf16[64,48,128]{2,1,0:T(8,128)(2,1)S(1)}, u32[]{:S(2)}, u32[]{:S(2)}) %all-to-all-start) | async-done | bytes 786464 | tf_op jit(solution)/shard_map/all_to_all | solution.py:224
  65.3 1.9 %collective-permute-start.3 = (bf16[64,48,128]{2,1,0:T(8,128)(2,1)S(1)}, bf16[64,48,128]{2,1,0:T(8,128)(2,1)}, u32[]{:S(2)}, u32[]{:S(2)}) collective-permute-start(bf16[64,48,128]{2,1,0:T(8,128)(2,1)S(1)} %all-to-all-done.packed_in), channel_id=1, source_target_pairs={{0,1},{1,0},{2,3},{3,2},{4,5},{5,4},{6,7},{7,6},{8,9},{9,8},{10,11... | collective-permute-start | bytes 2359304 | tf_op jit(solution)/shard_map/ppermute | solution.py:221
  67.2 0.0 collective-permute-done.10.up2_in
  67.3 3.4 %collective-permute-start.11 = (bf16[176,2048]{1,0:T(8,128)(2,1)}, bf16[176,2048]{1,0:T(8,128)(2,1)}, u32[]{:S(2)}, u32[]{:S(2)}) collective-permute-start(bf16[176,2048]{1,0:T(8,128)(2,1)} %collective-permute-done.10.up2_in), channel_id=1, source_target_pairs={{0,2},{1,7},{2,4},{3,1},{4,6},{5,3},{6,0},{7,5},{8,10},{9,15},{10,... | collective-permute-start | bytes 2162696 | tf_op jit(solution)/shard_map/ppermute | solution.py:218
  70.7 3.9 %collective-permute-done.7.gate2_in = bf16[176,2048]{1,0:T(8,128)(2,1)} collective-permute-done((bf16[176,2048]{1,0:T(8,128)(2,1)}, bf16[176,2048]{1,0:T(8,128)(2,1)}, u32[]{:S(2)}, u32[]{:S(2)}) %collective-permute-start.7) | collective-permute-done | bytes 720928 | tf_op jit(solution)/shard_map/ppermute | solution.py:218
  74.5 2.2 %collective-permute-start.8 = (bf16[176,2048]{1,0:T(8,128)(2,1)}, bf16[176,2048]{1,0:T(8,128)(2,1)}, u32[]{:S(2)}, u32[]{:S(2)}) collective-permute-start(bf16[176,2048]{1,0:T(8,128)(2,1)} %collective-permute-done.7.gate2_in), channel_id=1, source_target_pairs={{0,2},{1,7},{2,4},{3,1},{4,6},{5,3},{6,0},{7,5},{8,10},{9,15},{10,... | collective-permute-start | bytes 2162696 | tf_op jit(solution)/shard_map/ppermute | solution.py:218
  76.7 0.0 copy-done.1
  76.7 2.2 %collective-permute-start.4 = (bf16[192,1408]{1,0:T(8,128)(2,1)S(1)}, bf16[192,1408]{1,0:T(8,128)(2,1)}, u32[]{:S(2)}, u32[]{:S(2)}) collective-permute-start(bf16[192,1408]{1,0:T(8,128)(2,1)S(1)} %bitcast.20), channel_id=1, source_target_pairs={{0,1},{1,0},{2,3},{3,2},{4,5},{5,4},{6,7},{7,6},{8,9},{9,8},{10,11... | collective-permute-start | bytes 1622024 | tf_op jit(solution)/shard_map/ppermute | solution.py:221
  79.0 3.3 %collective-permute-done.2.down3_in = bf16[176,2048]{1,0:T(8,128)(2,1)} collective-permute-done((bf16[176,2048]{1,0:T(8,128)(2,1)S(1)}, bf16[176,2048]{1,0:T(8,128)(2,1)}, u32[]{:S(2)}, u32[]{:S(2)}) %collective-permute-start.2) | collective-permute-done | bytes 720928 | tf_op jit(solution)/shard_map/ppermute | solution.py:218
  82.2 1.9 %collective-permute-start.5 = (bf16[192,1408]{1,0:T(8,128)(2,1)}, bf16[192,1408]{1,0:T(8,128)(2,1)}, u32[]{:S(2)}, u32[]{:S(2)}) collective-permute-start(bf16[192,1408]{1,0:T(8,128)(2,1)} %bitcast.22), channel_id=1, source_target_pairs={{0,1},{1,0},{2,3},{3,2},{4,5},{5,4},{6,7},{7,6},{8,9},{9,8},{10,11... | collective-permute-start | bytes 1622024 | tf_op jit(solution)/shard_map/ppermute | solution.py:221
  84.2 0.0 copy-start.2
  84.2 1.0 copy-done.2
  85.2 3.2 %shard_map.84 = (bf16[192,704]{1,0:T(8,128)(2,1)S(1)}, bf16[192,704]{1,0:T(8,128)(2,1)S(1)}) custom-call(s32[1]{0:T(128)} %bitcast.link_ref, s32[1]{0:T(128)} %bitcast.1.core_ref, bf16[64,48,128]{2,1,0:T(8,128)(2,1)S(1)} %all-to-all-done.packed_in, bf16[176,2048]{1,0:T(8,128)(2,1)S(1)} %bitcast.18, bf16[176,2048]{1,0:T(8,128)(2,1)S(1)} %collective-permute-done.down1_in, ...), custom_call_target="tpu_custom_call" | custom-call | flops 553648128 | bytes 5292040 | tf_op jit(solution)/shard_map/pallas_call | solution.py:19
  88.5 0.0 collective-permute-done.4.saved_gate_in
  88.5 0.0 collective-permute-done.5.saved_up_in
  88.5 0.0 collective-permute-done.3.packed_in
  88.5 3.4 %shard_map.85 = (bf16[192,704]{1,0:T(8,128)(2,1)S(1)}, bf16[192,704]{1,0:T(8,128)(2,1)S(1)}) custom-call(s32[1]{0:T(128)} %bitcast.link_ref, s32[1]{0:T(128)} %bitcast.1.core_ref, bf16[64,48,128]{2,1,0:T(8,128)(2,1)} %collective-permute-done.3.packed_in, bf16[176,2048]{1,0:T(8,128)(2,1)S(1)} %bitcast.19, ...), custom_call_target="tpu_custom_call" | custom-call | flops 553648128 | bytes 5292040 | tf_op jit(solution)/shard_map/pallas_call | solution.py:19
  91.9 0.0 collective-permute-done.11.up3_in
  91.9 5.8 %collective-permute-done.8.gate3_in = bf16[176,2048]{1,0:T(8,128)(2,1)} collective-permute-done((bf16[176,2048]{1,0:T(8,128)(2,1)}, bf16[176,2048]{1,0:T(8,128)(2,1)}, u32[]{:S(2)}, u32[]{:S(2)}) %collective-permute-start.8) | collective-permute-done | bytes 720928 | tf_op jit(solution)/shard_map/ppermute | solution.py:218
  97.7 5.1 %shard_map.86 = (bf16[192,2048]{1,0:T(8,128)(2,1)S(1)}, bf16[192,2048]{1,0:T(8,128)(2,1)S(1)}) custom-call(s32[1]{0:T(128)} %bitcast.link_ref, s32[1]{0:T(128)} %bitcast.1.core_ref, bf16[192,704]{1,0:T(8,128)(2,1)S(1)} %get-tuple-element.11.own_gate_in, bf16[192,704]{1,0:T(8,128)(2,1)S(1)} %get-tuple-element.12.own_up_in, ...), custom_call_target="tpu_custom_call" | custom-call | flops 2214592512 | bytes 8421384 | tf_op jit(solution)/shard_map/pallas_call | solution.py:19
  102.8 1.9 %collective-permute-start.12 = (bf16[192,2048]{1,0:T(8,128)(2,1)S(1)}, bf16[192,2048]{1,0:T(8,128)(2,1)S(1)}, u32[]{:S(2)}, u32[]{:S(2)}) collective-permute-start(bf16[192,2048]{1,0:T(8,128)(2,1)S(1)} %get-tuple-element.16), channel_id=1, source_target_pairs={{0,1},{1,0},{2,3},{3,2},{4,5},{5,4},{6,7},{7,6},{8,9},{9,8},{10,11... | collective-permute-start | bytes 2359304 | tf_op jit(solution)/shard_map/ppermute | solution.py:221
  104.8 2.3 %collective-permute-done.12.back_ref = bf16[192,2048]{1,0:T(8,128)(2,1)S(1)} collective-permute-done((bf16[192,2048]{1,0:T(8,128)(2,1)S(1)}, bf16[192,2048]{1,0:T(8,128)(2,1)S(1)}, u32[]{:S(2)}, u32[]{:S(2)}) %collective-permute-start.12) | collective-permute-done | bytes 786464 | tf_op jit(solution)/shard_map/ppermute | solution.py:221
  107.0 1.3 shard_map.87
  108.3 0.0 copy-start.3
  108.3 15.2 %all-to-all-start.1 = ((bf16[64,48,128]{2,1,0:T(8,128)(2,1)}), bf16[64,48,128]{2,1,0:T(8,128)(2,1)S(1)}, u32[]{:S(2)}, u32[]{:S(2)}) async-start(bf16[64,48,128]{2,1,0:T(8,128)(2,1)} %shard_map.87), calls=%async_computation.1 | async-start | bytes 1572864 | tf_op jit(solution)/shard_map/all_to_all | solution.py:224
  123.5 0.0 copy-done.3
  123.5 0.1 copy.9.routes_ref
  123.6 0.2 shard_map.82.hot_ref
  123.9 43.9 %all-to-all-done.1.back_ref = bf16[64,48,128]{2,1,0:T(8,128)(2,1)S(1)} async-done(((bf16[64,48,128]{2,1,0:T(8,128)(2,1)}), bf16[64,48,128]{2,1,0:T(8,128)(2,1)S(1)}, u32[]{:S(2)}, u32[]{:S(2)}) %all-to-all-start.1) | async-done | bytes 786464 | tf_op jit(solution)/shard_map/all_to_all | solution.py:224
  167.8 1.1 shard_map.88
Async XLA Ops:
  2.5 18.9 %copy-start = (bf16[1,176,2048]{2,1,0:T(8,128)(2,1)S(1)}, bf16[1,176,2048]{2,1,0:T(8,128)(2,1)}, u32[]{:S(2)}) copy-start(bf16[1,176,2048]{2,1,0:T(8,128)(2,1)} %param.13) | copy-start | bytes 2162692
  2.5 74.2 %copy-start.1 = (bf16[1,1,64,3,1408]{4,2,3,1,0:T(8,128)(2,1)S(1)}, bf16[1,1,64,3,1408]{4,2,3,1,0:T(8,128)(2,1)}, u32[]{:S(2)}) copy-start(bf16[1,1,64,3,1408]{4,2,3,1,0:T(8,128)(2,1)} %param.14) | copy-start | bytes 1622020
  2.5 62.8 %all-to-all-start = ((bf16[64,48,128]{2,1,0:T(8,128)(2,1)}), bf16[64,48,128]{2,1,0:T(8,128)(2,1)S(1)}, u32[]{:S(2)}, u32[]{:S(2)}) async-start(bf16[64,48,128]{2,1,0:T(8,128)(2,1)} %shard_map.83), calls=%async_computation | async-start | bytes 1572864 | tf_op jit(solution)/shard_map/all_to_all | solution.py:224
  21.4 14.4 %collective-permute-start = (bf16[176,2048]{1,0:T(8,128)(2,1)S(1)}, bf16[176,2048]{1,0:T(8,128)(2,1)S(1)}, u32[]{:S(2)}, u32[]{:S(2)}) collective-permute-start(bf16[176,2048]{1,0:T(8,128)(2,1)S(1)} %bitcast.17), channel_id=1, source_target_pairs={{0,2},{1,7},{2,4},{3,1},{4,6},{5,3},{6,0},{7,5},{8,10},{9,15},{10,... | collective-permute-start | bytes 2162696 | tf_op jit(solution)/shard_map/ppermute | solution.py:218
  24.8 18.8 %collective-permute-start.9 = (bf16[176,2048]{1,0:T(8,128)(2,1)}, bf16[176,2048]{1,0:T(8,128)(2,1)}, u32[]{:S(2)}, u32[]{:S(2)}) collective-permute-start(bf16[176,2048]{1,0:T(8,128)(2,1)} %bitcast.16.up0_in), channel_id=1, source_target_pairs={{0,2},{1,7},{2,4},{3,1},{4,6},{5,3},{6,0},{7,5},{8,10},{9,15},{10,... | collective-permute-start | bytes 2162696 | tf_op jit(solution)/shard_map/ppermute | solution.py:218
  28.2 23.1 %collective-permute-start.6 = (bf16[176,2048]{1,0:T(8,128)(2,1)}, bf16[176,2048]{1,0:T(8,128)(2,1)}, u32[]{:S(2)}, u32[]{:S(2)}) collective-permute-start(bf16[176,2048]{1,0:T(8,128)(2,1)} %bitcast.15.gate0_in), channel_id=1, source_target_pairs={{0,2},{1,7},{2,4},{3,1},{4,6},{5,3},{6,0},{7,5},{8,10},{9,15},{10,... | collective-permute-start | bytes 2162696 | tf_op jit(solution)/shard_map/ppermute | solution.py:218
  35.8 23.2 %collective-permute-start.1 = (bf16[176,2048]{1,0:T(8,128)(2,1)S(1)}, bf16[176,2048]{1,0:T(8,128)(2,1)S(1)}, u32[]{:S(2)}, u32[]{:S(2)}) collective-permute-start(bf16[176,2048]{1,0:T(8,128)(2,1)S(1)} %collective-permute-done.down1_in), channel_id=1, source_target_pairs={{0,2},{1,7},{2,4},{3,1},{4,6},{5,3},{6,0},{7,5},{8,10},{9,15},{10,... | collective-permute-start | bytes 2162696 | tf_op jit(solution)/shard_map/ppermute | solution.py:218
  43.6 23.6 %collective-permute-start.10 = (bf16[176,2048]{1,0:T(8,128)(2,1)}, bf16[176,2048]{1,0:T(8,128)(2,1)}, u32[]{:S(2)}, u32[]{:S(2)}) collective-permute-start(bf16[176,2048]{1,0:T(8,128)(2,1)} %collective-permute-done.9.up1_in), channel_id=1, source_target_pairs={{0,2},{1,7},{2,4},{3,1},{4,6},{5,3},{6,0},{7,5},{8,10},{9,15},{10,... | collective-permute-start | bytes 2162696 | tf_op jit(solution)/shard_map/ppermute | solution.py:218
  51.3 23.2 %collective-permute-start.7 = (bf16[176,2048]{1,0:T(8,128)(2,1)}, bf16[176,2048]{1,0:T(8,128)(2,1)}, u32[]{:S(2)}, u32[]{:S(2)}) collective-permute-start(bf16[176,2048]{1,0:T(8,128)(2,1)} %collective-permute-done.6.gate1_in), channel_id=1, source_target_pairs={{0,2},{1,7},{2,4},{3,1},{4,6},{5,3},{6,0},{7,5},{8,10},{9,15},{10,... | collective-permute-start | bytes 2162696 | tf_op jit(solution)/shard_map/ppermute | solution.py:218
  59.0 23.3 %collective-permute-start.2 = (bf16[176,2048]{1,0:T(8,128)(2,1)S(1)}, bf16[176,2048]{1,0:T(8,128)(2,1)}, u32[]{:S(2)}, u32[]{:S(2)}) collective-permute-start(bf16[176,2048]{1,0:T(8,128)(2,1)S(1)} %collective-permute-done.1.down2_in), channel_id=1, source_target_pairs={{0,2},{1,7},{2,4},{3,1},{4,6},{5,3},{6,0},{7,5},{8,10},{9,15},{10,... | collective-permute-start | bytes 2162696 | tf_op jit(solution)/shard_map/ppermute | solution.py:218
  65.3 23.2 %collective-permute-start.3 = (bf16[64,48,128]{2,1,0:T(8,128)(2,1)S(1)}, bf16[64,48,128]{2,1,0:T(8,128)(2,1)}, u32[]{:S(2)}, u32[]{:S(2)}) collective-permute-start(bf16[64,48,128]{2,1,0:T(8,128)(2,1)S(1)} %all-to-all-done.packed_in), channel_id=1, source_target_pairs={{0,1},{1,0},{2,3},{3,2},{4,5},{5,4},{6,7},{7,6},{8,9},{9,8},{10,11... | collective-permute-start | bytes 2359304 | tf_op jit(solution)/shard_map/ppermute | solution.py:221
  67.3 24.6 %collective-permute-start.11 = (bf16[176,2048]{1,0:T(8,128)(2,1)}, bf16[176,2048]{1,0:T(8,128)(2,1)}, u32[]{:S(2)}, u32[]{:S(2)}) collective-permute-start(bf16[176,2048]{1,0:T(8,128)(2,1)} %collective-permute-done.10.up2_in), channel_id=1, source_target_pairs={{0,2},{1,7},{2,4},{3,1},{4,6},{5,3},{6,0},{7,5},{8,10},{9,15},{10,... | collective-permute-start | bytes 2162696 | tf_op jit(solution)/shard_map/ppermute | solution.py:218
  74.5 23.2 %collective-permute-start.8 = (bf16[176,2048]{1,0:T(8,128)(2,1)}, bf16[176,2048]{1,0:T(8,128)(2,1)}, u32[]{:S(2)}, u32[]{:S(2)}) collective-permute-start(bf16[176,2048]{1,0:T(8,128)(2,1)} %collective-permute-done.7.gate2_in), channel_id=1, source_target_pairs={{0,2},{1,7},{2,4},{3,1},{4,6},{5,3},{6,0},{7,5},{8,10},{9,15},{10,... | collective-permute-start | bytes 2162696 | tf_op jit(solution)/shard_map/ppermute | solution.py:218
  76.7 11.8 %collective-permute-start.4 = (bf16[192,1408]{1,0:T(8,128)(2,1)S(1)}, bf16[192,1408]{1,0:T(8,128)(2,1)}, u32[]{:S(2)}, u32[]{:S(2)}) collective-permute-start(bf16[192,1408]{1,0:T(8,128)(2,1)S(1)} %bitcast.20), channel_id=1, source_target_pairs={{0,1},{1,0},{2,3},{3,2},{4,5},{5,4},{6,7},{7,6},{8,9},{9,8},{10,11... | collective-permute-start | bytes 1622024 | tf_op jit(solution)/shard_map/ppermute | solution.py:221
  82.2 6.2 %collective-permute-start.5 = (bf16[192,1408]{1,0:T(8,128)(2,1)}, bf16[192,1408]{1,0:T(8,128)(2,1)}, u32[]{:S(2)}, u32[]{:S(2)}) collective-permute-start(bf16[192,1408]{1,0:T(8,128)(2,1)} %bitcast.22), channel_id=1, source_target_pairs={{0,1},{1,0},{2,3},{3,2},{4,5},{5,4},{6,7},{7,6},{8,9},{9,8},{10,11... | collective-permute-start | bytes 1622024 | tf_op jit(solution)/shard_map/ppermute | solution.py:221
  84.2 1.1 copy-start.2
  102.8 4.2 %collective-permute-start.12 = (bf16[192,2048]{1,0:T(8,128)(2,1)S(1)}, bf16[192,2048]{1,0:T(8,128)(2,1)S(1)}, u32[]{:S(2)}, u32[]{:S(2)}) collective-permute-start(bf16[192,2048]{1,0:T(8,128)(2,1)S(1)} %get-tuple-element.16), channel_id=1, source_target_pairs={{0,1},{1,0},{2,3},{3,2},{4,5},{5,4},{6,7},{7,6},{8,9},{9,8},{10,11... | collective-permute-start | bytes 2359304 | tf_op jit(solution)/shard_map/ppermute | solution.py:221
  108.3 15.2 %copy-start.3 = (s32[32,6]{0,1:T(8,128)S(1)}, s32[32,6]{0,1:T(8,128)}, u32[]{:S(2)}) copy-start(s32[32,6]{0,1:T(8,128)} %param.9) | copy-start | bytes 2308
  108.3 59.5 %all-to-all-start.1 = ((bf16[64,48,128]{2,1,0:T(8,128)(2,1)}), bf16[64,48,128]{2,1,0:T(8,128)(2,1)S(1)}, u32[]{:S(2)}, u32[]{:S(2)}) async-start(bf16[64,48,128]{2,1,0:T(8,128)(2,1)} %shard_map.87), calls=%async_computation.1 | async-start | bytes 1572864 | tf_op jit(solution)/shard_map/all_to_all | solution.py:224

commit v6 on v5

v6 whole, which is shorter than its diff:
```python
import jax
import jax.numpy as jnp
from jax import lax
from jax.experimental import pallas as pl
from jax.experimental.pallas import tpu as pltpu
from jax.sharding import PartitionSpec as P

F32 = jnp.float32
BF16 = jnp.bfloat16
VM = pl.BlockSpec(memory_space=pltpu.VMEM)
AN = pl.BlockSpec(memory_space=pl.ANY)
LINKS = 4
SLOTS = 3


def call(kernel, ins, outs, flops=0, scratch=(), spec=VM, limit=24 << 20):
    moved = sum(a.size * a.dtype.itemsize for a in ins) + sum(o.size * o.dtype.itemsize for o in outs)
    single = len(outs) == 1
    return pl.pallas_call(
        kernel,
        out_shape=outs[0] if single else tuple(outs),
        in_specs=[spec] * len(ins),
        out_specs=VM if single else tuple([VM] * len(outs)),
        scratch_shapes=list(scratch),
        compiler_params=pltpu.CompilerParams(vmem_limit_bytes=limit),
        cost_estimate=pl.CostEstimate(flops=flops, bytes_accessed=moved, transcendentals=0),
    )(*ins)


def fetch(copies, sems):
    made = [pltpu.make_async_copy(src, dst, sems.at[n]) for n, (src, dst) in enumerate(copies)]
    for copy in made:
        copy.start()
    return made


def pack(value, out_ref, part=0, parts=1):
    experts, deep, lanes = out_ref.shape
    slots = value.shape[0] // experts
    chunks = deep // slots
    span = chunks // parts
    for s in range(slots):
        block = value[s * experts : (s + 1) * experts].astype(BF16)
        stack = jnp.stack([block[:, c * lanes : (c + 1) * lanes] for c in range(span)])
        low = s * chunks + part * span
        out_ref[:, low : low + span, :] = jnp.swapaxes(stack, 0, 1)


def unpack(packed_ref, s, slots):
    _, deep, _ = packed_ref.shape
    chunks = deep // slots
    parts = jnp.swapaxes(packed_ref[:, s * chunks : (s + 1) * chunks, :], 0, 1)
    return jnp.concatenate([parts[c] for c in range(chunks)], axis=1)


def place_kernel(routes_ref, gates_ref, grad_ref, out_ref):
    named, chosen = chosen_of(routes_ref, out_ref.shape[0])
    weight = jnp.zeros(named.shape, F32)
    for k in range(routes_ref.shape[0]):
        weight = jnp.where(routes_ref[k : k + 1, :] == named, gates_ref[k : k + 1, :], weight)
    weight = jnp.sum(jnp.where(chosen, weight, 0.0), axis=1, keepdims=True)
    hot = jnp.where(chosen, 1.0, 0.0).astype(BF16)
    pack(weight * jnp.dot(hot, grad_ref[...], preferred_element_type=F32), out_ref)


def factor_kernel(gate_ref, up_ref, gf_ref, uf_ref):
    slice_width = gf_ref.shape[1] // LINKS
    first = (lax.axis_index("replica") & 1) == 0
    for q in range(LINKS):
        low = 2 * q * slice_width
        mid, high = low + slice_width, low + 2 * slice_width
        g = jnp.where(first, gate_ref[:, low:mid].astype(F32), gate_ref[:, mid:high].astype(F32))
        u = jnp.where(first, up_ref[:, low:mid].astype(F32), up_ref[:, mid:high].astype(F32))
        sig = jax.nn.sigmoid(g)
        place = slice(q * slice_width, (q + 1) * slice_width)
        uf_ref[:, place] = g * sig
        gf_ref[:, place] = u * sig * (1.0 + g * (1.0 - sig))


def spots(width):
    replica = lax.axis_index("replica")
    link, turn = replica >> 1, 2 * (replica & 1) - 1
    steps = [(link + step * turn + LINKS) & (LINKS - 1) for step in range(LINKS)]
    return [pl.ds(pl.multiple_of(step * width, 16), width) for step in steps]


def hidden_kernel(
    packed_in, down0_in, down1_in, down2_in, down3_in, gf_in, uf_in,
    hidden_ref, packed_ref, down_ref, gf_ref, uf_ref, rows_ref, sems,
):
    copies = [(packed_in, packed_ref)]
    for piece, place in zip((down0_in, down1_in, down2_in, down3_in), spots(down0_in.shape[0])):
        copies.append((piece, down_ref.at[place, :]))
    copies = fetch(copies + [(gf_in, gf_ref), (uf_in, uf_ref)], sems)
    copies[0].wait()
    experts = packed_ref.shape[0]
    slots = rows_ref.shape[0] // experts
    for s in range(slots):
        rows_ref[s * experts : (s + 1) * experts, :] = unpack(packed_ref, s, slots)
    for copy in copies[1:]:
        copy.wait()
    grad = lax.dot_general(
        rows_ref[...], down_ref[...], (((1,), (1,)), ((), ())), preferred_element_type=F32
    )
    units = grad.shape[1]
    hidden_ref[:, :units] = (grad * gf_ref[...]).astype(BF16)
    hidden_ref[:, units:] = (grad * uf_ref[...]).astype(BF16)


def output_kernel(
    own_in, other_in, gate0_in, gate1_in, gate2_in, gate3_in, up0_in, up1_in, up2_in, up3_in,
    own_ref, theirs_ref, hidden_ref, weight_ref, sems,
):
    width = gate0_in.shape[0]
    rows, hidden = own_in.shape[0], own_in.shape[1] // 2
    parts = sems.shape[0] - 1
    span = weight_ref.shape[1] // parts
    gates, ups = (gate0_in, gate1_in, gate2_in, gate3_in), (up0_in, up1_in, up2_in, up3_in)
    begun = fetch(
        [(own_in, hidden_ref.at[pl.ds(0, rows), :]), (other_in, hidden_ref.at[pl.ds(rows, rows), :])], sems.at[0]
    )
    blocks = []
    for n in range(parts):
        columns = pl.ds(n * span, span)
        copies = []
        for gate_in, up_in, place in zip(gates, ups, spots(width)):
            copies.append((gate_in.at[:, columns], weight_ref.at[place, columns]))
            lower = pl.ds(pl.multiple_of(place.start + hidden, 16), width)
            copies.append((up_in.at[:, columns], weight_ref.at[lower, columns]))
        blocks.append(fetch(copies, sems.at[n + 1]))
    for copy in begun:
        copy.wait()
    for n in range(parts):
        for copy in blocks[n]:
            copy.wait()
        columns = slice(n * span, (n + 1) * span)
        total = jnp.dot(hidden_ref[...], weight_ref[:, columns], preferred_element_type=F32)
        own_ref[:, columns] = total[:rows].astype(BF16)
        theirs_ref[:, columns] = total[rows:].astype(BF16)


def join_kernel(own_ref, back_ref, out_ref):
    pack(own_ref[...].astype(F32) + back_ref[...].astype(F32), out_ref)


def chosen_of(routes_ref, experts):
    top, tokens = routes_ref.shape
    row = lax.broadcasted_iota(jnp.int32, (experts * SLOTS, tokens), 0)
    number = row // experts
    named = row - number * experts
    hits = jnp.zeros(row.shape, F32)
    for k in range(top):
        hits = jnp.where(routes_ref[k : k + 1, :] == named, 1.0, hits)
    before = (
        lax.broadcasted_iota(jnp.int32, (tokens, tokens), 0)
        < lax.broadcasted_iota(jnp.int32, (tokens, tokens), 1)
    ).astype(BF16)
    earlier = jnp.dot(hits.astype(BF16), before, preferred_element_type=F32)
    return named, (hits > 0.5) & (jnp.abs(earlier - number.astype(F32)) < 0.5)


def turn_kernel(routes_ref, hot_ref):
    _, chosen = chosen_of(routes_ref, hot_ref.shape[1] // SLOTS)
    hot_ref[...] = jnp.where(chosen, 1.0, 0.0).T.astype(BF16)


def combine_kernel(hot_ref, back_ref, out_ref):
    tokens, width = out_ref.shape
    experts = back_ref.shape[0]
    slots = hot_ref.shape[1] // experts
    total = jnp.zeros((tokens, width), F32)
    for s in range(slots):
        total += jnp.dot(
            hot_ref[:, s * experts : (s + 1) * experts], unpack(back_ref, s, slots), preferred_element_type=F32
        )
    out_ref[...] = total.astype(BF16)


def body(grad_out, routes, gates, w_gate, w_up, w_down, saved_gate, saved_up):
    experts = lax.axis_size("expert")
    copies = lax.axis_size("replica")
    tokens, width = grad_out.shape
    slots = saved_gate.shape[3]
    slice_width = w_gate.shape[1]
    rows = experts * slots
    half = width // 2
    chunks = half // 128
    deep = slots * chunks

    def along(a):
        pairs = [(2 * i + k, 2 * ((i + 1 - 2 * k) % LINKS) + k) for i in range(LINKS) for k in range(2)]
        return lax.ppermute(a, "replica", pairs)

    def across(a):
        return lax.ppermute(a, "replica", [(i, i ^ 1) for i in range(copies)])

    def exchange(a):
        return lax.all_to_all(a, "expert", split_axis=0, concat_axis=0, tiled=True)

    downs, gate_pieces, up_pieces = [w_down[0]], [w_gate[0]], [w_up[0]]
    for _ in range(1, LINKS):
        for pieces in (downs, gate_pieces, up_pieces):
            pieces.append(along(pieces[-1]))

    packed = call(
        place_kernel,
        (routes.T, gates.T, grad_out),
        (jax.ShapeDtypeStruct((experts, 2 * deep, 128), BF16),),
        2 * rows * tokens * width,
        limit=60 << 20,
    )
    arrived = exchange(packed)

    saved = tuple(a[0, 0].transpose(1, 0, 2).reshape(rows, -1) for a in (saved_gate, saved_up))
    hidden_units = LINKS * slice_width
    factor = jax.ShapeDtypeStruct((rows, hidden_units), F32)
    own_factors = call(factor_kernel, saved, (factor, factor))
    sent = (across(saved[0]), across(saved[1]))
    other_factors = call(factor_kernel, sent, (factor, factor))

    hidden = jax.ShapeDtypeStruct((rows, 2 * hidden_units), BF16)
    cost = 2 * rows * hidden_units * width
    scratch = (
        pltpu.VMEM((experts, 2 * deep, 128), BF16),
        pltpu.VMEM((hidden_units, width), BF16),
        pltpu.VMEM((rows, hidden_units), F32),
        pltpu.VMEM((rows, hidden_units), F32),
        pltpu.VMEM((rows, width), BF16),
        pltpu.SemaphoreType.DMA((7,)),
    )
    other_rows = across(arrived)

    def hide(packed_rows, factors):
        ins = (packed_rows,) + tuple(downs) + tuple(factors)
        return call(hidden_kernel, ins, (hidden,), cost, scratch=scratch, spec=AN)

    own_hidden = hide(arrived, own_factors)
    other_hidden = hide(other_rows, other_factors)

    pieces = tuple(gate_pieces + up_pieces)
    scratch2 = (
        pltpu.VMEM((2 * rows, 2 * hidden_units), BF16),
        pltpu.VMEM((2 * hidden_units, width), BF16),
        pltpu.SemaphoreType.DMA((3, 8)),
    )
    part = jax.ShapeDtypeStruct((rows, width), BF16)
    ours, theirs = call(
        output_kernel, (own_hidden, other_hidden) + pieces, (part, part), 4 * cost, scratch=scratch2, spec=AN
    )
    back = across(theirs)
    outgoing = call(join_kernel, (ours, back), (jax.ShapeDtypeStruct((experts, 2 * deep, 128), BF16),))
    returned = exchange(outgoing)
    turned = call(turn_kernel, (routes.T,), (jax.ShapeDtypeStruct((tokens, rows), BF16),))
    return call(combine_kernel, (turned, returned), (jax.ShapeDtypeStruct((tokens, width), BF16),))


def solution(mesh):
    in_specs = (
        P(("expert", "replica"), None),
        P(("expert", "replica"), None),
        P(("expert", "replica"), None),
        P("expert", "replica", None),
        P("expert", "replica", None),
        P("expert", "replica", None),
        P("expert", "replica", None, None, None),
        P("expert", "replica", None, None, None),
    )
    out_specs = P(("expert", "replica"), None)

    return jax.shard_map(body, mesh=mesh, in_specs=in_specs, out_specs=out_specs, check_vma=False)
```

time: 170 us -> 169 us (level)
  waiting for transfers between devices: 84.4 us -> 80.6 us
  starting transfers between devices: 66.2 us -> 68.2 us
    ppermute x9, waiting for transfers between devices: 34 us -> 24.7 us  [along(): return lax.ppermute(a, 'replica', pairs)]
    all_to_all x2, waiting for transfers between devices: 48.1 us -> 53.4 us  [exchange(): return lax.all_to_all(a, 'expert', split_axis=0, concat_axis=0, tiled=True)]
    ppermute x9, starting transfers between devices: 24.2 us -> 25.9 us  [along(): return lax.ppermute(a, 'replica', pairs)]
    pallas_call x7 -> x9, Pallas kernels: 16.9 us -> 18.2 us  [call(): pl.pallas_call(kernel, out_shape=outs[0] if single else tuple(outs), in_s...]
  transfers between devices with their start and end apart: 15 -> 15, of which waited for: 10 -> 10; matrix products, arithmetic and copies ran while one was open for 0% -> 0% of each run, Pallas kernels for 4% -> 5%
where the time goes in v6:
time: 169 us; the launch traced here: 168 us
  waiting for transfers between devices  80.6 us (48%)
  starting transfers between devices  68.2 us (40%)
  Pallas kernels  18.2 us (11%)
    all_to_all x2, waiting for transfers between devices, exchange(): return lax.all_to_all(a, 'expert', split_axis=0, concat_axis=0, tiled=True)  53.4 us
    all_to_all x2, starting transfers between devices, exchange(): return lax.all_to_all(a, 'expert', split_axis=0, concat_axis=0, tiled=True)  34.1 us
    ppermute x9, starting transfers between devices, along(): return lax.ppermute(a, 'replica', pairs)  25.9 us
    ppermute x9, waiting for transfers between devices, along(): return lax.ppermute(a, 'replica', pairs)  24.7 us
    pallas_call x9, Pallas kernels, call(): pl.pallas_call(kernel, out_shape=outs[0] if single else tuple(outs), in_s...  18.2 us
    ppermute x4, starting transfers between devices, across(): return lax.ppermute(a, 'replica', [(i, i ^ 1) for i in range(copies)])  8.18 us
  transfers between devices with their start and end apart: 15, of which 10 were waited for; matrix products, arithmetic and copies ran while one was open for 0% of the time, Pallas kernels for 5%

profile of v6, /device:TPU:8, one launch (start us, length us, event | category | flops | bytes accessed | tf_op | source)
XLA Modules:
  0.0 168.3 jit_solution(14894416364341200804)
XLA Ops:
  0.0 2.5 %shard_map.83 = bf16[64,48,128]{2,1,0:T(8,128)(2,1)} custom-call(s32[6,32]{1,0:T(8,128)} %bitcast.22, f32[6,32]{1,0:T(8,128)} %bitcast.24, bf16[32,2048]{1,0:T(8,128)(2,1)} %grad_ref.1), custom_call_target="tpu_custom_call" | custom-call | flops 25165824 | bytes 919040 | tf_op jit(solution)/shard_map/pallas_call | solution.py:19
  2.5 0.0 copy-start
  2.5 0.0 copy-start.1
  2.5 18.9 %all-to-all-start = ((bf16[64,48,128]{2,1,0:T(8,128)(2,1)}), bf16[64,48,128]{2,1,0:T(8,128)(2,1)S(1)}, u32[]{:S(2)}, u32[]{:S(2)}) async-start(bf16[64,48,128]{2,1,0:T(8,128)(2,1)} %shard_map.83), calls=%async_computation | async-start | bytes 1572864 | tf_op jit(solution)/shard_map/all_to_all | solution.py:198
  21.4 0.0 copy-done
  21.4 3.4 %collective-permute-start = (bf16[176,2048]{1,0:T(8,128)(2,1)S(1)}, bf16[176,2048]{1,0:T(8,128)(2,1)S(1)}, u32[]{:S(2)}, u32[]{:S(2)}) collective-permute-start(bf16[176,2048]{1,0:T(8,128)(2,1)S(1)} %bitcast.15), channel_id=1, source_target_pairs={{0,2},{1,7},{2,4},{3,1},{4,6},{5,3},{6,0},{7,5},{8,10},{9,15},{10,... | collective-permute-start | bytes 2162696 | tf_op jit(solution)/shard_map/ppermute | solution.py:192
  24.8 3.4 %collective-permute-start.9 = (bf16[176,2048]{1,0:T(8,128)(2,1)}, bf16[176,2048]{1,0:T(8,128)(2,1)}, u32[]{:S(2)}, u32[]{:S(2)}) collective-permute-start(bf16[176,2048]{1,0:T(8,128)(2,1)} %bitcast.14.up0_in), channel_id=1, source_target_pairs={{0,2},{1,7},{2,4},{3,1},{4,6},{5,3},{6,0},{7,5},{8,10},{9,15},{10,... | collective-permute-start | bytes 2162696 | tf_op jit(solution)/shard_map/ppermute | solution.py:192
  28.2 3.1 %collective-permute-start.6 = (bf16[176,2048]{1,0:T(8,128)(2,1)}, bf16[176,2048]{1,0:T(8,128)(2,1)}, u32[]{:S(2)}, u32[]{:S(2)}) collective-permute-start(bf16[176,2048]{1,0:T(8,128)(2,1)} %bitcast.13.gate0_in), channel_id=1, source_target_pairs={{0,2},{1,7},{2,4},{3,1},{4,6},{5,3},{6,0},{7,5},{8,10},{9,15},{10,... | collective-permute-start | bytes 2162696 | tf_op jit(solution)/shard_map/ppermute | solution.py:192
  31.3 4.5 %collective-permute-done.down1_in = bf16[176,2048]{1,0:T(8,128)(2,1)S(1)} collective-permute-done((bf16[176,2048]{1,0:T(8,128)(2,1)S(1)}, bf16[176,2048]{1,0:T(8,128)(2,1)S(1)}, u32[]{:S(2)}, u32[]{:S(2)}) %collective-permute-start) | collective-permute-done | bytes 720928 | tf_op jit(solution)/shard_map/ppermute | solution.py:192
  35.8 2.2 %collective-permute-start.1 = (bf16[176,2048]{1,0:T(8,128)(2,1)S(1)}, bf16[176,2048]{1,0:T(8,128)(2,1)S(1)}, u32[]{:S(2)}, u32[]{:S(2)}) collective-permute-start(bf16[176,2048]{1,0:T(8,128)(2,1)S(1)} %collective-permute-done.down1_in), channel_id=1, source_target_pairs={{0,2},{1,7},{2,4},{3,1},{4,6},{5,3},{6,0},{7,5},{8,10},{9,15},{10,... | collective-permute-start | bytes 2162696 | tf_op jit(solution)/shard_map/ppermute | solution.py:192
  38.0 5.6 %collective-permute-done.9.up1_in = bf16[176,2048]{1,0:T(8,128)(2,1)} collective-permute-done((bf16[176,2048]{1,0:T(8,128)(2,1)}, bf16[176,2048]{1,0:T(8,128)(2,1)}, u32[]{:S(2)}, u32[]{:S(2)}) %collective-permute-start.9) | collective-permute-done | bytes 720928 | tf_op jit(solution)/shard_map/ppermute | solution.py:192
  43.6 2.2 %collective-permute-start.10 = (bf16[176,2048]{1,0:T(8,128)(2,1)}, bf16[176,2048]{1,0:T(8,128)(2,1)}, u32[]{:S(2)}, u32[]{:S(2)}) collective-permute-start(bf16[176,2048]{1,0:T(8,128)(2,1)} %collective-permute-done.9.up1_in), channel_id=1, source_target_pairs={{0,2},{1,7},{2,4},{3,1},{4,6},{5,3},{6,0},{7,5},{8,10},{9,15},{10,... | collective-permute-start | bytes 2162696 | tf_op jit(solution)/shard_map/ppermute | solution.py:192
  45.8 5.5 %collective-permute-done.6.gate1_in = bf16[176,2048]{1,0:T(8,128)(2,1)} collective-permute-done((bf16[176,2048]{1,0:T(8,128)(2,1)}, bf16[176,2048]{1,0:T(8,128)(2,1)}, u32[]{:S(2)}, u32[]{:S(2)}) %collective-permute-start.6) | collective-permute-done | bytes 720928 | tf_op jit(solution)/shard_map/ppermute | solution.py:192
  51.3 2.2 %collective-permute-start.7 = (bf16[176,2048]{1,0:T(8,128)(2,1)}, bf16[176,2048]{1,0:T(8,128)(2,1)}, u32[]{:S(2)}, u32[]{:S(2)}) collective-permute-start(bf16[176,2048]{1,0:T(8,128)(2,1)} %collective-permute-done.6.gate1_in), channel_id=1, source_target_pairs={{0,2},{1,7},{2,4},{3,1},{4,6},{5,3},{6,0},{7,5},{8,10},{9,15},{10,... | collective-permute-start | bytes 2162696 | tf_op jit(solution)/shard_map/ppermute | solution.py:192
  53.5 0.0 copy-done.1
  53.5 2.4 %collective-permute-start.4 = (bf16[192,1408]{1,0:T(8,128)(2,1)S(1)}, bf16[192,1408]{1,0:T(8,128)(2,1)}, u32[]{:S(2)}, u32[]{:S(2)}) collective-permute-start(bf16[192,1408]{1,0:T(8,128)(2,1)S(1)} %bitcast.18), channel_id=1, source_target_pairs={{0,1},{1,0},{2,3},{3,2},{4,5},{5,4},{6,7},{7,6},{8,9},{9,8},{10,11... | collective-permute-start | bytes 1622024 | tf_op jit(solution)/shard_map/ppermute | solution.py:195
  56.0 9.4 %all-to-all-done.packed_in = bf16[64,48,128]{2,1,0:T(8,128)(2,1)S(1)} async-done(((bf16[64,48,128]{2,1,0:T(8,128)(2,1)}), bf16[64,48,128]{2,1,0:T(8,128)(2,1)S(1)}, u32[]{:S(2)}, u32[]{:S(2)}) %all-to-all-start) | async-done | bytes 786464 | tf_op jit(solution)/shard_map/all_to_all | solution.py:198
  65.3 1.9 %collective-permute-start.3 = (bf16[64,48,128]{2,1,0:T(8,128)(2,1)S(1)}, bf16[64,48,128]{2,1,0:T(8,128)(2,1)S(1)}, u32[]{:S(2)}, u32[]{:S(2)}) collective-permute-start(bf16[64,48,128]{2,1,0:T(8,128)(2,1)S(1)} %all-to-all-done.packed_in), channel_id=1, source_target_pairs={{0,1},{1,0},{2,3},{3,2},{4,5},{5,4},{6,7},{7,6},{8,9},{9,8},{10,11... | collective-permute-start | bytes 2359304 | tf_op jit(solution)/shard_map/ppermute | solution.py:195
  67.2 0.0 collective-permute-done.1.down2_in
  67.3 3.4 %collective-permute-start.2 = (bf16[176,2048]{1,0:T(8,128)(2,1)S(1)}, bf16[176,2048]{1,0:T(8,128)(2,1)S(1)}, u32[]{:S(2)}, u32[]{:S(2)}) collective-permute-start(bf16[176,2048]{1,0:T(8,128)(2,1)S(1)} %collective-permute-done.1.down2_in), channel_id=1, source_target_pairs={{0,2},{1,7},{2,4},{3,1},{4,6},{5,3},{6,0},{7,5},{8,10},{9,15},{10,... | collective-permute-start | bytes 2162696 | tf_op jit(solution)/shard_map/ppermute | solution.py:192
  70.7 0.0 collective-permute-done.10.up2_in
  70.7 3.4 %collective-permute-start.11 = (bf16[176,2048]{1,0:T(8,128)(2,1)}, bf16[176,2048]{1,0:T(8,128)(2,1)S(1)}, u32[]{:S(2)}, u32[]{:S(2)}) collective-permute-start(bf16[176,2048]{1,0:T(8,128)(2,1)} %collective-permute-done.10.up2_in), channel_id=1, source_target_pairs={{0,2},{1,7},{2,4},{3,1},{4,6},{5,3},{6,0},{7,5},{8,10},{9,15},{10,... | collective-permute-start | bytes 2162696 | tf_op jit(solution)/shard_map/ppermute | solution.py:192
  74.1 0.4 collective-permute-done.7.gate2_in
  74.5 2.7 %collective-permute-start.8 = (bf16[176,2048]{1,0:T(8,128)(2,1)}, bf16[176,2048]{1,0:T(8,128)(2,1)S(1)}, u32[]{:S(2)}, u32[]{:S(2)}) collective-permute-start(bf16[176,2048]{1,0:T(8,128)(2,1)} %collective-permute-done.7.gate2_in), channel_id=1, source_target_pairs={{0,2},{1,7},{2,4},{3,1},{4,6},{5,3},{6,0},{7,5},{8,10},{9,15},{10,... | collective-permute-start | bytes 2162696 | tf_op jit(solution)/shard_map/ppermute | solution.py:192
  77.2 0.0 collective-permute-done.4.gate_ref
  77.2 1.9 %collective-permute-start.5 = (bf16[192,1408]{1,0:T(8,128)(2,1)}, bf16[192,1408]{1,0:T(8,128)(2,1)S(1)}, u32[]{:S(2)}, u32[]{:S(2)}) collective-permute-start(bf16[192,1408]{1,0:T(8,128)(2,1)} %bitcast.20), channel_id=1, source_target_pairs={{0,1},{1,0},{2,3},{3,2},{4,5},{5,4},{6,7},{7,6},{8,9},{9,8},{10,11... | collective-permute-start | bytes 1622024 | tf_op jit(solution)/shard_map/ppermute | solution.py:195
  79.1 0.0 copy-start.2
  79.2 1.0 copy-done.2
  80.2 0.8 shard_map.84
  81.0 0.2 collective-permute-done.5.up_ref
  81.3 1.9 %shard_map.86 = (f32[192,704]{1,0:T(8,128)S(1)}, f32[192,704]{1,0:T(8,128)S(1)}) custom-call(bf16[192,1408]{1,0:T(8,128)(2,1)} %collective-permute-done.4.gate_ref, bf16[192,1408]{1,0:T(8,128)(2,1)S(1)} %collective-permute-done.5.up_ref), custom_call_target="tpu_custom_call" | custom-call | bytes 2162688 | tf_op jit(solution)/shard_map/pallas_call | solution.py:19
  83.2 0.0 collective-permute-done.2.down3_in
  83.2 2.9 %shard_map.85.own_in = bf16[192,1408]{1,0:T(8,128)(2,1)S(1)} custom-call(bf16[64,48,128]{2,1,0:T(8,128)(2,1)S(1)} %all-to-all-done.packed_in, bf16[176,2048]{1,0:T(8,128)(2,1)S(1)} %bitcast.16, bf16[176,2048]{1,0:T(8,128)(2,1)S(1)} %collective-permute-done.down1_in, bf16[176,2048]{1,0:T(8,128)(2,1)S(1)} %collective-permute-done.1.down2_in, ...), custom_call_target="tpu_custom_call" | custom-call | flops 553648128 | bytes 5292032 | tf_op jit(solution)/shard_map/pallas_call | solution.py:19
  86.0 0.0 collective-permute-done.3.packed_in
  86.0 2.9 %shard_map.87.other_in = bf16[192,1408]{1,0:T(8,128)(2,1)S(1)} custom-call(bf16[64,48,128]{2,1,0:T(8,128)(2,1)S(1)} %collective-permute-done.3.packed_in, bf16[176,2048]{1,0:T(8,128)(2,1)S(1)} %bitcast.17, bf16[176,2048]{1,0:T(8,128)(2,1)S(1)} %collective-permute-done.down1_in, bf16[176,2048]{1,0:T(8,128)(2,1)S(1)} %collective-permute-done.1.down2_in, ...), custom_call_target="tpu_custom_call" | custom-call | flops 553648128 | bytes 5292032 | tf_op jit(solution)/shard_map/pallas_call | solution.py:19
  88.9 0.9 collective-permute-done.11.up3_in
  89.9 7.7 %collective-permute-done.8.gate3_in = bf16[176,2048]{1,0:T(8,128)(2,1)S(1)} collective-permute-done((bf16[176,2048]{1,0:T(8,128)(2,1)}, bf16[176,2048]{1,0:T(8,128)(2,1)S(1)}, u32[]{:S(2)}, u32[]{:S(2)}) %collective-permute-start.8) | collective-permute-done | bytes 720928 | tf_op jit(solution)/shard_map/ppermute | solution.py:192
  97.6 4.6 %shard_map.88 = (bf16[192,2048]{1,0:T(8,128)(2,1)S(1)}, bf16[192,2048]{1,0:T(8,128)(2,1)S(1)}) custom-call(bf16[192,1408]{1,0:T(8,128)(2,1)S(1)} %shard_map.85.own_in, bf16[192,1408]{1,0:T(8,128)(2,1)S(1)} %shard_map.87.other_in, bf16[176,2048]{1,0:T(8,128)(2,1)} %bitcast.13.gate0_in, bf16[176,2048]{1,0:T(8,128)(2,1)} %collective-permute-done.6.gate1_in, ...), custom_call_target="tpu_custom_call" | custom-call | flops 2214592512 | bytes 8421376 | tf_op jit(solution)/shard_map/pallas_call | solution.py:19
  102.2 1.9 %collective-permute-start.12 = (bf16[192,2048]{1,0:T(8,128)(2,1)S(1)}, bf16[192,2048]{1,0:T(8,128)(2,1)S(1)}, u32[]{:S(2)}, u32[]{:S(2)}) collective-permute-start(bf16[192,2048]{1,0:T(8,128)(2,1)S(1)} %get-tuple-element.16), channel_id=1, source_target_pairs={{0,1},{1,0},{2,3},{3,2},{4,5},{5,4},{6,7},{7,6},{8,9},{9,8},{10,11... | collective-permute-start | bytes 2359304 | tf_op jit(solution)/shard_map/ppermute | solution.py:195
  104.2 2.3 %collective-permute-done.12.back_ref = bf16[192,2048]{1,0:T(8,128)(2,1)S(1)} collective-permute-done((bf16[192,2048]{1,0:T(8,128)(2,1)S(1)}, bf16[192,2048]{1,0:T(8,128)(2,1)S(1)}, u32[]{:S(2)}, u32[]{:S(2)}) %collective-permute-start.12) | collective-permute-done | bytes 786464 | tf_op jit(solution)/shard_map/ppermute | solution.py:195
  106.4 1.3 shard_map.89
  107.7 0.0 copy-start.3
  107.7 15.2 %all-to-all-start.1 = ((bf16[64,48,128]{2,1,0:T(8,128)(2,1)}), bf16[64,48,128]{2,1,0:T(8,128)(2,1)S(1)}, u32[]{:S(2)}, u32[]{:S(2)}) async-start(bf16[64,48,128]{2,1,0:T(8,128)(2,1)} %shard_map.89), calls=%async_computation.1 | async-start | bytes 1572864 | tf_op jit(solution)/shard_map/all_to_all | solution.py:198
  122.9 0.0 copy-done.3
  122.9 0.2 shard_map.82.hot_ref
  123.1 44.0 %all-to-all-done.1.back_ref = bf16[64,48,128]{2,1,0:T(8,128)(2,1)S(1)} async-done(((bf16[64,48,128]{2,1,0:T(8,128)(2,1)}), bf16[64,48,128]{2,1,0:T(8,128)(2,1)S(1)}, u32[]{:S(2)}, u32[]{:S(2)}) %all-to-all-start.1) | async-done | bytes 786464 | tf_op jit(solution)/shard_map/all_to_all | solution.py:198
  167.2 1.1 shard_map.90
Async XLA Ops:
  2.5 18.9 %copy-start = (bf16[1,176,2048]{2,1,0:T(8,128)(2,1)S(1)}, bf16[1,176,2048]{2,1,0:T(8,128)(2,1)}, u32[]{:S(2)}) copy-start(bf16[1,176,2048]{2,1,0:T(8,128)(2,1)} %param.13) | copy-start | bytes 2162692
  2.5 51.0 %copy-start.1 = (bf16[1,1,64,3,1408]{4,2,3,1,0:T(8,128)(2,1)S(1)}, bf16[1,1,64,3,1408]{4,2,3,1,0:T(8,128)(2,1)}, u32[]{:S(2)}) copy-start(bf16[1,1,64,3,1408]{4,2,3,1,0:T(8,128)(2,1)} %param.14) | copy-start | bytes 1622020
  2.5 62.8 %all-to-all-start = ((bf16[64,48,128]{2,1,0:T(8,128)(2,1)}), bf16[64,48,128]{2,1,0:T(8,128)(2,1)S(1)}, u32[]{:S(2)}, u32[]{:S(2)}) async-start(bf16[64,48,128]{2,1,0:T(8,128)(2,1)} %shard_map.83), calls=%async_computation | async-start | bytes 1572864 | tf_op jit(solution)/shard_map/all_to_all | solution.py:198
  21.4 14.4 %collective-permute-start = (bf16[176,2048]{1,0:T(8,128)(2,1)S(1)}, bf16[176,2048]{1,0:T(8,128)(2,1)S(1)}, u32[]{:S(2)}, u32[]{:S(2)}) collective-permute-start(bf16[176,2048]{1,0:T(8,128)(2,1)S(1)} %bitcast.15), channel_id=1, source_target_pairs={{0,2},{1,7},{2,4},{3,1},{4,6},{5,3},{6,0},{7,5},{8,10},{9,15},{10,... | collective-permute-start | bytes 2162696 | tf_op jit(solution)/shard_map/ppermute | solution.py:192
  24.8 18.8 %collective-permute-start.9 = (bf16[176,2048]{1,0:T(8,128)(2,1)}, bf16[176,2048]{1,0:T(8,128)(2,1)}, u32[]{:S(2)}, u32[]{:S(2)}) collective-permute-start(bf16[176,2048]{1,0:T(8,128)(2,1)} %bitcast.14.up0_in), channel_id=1, source_target_pairs={{0,2},{1,7},{2,4},{3,1},{4,6},{5,3},{6,0},{7,5},{8,10},{9,15},{10,... | collective-permute-start | bytes 2162696 | tf_op jit(solution)/shard_map/ppermute | solution.py:192
  28.2 23.1 %collective-permute-start.6 = (bf16[176,2048]{1,0:T(8,128)(2,1)}, bf16[176,2048]{1,0:T(8,128)(2,1)}, u32[]{:S(2)}, u32[]{:S(2)}) collective-permute-start(bf16[176,2048]{1,0:T(8,128)(2,1)} %bitcast.13.gate0_in), channel_id=1, source_target_pairs={{0,2},{1,7},{2,4},{3,1},{4,6},{5,3},{6,0},{7,5},{8,10},{9,15},{10,... | collective-permute-start | bytes 2162696 | tf_op jit(solution)/shard_map/ppermute | solution.py:192
  35.8 31.5 %collective-permute-start.1 = (bf16[176,2048]{1,0:T(8,128)(2,1)S(1)}, bf16[176,2048]{1,0:T(8,128)(2,1)S(1)}, u32[]{:S(2)}, u32[]{:S(2)}) collective-permute-start(bf16[176,2048]{1,0:T(8,128)(2,1)S(1)} %collective-permute-done.down1_in), channel_id=1, source_target_pairs={{0,2},{1,7},{2,4},{3,1},{4,6},{5,3},{6,0},{7,5},{8,10},{9,15},{10,... | collective-permute-start | bytes 2162696 | tf_op jit(solution)/shard_map/ppermute | solution.py:192
  43.6 27.0 %collective-permute-start.10 = (bf16[176,2048]{1,0:T(8,128)(2,1)}, bf16[176,2048]{1,0:T(8,128)(2,1)}, u32[]{:S(2)}, u32[]{:S(2)}) collective-permute-start(bf16[176,2048]{1,0:T(8,128)(2,1)} %collective-permute-done.9.up1_in), channel_id=1, source_target_pairs={{0,2},{1,7},{2,4},{3,1},{4,6},{5,3},{6,0},{7,5},{8,10},{9,15},{10,... | collective-permute-start | bytes 2162696 | tf_op jit(solution)/shard_map/ppermute | solution.py:192
  51.3 23.2 %collective-permute-start.7 = (bf16[176,2048]{1,0:T(8,128)(2,1)}, bf16[176,2048]{1,0:T(8,128)(2,1)}, u32[]{:S(2)}, u32[]{:S(2)}) collective-permute-start(bf16[176,2048]{1,0:T(8,128)(2,1)} %collective-permute-done.6.gate1_in), channel_id=1, source_target_pairs={{0,2},{1,7},{2,4},{3,1},{4,6},{5,3},{6,0},{7,5},{8,10},{9,15},{10,... | collective-permute-start | bytes 2162696 | tf_op jit(solution)/shard_map/ppermute | solution.py:192
  53.5 23.7 %collective-permute-start.4 = (bf16[192,1408]{1,0:T(8,128)(2,1)S(1)}, bf16[192,1408]{1,0:T(8,128)(2,1)}, u32[]{:S(2)}, u32[]{:S(2)}) collective-permute-start(bf16[192,1408]{1,0:T(8,128)(2,1)S(1)} %bitcast.18), channel_id=1, source_target_pairs={{0,1},{1,0},{2,3},{3,2},{4,5},{5,4},{6,7},{7,6},{8,9},{9,8},{10,11... | collective-permute-start | bytes 1622024 | tf_op jit(solution)/shard_map/ppermute | solution.py:195
  65.3 20.7 %collective-permute-start.3 = (bf16[64,48,128]{2,1,0:T(8,128)(2,1)S(1)}, bf16[64,48,128]{2,1,0:T(8,128)(2,1)S(1)}, u32[]{:S(2)}, u32[]{:S(2)}) collective-permute-start(bf16[64,48,128]{2,1,0:T(8,128)(2,1)S(1)} %all-to-all-done.packed_in), channel_id=1, source_target_pairs={{0,1},{1,0},{2,3},{3,2},{4,5},{5,4},{6,7},{7,6},{8,9},{9,8},{10,11... | collective-permute-start | bytes 2359304 | tf_op jit(solution)/shard_map/ppermute | solution.py:195
  67.3 15.9 %collective-permute-start.2 = (bf16[176,2048]{1,0:T(8,128)(2,1)S(1)}, bf16[176,2048]{1,0:T(8,128)(2,1)S(1)}, u32[]{:S(2)}, u32[]{:S(2)}) collective-permute-start(bf16[176,2048]{1,0:T(8,128)(2,1)S(1)} %collective-permute-done.1.down2_in), channel_id=1, source_target_pairs={{0,2},{1,7},{2,4},{3,1},{4,6},{5,3},{6,0},{7,5},{8,10},{9,15},{10,... | collective-permute-start | bytes 2162696 | tf_op jit(solution)/shard_map/ppermute | solution.py:192
  70.7 19.2 %collective-permute-start.11 = (bf16[176,2048]{1,0:T(8,128)(2,1)}, bf16[176,2048]{1,0:T(8,128)(2,1)S(1)}, u32[]{:S(2)}, u32[]{:S(2)}) collective-permute-start(bf16[176,2048]{1,0:T(8,128)(2,1)} %collective-permute-done.10.up2_in), channel_id=1, source_target_pairs={{0,2},{1,7},{2,4},{3,1},{4,6},{5,3},{6,0},{7,5},{8,10},{9,15},{10,... | collective-permute-start | bytes 2162696 | tf_op jit(solution)/shard_map/ppermute | solution.py:192
  74.5 23.1 %collective-permute-start.8 = (bf16[176,2048]{1,0:T(8,128)(2,1)}, bf16[176,2048]{1,0:T(8,128)(2,1)S(1)}, u32[]{:S(2)}, u32[]{:S(2)}) collective-permute-start(bf16[176,2048]{1,0:T(8,128)(2,1)} %collective-permute-done.7.gate2_in), channel_id=1, source_target_pairs={{0,2},{1,7},{2,4},{3,1},{4,6},{5,3},{6,0},{7,5},{8,10},{9,15},{10,... | collective-permute-start | bytes 2162696 | tf_op jit(solution)/shard_map/ppermute | solution.py:192
  77.2 4.0 %collective-permute-start.5 = (bf16[192,1408]{1,0:T(8,128)(2,1)}, bf16[192,1408]{1,0:T(8,128)(2,1)S(1)}, u32[]{:S(2)}, u32[]{:S(2)}) collective-permute-start(bf16[192,1408]{1,0:T(8,128)(2,1)} %bitcast.20), channel_id=1, source_target_pairs={{0,1},{1,0},{2,3},{3,2},{4,5},{5,4},{6,7},{7,6},{8,9},{9,8},{10,11... | collective-permute-start | bytes 1622024 | tf_op jit(solution)/shard_map/ppermute | solution.py:195
  79.1 1.1 copy-start.2
  102.2 4.2 %collective-permute-start.12 = (bf16[192,2048]{1,0:T(8,128)(2,1)S(1)}, bf16[192,2048]{1,0:T(8,128)(2,1)S(1)}, u32[]{:S(2)}, u32[]{:S(2)}) collective-permute-start(bf16[192,2048]{1,0:T(8,128)(2,1)S(1)} %get-tuple-element.16), channel_id=1, source_target_pairs={{0,1},{1,0},{2,3},{3,2},{4,5},{5,4},{6,7},{7,6},{8,9},{9,8},{10,11... | collective-permute-start | bytes 2359304 | tf_op jit(solution)/shard_map/ppermute | solution.py:195
  107.7 15.2 %copy-start.3 = (s32[32,6]{0,1:T(8,128)S(1)}, s32[32,6]{0,1:T(8,128)}, u32[]{:S(2)}) copy-start(s32[32,6]{0,1:T(8,128)} %param.9) | copy-start | bytes 2308
  107.7 59.5 %all-to-all-start.1 = ((bf16[64,48,128]{2,1,0:T(8,128)(2,1)}), bf16[64,48,128]{2,1,0:T(8,128)(2,1)S(1)}, u32[]{:S(2)}, u32[]{:S(2)}) async-start(bf16[64,48,128]{2,1,0:T(8,128)(2,1)} %shard_map.89), calls=%async_computation.1 | async-start | bytes 1572864 | tf_op jit(solution)/shard_map/all_to_all | solution.py:198

commit v7 on v6

--- a/solution.py
+++ b/solution.py
@@ -3,7 +3,7 @@
 from jax import lax
 from jax.experimental import pallas as pl
 from jax.experimental.pallas import tpu as pltpu
-from jax.sharding import PartitionSpec as P
+from jax.sharding import Mesh, PartitionSpec as P
 
 F32 = jnp.float32
 BF16 = jnp.bfloat16
@@ -11,6 +11,7 @@
 AN = pl.BlockSpec(memory_space=pl.ANY)
 LINKS = 4
 SLOTS = 3
+ROWS_Y = 4
 
 
 def call(kernel, ins, outs, flops=0, scratch=(), spec=VM, limit=24 << 20):
@@ -34,16 +35,23 @@
     return made
 
 
-def pack(value, out_ref, part=0, parts=1):
+def pack(value, out_ref, turned=False):
     experts, deep, lanes = out_ref.shape
     slots = value.shape[0] // experts
     chunks = deep // slots
-    span = chunks // parts
+    span = chunks
     for s in range(slots):
         block = value[s * experts : (s + 1) * experts].astype(BF16)
         stack = jnp.stack([block[:, c * lanes : (c + 1) * lanes] for c in range(span)])
-        low = s * chunks + part * span
-        out_ref[:, low : low + span, :] = jnp.swapaxes(stack, 0, 1)
+        low = s * chunks
+        blocks = jnp.swapaxes(stack, 0, 1)
+        if not turned:
+            out_ref[:, low : low + span, :] = blocks
+            continue
+        planes = experts // ROWS_Y
+        blocks = blocks.reshape(planes, ROWS_Y, span, lanes)
+        for y in range(ROWS_Y):
+            out_ref[y * planes : (y + 1) * planes, low : low + span, :] = blocks[:, y]
 
 
 def unpack(packed_ref, s, slots):
@@ -88,20 +96,32 @@
     packed_in, down0_in, down1_in, down2_in, down3_in, gf_in, uf_in,
     hidden_ref, packed_ref, down_ref, gf_ref, uf_ref, rows_ref, sems,
 ):
-    copies = [(packed_in, packed_ref)]
-    for piece, place in zip((down0_in, down1_in, down2_in, down3_in), spots(down0_in.shape[0])):
-        copies.append((piece, down_ref.at[place, :]))
+    planes, across_y, deep, lanes = packed_ref.shape
+    copies = [(packed_in.at[pl.ds(y * planes, planes)], packed_ref.at[:, y]) for y in range(across_y)]
+    half = down_ref.shape[1] // 2
+    downs = (down0_in, down1_in, down2_in, down3_in)
+    for n in range(2):
+        columns = pl.ds(n * half, half)
+        for piece, place in zip(downs, spots(down0_in.shape[0])):
+            copies.append((piece.at[:, columns], down_ref.at[place, columns]))
     copies = fetch(copies + [(gf_in, gf_ref), (uf_in, uf_ref)], sems)
-    copies[0].wait()
-    experts = packed_ref.shape[0]
+    for copy in copies[:across_y]:
+        copy.wait()
+    experts = planes * across_y
     slots = rows_ref.shape[0] // experts
+    packed = packed_ref[...].reshape(experts, deep, lanes)
     for s in range(slots):
-        rows_ref[s * experts : (s + 1) * experts, :] = unpack(packed_ref, s, slots)
-    for copy in copies[1:]:
+        rows_ref[s * experts : (s + 1) * experts, :] = unpack(packed, s, slots)
+    grad = jnp.zeros(gf_ref.shape, F32)
+    for n in range(2):
+        for copy in copies[across_y + n * LINKS : across_y + (n + 1) * LINKS]:
+            copy.wait()
+        columns = slice(n * half, (n + 1) * half)
+        grad += lax.dot_general(
+            rows_ref[:, columns], down_ref[:, columns], (((1,), (1,)), ((), ())), preferred_element_type=F32
+        )
+    for copy in copies[across_y + 2 * LINKS :]:
         copy.wait()
-    grad = lax.dot_general(
-        rows_ref[...], down_ref[...], (((1,), (1,)), ((), ())), preferred_element_type=F32
-    )
     units = grad.shape[1]
     hidden_ref[:, :units] = (grad * gf_ref[...]).astype(BF16)
     hidden_ref[:, units:] = (grad * uf_ref[...]).astype(BF16)
@@ -140,14 +160,16 @@
 
 
 def join_kernel(own_ref, back_ref, out_ref):
-    pack(own_ref[...].astype(F32) + back_ref[...].astype(F32), out_ref)
+    pack(own_ref[...].astype(F32) + back_ref[...].astype(F32), out_ref, True)
 
 
 def chosen_of(routes_ref, experts):
     top, tokens = routes_ref.shape
     row = lax.broadcasted_iota(jnp.int32, (experts * SLOTS, tokens), 0)
     number = row // experts
-    named = row - number * experts
+    block = row - number * experts
+    planes = experts // ROWS_Y
+    named = (block % planes) * ROWS_Y + block // planes
     hits = jnp.zeros(row.shape, F32)
     for k in range(top):
         hits = jnp.where(routes_ref[k : k + 1, :] == named, 1.0, hits)
@@ -177,7 +199,7 @@
 
 
 def body(grad_out, routes, gates, w_gate, w_up, w_down, saved_gate, saved_up):
-    experts = lax.axis_size("expert")
+    experts = lax.axis_size("z") * lax.axis_size("y")
     copies = lax.axis_size("replica")
     tokens, width = grad_out.shape
     slots = saved_gate.shape[3]
@@ -195,7 +217,7 @@
         return lax.ppermute(a, "replica", [(i, i ^ 1) for i in range(copies)])
 
     def exchange(a):
-        return lax.all_to_all(a, "expert", split_axis=0, concat_axis=0, tiled=True)
+        return lax.all_to_all(a, ("y", "z"), split_axis=0, concat_axis=0, tiled=True)
 
     downs, gate_pieces, up_pieces = [w_down[0]], [w_gate[0]], [w_up[0]]
     for _ in range(1, LINKS):
@@ -221,12 +243,12 @@
     hidden = jax.ShapeDtypeStruct((rows, 2 * hidden_units), BF16)
     cost = 2 * rows * hidden_units * width
     scratch = (
-        pltpu.VMEM((experts, 2 * deep, 128), BF16),
+        pltpu.VMEM((experts // ROWS_Y, ROWS_Y, 2 * deep, 128), BF16),
         pltpu.VMEM((hidden_units, width), BF16),
         pltpu.VMEM((rows, hidden_units), F32),
         pltpu.VMEM((rows, hidden_units), F32),
         pltpu.VMEM((rows, width), BF16),
-        pltpu.SemaphoreType.DMA((7,)),
+        pltpu.SemaphoreType.DMA((ROWS_Y + 2 * LINKS + 2,)),
     )
     other_rows = across(arrived)
 
@@ -255,16 +277,18 @@
 
 
 def solution(mesh):
+    devices = mesh.devices
+    split = Mesh(devices.reshape(-1, ROWS_Y, devices.shape[1]), ("z", "y", "replica"))
     in_specs = (
-        P(("expert", "replica"), None),
-        P(("expert", "replica"), None),
-        P(("expert", "replica"), None),
-        P("expert", "replica", None),
-        P("expert", "replica", None),
-        P("expert", "replica", None),
-        P("expert", "replica", None, None, None),
-        P("expert", "replica", None, None, None),
-    )
-    out_specs = P(("expert", "replica"), None)
-
-    return jax.shard_map(body, mesh=mesh, in_specs=in_specs, out_specs=out_specs, check_vma=False)
+        P(("z", "y", "replica"), None),
+        P(("z", "y", "replica"), None),
+        P(("z", "y", "replica"), None),
+        P(("z", "y"), "replica", None),
+        P(("z", "y"), "replica", None),
+        P(("z", "y"), "replica", None),
+        P(("z", "y"), "replica", None, None, None),
+        P(("z", "y"), "replica", None, None, None),
+    )
+    out_specs = P(("z", "y", "replica"), None)
+
+    return jax.shard_map(body, mesh=split, in_specs=in_specs, out_specs=out_specs, check_vma=False)

time: 169 us -> 168 us (level)
    ppermute x9, waiting for transfers between devices: 24.7 us -> 27.4 us  [along(): return lax.ppermute(a, 'replica', pairs)]
    all_to_all x2, waiting for transfers between devices: 53.4 us -> 51 us  [exchange(): lax.all_to_all(a, ('y', 'z'), split_axis=0, concat_axis=0, tiled=True)]
  transfers between devices with their start and end apart: 15 -> 15, of which waited for: 10 -> 9; matrix products, arithmetic and copies ran while one was open for 0% -> 0% of each run, Pallas kernels for 5% -> 5%
where the time goes in v7:
time: 168 us; the launch traced here: 167 us
  waiting for transfers between devices  80.7 us (48%)
  starting transfers between devices  68 us (40%)
  Pallas kernels  17.2 us (10%)
    all_to_all x2, waiting for transfers between devices, exchange(): lax.all_to_all(a, ('y', 'z'), split_axis=0, concat_axis=0, tiled=True)  51 us
    all_to_all x2, starting transfers between devices, exchange(): lax.all_to_all(a, ('y', 'z'), split_axis=0, concat_axis=0, tiled=True)  34.1 us
    ppermute x9, waiting for transfers between devices, along(): return lax.ppermute(a, 'replica', pairs)  27.4 us
    ppermute x9, starting transfers between devices, along(): return lax.ppermute(a, 'replica', pairs)  25.4 us
    pallas_call x9, Pallas kernels, call(): pl.pallas_call(kernel, out_shape=outs[0] if single else tuple(outs), in_s...  17.2 us
    ppermute x4, starting transfers between devices, across(): return lax.ppermute(a, 'replica', [(i, i ^ 1) for i in range(copies)])  8.48 us
  transfers between devices with their start and end apart: 15, of which 9 were waited for; matrix products, arithmetic and copies ran while one was open for 0% of the time, Pallas kernels for 5%

profile of v7, /device:TPU:8, one launch (start us, length us, event | category | flops | bytes accessed | tf_op | source)
XLA Modules:
  0.0 167.2 jit_solution(11655686953564280062)
XLA Ops:
  0.0 2.6 %shard_map.83 = bf16[64,48,128]{2,1,0:T(8,128)(2,1)} custom-call(s32[6,32]{1,0:T(8,128)} %bitcast.22, f32[6,32]{1,0:T(8,128)} %bitcast.24, bf16[32,2048]{1,0:T(8,128)(2,1)} %grad_ref.1), custom_call_target="tpu_custom_call" | custom-call | flops 25165824 | bytes 919040 | tf_op jit(solution)/shard_map/pallas_call | solution.py:20
  2.6 0.0 copy-start
  2.6 0.0 copy-start.1
  2.6 18.9 %all-to-all-start = ((bf16[64,48,128]{2,1,0:T(8,128)(2,1)}), bf16[64,48,128]{2,1,0:T(8,128)(2,1)S(1)}, u32[]{:S(2)}, u32[]{:S(2)}) async-start(bf16[64,48,128]{2,1,0:T(8,128)(2,1)} %shard_map.83), calls=%async_computation | async-start | bytes 1572864 | tf_op jit(solution)/shard_map/all_to_all | solution.py:220
  21.5 0.0 copy-done
  21.5 3.4 %collective-permute-start = (bf16[176,2048]{1,0:T(8,128)(2,1)S(1)}, bf16[176,2048]{1,0:T(8,128)(2,1)S(1)}, u32[]{:S(2)}, u32[]{:S(2)}) collective-permute-start(bf16[176,2048]{1,0:T(8,128)(2,1)S(1)} %bitcast.15), channel_id=1, source_target_pairs={{0,2},{1,7},{2,4},{3,1},{4,6},{5,3},{6,0},{7,5},{8,10},{9,15},{10,... | collective-permute-start | bytes 2162696 | tf_op jit(solution)/shard_map/ppermute | solution.py:214
  24.9 3.4 %collective-permute-start.9 = (bf16[176,2048]{1,0:T(8,128)(2,1)}, bf16[176,2048]{1,0:T(8,128)(2,1)}, u32[]{:S(2)}, u32[]{:S(2)}) collective-permute-start(bf16[176,2048]{1,0:T(8,128)(2,1)} %bitcast.14.up0_in), channel_id=1, source_target_pairs={{0,2},{1,7},{2,4},{3,1},{4,6},{5,3},{6,0},{7,5},{8,10},{9,15},{10,... | collective-permute-start | bytes 2162696 | tf_op jit(solution)/shard_map/ppermute | solution.py:214
  28.3 3.1 %collective-permute-start.6 = (bf16[176,2048]{1,0:T(8,128)(2,1)}, bf16[176,2048]{1,0:T(8,128)(2,1)}, u32[]{:S(2)}, u32[]{:S(2)}) collective-permute-start(bf16[176,2048]{1,0:T(8,128)(2,1)} %bitcast.13.gate0_in), channel_id=1, source_target_pairs={{0,2},{1,7},{2,4},{3,1},{4,6},{5,3},{6,0},{7,5},{8,10},{9,15},{10,... | collective-permute-start | bytes 2162696 | tf_op jit(solution)/shard_map/ppermute | solution.py:214
  31.4 4.5 %collective-permute-done.down1_in = bf16[176,2048]{1,0:T(8,128)(2,1)S(1)} collective-permute-done((bf16[176,2048]{1,0:T(8,128)(2,1)S(1)}, bf16[176,2048]{1,0:T(8,128)(2,1)S(1)}, u32[]{:S(2)}, u32[]{:S(2)}) %collective-permute-start) | collective-permute-done | bytes 720928 | tf_op jit(solution)/shard_map/ppermute | solution.py:214
  35.9 2.2 %collective-permute-start.1 = (bf16[176,2048]{1,0:T(8,128)(2,1)S(1)}, bf16[176,2048]{1,0:T(8,128)(2,1)S(1)}, u32[]{:S(2)}, u32[]{:S(2)}) collective-permute-start(bf16[176,2048]{1,0:T(8,128)(2,1)S(1)} %collective-permute-done.down1_in), channel_id=1, source_target_pairs={{0,2},{1,7},{2,4},{3,1},{4,6},{5,3},{6,0},{7,5},{8,10},{9,15},{10,... | collective-permute-start | bytes 2162696 | tf_op jit(solution)/shard_map/ppermute | solution.py:214
  38.1 5.6 %collective-permute-done.9.up1_in = bf16[176,2048]{1,0:T(8,128)(2,1)} collective-permute-done((bf16[176,2048]{1,0:T(8,128)(2,1)}, bf16[176,2048]{1,0:T(8,128)(2,1)}, u32[]{:S(2)}, u32[]{:S(2)}) %collective-permute-start.9) | collective-permute-done | bytes 720928 | tf_op jit(solution)/shard_map/ppermute | solution.py:214
  43.7 2.2 %collective-permute-start.10 = (bf16[176,2048]{1,0:T(8,128)(2,1)}, bf16[176,2048]{1,0:T(8,128)(2,1)}, u32[]{:S(2)}, u32[]{:S(2)}) collective-permute-start(bf16[176,2048]{1,0:T(8,128)(2,1)} %collective-permute-done.9.up1_in), channel_id=1, source_target_pairs={{0,2},{1,7},{2,4},{3,1},{4,6},{5,3},{6,0},{7,5},{8,10},{9,15},{10,... | collective-permute-start | bytes 2162696 | tf_op jit(solution)/shard_map/ppermute | solution.py:214
  45.9 5.5 %collective-permute-done.6.gate1_in = bf16[176,2048]{1,0:T(8,128)(2,1)} collective-permute-done((bf16[176,2048]{1,0:T(8,128)(2,1)}, bf16[176,2048]{1,0:T(8,128)(2,1)}, u32[]{:S(2)}, u32[]{:S(2)}) %collective-permute-start.6) | collective-permute-done | bytes 720928 | tf_op jit(solution)/shard_map/ppermute | solution.py:214
  51.4 2.2 %collective-permute-start.7 = (bf16[176,2048]{1,0:T(8,128)(2,1)}, bf16[176,2048]{1,0:T(8,128)(2,1)}, u32[]{:S(2)}, u32[]{:S(2)}) collective-permute-start(bf16[176,2048]{1,0:T(8,128)(2,1)} %collective-permute-done.6.gate1_in), channel_id=1, source_target_pairs={{0,2},{1,7},{2,4},{3,1},{4,6},{5,3},{6,0},{7,5},{8,10},{9,15},{10,... | collective-permute-start | bytes 2162696 | tf_op jit(solution)/shard_map/ppermute | solution.py:214
  53.6 0.0 copy-done.1
  53.6 2.4 %collective-permute-start.4 = (bf16[192,1408]{1,0:T(8,128)(2,1)S(1)}, bf16[192,1408]{1,0:T(8,128)(2,1)}, u32[]{:S(2)}, u32[]{:S(2)}) collective-permute-start(bf16[192,1408]{1,0:T(8,128)(2,1)S(1)} %bitcast.18), channel_id=1, source_target_pairs={{0,1},{1,0},{2,3},{3,2},{4,5},{5,4},{6,7},{7,6},{8,9},{9,8},{10,11... | collective-permute-start | bytes 1622024 | tf_op jit(solution)/shard_map/ppermute | solution.py:217
  56.1 8.2 %all-to-all-done.packed_in = bf16[64,48,128]{2,1,0:T(8,128)(2,1)S(1)} async-done(((bf16[64,48,128]{2,1,0:T(8,128)(2,1)}), bf16[64,48,128]{2,1,0:T(8,128)(2,1)S(1)}, u32[]{:S(2)}, u32[]{:S(2)}) %all-to-all-start) | async-done | bytes 786464 | tf_op jit(solution)/shard_map/all_to_all | solution.py:220
  64.3 1.9 %collective-permute-start.3 = (bf16[64,48,128]{2,1,0:T(8,128)(2,1)S(1)}, bf16[64,48,128]{2,1,0:T(8,128)(2,1)S(1)}, u32[]{:S(2)}, u32[]{:S(2)}) collective-permute-start(bf16[64,48,128]{2,1,0:T(8,128)(2,1)S(1)} %all-to-all-done.packed_in), channel_id=1, source_target_pairs={{0,1},{1,0},{2,3},{3,2},{4,5},{5,4},{6,7},{7,6},{8,9},{9,8},{10,11... | collective-permute-start | bytes 2359304 | tf_op jit(solution)/shard_map/ppermute | solution.py:217
  66.2 0.0 collective-permute-done.1.down2_in
  66.2 3.4 %collective-permute-start.2 = (bf16[176,2048]{1,0:T(8,128)(2,1)S(1)}, bf16[176,2048]{1,0:T(8,128)(2,1)S(1)}, u32[]{:S(2)}, u32[]{:S(2)}) collective-permute-start(bf16[176,2048]{1,0:T(8,128)(2,1)S(1)} %collective-permute-done.1.down2_in), channel_id=1, source_target_pairs={{0,2},{1,7},{2,4},{3,1},{4,6},{5,3},{6,0},{7,5},{8,10},{9,15},{10,... | collective-permute-start | bytes 2162696 | tf_op jit(solution)/shard_map/ppermute | solution.py:214
  69.6 0.0 collective-permute-done.10.up2_in
  69.6 3.4 %collective-permute-start.11 = (bf16[176,2048]{1,0:T(8,128)(2,1)}, bf16[176,2048]{1,0:T(8,128)(2,1)S(1)}, u32[]{:S(2)}, u32[]{:S(2)}) collective-permute-start(bf16[176,2048]{1,0:T(8,128)(2,1)} %collective-permute-done.10.up2_in), channel_id=1, source_target_pairs={{0,2},{1,7},{2,4},{3,1},{4,6},{5,3},{6,0},{7,5},{8,10},{9,15},{10,... | collective-permute-start | bytes 2162696 | tf_op jit(solution)/shard_map/ppermute | solution.py:214
  73.0 1.6 collective-permute-done.7.gate2_in
  74.6 2.2 %collective-permute-start.8 = (bf16[176,2048]{1,0:T(8,128)(2,1)}, bf16[176,2048]{1,0:T(8,128)(2,1)S(1)}, u32[]{:S(2)}, u32[]{:S(2)}) collective-permute-start(bf16[176,2048]{1,0:T(8,128)(2,1)} %collective-permute-done.7.gate2_in), channel_id=1, source_target_pairs={{0,2},{1,7},{2,4},{3,1},{4,6},{5,3},{6,0},{7,5},{8,10},{9,15},{10,... | collective-permute-start | bytes 2162696 | tf_op jit(solution)/shard_map/ppermute | solution.py:214
  76.8 0.0 collective-permute-done.4.gate_ref
  76.8 2.2 %collective-permute-start.5 = (bf16[192,1408]{1,0:T(8,128)(2,1)}, bf16[192,1408]{1,0:T(8,128)(2,1)S(1)}, u32[]{:S(2)}, u32[]{:S(2)}) collective-permute-start(bf16[192,1408]{1,0:T(8,128)(2,1)} %bitcast.20), channel_id=1, source_target_pairs={{0,1},{1,0},{2,3},{3,2},{4,5},{5,4},{6,7},{7,6},{8,9},{9,8},{10,11... | collective-permute-start | bytes 1622024 | tf_op jit(solution)/shard_map/ppermute | solution.py:217
  79.0 0.0 copy-start.2
  79.1 1.0 copy-done.2
  80.1 0.8 shard_map.84
  80.9 0.0 collective-permute-done.5.up_ref
  81.0 1.9 %shard_map.86 = (f32[192,704]{1,0:T(8,128)S(1)}, f32[192,704]{1,0:T(8,128)S(1)}) custom-call(bf16[192,1408]{1,0:T(8,128)(2,1)} %collective-permute-done.4.gate_ref, bf16[192,1408]{1,0:T(8,128)(2,1)S(1)} %collective-permute-done.5.up_ref), custom_call_target="tpu_custom_call" | custom-call | bytes 2162688 | tf_op jit(solution)/shard_map/pallas_call | solution.py:20
  82.8 0.0 collective-permute-done.2.down3_in
  82.9 2.3 %shard_map.85.own_in = bf16[192,1408]{1,0:T(8,128)(2,1)S(1)} custom-call(bf16[64,48,128]{2,1,0:T(8,128)(2,1)S(1)} %all-to-all-done.packed_in, bf16[176,2048]{1,0:T(8,128)(2,1)S(1)} %bitcast.16, bf16[176,2048]{1,0:T(8,128)(2,1)S(1)} %collective-permute-done.down1_in, bf16[176,2048]{1,0:T(8,128)(2,1)S(1)} %collective-permute-done.1.down2_in, ...), custom_call_target="tpu_custom_call" | custom-call | flops 553648128 | bytes 5292032 | tf_op jit(solution)/shard_map/pallas_call | solution.py:20
  85.2 0.0 collective-permute-done.3.packed_in
  85.2 2.3 %shard_map.87.other_in = bf16[192,1408]{1,0:T(8,128)(2,1)S(1)} custom-call(bf16[64,48,128]{2,1,0:T(8,128)(2,1)S(1)} %collective-permute-done.3.packed_in, bf16[176,2048]{1,0:T(8,128)(2,1)S(1)} %bitcast.17, bf16[176,2048]{1,0:T(8,128)(2,1)S(1)} %collective-permute-done.down1_in, bf16[176,2048]{1,0:T(8,128)(2,1)S(1)} %collective-permute-done.1.down2_in, ...), custom_call_target="tpu_custom_call" | custom-call | flops 553648128 | bytes 5292032 | tf_op jit(solution)/shard_map/pallas_call | solution.py:20
  87.5 2.5 %collective-permute-done.11.up3_in = bf16[176,2048]{1,0:T(8,128)(2,1)S(1)} collective-permute-done((bf16[176,2048]{1,0:T(8,128)(2,1)}, bf16[176,2048]{1,0:T(8,128)(2,1)S(1)}, u32[]{:S(2)}, u32[]{:S(2)}) %collective-permute-start.11) | collective-permute-done | bytes 720928 | tf_op jit(solution)/shard_map/ppermute | solution.py:214
  89.9 7.7 %collective-permute-done.8.gate3_in = bf16[176,2048]{1,0:T(8,128)(2,1)S(1)} collective-permute-done((bf16[176,2048]{1,0:T(8,128)(2,1)}, bf16[176,2048]{1,0:T(8,128)(2,1)S(1)}, u32[]{:S(2)}, u32[]{:S(2)}) %collective-permute-start.8) | collective-permute-done | bytes 720928 | tf_op jit(solution)/shard_map/ppermute | solution.py:214
  97.7 4.6 %shard_map.88 = (bf16[192,2048]{1,0:T(8,128)(2,1)S(1)}, bf16[192,2048]{1,0:T(8,128)(2,1)S(1)}) custom-call(bf16[192,1408]{1,0:T(8,128)(2,1)S(1)} %shard_map.85.own_in, bf16[192,1408]{1,0:T(8,128)(2,1)S(1)} %shard_map.87.other_in, bf16[176,2048]{1,0:T(8,128)(2,1)} %bitcast.13.gate0_in, bf16[176,2048]{1,0:T(8,128)(2,1)} %collective-permute-done.6.gate1_in, ...), custom_call_target="tpu_custom_call" | custom-call | flops 2214592512 | bytes 8421376 | tf_op jit(solution)/shard_map/pallas_call | solution.py:20
  102.3 1.9 %collective-permute-start.12 = (bf16[192,2048]{1,0:T(8,128)(2,1)S(1)}, bf16[192,2048]{1,0:T(8,128)(2,1)S(1)}, u32[]{:S(2)}, u32[]{:S(2)}) collective-permute-start(bf16[192,2048]{1,0:T(8,128)(2,1)S(1)} %get-tuple-element.16), channel_id=1, source_target_pairs={{0,1},{1,0},{2,3},{3,2},{4,5},{5,4},{6,7},{7,6},{8,9},{9,8},{10,11... | collective-permute-start | bytes 2359304 | tf_op jit(solution)/shard_map/ppermute | solution.py:217
  104.3 2.3 %collective-permute-done.12.back_ref = bf16[192,2048]{1,0:T(8,128)(2,1)S(1)} collective-permute-done((bf16[192,2048]{1,0:T(8,128)(2,1)S(1)}, bf16[192,2048]{1,0:T(8,128)(2,1)S(1)}, u32[]{:S(2)}, u32[]{:S(2)}) %collective-permute-start.12) | collective-permute-done | bytes 786464 | tf_op jit(solution)/shard_map/ppermute | solution.py:217
  106.5 1.3 shard_map.89
  107.8 0.0 copy-start.3
  107.8 15.3 %all-to-all-start.1 = ((bf16[64,48,128]{2,1,0:T(8,128)(2,1)}), bf16[64,48,128]{2,1,0:T(8,128)(2,1)S(1)}, u32[]{:S(2)}, u32[]{:S(2)}) async-start(bf16[64,48,128]{2,1,0:T(8,128)(2,1)} %shard_map.89), calls=%async_computation.1 | async-start | bytes 1572864 | tf_op jit(solution)/shard_map/all_to_all | solution.py:220
  123.0 0.0 copy-done.3
  123.1 0.3 shard_map.82.hot_ref
  123.3 42.8 %all-to-all-done.1.back_ref = bf16[64,48,128]{2,1,0:T(8,128)(2,1)S(1)} async-done(((bf16[64,48,128]{2,1,0:T(8,128)(2,1)}), bf16[64,48,128]{2,1,0:T(8,128)(2,1)S(1)}, u32[]{:S(2)}, u32[]{:S(2)}) %all-to-all-start.1) | async-done | bytes 786464 | tf_op jit(solution)/shard_map/all_to_all | solution.py:220
  166.1 1.1 shard_map.90
Async XLA Ops:
  2.6 18.9 %copy-start = (bf16[1,176,2048]{2,1,0:T(8,128)(2,1)S(1)}, bf16[1,176,2048]{2,1,0:T(8,128)(2,1)}, u32[]{:S(2)}) copy-start(bf16[1,176,2048]{2,1,0:T(8,128)(2,1)} %param.13) | copy-start | bytes 2162692
  2.6 51.0 %copy-start.1 = (bf16[1,1,64,3,1408]{4,2,3,1,0:T(8,128)(2,1)S(1)}, bf16[1,1,64,3,1408]{4,2,3,1,0:T(8,128)(2,1)}, u32[]{:S(2)}) copy-start(bf16[1,1,64,3,1408]{4,2,3,1,0:T(8,128)(2,1)} %param.14) | copy-start | bytes 1622020
  2.6 61.6 %all-to-all-start = ((bf16[64,48,128]{2,1,0:T(8,128)(2,1)}), bf16[64,48,128]{2,1,0:T(8,128)(2,1)S(1)}, u32[]{:S(2)}, u32[]{:S(2)}) async-start(bf16[64,48,128]{2,1,0:T(8,128)(2,1)} %shard_map.83), calls=%async_computation | async-start | bytes 1572864 | tf_op jit(solution)/shard_map/all_to_all | solution.py:220
  21.5 14.4 %collective-permute-start = (bf16[176,2048]{1,0:T(8,128)(2,1)S(1)}, bf16[176,2048]{1,0:T(8,128)(2,1)S(1)}, u32[]{:S(2)}, u32[]{:S(2)}) collective-permute-start(bf16[176,2048]{1,0:T(8,128)(2,1)S(1)} %bitcast.15), channel_id=1, source_target_pairs={{0,2},{1,7},{2,4},{3,1},{4,6},{5,3},{6,0},{7,5},{8,10},{9,15},{10,... | collective-permute-start | bytes 2162696 | tf_op jit(solution)/shard_map/ppermute | solution.py:214
  24.9 18.8 %collective-permute-start.9 = (bf16[176,2048]{1,0:T(8,128)(2,1)}, bf16[176,2048]{1,0:T(8,128)(2,1)}, u32[]{:S(2)}, u32[]{:S(2)}) collective-permute-start(bf16[176,2048]{1,0:T(8,128)(2,1)} %bitcast.14.up0_in), channel_id=1, source_target_pairs={{0,2},{1,7},{2,4},{3,1},{4,6},{5,3},{6,0},{7,5},{8,10},{9,15},{10,... | collective-permute-start | bytes 2162696 | tf_op jit(solution)/shard_map/ppermute | solution.py:214
  28.3 23.1 %collective-permute-start.6 = (bf16[176,2048]{1,0:T(8,128)(2,1)}, bf16[176,2048]{1,0:T(8,128)(2,1)}, u32[]{:S(2)}, u32[]{:S(2)}) collective-permute-start(bf16[176,2048]{1,0:T(8,128)(2,1)} %bitcast.13.gate0_in), channel_id=1, source_target_pairs={{0,2},{1,7},{2,4},{3,1},{4,6},{5,3},{6,0},{7,5},{8,10},{9,15},{10,... | collective-permute-start | bytes 2162696 | tf_op jit(solution)/shard_map/ppermute | solution.py:214
  35.9 30.3 %collective-permute-start.1 = (bf16[176,2048]{1,0:T(8,128)(2,1)S(1)}, bf16[176,2048]{1,0:T(8,128)(2,1)S(1)}, u32[]{:S(2)}, u32[]{:S(2)}) collective-permute-start(bf16[176,2048]{1,0:T(8,128)(2,1)S(1)} %collective-permute-done.down1_in), channel_id=1, source_target_pairs={{0,2},{1,7},{2,4},{3,1},{4,6},{5,3},{6,0},{7,5},{8,10},{9,15},{10,... | collective-permute-start | bytes 2162696 | tf_op jit(solution)/shard_map/ppermute | solution.py:214
  43.7 25.9 %collective-permute-start.10 = (bf16[176,2048]{1,0:T(8,128)(2,1)}, bf16[176,2048]{1,0:T(8,128)(2,1)}, u32[]{:S(2)}, u32[]{:S(2)}) collective-permute-start(bf16[176,2048]{1,0:T(8,128)(2,1)} %collective-permute-done.9.up1_in), channel_id=1, source_target_pairs={{0,2},{1,7},{2,4},{3,1},{4,6},{5,3},{6,0},{7,5},{8,10},{9,15},{10,... | collective-permute-start | bytes 2162696 | tf_op jit(solution)/shard_map/ppermute | solution.py:214
  51.4 23.2 %collective-permute-start.7 = (bf16[176,2048]{1,0:T(8,128)(2,1)}, bf16[176,2048]{1,0:T(8,128)(2,1)}, u32[]{:S(2)}, u32[]{:S(2)}) collective-permute-start(bf16[176,2048]{1,0:T(8,128)(2,1)} %collective-permute-done.6.gate1_in), channel_id=1, source_target_pairs={{0,2},{1,7},{2,4},{3,1},{4,6},{5,3},{6,0},{7,5},{8,10},{9,15},{10,... | collective-permute-start | bytes 2162696 | tf_op jit(solution)/shard_map/ppermute | solution.py:214
  53.6 23.2 %collective-permute-start.4 = (bf16[192,1408]{1,0:T(8,128)(2,1)S(1)}, bf16[192,1408]{1,0:T(8,128)(2,1)}, u32[]{:S(2)}, u32[]{:S(2)}) collective-permute-start(bf16[192,1408]{1,0:T(8,128)(2,1)S(1)} %bitcast.18), channel_id=1, source_target_pairs={{0,1},{1,0},{2,3},{3,2},{4,5},{5,4},{6,7},{7,6},{8,9},{9,8},{10,11... | collective-permute-start | bytes 1622024 | tf_op jit(solution)/shard_map/ppermute | solution.py:217
  64.3 20.9 %collective-permute-start.3 = (bf16[64,48,128]{2,1,0:T(8,128)(2,1)S(1)}, bf16[64,48,128]{2,1,0:T(8,128)(2,1)S(1)}, u32[]{:S(2)}, u32[]{:S(2)}) collective-permute-start(bf16[64,48,128]{2,1,0:T(8,128)(2,1)S(1)} %all-to-all-done.packed_in), channel_id=1, source_target_pairs={{0,1},{1,0},{2,3},{3,2},{4,5},{5,4},{6,7},{7,6},{8,9},{9,8},{10,11... | collective-permute-start | bytes 2359304 | tf_op jit(solution)/shard_map/ppermute | solution.py:217
  66.2 16.7 %collective-permute-start.2 = (bf16[176,2048]{1,0:T(8,128)(2,1)S(1)}, bf16[176,2048]{1,0:T(8,128)(2,1)S(1)}, u32[]{:S(2)}, u32[]{:S(2)}) collective-permute-start(bf16[176,2048]{1,0:T(8,128)(2,1)S(1)} %collective-permute-done.1.down2_in), channel_id=1, source_target_pairs={{0,2},{1,7},{2,4},{3,1},{4,6},{5,3},{6,0},{7,5},{8,10},{9,15},{10,... | collective-permute-start | bytes 2162696 | tf_op jit(solution)/shard_map/ppermute | solution.py:214
  69.6 20.4 %collective-permute-start.11 = (bf16[176,2048]{1,0:T(8,128)(2,1)}, bf16[176,2048]{1,0:T(8,128)(2,1)S(1)}, u32[]{:S(2)}, u32[]{:S(2)}) collective-permute-start(bf16[176,2048]{1,0:T(8,128)(2,1)} %collective-permute-done.10.up2_in), channel_id=1, source_target_pairs={{0,2},{1,7},{2,4},{3,1},{4,6},{5,3},{6,0},{7,5},{8,10},{9,15},{10,... | collective-permute-start | bytes 2162696 | tf_op jit(solution)/shard_map/ppermute | solution.py:214
  74.6 23.1 %collective-permute-start.8 = (bf16[176,2048]{1,0:T(8,128)(2,1)}, bf16[176,2048]{1,0:T(8,128)(2,1)S(1)}, u32[]{:S(2)}, u32[]{:S(2)}) collective-permute-start(bf16[176,2048]{1,0:T(8,128)(2,1)} %collective-permute-done.7.gate2_in), channel_id=1, source_target_pairs={{0,2},{1,7},{2,4},{3,1},{4,6},{5,3},{6,0},{7,5},{8,10},{9,15},{10,... | collective-permute-start | bytes 2162696 | tf_op jit(solution)/shard_map/ppermute | solution.py:214
  76.8 4.1 %collective-permute-start.5 = (bf16[192,1408]{1,0:T(8,128)(2,1)}, bf16[192,1408]{1,0:T(8,128)(2,1)S(1)}, u32[]{:S(2)}, u32[]{:S(2)}) collective-permute-start(bf16[192,1408]{1,0:T(8,128)(2,1)} %bitcast.20), channel_id=1, source_target_pairs={{0,1},{1,0},{2,3},{3,2},{4,5},{5,4},{6,7},{7,6},{8,9},{9,8},{10,11... | collective-permute-start | bytes 1622024 | tf_op jit(solution)/shard_map/ppermute | solution.py:217
  79.0 1.1 copy-start.2
  102.3 4.2 %collective-permute-start.12 = (bf16[192,2048]{1,0:T(8,128)(2,1)S(1)}, bf16[192,2048]{1,0:T(8,128)(2,1)S(1)}, u32[]{:S(2)}, u32[]{:S(2)}) collective-permute-start(bf16[192,2048]{1,0:T(8,128)(2,1)S(1)} %get-tuple-element.16), channel_id=1, source_target_pairs={{0,1},{1,0},{2,3},{3,2},{4,5},{5,4},{6,7},{7,6},{8,9},{9,8},{10,11... | collective-permute-start | bytes 2359304 | tf_op jit(solution)/shard_map/ppermute | solution.py:217
  107.8 15.3 %copy-start.3 = (s32[32,6]{0,1:T(8,128)S(1)}, s32[32,6]{0,1:T(8,128)}, u32[]{:S(2)}) copy-start(s32[32,6]{0,1:T(8,128)} %param.9) | copy-start | bytes 2308
  107.8 58.4 %all-to-all-start.1 = ((bf16[64,48,128]{2,1,0:T(8,128)(2,1)}), bf16[64,48,128]{2,1,0:T(8,128)(2,1)S(1)}, u32[]{:S(2)}, u32[]{:S(2)}) async-start(bf16[64,48,128]{2,1,0:T(8,128)(2,1)} %shard_map.89), calls=%async_computation.1 | async-start | bytes 1572864 | tf_op jit(solution)/shard_map/all_to_all | solution.py:220

commit v8 on v7

--- a/solution.py
+++ b/solution.py
@@ -20,7 +20,7 @@
     return pl.pallas_call(
         kernel,
         out_shape=outs[0] if single else tuple(outs),
-        in_specs=[spec] * len(ins),
+        in_specs=spec if isinstance(spec, list) else [spec] * len(ins),
         out_specs=VM if single else tuple([VM] * len(outs)),
         scratch_shapes=list(scratch),
         compiler_params=pltpu.CompilerParams(vmem_limit_bytes=limit),
@@ -72,37 +72,34 @@
 
 
 def factor_kernel(gate_ref, up_ref, gf_ref, uf_ref):
-    slice_width = gf_ref.shape[1] // LINKS
-    first = (lax.axis_index("replica") & 1) == 0
+    slice_width = gf_ref.shape[2]
+    replica = lax.axis_index("replica")
+    link, turn = replica >> 1, 2 * (replica & 1) - 1
+    first = turn < 0
     for q in range(LINKS):
         low = 2 * q * slice_width
         mid, high = low + slice_width, low + 2 * slice_width
         g = jnp.where(first, gate_ref[:, low:mid].astype(F32), gate_ref[:, mid:high].astype(F32))
         u = jnp.where(first, up_ref[:, low:mid].astype(F32), up_ref[:, mid:high].astype(F32))
         sig = jax.nn.sigmoid(g)
-        place = slice(q * slice_width, (q + 1) * slice_width)
-        uf_ref[:, place] = g * sig
-        gf_ref[:, place] = u * sig * (1.0 + g * (1.0 - sig))
-
-
-def spots(width):
-    replica = lax.axis_index("replica")
-    link, turn = replica >> 1, 2 * (replica & 1) - 1
-    steps = [(link + step * turn + LINKS) & (LINKS - 1) for step in range(LINKS)]
-    return [pl.ds(pl.multiple_of(step * width, 16), width) for step in steps]
+        step = ((q - link) * turn + 2 * LINKS) & (LINKS - 1)
+        uf_ref[step] = g * sig
+        gf_ref[step] = u * sig * (1.0 + g * (1.0 - sig))
 
 
 def hidden_kernel(
     packed_in, down0_in, down1_in, down2_in, down3_in, gf_in, uf_in,
-    hidden_ref, packed_ref, down_ref, gf_ref, uf_ref, rows_ref, sems,
+    early_ref, late_ref, packed_ref, down_ref, gf_ref, uf_ref, rows_ref, sems,
 ):
     planes, across_y, deep, lanes = packed_ref.shape
     copies = [(packed_in.at[pl.ds(y * planes, planes)], packed_ref.at[:, y]) for y in range(across_y)]
     half = down_ref.shape[1] // 2
+    width = down0_in.shape[0]
     downs = (down0_in, down1_in, down2_in, down3_in)
     for n in range(2):
         columns = pl.ds(n * half, half)
-        for piece, place in zip(downs, spots(down0_in.shape[0])):
+        for step, piece in enumerate(downs):
+            place = pl.ds(step * width, width)
             copies.append((piece.at[:, columns], down_ref.at[place, columns]))
     copies = fetch(copies + [(gf_in, gf_ref), (uf_in, uf_ref)], sems)
     for copy in copies[:across_y]:
@@ -112,7 +109,7 @@
     packed = packed_ref[...].reshape(experts, deep, lanes)
     for s in range(slots):
         rows_ref[s * experts : (s + 1) * experts, :] = unpack(packed, s, slots)
-    grad = jnp.zeros(gf_ref.shape, F32)
+    grad = jnp.zeros((rows_ref.shape[0], down_ref.shape[0]), F32)
     for n in range(2):
         for copy in copies[across_y + n * LINKS : across_y + (n + 1) * LINKS]:
             copy.wait()
@@ -122,31 +119,26 @@
         )
     for copy in copies[across_y + 2 * LINKS :]:
         copy.wait()
-    units = grad.shape[1]
-    hidden_ref[:, :units] = (grad * gf_ref[...]).astype(BF16)
-    hidden_ref[:, units:] = (grad * uf_ref[...]).astype(BF16)
-
-
-def output_kernel(
-    own_in, other_in, gate0_in, gate1_in, gate2_in, gate3_in, up0_in, up1_in, up2_in, up3_in,
-    own_ref, theirs_ref, hidden_ref, weight_ref, sems,
-):
-    width = gate0_in.shape[0]
-    rows, hidden = own_in.shape[0], own_in.shape[1] // 2
+    for step in range(LINKS):
+        part = grad[:, step * width : (step + 1) * width]
+        out_ref, low = (early_ref, 2 * step * width) if step < LINKS - 1 else (late_ref, 0)
+        out_ref[:, low : low + width] = (part * gf_ref[step]).astype(BF16)
+        out_ref[:, low + width : low + 2 * width] = (part * uf_ref[step]).astype(BF16)
+
+
+def gather(own_in, other_in, pieces, hidden_ref, weight_ref, sems):
+    rows, width = own_in.shape[0], pieces[0].shape[0]
     parts = sems.shape[0] - 1
     span = weight_ref.shape[1] // parts
-    gates, ups = (gate0_in, gate1_in, gate2_in, gate3_in), (up0_in, up1_in, up2_in, up3_in)
     begun = fetch(
         [(own_in, hidden_ref.at[pl.ds(0, rows), :]), (other_in, hidden_ref.at[pl.ds(rows, rows), :])], sems.at[0]
     )
     blocks = []
     for n in range(parts):
         columns = pl.ds(n * span, span)
-        copies = []
-        for gate_in, up_in, place in zip(gates, ups, spots(width)):
-            copies.append((gate_in.at[:, columns], weight_ref.at[place, columns]))
-            lower = pl.ds(pl.multiple_of(place.start + hidden, 16), width)
-            copies.append((up_in.at[:, columns], weight_ref.at[lower, columns]))
+        copies = [
+            (piece.at[:, columns], weight_ref.at[pl.ds(k * width, width), columns]) for k, piece in enumerate(pieces)
+        ]
         blocks.append(fetch(copies, sems.at[n + 1]))
     for copy in begun:
         copy.wait()
@@ -154,7 +146,19 @@
         for copy in blocks[n]:
             copy.wait()
         columns = slice(n * span, (n + 1) * span)
-        total = jnp.dot(hidden_ref[...], weight_ref[:, columns], preferred_element_type=F32)
+        yield columns, jnp.dot(hidden_ref[...], weight_ref[:, columns], preferred_element_type=F32)
+
+
+def early_kernel(own_in, other_in, g0_in, u0_in, g1_in, u1_in, g2_in, u2_in, sum_ref, hidden_ref, weight_ref, sems):
+    pieces = (g0_in, u0_in, g1_in, u1_in, g2_in, u2_in)
+    for columns, total in gather(own_in, other_in, pieces, hidden_ref, weight_ref, sems):
+        sum_ref[:, columns] = total
+
+
+def late_kernel(sum_ref, own_in, other_in, gate_in, up_in, own_ref, theirs_ref, hidden_ref, weight_ref, sems):
+    rows = own_in.shape[0]
+    for columns, total in gather(own_in, other_in, (gate_in, up_in), hidden_ref, weight_ref, sems):
+        total += sum_ref[:, columns]
         own_ref[:, columns] = total[:rows].astype(BF16)
         theirs_ref[:, columns] = total[rows:].astype(BF16)
 
@@ -235,18 +239,19 @@
 
     saved = tuple(a[0, 0].transpose(1, 0, 2).reshape(rows, -1) for a in (saved_gate, saved_up))
     hidden_units = LINKS * slice_width
-    factor = jax.ShapeDtypeStruct((rows, hidden_units), F32)
+    factor = jax.ShapeDtypeStruct((LINKS, rows, slice_width), F32)
     own_factors = call(factor_kernel, saved, (factor, factor))
     sent = (across(saved[0]), across(saved[1]))
     other_factors = call(factor_kernel, sent, (factor, factor))
 
-    hidden = jax.ShapeDtypeStruct((rows, 2 * hidden_units), BF16)
+    last = 2 * slice_width
+    hidden = tuple(jax.ShapeDtypeStruct((rows, n), BF16) for n in (2 * hidden_units - last, last))
     cost = 2 * rows * hidden_units * width
     scratch = (
         pltpu.VMEM((experts // ROWS_Y, ROWS_Y, 2 * deep, 128), BF16),
         pltpu.VMEM((hidden_units, width), BF16),
-        pltpu.VMEM((rows, hidden_units), F32),
-        pltpu.VMEM((rows, hidden_units), F32),
+        pltpu.VMEM((LINKS, rows, slice_width), F32),
+        pltpu.VMEM((LINKS, rows, slice_width), F32),
         pltpu.VMEM((rows, width), BF16),
         pltpu.SemaphoreType.DMA((ROWS_Y + 2 * LINKS + 2,)),
     )
@@ -254,20 +259,36 @@
 
     def hide(packed_rows, factors):
         ins = (packed_rows,) + tuple(downs) + tuple(factors)
-        return call(hidden_kernel, ins, (hidden,), cost, scratch=scratch, spec=AN)
+        return call(hidden_kernel, ins, hidden, cost, scratch=scratch, spec=AN)
 
     own_hidden = hide(arrived, own_factors)
     other_hidden = hide(other_rows, other_factors)
 
-    pieces = tuple(gate_pieces + up_pieces)
-    scratch2 = (
-        pltpu.VMEM((2 * rows, 2 * hidden_units), BF16),
-        pltpu.VMEM((2 * hidden_units, width), BF16),
-        pltpu.SemaphoreType.DMA((3, 8)),
-    )
+    pieces = [piece for both in zip(gate_pieces, up_pieces) for piece in both]
+
+    def room(n):
+        return (
+            pltpu.VMEM((2 * rows, n), BF16),
+            pltpu.VMEM((n, width), BF16),
+            pltpu.SemaphoreType.DMA((3, n // slice_width)),
+        )
+
     part = jax.ShapeDtypeStruct((rows, width), BF16)
+    early = call(
+        early_kernel,
+        (own_hidden[0], other_hidden[0]) + tuple(pieces[:-2]),
+        (jax.ShapeDtypeStruct((2 * rows, width), F32),),
+        3 * cost,
+        scratch=room(2 * hidden_units - last),
+        spec=AN,
+    )
     ours, theirs = call(
-        output_kernel, (own_hidden, other_hidden) + pieces, (part, part), 4 * cost, scratch=scratch2, spec=AN
+        late_kernel,
+        (early, own_hidden[1], other_hidden[1]) + tuple(pieces[-2:]),
+        (part, part),
+        cost,
+        scratch=room(last),
+        spec=[VM] + [AN] * 4,
     )
     back = across(theirs)
     outgoing = call(join_kernel, (ours, back), (jax.ShapeDtypeStruct((experts, 2 * deep, 128), BF16),))

time: 168 us -> 165 us (0.982)
  waiting for transfers between devices: 80.7 us -> 74.8 us
    ppermute x9, waiting for transfers between devices: 27.4 us -> 21.7 us  [along(): return lax.ppermute(a, 'replica', pairs)]
    pallas_call x9 -> x10, Pallas kernels: 17.2 us -> 18.8 us  [call(): pl.pallas_call(kernel, out_shape=outs[0] if single else tuple(outs), in_s...]
  transfers between devices with their start and end apart: 15 -> 15, of which waited for: 9 -> 8; matrix products, arithmetic and copies ran while one was open for 0% -> 0% of each run, Pallas kernels for 5% -> 7%
where the time goes in v8:
time: 165 us; the launch traced here: 164 us
  waiting for transfers between devices  74.8 us (45%)
  starting transfers between devices  68.4 us (41%)
  Pallas kernels  18.8 us (11%)
  local copies, waits for them, and re-layouts  2.11 us (1%)
    all_to_all x2, waiting for transfers between devices, exchange(): lax.all_to_all(a, ('y', 'z'), split_axis=0, concat_axis=0, tiled=True)  50.8 us
    all_to_all x2, starting transfers between devices, exchange(): lax.all_to_all(a, ('y', 'z'), split_axis=0, concat_axis=0, tiled=True)  33.9 us
    ppermute x9, starting transfers between devices, along(): return lax.ppermute(a, 'replica', pairs)  24.9 us
    ppermute x9, waiting for transfers between devices, along(): return lax.ppermute(a, 'replica', pairs)  21.7 us
    pallas_call x10, Pallas kernels, call(): pl.pallas_call(kernel, out_shape=outs[0] if single else tuple(outs), in_s...  18.8 us
    ppermute x4, starting transfers between devices, across(): return lax.ppermute(a, 'replica', [(i, i ^ 1) for i in range(copies)])  9.66 us
  transfers between devices with their start and end apart: 15, of which 8 were waited for; matrix products, arithmetic and copies ran while one was open for 0% of the time, Pallas kernels for 7%

profile of v8, /device:TPU:8, one launch (start us, length us, event | category | flops | bytes accessed | tf_op | source)
XLA Modules:
  0.0 164.3 jit_solution(14726561562133797624)
XLA Ops:
  0.0 2.7 %shard_map.83 = bf16[64,48,128]{2,1,0:T(8,128)(2,1)} custom-call(s32[6,32]{1,0:T(8,128)} %bitcast.26, f32[6,32]{1,0:T(8,128)} %bitcast.28, bf16[32,2048]{1,0:T(8,128)(2,1)} %grad_ref.1), custom_call_target="tpu_custom_call" | custom-call | flops 25165824 | bytes 919040 | tf_op jit(solution)/shard_map/pallas_call | solution.py:20
  2.7 18.7 %all-to-all-start = ((bf16[64,48,128]{2,1,0:T(8,128)(2,1)}), bf16[64,48,128]{2,1,0:T(8,128)(2,1)S(1)}, u32[]{:S(2)}, u32[]{:S(2)}) async-start(bf16[64,48,128]{2,1,0:T(8,128)(2,1)} %shard_map.83), calls=%async_computation | async-start | bytes 1572864 | tf_op jit(solution)/shard_map/all_to_all | solution.py:224
  21.4 3.4 %collective-permute-start = (bf16[176,2048]{1,0:T(8,128)(2,1)}, bf16[176,2048]{1,0:T(8,128)(2,1)S(1)}, u32[]{:S(2)}, u32[]{:S(2)}) collective-permute-start(bf16[176,2048]{1,0:T(8,128)(2,1)} %bitcast.15), channel_id=1, source_target_pairs={{0,2},{1,7},{2,4},{3,1},{4,6},{5,3},{6,0},{7,5},{8,10},{9,15},{10,... | collective-permute-start | bytes 2162696 | tf_op jit(solution)/shard_map/ppermute | solution.py:218
  24.8 3.4 %collective-permute-start.6 = (bf16[176,2048]{1,0:T(8,128)(2,1)}, bf16[176,2048]{1,0:T(8,128)(2,1)}, u32[]{:S(2)}, u32[]{:S(2)}) collective-permute-start(bf16[176,2048]{1,0:T(8,128)(2,1)} %bitcast.18), channel_id=1, source_target_pairs={{0,2},{1,7},{2,4},{3,1},{4,6},{5,3},{6,0},{7,5},{8,10},{9,15},{10,... | collective-permute-start | bytes 2162696 | tf_op jit(solution)/shard_map/ppermute | solution.py:218
  28.2 3.1 %collective-permute-start.7 = (bf16[176,2048]{1,0:T(8,128)(2,1)}, bf16[176,2048]{1,0:T(8,128)(2,1)}, u32[]{:S(2)}, u32[]{:S(2)}) collective-permute-start(bf16[176,2048]{1,0:T(8,128)(2,1)} %bitcast.20), channel_id=1, source_target_pairs={{0,2},{1,7},{2,4},{3,1},{4,6},{5,3},{6,0},{7,5},{8,10},{9,15},{10,... | collective-permute-start | bytes 2162696 | tf_op jit(solution)/shard_map/ppermute | solution.py:218
  31.3 4.7 %collective-permute-done.down1_in = bf16[176,2048]{1,0:T(8,128)(2,1)S(1)} collective-permute-done((bf16[176,2048]{1,0:T(8,128)(2,1)}, bf16[176,2048]{1,0:T(8,128)(2,1)S(1)}, u32[]{:S(2)}, u32[]{:S(2)}) %collective-permute-start) | collective-permute-done | bytes 720928 | tf_op jit(solution)/shard_map/ppermute | solution.py:218
  36.0 2.2 %collective-permute-start.1 = (bf16[176,2048]{1,0:T(8,128)(2,1)S(1)}, bf16[176,2048]{1,0:T(8,128)(2,1)S(1)}, u32[]{:S(2)}, u32[]{:S(2)}) collective-permute-start(bf16[176,2048]{1,0:T(8,128)(2,1)S(1)} %collective-permute-done.down1_in), channel_id=1, source_target_pairs={{0,2},{1,7},{2,4},{3,1},{4,6},{5,3},{6,0},{7,5},{8,10},{9,15},{10,... | collective-permute-start | bytes 2162696 | tf_op jit(solution)/shard_map/ppermute | solution.py:218
  38.2 5.6 %collective-permute-done.6.g1_in = bf16[176,2048]{1,0:T(8,128)(2,1)} collective-permute-done((bf16[176,2048]{1,0:T(8,128)(2,1)}, bf16[176,2048]{1,0:T(8,128)(2,1)}, u32[]{:S(2)}, u32[]{:S(2)}) %collective-permute-start.6) | collective-permute-done | bytes 720928 | tf_op jit(solution)/shard_map/ppermute | solution.py:218
  43.8 2.2 %collective-permute-start.8 = (bf16[176,2048]{1,0:T(8,128)(2,1)}, bf16[176,2048]{1,0:T(8,128)(2,1)}, u32[]{:S(2)}, u32[]{:S(2)}) collective-permute-start(bf16[176,2048]{1,0:T(8,128)(2,1)} %collective-permute-done.6.g1_in), channel_id=1, source_target_pairs={{0,2},{1,7},{2,4},{3,1},{4,6},{5,3},{6,0},{7,5},{8,10},{9,15},{10,... | collective-permute-start | bytes 2162696 | tf_op jit(solution)/shard_map/ppermute | solution.py:218
  46.0 5.5 %collective-permute-done.7.u1_in = bf16[176,2048]{1,0:T(8,128)(2,1)} collective-permute-done((bf16[176,2048]{1,0:T(8,128)(2,1)}, bf16[176,2048]{1,0:T(8,128)(2,1)}, u32[]{:S(2)}, u32[]{:S(2)}) %collective-permute-start.7) | collective-permute-done | bytes 720928 | tf_op jit(solution)/shard_map/ppermute | solution.py:218
  51.6 2.2 %collective-permute-start.9 = (bf16[176,2048]{1,0:T(8,128)(2,1)}, bf16[176,2048]{1,0:T(8,128)(2,1)}, u32[]{:S(2)}, u32[]{:S(2)}) collective-permute-start(bf16[176,2048]{1,0:T(8,128)(2,1)} %collective-permute-done.7.u1_in), channel_id=1, source_target_pairs={{0,2},{1,7},{2,4},{3,1},{4,6},{5,3},{6,0},{7,5},{8,10},{9,15},{10,... | collective-permute-start | bytes 2162696 | tf_op jit(solution)/shard_map/ppermute | solution.py:218
  53.8 2.4 %collective-permute-start.4 = (bf16[192,1408]{1,0:T(8,128)(2,1)}, bf16[192,1408]{1,0:T(8,128)(2,1)S(1)}, u32[]{:S(2)}, u32[]{:S(2)}) collective-permute-start(bf16[192,1408]{1,0:T(8,128)(2,1)} %bitcast.22), channel_id=1, source_target_pairs={{0,1},{1,0},{2,3},{3,2},{4,5},{5,4},{6,7},{7,6},{8,9},{9,8},{10,11... | collective-permute-start | bytes 1622024 | tf_op jit(solution)/shard_map/ppermute | solution.py:221
  56.2 8.0 %all-to-all-done.packed_in = bf16[64,48,128]{2,1,0:T(8,128)(2,1)S(1)} async-done(((bf16[64,48,128]{2,1,0:T(8,128)(2,1)}), bf16[64,48,128]{2,1,0:T(8,128)(2,1)S(1)}, u32[]{:S(2)}, u32[]{:S(2)}) %all-to-all-start) | async-done | bytes 786464 | tf_op jit(solution)/shard_map/all_to_all | solution.py:224
  64.2 1.9 %collective-permute-start.3 = (bf16[64,48,128]{2,1,0:T(8,128)(2,1)S(1)}, bf16[64,48,128]{2,1,0:T(8,128)(2,1)S(1)}, u32[]{:S(2)}, u32[]{:S(2)}) collective-permute-start(bf16[64,48,128]{2,1,0:T(8,128)(2,1)S(1)} %all-to-all-done.packed_in), channel_id=1, source_target_pairs={{0,1},{1,0},{2,3},{3,2},{4,5},{5,4},{6,7},{7,6},{8,9},{9,8},{10,11... | collective-permute-start | bytes 2359304 | tf_op jit(solution)/shard_map/ppermute | solution.py:221
  66.1 0.0 collective-permute-done.1.down2_in
  66.1 3.4 %collective-permute-start.2 = (bf16[176,2048]{1,0:T(8,128)(2,1)S(1)}, bf16[176,2048]{1,0:T(8,128)(2,1)S(1)}, u32[]{:S(2)}, u32[]{:S(2)}) collective-permute-start(bf16[176,2048]{1,0:T(8,128)(2,1)S(1)} %collective-permute-done.1.down2_in), channel_id=1, source_target_pairs={{0,2},{1,7},{2,4},{3,1},{4,6},{5,3},{6,0},{7,5},{8,10},{9,15},{10,... | collective-permute-start | bytes 2162696 | tf_op jit(solution)/shard_map/ppermute | solution.py:218
  69.5 0.0 collective-permute-done.4.gate_ref
  69.5 3.4 %collective-permute-start.5 = (bf16[192,1408]{1,0:T(8,128)(2,1)}, bf16[192,1408]{1,0:T(8,128)(2,1)S(1)}, u32[]{:S(2)}, u32[]{:S(2)}) collective-permute-start(bf16[192,1408]{1,0:T(8,128)(2,1)} %bitcast.24), channel_id=1, source_target_pairs={{0,1},{1,0},{2,3},{3,2},{4,5},{5,4},{6,7},{7,6},{8,9},{9,8},{10,11... | collective-permute-start | bytes 1622024 | tf_op jit(solution)/shard_map/ppermute | solution.py:221
  72.9 0.0 collective-permute-done.8.g2_in
  72.9 1.9 %collective-permute-start.10 = (bf16[176,2048]{1,0:T(8,128)(2,1)}, bf16[176,2048]{1,0:T(8,128)(2,1)S(1)}, u32[]{:S(2)}, u32[]{:S(2)}) collective-permute-start(bf16[176,2048]{1,0:T(8,128)(2,1)} %collective-permute-done.8.g2_in), channel_id=1, source_target_pairs={{0,2},{1,7},{2,4},{3,1},{4,6},{5,3},{6,0},{7,5},{8,10},{9,15},{10,... | collective-permute-start | bytes 2162696 | tf_op jit(solution)/shard_map/ppermute | solution.py:218
  74.9 0.0 collective-permute-done.9.u2_in
  74.9 3.1 %collective-permute-start.11 = (bf16[176,2048]{1,0:T(8,128)(2,1)}, bf16[176,2048]{1,0:T(8,128)(2,1)S(1)}, u32[]{:S(2)}, u32[]{:S(2)}) collective-permute-start(bf16[176,2048]{1,0:T(8,128)(2,1)} %collective-permute-done.9.u2_in), channel_id=1, source_target_pairs={{0,2},{1,7},{2,4},{3,1},{4,6},{5,3},{6,0},{7,5},{8,10},{9,15},{10,... | collective-permute-start | bytes 2162696 | tf_op jit(solution)/shard_map/ppermute | solution.py:218
  78.0 0.0 copy-start.3
  78.0 1.0 copy-done.3
  79.1 1.0 copy-done.4
  80.1 0.9 shard_map.84
  81.0 0.0 collective-permute-done.5.up_ref
  81.0 0.9 shard_map.86
  81.9 0.5 collective-permute-done.2.down3_in
  82.4 0.0 copy-done
  82.4 2.8 %shard_map.85 = (bf16[192,1056]{1,0:T(8,128)(2,1)S(1)}, bf16[192,352]{1,0:T(8,128)(2,1)S(1)}) custom-call(bf16[64,48,128]{2,1,0:T(8,128)(2,1)S(1)} %all-to-all-done.packed_in, bf16[176,2048]{1,0:T(8,128)(2,1)S(1)} %bitcast.16, bf16[176,2048]{1,0:T(8,128)(2,1)S(1)} %collective-permute-done.down1_in, bf16[176,2048]{1,0:T(8,128)(2,1)S(1)} %collective-permute-done.1.down2_in, ...), custom_call_target="tpu_custom_call" | custom-call | flops 553648128 | bytes 5292032 | tf_op jit(solution)/shard_map/pallas_call | solution.py:20
  85.2 0.0 copy-start.1
  85.2 0.0 copy-start.2
  85.2 0.0 collective-permute-done.3.packed_in
  85.2 2.8 %shard_map.87 = (bf16[192,1056]{1,0:T(8,128)(2,1)S(1)}, bf16[192,352]{1,0:T(8,128)(2,1)S(1)}) custom-call(bf16[64,48,128]{2,1,0:T(8,128)(2,1)S(1)} %collective-permute-done.3.packed_in, bf16[176,2048]{1,0:T(8,128)(2,1)S(1)} %bitcast.17, bf16[176,2048]{1,0:T(8,128)(2,1)S(1)} %collective-permute-done.down1_in, ...), custom_call_target="tpu_custom_call" | custom-call | flops 553648128 | bytes 5292032 | tf_op jit(solution)/shard_map/pallas_call | solution.py:20
  88.0 0.0 copy-done.1
  88.0 4.4 %shard_map.88.sum_ref = f32[384,2048]{1,0:T(8,128)S(1)} custom-call(bf16[192,1056]{1,0:T(8,128)(2,1)S(1)} %get-tuple-element.17.own_in, bf16[192,1056]{1,0:T(8,128)(2,1)S(1)} %get-tuple-element.20.other_in, bf16[176,2048]{1,0:T(8,128)(2,1)S(1)} %bitcast.19, bf16[176,2048]{1,0:T(8,128)(2,1)S(1)} %bitcast.21, bf16[176,2048]{1,0:T(8,128)(2,1)} %collective-permute-done.6.g1_in, ...), custom_call_target="tpu_custom_call" | custom-call | flops 1660944384 | bytes 8282112 | tf_op jit(solution)/shard_map/pallas_call | solution.py:20
  92.4 0.0 collective-permute-done.10.gate_in
  92.5 5.4 %collective-permute-done.11.up_in = bf16[176,2048]{1,0:T(8,128)(2,1)S(1)} collective-permute-done((bf16[176,2048]{1,0:T(8,128)(2,1)}, bf16[176,2048]{1,0:T(8,128)(2,1)S(1)}, u32[]{:S(2)}, u32[]{:S(2)}) %collective-permute-start.11) | collective-permute-done | bytes 720928 | tf_op jit(solution)/shard_map/ppermute | solution.py:218
  97.8 1.7 %shard_map.89 = (bf16[192,2048]{1,0:T(8,128)(2,1)S(1)}, bf16[192,2048]{1,0:T(8,128)(2,1)S(1)}) custom-call(f32[384,2048]{1,0:T(8,128)S(1)} %shard_map.88.sum_ref, bf16[192,352]{1,0:T(8,128)(2,1)S(1)} %get-tuple-element.21.own_in, bf16[192,352]{1,0:T(8,128)(2,1)S(1)} %get-tuple-element.22.other_in, bf16[176,2048]{1,0:T(8,128)(2,1)S(1)} %collective-permute-done.10.gate_in, ...), custom_call_target="tpu_custom_call" | custom-call | flops 553648128 | bytes 6430720 | tf_op jit(solution)/shard_map/pallas_call | solution.py:20
  99.5 0.0 copy-start.5
  99.5 1.9 %collective-permute-start.12 = (bf16[192,2048]{1,0:T(8,128)(2,1)S(1)}, bf16[192,2048]{1,0:T(8,128)(2,1)S(1)}, u32[]{:S(2)}, u32[]{:S(2)}) collective-permute-start(bf16[192,2048]{1,0:T(8,128)(2,1)S(1)} %get-tuple-element.24), channel_id=1, source_target_pairs={{0,1},{1,0},{2,3},{3,2},{4,5},{5,4},{6,7},{7,6},{8,9},{9,8},{10,11... | collective-permute-start | bytes 2359304 | tf_op jit(solution)/shard_map/ppermute | solution.py:221
  101.5 2.3 %collective-permute-done.12.back_ref = bf16[192,2048]{1,0:T(8,128)(2,1)S(1)} collective-permute-done((bf16[192,2048]{1,0:T(8,128)(2,1)S(1)}, bf16[192,2048]{1,0:T(8,128)(2,1)S(1)}, u32[]{:S(2)}, u32[]{:S(2)}) %collective-permute-start.12) | collective-permute-done | bytes 786464 | tf_op jit(solution)/shard_map/ppermute | solution.py:221
  103.7 1.3 shard_map.90
  105.0 15.1 %all-to-all-start.1 = ((bf16[64,48,128]{2,1,0:T(8,128)(2,1)}), bf16[64,48,128]{2,1,0:T(8,128)(2,1)S(1)}, u32[]{:S(2)}, u32[]{:S(2)}) async-start(bf16[64,48,128]{2,1,0:T(8,128)(2,1)} %shard_map.90), calls=%async_computation.1 | async-start | bytes 1572864 | tf_op jit(solution)/shard_map/all_to_all | solution.py:224
  120.1 0.3 shard_map.82.hot_ref
  120.4 42.8 %all-to-all-done.1.back_ref = bf16[64,48,128]{2,1,0:T(8,128)(2,1)S(1)} async-done(((bf16[64,48,128]{2,1,0:T(8,128)(2,1)}), bf16[64,48,128]{2,1,0:T(8,128)(2,1)S(1)}, u32[]{:S(2)}, u32[]{:S(2)}) %all-to-all-start.1) | async-done | bytes 786464 | tf_op jit(solution)/shard_map/all_to_all | solution.py:224
  163.2 1.1 shard_map.91
  (4 shorter events, 0.0 us)
Async XLA Ops:
  0.0 82.4 %copy-start = (bf16[1,176,2048]{2,1,0:T(8,128)(2,1)S(1)}, bf16[1,176,2048]{2,1,0:T(8,128)(2,1)}, u32[]{:S(2)}) copy-start(bf16[1,176,2048]{2,1,0:T(8,128)(2,1)} %param.13) | copy-start | bytes 2162692
  2.7 61.5 %all-to-all-start = ((bf16[64,48,128]{2,1,0:T(8,128)(2,1)}), bf16[64,48,128]{2,1,0:T(8,128)(2,1)S(1)}, u32[]{:S(2)}, u32[]{:S(2)}) async-start(bf16[64,48,128]{2,1,0:T(8,128)(2,1)} %shard_map.83), calls=%async_computation | async-start | bytes 1572864 | tf_op jit(solution)/shard_map/all_to_all | solution.py:224
  21.4 14.6 %collective-permute-start = (bf16[176,2048]{1,0:T(8,128)(2,1)}, bf16[176,2048]{1,0:T(8,128)(2,1)S(1)}, u32[]{:S(2)}, u32[]{:S(2)}) collective-permute-start(bf16[176,2048]{1,0:T(8,128)(2,1)} %bitcast.15), channel_id=1, source_target_pairs={{0,2},{1,7},{2,4},{3,1},{4,6},{5,3},{6,0},{7,5},{8,10},{9,15},{10,... | collective-permute-start | bytes 2162696 | tf_op jit(solution)/shard_map/ppermute | solution.py:218
  24.8 19.0 %collective-permute-start.6 = (bf16[176,2048]{1,0:T(8,128)(2,1)}, bf16[176,2048]{1,0:T(8,128)(2,1)}, u32[]{:S(2)}, u32[]{:S(2)}) collective-permute-start(bf16[176,2048]{1,0:T(8,128)(2,1)} %bitcast.18), channel_id=1, source_target_pairs={{0,2},{1,7},{2,4},{3,1},{4,6},{5,3},{6,0},{7,5},{8,10},{9,15},{10,... | collective-permute-start | bytes 2162696 | tf_op jit(solution)/shard_map/ppermute | solution.py:218
  28.2 23.3 %collective-permute-start.7 = (bf16[176,2048]{1,0:T(8,128)(2,1)}, bf16[176,2048]{1,0:T(8,128)(2,1)}, u32[]{:S(2)}, u32[]{:S(2)}) collective-permute-start(bf16[176,2048]{1,0:T(8,128)(2,1)} %bitcast.20), channel_id=1, source_target_pairs={{0,2},{1,7},{2,4},{3,1},{4,6},{5,3},{6,0},{7,5},{8,10},{9,15},{10,... | collective-permute-start | bytes 2162696 | tf_op jit(solution)/shard_map/ppermute | solution.py:218
  36.0 30.1 %collective-permute-start.1 = (bf16[176,2048]{1,0:T(8,128)(2,1)S(1)}, bf16[176,2048]{1,0:T(8,128)(2,1)S(1)}, u32[]{:S(2)}, u32[]{:S(2)}) collective-permute-start(bf16[176,2048]{1,0:T(8,128)(2,1)S(1)} %collective-permute-done.down1_in), channel_id=1, source_target_pairs={{0,2},{1,7},{2,4},{3,1},{4,6},{5,3},{6,0},{7,5},{8,10},{9,15},{10,... | collective-permute-start | bytes 2162696 | tf_op jit(solution)/shard_map/ppermute | solution.py:218
  43.8 29.1 %collective-permute-start.8 = (bf16[176,2048]{1,0:T(8,128)(2,1)}, bf16[176,2048]{1,0:T(8,128)(2,1)}, u32[]{:S(2)}, u32[]{:S(2)}) collective-permute-start(bf16[176,2048]{1,0:T(8,128)(2,1)} %collective-permute-done.6.g1_in), channel_id=1, source_target_pairs={{0,2},{1,7},{2,4},{3,1},{4,6},{5,3},{6,0},{7,5},{8,10},{9,15},{10,... | collective-permute-start | bytes 2162696 | tf_op jit(solution)/shard_map/ppermute | solution.py:218
  51.6 23.3 %collective-permute-start.9 = (bf16[176,2048]{1,0:T(8,128)(2,1)}, bf16[176,2048]{1,0:T(8,128)(2,1)}, u32[]{:S(2)}, u32[]{:S(2)}) collective-permute-start(bf16[176,2048]{1,0:T(8,128)(2,1)} %collective-permute-done.7.u1_in), channel_id=1, source_target_pairs={{0,2},{1,7},{2,4},{3,1},{4,6},{5,3},{6,0},{7,5},{8,10},{9,15},{10,... | collective-permute-start | bytes 2162696 | tf_op jit(solution)/shard_map/ppermute | solution.py:218
  53.8 15.8 %collective-permute-start.4 = (bf16[192,1408]{1,0:T(8,128)(2,1)}, bf16[192,1408]{1,0:T(8,128)(2,1)S(1)}, u32[]{:S(2)}, u32[]{:S(2)}) collective-permute-start(bf16[192,1408]{1,0:T(8,128)(2,1)} %bitcast.22), channel_id=1, source_target_pairs={{0,1},{1,0},{2,3},{3,2},{4,5},{5,4},{6,7},{7,6},{8,9},{9,8},{10,11... | collective-permute-start | bytes 1622024 | tf_op jit(solution)/shard_map/ppermute | solution.py:221
  64.2 21.0 %collective-permute-start.3 = (bf16[64,48,128]{2,1,0:T(8,128)(2,1)S(1)}, bf16[64,48,128]{2,1,0:T(8,128)(2,1)S(1)}, u32[]{:S(2)}, u32[]{:S(2)}) collective-permute-start(bf16[64,48,128]{2,1,0:T(8,128)(2,1)S(1)} %all-to-all-done.packed_in), channel_id=1, source_target_pairs={{0,1},{1,0},{2,3},{3,2},{4,5},{5,4},{6,7},{7,6},{8,9},{9,8},{10,11... | collective-permute-start | bytes 2359304 | tf_op jit(solution)/shard_map/ppermute | solution.py:221
  66.1 16.2 %collective-permute-start.2 = (bf16[176,2048]{1,0:T(8,128)(2,1)S(1)}, bf16[176,2048]{1,0:T(8,128)(2,1)S(1)}, u32[]{:S(2)}, u32[]{:S(2)}) collective-permute-start(bf16[176,2048]{1,0:T(8,128)(2,1)S(1)} %collective-permute-done.1.down2_in), channel_id=1, source_target_pairs={{0,2},{1,7},{2,4},{3,1},{4,6},{5,3},{6,0},{7,5},{8,10},{9,15},{10,... | collective-permute-start | bytes 2162696 | tf_op jit(solution)/shard_map/ppermute | solution.py:218
  69.5 11.5 %collective-permute-start.5 = (bf16[192,1408]{1,0:T(8,128)(2,1)}, bf16[192,1408]{1,0:T(8,128)(2,1)S(1)}, u32[]{:S(2)}, u32[]{:S(2)}) collective-permute-start(bf16[192,1408]{1,0:T(8,128)(2,1)} %bitcast.24), channel_id=1, source_target_pairs={{0,1},{1,0},{2,3},{3,2},{4,5},{5,4},{6,7},{7,6},{8,9},{9,8},{10,11... | collective-permute-start | bytes 1622024 | tf_op jit(solution)/shard_map/ppermute | solution.py:221
  72.9 19.5 %collective-permute-start.10 = (bf16[176,2048]{1,0:T(8,128)(2,1)}, bf16[176,2048]{1,0:T(8,128)(2,1)S(1)}, u32[]{:S(2)}, u32[]{:S(2)}) collective-permute-start(bf16[176,2048]{1,0:T(8,128)(2,1)} %collective-permute-done.8.g2_in), channel_id=1, source_target_pairs={{0,2},{1,7},{2,4},{3,1},{4,6},{5,3},{6,0},{7,5},{8,10},{9,15},{10,... | collective-permute-start | bytes 2162696 | tf_op jit(solution)/shard_map/ppermute | solution.py:218
  74.9 22.9 %collective-permute-start.11 = (bf16[176,2048]{1,0:T(8,128)(2,1)}, bf16[176,2048]{1,0:T(8,128)(2,1)S(1)}, u32[]{:S(2)}, u32[]{:S(2)}) collective-permute-start(bf16[176,2048]{1,0:T(8,128)(2,1)} %collective-permute-done.9.u2_in), channel_id=1, source_target_pairs={{0,2},{1,7},{2,4},{3,1},{4,6},{5,3},{6,0},{7,5},{8,10},{9,15},{10,... | collective-permute-start | bytes 2162696 | tf_op jit(solution)/shard_map/ppermute | solution.py:218
  78.0 1.1 copy-start.3
  79.1 1.0 copy-start.4
  85.2 2.8 %copy-start.1 = (bf16[1,176,2048]{2,1,0:T(8,128)(2,1)S(1)}, bf16[1,176,2048]{2,1,0:T(8,128)(2,1)}, u32[]{:S(2)}) copy-start(bf16[1,176,2048]{2,1,0:T(8,128)(2,1)} %param.11) | copy-start | bytes 2162692
  85.2 2.8 %copy-start.2 = (bf16[1,176,2048]{2,1,0:T(8,128)(2,1)S(1)}, bf16[1,176,2048]{2,1,0:T(8,128)(2,1)}, u32[]{:S(2)}) copy-start(bf16[1,176,2048]{2,1,0:T(8,128)(2,1)} %param.12) | copy-start | bytes 2162692
  99.5 20.6 %copy-start.5 = (s32[32,6]{0,1:T(8,128)S(1)}, s32[32,6]{0,1:T(8,128)}, u32[]{:S(2)}) copy-start(s32[32,6]{0,1:T(8,128)} %param.9) | copy-start | bytes 2308
  99.5 4.2 %collective-permute-start.12 = (bf16[192,2048]{1,0:T(8,128)(2,1)S(1)}, bf16[192,2048]{1,0:T(8,128)(2,1)S(1)}, u32[]{:S(2)}, u32[]{:S(2)}) collective-permute-start(bf16[192,2048]{1,0:T(8,128)(2,1)S(1)} %get-tuple-element.24), channel_id=1, source_target_pairs={{0,1},{1,0},{2,3},{3,2},{4,5},{5,4},{6,7},{7,6},{8,9},{9,8},{10,11... | collective-permute-start | bytes 2359304 | tf_op jit(solution)/shard_map/ppermute | solution.py:221
  105.0 58.2 %all-to-all-start.1 = ((bf16[64,48,128]{2,1,0:T(8,128)(2,1)}), bf16[64,48,128]{2,1,0:T(8,128)(2,1)S(1)}, u32[]{:S(2)}, u32[]{:S(2)}) async-start(bf16[64,48,128]{2,1,0:T(8,128)(2,1)} %shard_map.90), calls=%async_computation.1 | async-start | bytes 1572864 | tf_op jit(solution)/shard_map/all_to_all | solution.py:224

commit v9 on v8

--- a/solution.py
+++ b/solution.py
@@ -257,12 +257,12 @@
     )
     other_rows = across(arrived)
 
-    def hide(packed_rows, factors):
+    def hide(packed_rows, factors, limit):
         ins = (packed_rows,) + tuple(downs) + tuple(factors)
-        return call(hidden_kernel, ins, hidden, cost, scratch=scratch, spec=AN)
-
-    own_hidden = hide(arrived, own_factors)
-    other_hidden = hide(other_rows, other_factors)
+        return call(hidden_kernel, ins, hidden, cost, scratch=scratch, spec=AN, limit=limit)
+
+    own_hidden = hide(arrived, own_factors, 50 << 20)
+    other_hidden = hide(other_rows, other_factors, 50 << 20)
 
     pieces = [piece for both in zip(gate_pieces, up_pieces) for piece in both]
 

time: 165 us -> 165 us (level)
  waiting for transfers between devices: 74.8 us -> 69.4 us
  local copies, waits for them, and re-layouts: 2.11 us -> 5.69 us
  Pallas kernels: 18.8 us -> 20.5 us
    ppermute x9, waiting for transfers between devices: 21.7 us -> 16.5 us  [along(): return lax.ppermute(a, 'replica', pairs)]
    unnamed x12 -> x22, local copies, waits for them, and re-layouts: 2.11 us -> 5.69 us
    pallas_call x10, Pallas kernels: 18.8 us -> 20.5 us  [call(): pl.pallas_call(kernel, out_shape=outs[0] if single else tuple(outs), in_s...]
  transfers between devices with their start and end apart: 15 -> 15, of which waited for: 8 -> 7; matrix products, arithmetic and copies ran while one was open for 0% -> 0% of each run, Pallas kernels for 7% -> 8%
where the time goes in v9:
time: 165 us
  waiting for transfers between devices  69.4 us (42%)
  starting transfers between devices  68.7 us (42%)
  Pallas kernels  20.5 us (12%)
  local copies, waits for them, and re-layouts  5.69 us (3%)
    all_to_all x2, waiting for transfers between devices, exchange(): lax.all_to_all(a, ('y', 'z'), split_axis=0, concat_axis=0, tiled=True)  50.6 us
    all_to_all x2, starting transfers between devices, exchange(): lax.all_to_all(a, ('y', 'z'), split_axis=0, concat_axis=0, tiled=True)  34 us
    ppermute x9, starting transfers between devices, along(): return lax.ppermute(a, 'replica', pairs)  24.9 us
    pallas_call x10, Pallas kernels, call(): pl.pallas_call(kernel, out_shape=outs[0] if single else tuple(outs), in_s...  20.5 us
    ppermute x9, waiting for transfers between devices, along(): return lax.ppermute(a, 'replica', pairs)  16.5 us
    ppermute x4, starting transfers between devices, across(): return lax.ppermute(a, 'replica', [(i, i ^ 1) for i in range(copies)])  9.77 us
    unnamed x22, local copies, waits for them, and re-layouts  5.69 us
  transfers between devices with their start and end apart: 15, of which 7 were waited for; matrix products, arithmetic and copies ran while one was open for 0% of the time, Pallas kernels for 8%

profile of v9, /device:TPU:8, one launch (start us, length us, event | category | flops | bytes accessed | tf_op | source)
XLA Modules:
  0.0 164.5 jit_solution(9537407598796464590)
XLA Ops:
  0.0 2.7 %shard_map.83 = bf16[64,48,128]{2,1,0:T(8,128)(2,1)} custom-call(s32[6,32]{1,0:T(8,128)} %bitcast.26, f32[6,32]{1,0:T(8,128)} %bitcast.28, bf16[32,2048]{1,0:T(8,128)(2,1)} %grad_ref.1), custom_call_target="tpu_custom_call" | custom-call | flops 25165824 | bytes 919040 | tf_op jit(solution)/shard_map/pallas_call | solution.py:20
  2.7 18.9 %all-to-all-start = ((bf16[64,48,128]{2,1,0:T(8,128)(2,1)}), bf16[64,48,128]{2,1,0:T(8,128)(2,1)}, u32[]{:S(2)}, u32[]{:S(2)}) async-start(bf16[64,48,128]{2,1,0:T(8,128)(2,1)} %shard_map.83), calls=%async_computation | async-start | bytes 1572864 | tf_op jit(solution)/shard_map/all_to_all | solution.py:224
  21.6 3.4 %collective-permute-start = (bf16[176,2048]{1,0:T(8,128)(2,1)}, bf16[176,2048]{1,0:T(8,128)(2,1)S(1)}, u32[]{:S(2)}, u32[]{:S(2)}) collective-permute-start(bf16[176,2048]{1,0:T(8,128)(2,1)} %bitcast.15), channel_id=1, source_target_pairs={{0,2},{1,7},{2,4},{3,1},{4,6},{5,3},{6,0},{7,5},{8,10},{9,15},{10,... | collective-permute-start | bytes 2162696 | tf_op jit(solution)/shard_map/ppermute | solution.py:218
  25.0 3.4 %collective-permute-start.6 = (bf16[176,2048]{1,0:T(8,128)(2,1)}, bf16[176,2048]{1,0:T(8,128)(2,1)S(1)}, u32[]{:S(2)}, u32[]{:S(2)}) collective-permute-start(bf16[176,2048]{1,0:T(8,128)(2,1)} %bitcast.18), channel_id=1, source_target_pairs={{0,2},{1,7},{2,4},{3,1},{4,6},{5,3},{6,0},{7,5},{8,10},{9,15},{10,... | collective-permute-start | bytes 2162696 | tf_op jit(solution)/shard_map/ppermute | solution.py:218
  28.4 3.1 %collective-permute-start.7 = (bf16[176,2048]{1,0:T(8,128)(2,1)}, bf16[176,2048]{1,0:T(8,128)(2,1)}, u32[]{:S(2)}, u32[]{:S(2)}) collective-permute-start(bf16[176,2048]{1,0:T(8,128)(2,1)} %bitcast.20), channel_id=1, source_target_pairs={{0,2},{1,7},{2,4},{3,1},{4,6},{5,3},{6,0},{7,5},{8,10},{9,15},{10,... | collective-permute-start | bytes 2162696 | tf_op jit(solution)/shard_map/ppermute | solution.py:218
  31.6 4.7 %collective-permute-done.down1_in = bf16[176,2048]{1,0:T(8,128)(2,1)S(1)} collective-permute-done((bf16[176,2048]{1,0:T(8,128)(2,1)}, bf16[176,2048]{1,0:T(8,128)(2,1)S(1)}, u32[]{:S(2)}, u32[]{:S(2)}) %collective-permute-start) | collective-permute-done | bytes 720928 | tf_op jit(solution)/shard_map/ppermute | solution.py:218
  36.2 2.2 %collective-permute-start.1 = (bf16[176,2048]{1,0:T(8,128)(2,1)S(1)}, bf16[176,2048]{1,0:T(8,128)(2,1)S(1)}, u32[]{:S(2)}, u32[]{:S(2)}) collective-permute-start(bf16[176,2048]{1,0:T(8,128)(2,1)S(1)} %collective-permute-done.down1_in), channel_id=1, source_target_pairs={{0,2},{1,7},{2,4},{3,1},{4,6},{5,3},{6,0},{7,5},{8,10},{9,15},{10,... | collective-permute-start | bytes 2162696 | tf_op jit(solution)/shard_map/ppermute | solution.py:218
  38.4 5.5 %collective-permute-done.6.g1_in = bf16[176,2048]{1,0:T(8,128)(2,1)S(1)} collective-permute-done((bf16[176,2048]{1,0:T(8,128)(2,1)}, bf16[176,2048]{1,0:T(8,128)(2,1)S(1)}, u32[]{:S(2)}, u32[]{:S(2)}) %collective-permute-start.6) | collective-permute-done | bytes 720928 | tf_op jit(solution)/shard_map/ppermute | solution.py:218
  44.0 2.2 %collective-permute-start.8 = (bf16[176,2048]{1,0:T(8,128)(2,1)S(1)}, bf16[176,2048]{1,0:T(8,128)(2,1)}, u32[]{:S(2)}, u32[]{:S(2)}) collective-permute-start(bf16[176,2048]{1,0:T(8,128)(2,1)S(1)} %collective-permute-done.6.g1_in), channel_id=1, source_target_pairs={{0,2},{1,7},{2,4},{3,1},{4,6},{5,3},{6,0},{7,5},{8,10},{9,15},{10,... | collective-permute-start | bytes 2162696 | tf_op jit(solution)/shard_map/ppermute | solution.py:218
  46.1 5.6 %collective-permute-done.7.u1_in = bf16[176,2048]{1,0:T(8,128)(2,1)} collective-permute-done((bf16[176,2048]{1,0:T(8,128)(2,1)}, bf16[176,2048]{1,0:T(8,128)(2,1)}, u32[]{:S(2)}, u32[]{:S(2)}) %collective-permute-start.7) | collective-permute-done | bytes 720928 | tf_op jit(solution)/shard_map/ppermute | solution.py:218
  51.8 2.2 %collective-permute-start.9 = (bf16[176,2048]{1,0:T(8,128)(2,1)}, bf16[176,2048]{1,0:T(8,128)(2,1)}, u32[]{:S(2)}, u32[]{:S(2)}) collective-permute-start(bf16[176,2048]{1,0:T(8,128)(2,1)} %collective-permute-done.7.u1_in), channel_id=1, source_target_pairs={{0,2},{1,7},{2,4},{3,1},{4,6},{5,3},{6,0},{7,5},{8,10},{9,15},{10,... | collective-permute-start | bytes 2162696 | tf_op jit(solution)/shard_map/ppermute | solution.py:218
  54.0 2.5 %collective-permute-start.4 = (bf16[192,1408]{1,0:T(8,128)(2,1)}, bf16[192,1408]{1,0:T(8,128)(2,1)S(1)}, u32[]{:S(2)}, u32[]{:S(2)}) collective-permute-start(bf16[192,1408]{1,0:T(8,128)(2,1)} %bitcast.22), channel_id=1, source_target_pairs={{0,1},{1,0},{2,3},{3,2},{4,5},{5,4},{6,7},{7,6},{8,9},{9,8},{10,11... | collective-permute-start | bytes 1622024 | tf_op jit(solution)/shard_map/ppermute | solution.py:221
  56.5 7.8 %all-to-all-done.packed_in = bf16[64,48,128]{2,1,0:T(8,128)(2,1)} async-done(((bf16[64,48,128]{2,1,0:T(8,128)(2,1)}), bf16[64,48,128]{2,1,0:T(8,128)(2,1)}, u32[]{:S(2)}, u32[]{:S(2)}) %all-to-all-start) | async-done | bytes 786464 | tf_op jit(solution)/shard_map/all_to_all | solution.py:224
  64.3 1.9 %collective-permute-start.3 = (bf16[64,48,128]{2,1,0:T(8,128)(2,1)}, bf16[64,48,128]{2,1,0:T(8,128)(2,1)S(1)}, u32[]{:S(2)}, u32[]{:S(2)}) collective-permute-start(bf16[64,48,128]{2,1,0:T(8,128)(2,1)} %all-to-all-done.packed_in), channel_id=1, source_target_pairs={{0,1},{1,0},{2,3},{3,2},{4,5},{5,4},{6,7},{7,6},{8,9},{9,8},{10,11... | collective-permute-start | bytes 2359304 | tf_op jit(solution)/shard_map/ppermute | solution.py:221
  66.3 0.0 collective-permute-done.1.down2_in
  66.3 3.4 %collective-permute-start.2 = (bf16[176,2048]{1,0:T(8,128)(2,1)S(1)}, bf16[176,2048]{1,0:T(8,128)(2,1)S(1)}, u32[]{:S(2)}, u32[]{:S(2)}) collective-permute-start(bf16[176,2048]{1,0:T(8,128)(2,1)S(1)} %collective-permute-done.1.down2_in), channel_id=1, source_target_pairs={{0,2},{1,7},{2,4},{3,1},{4,6},{5,3},{6,0},{7,5},{8,10},{9,15},{10,... | collective-permute-start | bytes 2162696 | tf_op jit(solution)/shard_map/ppermute | solution.py:218
  69.7 0.0 collective-permute-done.4.gate_ref
  69.7 3.4 %collective-permute-start.5 = (bf16[192,1408]{1,0:T(8,128)(2,1)}, bf16[192,1408]{1,0:T(8,128)(2,1)S(1)}, u32[]{:S(2)}, u32[]{:S(2)}) collective-permute-start(bf16[192,1408]{1,0:T(8,128)(2,1)} %bitcast.24), channel_id=1, source_target_pairs={{0,1},{1,0},{2,3},{3,2},{4,5},{5,4},{6,7},{7,6},{8,9},{9,8},{10,11... | collective-permute-start | bytes 1622024 | tf_op jit(solution)/shard_map/ppermute | solution.py:221
  73.1 0.0 collective-permute-done.8.g2_in
  73.1 1.9 %collective-permute-start.10 = (bf16[176,2048]{1,0:T(8,128)(2,1)}, bf16[176,2048]{1,0:T(8,128)(2,1)S(1)}, u32[]{:S(2)}, u32[]{:S(2)}) collective-permute-start(bf16[176,2048]{1,0:T(8,128)(2,1)} %collective-permute-done.8.g2_in), channel_id=1, source_target_pairs={{0,2},{1,7},{2,4},{3,1},{4,6},{5,3},{6,0},{7,5},{8,10},{9,15},{10,... | collective-permute-start | bytes 2162696 | tf_op jit(solution)/shard_map/ppermute | solution.py:218
  75.0 0.0 collective-permute-done.9.u2_in
  75.0 3.1 %collective-permute-start.11 = (bf16[176,2048]{1,0:T(8,128)(2,1)}, bf16[176,2048]{1,0:T(8,128)(2,1)S(1)}, u32[]{:S(2)}, u32[]{:S(2)}) collective-permute-start(bf16[176,2048]{1,0:T(8,128)(2,1)} %collective-permute-done.9.u2_in), channel_id=1, source_target_pairs={{0,2},{1,7},{2,4},{3,1},{4,6},{5,3},{6,0},{7,5},{8,10},{9,15},{10,... | collective-permute-start | bytes 2162696 | tf_op jit(solution)/shard_map/ppermute | solution.py:218
  78.2 0.0 copy-start.7
  78.2 1.0 copy-done.7
  79.2 1.0 copy-done.8
  80.3 0.9 shard_map.84
  81.1 0.9 copy-done.3
  82.0 0.9 copy-done.4
  82.9 0.0 collective-permute-done.5.up_ref
  82.9 0.9 shard_map.86
  83.8 0.9 copy-done.1
  84.7 3.8 %shard_map.85 = (bf16[192,1056]{1,0:T(8,128)(2,1)S(1)}, bf16[192,352]{1,0:T(8,128)(2,1)S(1)}) custom-call(bf16[64,48,128]{2,1,0:T(8,128)(2,1)} %all-to-all-done.packed_in, bf16[176,2048]{1,0:T(8,128)(2,1)S(1)} %bitcast.16, bf16[176,2048]{1,0:T(8,128)(2,1)S(1)} %collective-permute-done.down1_in, bf16[176,2048]{1,0:T(8,128)(2,1)S(1)} %collective-permute-done.1.down2_in, ...), custom_call_target="tpu_custom_call" | custom-call | flops 553648128 | bytes 5292032 | tf_op jit(solution)/shard_map/pallas_call | solution.py:20
  88.5 0.0 copy-start.5
  88.5 0.0 copy-start.6
  88.6 0.9 copy-done.10
  89.5 3.5 %shard_map.87 = (bf16[192,1056]{1,0:T(8,128)(2,1)S(1)}, bf16[192,352]{1,0:T(8,128)(2,1)S(1)}) custom-call(bf16[64,48,128]{2,1,0:T(8,128)(2,1)} %copy-done.10, bf16[176,2048]{1,0:T(8,128)(2,1)S(1)} %bitcast.17, bf16[176,2048]{1,0:T(8,128)(2,1)S(1)} %collective-permute-done.down1_in, bf16[176,2048]{1,0:T(8,128)(2,1)S(1)} %collective-permute-done.1.down2_in, ...), custom_call_target="tpu_custom_call" | custom-call | flops 553648128 | bytes 5292032 | tf_op jit(solution)/shard_map/pallas_call | solution.py:20
  93.0 4.3 %shard_map.88.sum_ref = f32[384,2048]{1,0:T(8,128)S(1)} custom-call(bf16[192,1056]{1,0:T(8,128)(2,1)S(1)} %get-tuple-element.17.own_in, bf16[192,1056]{1,0:T(8,128)(2,1)S(1)} %get-tuple-element.20.other_in, bf16[176,2048]{1,0:T(8,128)(2,1)S(1)} %bitcast.19, bf16[176,2048]{1,0:T(8,128)(2,1)S(1)} %bitcast.21, ...), custom_call_target="tpu_custom_call" | custom-call | flops 1660944384 | bytes 8282112 | tf_op jit(solution)/shard_map/pallas_call | solution.py:20
  97.4 0.0 collective-permute-done.10.gate_in
  97.4 0.6 collective-permute-done.11.up_in
  98.0 1.7 %shard_map.89 = (bf16[192,2048]{1,0:T(8,128)(2,1)S(1)}, bf16[192,2048]{1,0:T(8,128)(2,1)S(1)}) custom-call(f32[384,2048]{1,0:T(8,128)S(1)} %shard_map.88.sum_ref, bf16[192,352]{1,0:T(8,128)(2,1)S(1)} %get-tuple-element.21.own_in, bf16[192,352]{1,0:T(8,128)(2,1)S(1)} %get-tuple-element.22.other_in, bf16[176,2048]{1,0:T(8,128)(2,1)S(1)} %collective-permute-done.10.gate_in, ...), custom_call_target="tpu_custom_call" | custom-call | flops 553648128 | bytes 6430720 | tf_op jit(solution)/shard_map/pallas_call | solution.py:20
  99.7 0.0 copy-start.9
  99.7 1.9 %collective-permute-start.12 = (bf16[192,2048]{1,0:T(8,128)(2,1)S(1)}, bf16[192,2048]{1,0:T(8,128)(2,1)S(1)}, u32[]{:S(2)}, u32[]{:S(2)}) collective-permute-start(bf16[192,2048]{1,0:T(8,128)(2,1)S(1)} %get-tuple-element.24), channel_id=1, source_target_pairs={{0,1},{1,0},{2,3},{3,2},{4,5},{5,4},{6,7},{7,6},{8,9},{9,8},{10,11... | collective-permute-start | bytes 2359304 | tf_op jit(solution)/shard_map/ppermute | solution.py:221
  101.7 2.3 %collective-permute-done.12.back_ref = bf16[192,2048]{1,0:T(8,128)(2,1)S(1)} collective-permute-done((bf16[192,2048]{1,0:T(8,128)(2,1)S(1)}, bf16[192,2048]{1,0:T(8,128)(2,1)S(1)}, u32[]{:S(2)}, u32[]{:S(2)}) %collective-permute-start.12) | collective-permute-done | bytes 786464 | tf_op jit(solution)/shard_map/ppermute | solution.py:221
  103.9 1.3 shard_map.90
  105.2 15.1 %all-to-all-start.1 = ((bf16[64,48,128]{2,1,0:T(8,128)(2,1)}), bf16[64,48,128]{2,1,0:T(8,128)(2,1)S(1)}, u32[]{:S(2)}, u32[]{:S(2)}) async-start(bf16[64,48,128]{2,1,0:T(8,128)(2,1)} %shard_map.90), calls=%async_computation.1 | async-start | bytes 1572864 | tf_op jit(solution)/shard_map/all_to_all | solution.py:224
  120.4 0.3 shard_map.82.hot_ref
  120.7 42.8 %all-to-all-done.1.back_ref = bf16[64,48,128]{2,1,0:T(8,128)(2,1)S(1)} async-done(((bf16[64,48,128]{2,1,0:T(8,128)(2,1)}), bf16[64,48,128]{2,1,0:T(8,128)(2,1)S(1)}, u32[]{:S(2)}, u32[]{:S(2)}) %all-to-all-start.1) | async-done | bytes 786464 | tf_op jit(solution)/shard_map/all_to_all | solution.py:224
  163.4 1.1 shard_map.91
  (14 shorter events, 0.0 us)
Async XLA Ops:
  0.0 84.7 %copy-start = (bf16[1,176,2048]{2,1,0:T(8,128)(2,1)S(1)}, bf16[1,176,2048]{2,1,0:T(8,128)(2,1)}, u32[]{:S(2)}) copy-start(bf16[1,176,2048]{2,1,0:T(8,128)(2,1)} %param.13) | copy-start | bytes 2162692
  2.7 61.6 %all-to-all-start = ((bf16[64,48,128]{2,1,0:T(8,128)(2,1)}), bf16[64,48,128]{2,1,0:T(8,128)(2,1)}, u32[]{:S(2)}, u32[]{:S(2)}) async-start(bf16[64,48,128]{2,1,0:T(8,128)(2,1)} %shard_map.83), calls=%async_computation | async-start | bytes 1572864 | tf_op jit(solution)/shard_map/all_to_all | solution.py:224
  21.6 14.6 %collective-permute-start = (bf16[176,2048]{1,0:T(8,128)(2,1)}, bf16[176,2048]{1,0:T(8,128)(2,1)S(1)}, u32[]{:S(2)}, u32[]{:S(2)}) collective-permute-start(bf16[176,2048]{1,0:T(8,128)(2,1)} %bitcast.15), channel_id=1, source_target_pairs={{0,2},{1,7},{2,4},{3,1},{4,6},{5,3},{6,0},{7,5},{8,10},{9,15},{10,... | collective-permute-start | bytes 2162696 | tf_op jit(solution)/shard_map/ppermute | solution.py:218
  25.0 18.9 %collective-permute-start.6 = (bf16[176,2048]{1,0:T(8,128)(2,1)}, bf16[176,2048]{1,0:T(8,128)(2,1)S(1)}, u32[]{:S(2)}, u32[]{:S(2)}) collective-permute-start(bf16[176,2048]{1,0:T(8,128)(2,1)} %bitcast.18), channel_id=1, source_target_pairs={{0,2},{1,7},{2,4},{3,1},{4,6},{5,3},{6,0},{7,5},{8,10},{9,15},{10,... | collective-permute-start | bytes 2162696 | tf_op jit(solution)/shard_map/ppermute | solution.py:218
  28.4 23.3 %collective-permute-start.7 = (bf16[176,2048]{1,0:T(8,128)(2,1)}, bf16[176,2048]{1,0:T(8,128)(2,1)}, u32[]{:S(2)}, u32[]{:S(2)}) collective-permute-start(bf16[176,2048]{1,0:T(8,128)(2,1)} %bitcast.20), channel_id=1, source_target_pairs={{0,2},{1,7},{2,4},{3,1},{4,6},{5,3},{6,0},{7,5},{8,10},{9,15},{10,... | collective-permute-start | bytes 2162696 | tf_op jit(solution)/shard_map/ppermute | solution.py:218
  36.2 30.0 %collective-permute-start.1 = (bf16[176,2048]{1,0:T(8,128)(2,1)S(1)}, bf16[176,2048]{1,0:T(8,128)(2,1)S(1)}, u32[]{:S(2)}, u32[]{:S(2)}) collective-permute-start(bf16[176,2048]{1,0:T(8,128)(2,1)S(1)} %collective-permute-done.down1_in), channel_id=1, source_target_pairs={{0,2},{1,7},{2,4},{3,1},{4,6},{5,3},{6,0},{7,5},{8,10},{9,15},{10,... | collective-permute-start | bytes 2162696 | tf_op jit(solution)/shard_map/ppermute | solution.py:218
  44.0 29.1 %collective-permute-start.8 = (bf16[176,2048]{1,0:T(8,128)(2,1)S(1)}, bf16[176,2048]{1,0:T(8,128)(2,1)}, u32[]{:S(2)}, u32[]{:S(2)}) collective-permute-start(bf16[176,2048]{1,0:T(8,128)(2,1)S(1)} %collective-permute-done.6.g1_in), channel_id=1, source_target_pairs={{0,2},{1,7},{2,4},{3,1},{4,6},{5,3},{6,0},{7,5},{8,10},{9,15},{10,... | collective-permute-start | bytes 2162696 | tf_op jit(solution)/shard_map/ppermute | solution.py:218
  51.8 23.2 %collective-permute-start.9 = (bf16[176,2048]{1,0:T(8,128)(2,1)}, bf16[176,2048]{1,0:T(8,128)(2,1)}, u32[]{:S(2)}, u32[]{:S(2)}) collective-permute-start(bf16[176,2048]{1,0:T(8,128)(2,1)} %collective-permute-done.7.u1_in), channel_id=1, source_target_pairs={{0,2},{1,7},{2,4},{3,1},{4,6},{5,3},{6,0},{7,5},{8,10},{9,15},{10,... | collective-permute-start | bytes 2162696 | tf_op jit(solution)/shard_map/ppermute | solution.py:218
  54.0 15.7 %collective-permute-start.4 = (bf16[192,1408]{1,0:T(8,128)(2,1)}, bf16[192,1408]{1,0:T(8,128)(2,1)S(1)}, u32[]{:S(2)}, u32[]{:S(2)}) collective-permute-start(bf16[192,1408]{1,0:T(8,128)(2,1)} %bitcast.22), channel_id=1, source_target_pairs={{0,1},{1,0},{2,3},{3,2},{4,5},{5,4},{6,7},{7,6},{8,9},{9,8},{10,11... | collective-permute-start | bytes 1622024 | tf_op jit(solution)/shard_map/ppermute | solution.py:221
  64.3 24.2 %collective-permute-start.3 = (bf16[64,48,128]{2,1,0:T(8,128)(2,1)}, bf16[64,48,128]{2,1,0:T(8,128)(2,1)S(1)}, u32[]{:S(2)}, u32[]{:S(2)}) collective-permute-start(bf16[64,48,128]{2,1,0:T(8,128)(2,1)} %all-to-all-done.packed_in), channel_id=1, source_target_pairs={{0,1},{1,0},{2,3},{3,2},{4,5},{5,4},{6,7},{7,6},{8,9},{9,8},{10,11... | collective-permute-start | bytes 2359304 | tf_op jit(solution)/shard_map/ppermute | solution.py:221
  66.3 18.4 %collective-permute-start.2 = (bf16[176,2048]{1,0:T(8,128)(2,1)S(1)}, bf16[176,2048]{1,0:T(8,128)(2,1)S(1)}, u32[]{:S(2)}, u32[]{:S(2)}) collective-permute-start(bf16[176,2048]{1,0:T(8,128)(2,1)S(1)} %collective-permute-done.1.down2_in), channel_id=1, source_target_pairs={{0,2},{1,7},{2,4},{3,1},{4,6},{5,3},{6,0},{7,5},{8,10},{9,15},{10,... | collective-permute-start | bytes 2162696 | tf_op jit(solution)/shard_map/ppermute | solution.py:218
  69.7 13.2 %collective-permute-start.5 = (bf16[192,1408]{1,0:T(8,128)(2,1)}, bf16[192,1408]{1,0:T(8,128)(2,1)S(1)}, u32[]{:S(2)}, u32[]{:S(2)}) collective-permute-start(bf16[192,1408]{1,0:T(8,128)(2,1)} %bitcast.24), channel_id=1, source_target_pairs={{0,1},{1,0},{2,3},{3,2},{4,5},{5,4},{6,7},{7,6},{8,9},{9,8},{10,11... | collective-permute-start | bytes 1622024 | tf_op jit(solution)/shard_map/ppermute | solution.py:221
  73.1 24.3 %collective-permute-start.10 = (bf16[176,2048]{1,0:T(8,128)(2,1)}, bf16[176,2048]{1,0:T(8,128)(2,1)S(1)}, u32[]{:S(2)}, u32[]{:S(2)}) collective-permute-start(bf16[176,2048]{1,0:T(8,128)(2,1)} %collective-permute-done.8.g2_in), channel_id=1, source_target_pairs={{0,2},{1,7},{2,4},{3,1},{4,6},{5,3},{6,0},{7,5},{8,10},{9,15},{10,... | collective-permute-start | bytes 2162696 | tf_op jit(solution)/shard_map/ppermute | solution.py:218
  75.0 23.0 %collective-permute-start.11 = (bf16[176,2048]{1,0:T(8,128)(2,1)}, bf16[176,2048]{1,0:T(8,128)(2,1)S(1)}, u32[]{:S(2)}, u32[]{:S(2)}) collective-permute-start(bf16[176,2048]{1,0:T(8,128)(2,1)} %collective-permute-done.9.u2_in), channel_id=1, source_target_pairs={{0,2},{1,7},{2,4},{3,1},{4,6},{5,3},{6,0},{7,5},{8,10},{9,15},{10,... | collective-permute-start | bytes 2162696 | tf_op jit(solution)/shard_map/ppermute | solution.py:218
  78.2 1.1 copy-start.7
  79.2 1.0 copy-start.8
  81.1 0.9 copy-start.3
  82.0 0.9 copy-start.4
  83.8 0.9 copy-start.1
  84.7 3.9 %copy-start.2 = (f32[4,192,176]{2,1,0:T(8,128)}, f32[4,192,176]{2,1,0:T(8,128)S(1)}, u32[]{:S(2)}) copy-start(f32[4,192,176]{2,1,0:T(8,128)S(1)} %get-tuple-element.19.uf_in) | copy-start | bytes 1622020
  88.5 4.5 %copy-start.5 = (bf16[1,176,2048]{2,1,0:T(8,128)(2,1)S(1)}, bf16[1,176,2048]{2,1,0:T(8,128)(2,1)}, u32[]{:S(2)}) copy-start(bf16[1,176,2048]{2,1,0:T(8,128)(2,1)} %param.11) | copy-start | bytes 2162692
  88.5 4.5 %copy-start.6 = (bf16[1,176,2048]{2,1,0:T(8,128)(2,1)S(1)}, bf16[1,176,2048]{2,1,0:T(8,128)(2,1)}, u32[]{:S(2)}) copy-start(bf16[1,176,2048]{2,1,0:T(8,128)(2,1)} %param.12) | copy-start | bytes 2162692
  88.6 0.9 copy-start.10
  99.7 20.6 %copy-start.9 = (s32[32,6]{0,1:T(8,128)S(1)}, s32[32,6]{0,1:T(8,128)}, u32[]{:S(2)}) copy-start(s32[32,6]{0,1:T(8,128)} %param.9) | copy-start | bytes 2308
  99.7 4.2 %collective-permute-start.12 = (bf16[192,2048]{1,0:T(8,128)(2,1)S(1)}, bf16[192,2048]{1,0:T(8,128)(2,1)S(1)}, u32[]{:S(2)}, u32[]{:S(2)}) collective-permute-start(bf16[192,2048]{1,0:T(8,128)(2,1)S(1)} %get-tuple-element.24), channel_id=1, source_target_pairs={{0,1},{1,0},{2,3},{3,2},{4,5},{5,4},{6,7},{7,6},{8,9},{9,8},{10,11... | collective-permute-start | bytes 2359304 | tf_op jit(solution)/shard_map/ppermute | solution.py:221
  105.2 58.2 %all-to-all-start.1 = ((bf16[64,48,128]{2,1,0:T(8,128)(2,1)}), bf16[64,48,128]{2,1,0:T(8,128)(2,1)S(1)}, u32[]{:S(2)}, u32[]{:S(2)}) async-start(bf16[64,48,128]{2,1,0:T(8,128)(2,1)} %shard_map.90), calls=%async_computation.1 | async-start | bytes 1572864 | tf_op jit(solution)/shard_map/all_to_all | solution.py:224

commit v10 on v9

--- a/solution.py
+++ b/solution.py
@@ -72,19 +72,27 @@
 
 
 def factor_kernel(gate_ref, up_ref, gf_ref, uf_ref):
-    slice_width = gf_ref.shape[2]
+    slice_width = gf_ref.shape[1] // LINKS
     replica = lax.axis_index("replica")
     link, turn = replica >> 1, 2 * (replica & 1) - 1
     first = turn < 0
+    gates, ups = [], []
     for q in range(LINKS):
         low = 2 * q * slice_width
         mid, high = low + slice_width, low + 2 * slice_width
         g = jnp.where(first, gate_ref[:, low:mid].astype(F32), gate_ref[:, mid:high].astype(F32))
         u = jnp.where(first, up_ref[:, low:mid].astype(F32), up_ref[:, mid:high].astype(F32))
         sig = jax.nn.sigmoid(g)
-        step = ((q - link) * turn + 2 * LINKS) & (LINKS - 1)
-        uf_ref[step] = g * sig
-        gf_ref[step] = u * sig * (1.0 + g * (1.0 - sig))
+        ups.append(g * sig)
+        gates.append(u * sig * (1.0 + g * (1.0 - sig)))
+    for step in range(LINKS):
+        held = (link + step * turn + LINKS) & (LINKS - 1)
+        place = slice(step * slice_width, (step + 1) * slice_width)
+        for values, ref in ((gates, gf_ref), (ups, uf_ref)):
+            value = values[0]
+            for q in range(1, LINKS):
+                value = jnp.where(held == q, values[q], value)
+            ref[:, place] = value
 
 
 def hidden_kernel(
@@ -119,11 +127,11 @@
         )
     for copy in copies[across_y + 2 * LINKS :]:
         copy.wait()
-    for step in range(LINKS):
-        part = grad[:, step * width : (step + 1) * width]
-        out_ref, low = (early_ref, 2 * step * width) if step < LINKS - 1 else (late_ref, 0)
-        out_ref[:, low : low + width] = (part * gf_ref[step]).astype(BF16)
-        out_ref[:, low + width : low + 2 * width] = (part * uf_ref[step]).astype(BF16)
+    cut = (LINKS - 1) * width
+    for factor_ref, half in ((gf_ref, 0), (uf_ref, 1)):
+        value = (grad * factor_ref[...]).astype(BF16)
+        early_ref[:, half * cut : (half + 1) * cut] = value[:, :cut]
+        late_ref[:, half * width : (half + 1) * width] = value[:, cut:]
 
 
 def gather(own_in, other_in, pieces, hidden_ref, weight_ref, sems):
@@ -149,8 +157,8 @@
         yield columns, jnp.dot(hidden_ref[...], weight_ref[:, columns], preferred_element_type=F32)
 
 
-def early_kernel(own_in, other_in, g0_in, u0_in, g1_in, u1_in, g2_in, u2_in, sum_ref, hidden_ref, weight_ref, sems):
-    pieces = (g0_in, u0_in, g1_in, u1_in, g2_in, u2_in)
+def early_kernel(own_in, other_in, g0_in, g1_in, g2_in, u0_in, u1_in, u2_in, sum_ref, hidden_ref, weight_ref, sems):
+    pieces = (g0_in, g1_in, g2_in, u0_in, u1_in, u2_in)
     for columns, total in gather(own_in, other_in, pieces, hidden_ref, weight_ref, sems):
         sum_ref[:, columns] = total
 
@@ -239,7 +247,7 @@
 
     saved = tuple(a[0, 0].transpose(1, 0, 2).reshape(rows, -1) for a in (saved_gate, saved_up))
     hidden_units = LINKS * slice_width
-    factor = jax.ShapeDtypeStruct((LINKS, rows, slice_width), F32)
+    factor = jax.ShapeDtypeStruct((rows, hidden_units), F32)
     own_factors = call(factor_kernel, saved, (factor, factor))
     sent = (across(saved[0]), across(saved[1]))
     other_factors = call(factor_kernel, sent, (factor, factor))
@@ -250,8 +258,8 @@
     scratch = (
         pltpu.VMEM((experts // ROWS_Y, ROWS_Y, 2 * deep, 128), BF16),
         pltpu.VMEM((hidden_units, width), BF16),
-        pltpu.VMEM((LINKS, rows, slice_width), F32),
-        pltpu.VMEM((LINKS, rows, slice_width), F32),
+        pltpu.VMEM((rows, hidden_units), F32),
+        pltpu.VMEM((rows, hidden_units), F32),
         pltpu.VMEM((rows, width), BF16),
         pltpu.SemaphoreType.DMA((ROWS_Y + 2 * LINKS + 2,)),
     )
@@ -261,10 +269,9 @@
         ins = (packed_rows,) + tuple(downs) + tuple(factors)
         return call(hidden_kernel, ins, hidden, cost, scratch=scratch, spec=AN, limit=limit)
 
-    own_hidden = hide(arrived, own_factors, 50 << 20)
-    other_hidden = hide(other_rows, other_factors, 50 << 20)
-
-    pieces = [piece for both in zip(gate_pieces, up_pieces) for piece in both]
+    own_hidden = hide(arrived, own_factors, 53 << 20)
+    other_hidden = hide(other_rows, other_factors, 53 << 20)
+
 
     def room(n):
         return (
@@ -276,7 +283,7 @@
     part = jax.ShapeDtypeStruct((rows, width), BF16)
     early = call(
         early_kernel,
-        (own_hidden[0], other_hidden[0]) + tuple(pieces[:-2]),
+        (own_hidden[0], other_hidden[0]) + tuple(gate_pieces[:-1] + up_pieces[:-1]),
         (jax.ShapeDtypeStruct((2 * rows, width), F32),),
         3 * cost,
         scratch=room(2 * hidden_units - last),
@@ -284,7 +291,7 @@
     )
     ours, theirs = call(
         late_kernel,
-        (early, own_hidden[1], other_hidden[1]) + tuple(pieces[-2:]),
+        (early, own_hidden[1], other_hidden[1]) + (gate_pieces[-1], up_pieces[-1]),
         (part, part),
         cost,
         scratch=room(last),

time: 165 us -> 167 us (1.012)
  the two profiles are of different devices: /device:TPU:8 before, /device:TPU:6 now
where the time goes in v10:
time: 167 us; the launch traced here: 166 us
  starting transfers between devices  70.7 us (42%)
  waiting for transfers between devices  66.1 us (40%)
  Pallas kernels  22 us (13%)
  local copies, waits for them, and re-layouts  7.13 us (4%)
    all_to_all x2, waiting for transfers between devices, exchange(): lax.all_to_all(a, ('y', 'z'), split_axis=0, concat_axis=0, tiled=True)  51.4 us
    all_to_all x2, starting transfers between devices, exchange(): lax.all_to_all(a, ('y', 'z'), split_axis=0, concat_axis=0, tiled=True)  33.8 us
    ppermute x9, starting transfers between devices, along(): return lax.ppermute(a, 'replica', pairs)  28.8 us
    pallas_call x10, Pallas kernels, call(): pl.pallas_call(kernel, out_shape=outs[0] if single else tuple(outs), in_s...  22 us
    ppermute x9, waiting for transfers between devices, along(): return lax.ppermute(a, 'replica', pairs)  12.5 us
    ppermute x4, starting transfers between devices, across(): return lax.ppermute(a, 'replica', [(i, i ^ 1) for i in range(copies)])  8.23 us
    unnamed x22, local copies, waits for them, and re-layouts  7.13 us
  transfers between devices with their start and end apart: 15, of which 6 were waited for; matrix products, arithmetic and copies ran while one was open for 0% of the time, Pallas kernels for 9%

profile of v10, /device:TPU:6, one launch (start us, length us, event | category | flops | bytes accessed | tf_op | source)
XLA Modules:
  0.0 166.3 jit_solution(702279774239056019)
XLA Ops:
  0.0 2.6 %shard_map.83 = bf16[64,48,128]{2,1,0:T(8,128)(2,1)} custom-call(s32[6,32]{1,0:T(8,128)} %bitcast.23, f32[6,32]{1,0:T(8,128)} %bitcast.28, bf16[32,2048]{1,0:T(8,128)(2,1)} %grad_ref.1), custom_call_target="tpu_custom_call" | custom-call | flops 25165824 | bytes 919040 | tf_op jit(solution)/shard_map/pallas_call | solution.py:20
  2.6 19.0 %all-to-all-start = ((bf16[64,48,128]{2,1,0:T(8,128)(2,1)}), bf16[64,48,128]{2,1,0:T(8,128)(2,1)}, u32[]{:S(2)}, u32[]{:S(2)}) async-start(bf16[64,48,128]{2,1,0:T(8,128)(2,1)} %shard_map.83), calls=%async_computation | async-start | bytes 1572864 | tf_op jit(solution)/shard_map/all_to_all | solution.py:232
  21.6 2.4 %collective-permute-start = (bf16[176,2048]{1,0:T(8,128)(2,1)}, bf16[176,2048]{1,0:T(8,128)(2,1)}, u32[]{:S(2)}, u32[]{:S(2)}) collective-permute-start(bf16[176,2048]{1,0:T(8,128)(2,1)} %bitcast.25), channel_id=1, source_target_pairs={{0,2},{1,7},{2,4},{3,1},{4,6},{5,3},{6,0},{7,5},{8,10},{9,15},{10,... | collective-permute-start | bytes 2162696 | tf_op jit(solution)/shard_map/ppermute | solution.py:226
  24.0 3.4 %collective-permute-start.6 = (bf16[176,2048]{1,0:T(8,128)(2,1)}, bf16[176,2048]{1,0:T(8,128)(2,1)S(1)}, u32[]{:S(2)}, u32[]{:S(2)}) collective-permute-start(bf16[176,2048]{1,0:T(8,128)(2,1)} %bitcast.15), channel_id=1, source_target_pairs={{0,2},{1,7},{2,4},{3,1},{4,6},{5,3},{6,0},{7,5},{8,10},{9,15},{10,... | collective-permute-start | bytes 2162696 | tf_op jit(solution)/shard_map/ppermute | solution.py:226
  27.4 3.4 %collective-permute-start.8 = (bf16[176,2048]{1,0:T(8,128)(2,1)}, bf16[176,2048]{1,0:T(8,128)(2,1)S(1)}, u32[]{:S(2)}, u32[]{:S(2)}) collective-permute-start(bf16[176,2048]{1,0:T(8,128)(2,1)} %bitcast.17), channel_id=1, source_target_pairs={{0,2},{1,7},{2,4},{3,1},{4,6},{5,3},{6,0},{7,5},{8,10},{9,15},{10,... | collective-permute-start | bytes 2162696 | tf_op jit(solution)/shard_map/ppermute | solution.py:226
  30.8 4.3 %collective-permute-done.down1_in = bf16[176,2048]{1,0:T(8,128)(2,1)} collective-permute-done((bf16[176,2048]{1,0:T(8,128)(2,1)}, bf16[176,2048]{1,0:T(8,128)(2,1)}, u32[]{:S(2)}, u32[]{:S(2)}) %collective-permute-start) | collective-permute-done | bytes 720928 | tf_op jit(solution)/shard_map/ppermute | solution.py:226
  35.1 3.6 %collective-permute-start.1 = (bf16[176,2048]{1,0:T(8,128)(2,1)}, bf16[176,2048]{1,0:T(8,128)(2,1)}, u32[]{:S(2)}, u32[]{:S(2)}) collective-permute-start(bf16[176,2048]{1,0:T(8,128)(2,1)} %collective-permute-done.down1_in), channel_id=1, source_target_pairs={{0,2},{1,7},{2,4},{3,1},{4,6},{5,3},{6,0},{7,5},{8,10},{9,15},{10,... | collective-permute-start | bytes 2162696 | tf_op jit(solution)/shard_map/ppermute | solution.py:226
  38.7 4.0 %collective-permute-done.6.g1_in = bf16[176,2048]{1,0:T(8,128)(2,1)S(1)} collective-permute-done((bf16[176,2048]{1,0:T(8,128)(2,1)}, bf16[176,2048]{1,0:T(8,128)(2,1)S(1)}, u32[]{:S(2)}, u32[]{:S(2)}) %collective-permute-start.6) | collective-permute-done | bytes 720928 | tf_op jit(solution)/shard_map/ppermute | solution.py:226
  42.7 3.6 %collective-permute-start.7 = (bf16[176,2048]{1,0:T(8,128)(2,1)S(1)}, bf16[176,2048]{1,0:T(8,128)(2,1)S(1)}, u32[]{:S(2)}, u32[]{:S(2)}) collective-permute-start(bf16[176,2048]{1,0:T(8,128)(2,1)S(1)} %collective-permute-done.6.g1_in), channel_id=1, source_target_pairs={{0,2},{1,7},{2,4},{3,1},{4,6},{5,3},{6,0},{7,5},{8,10},{9,15},{10,... | collective-permute-start | bytes 2162696 | tf_op jit(solution)/shard_map/ppermute | solution.py:226
  46.3 4.1 %collective-permute-done.8.u1_in = bf16[176,2048]{1,0:T(8,128)(2,1)S(1)} collective-permute-done((bf16[176,2048]{1,0:T(8,128)(2,1)}, bf16[176,2048]{1,0:T(8,128)(2,1)S(1)}, u32[]{:S(2)}, u32[]{:S(2)}) %collective-permute-start.8) | collective-permute-done | bytes 720928 | tf_op jit(solution)/shard_map/ppermute | solution.py:226
  50.4 3.6 %collective-permute-start.9 = (bf16[176,2048]{1,0:T(8,128)(2,1)S(1)}, bf16[176,2048]{1,0:T(8,128)(2,1)S(1)}, u32[]{:S(2)}, u32[]{:S(2)}) collective-permute-start(bf16[176,2048]{1,0:T(8,128)(2,1)S(1)} %collective-permute-done.8.u1_in), channel_id=1, source_target_pairs={{0,2},{1,7},{2,4},{3,1},{4,6},{5,3},{6,0},{7,5},{8,10},{9,15},{10,... | collective-permute-start | bytes 2162696 | tf_op jit(solution)/shard_map/ppermute | solution.py:226
  54.0 1.9 %collective-permute-start.4 = (bf16[192,1408]{1,0:T(8,128)(2,1)}, bf16[192,1408]{1,0:T(8,128)(2,1)S(1)}, u32[]{:S(2)}, u32[]{:S(2)}) collective-permute-start(bf16[192,1408]{1,0:T(8,128)(2,1)} %bitcast.19), channel_id=1, source_target_pairs={{0,1},{1,0},{2,3},{3,2},{4,5},{5,4},{6,7},{7,6},{8,9},{9,8},{10,11... | collective-permute-start | bytes 1622024 | tf_op jit(solution)/shard_map/ppermute | solution.py:229
  56.0 8.4 %all-to-all-done.packed_in = bf16[64,48,128]{2,1,0:T(8,128)(2,1)} async-done(((bf16[64,48,128]{2,1,0:T(8,128)(2,1)}), bf16[64,48,128]{2,1,0:T(8,128)(2,1)}, u32[]{:S(2)}, u32[]{:S(2)}) %all-to-all-start) | async-done | bytes 786464 | tf_op jit(solution)/shard_map/all_to_all | solution.py:232
  64.4 1.9 %collective-permute-start.3 = (bf16[64,48,128]{2,1,0:T(8,128)(2,1)}, bf16[64,48,128]{2,1,0:T(8,128)(2,1)S(1)}, u32[]{:S(2)}, u32[]{:S(2)}) collective-permute-start(bf16[64,48,128]{2,1,0:T(8,128)(2,1)} %all-to-all-done.packed_in), channel_id=1, source_target_pairs={{0,1},{1,0},{2,3},{3,2},{4,5},{5,4},{6,7},{7,6},{8,9},{9,8},{10,11... | collective-permute-start | bytes 2359304 | tf_op jit(solution)/shard_map/ppermute | solution.py:229
  66.3 0.0 collective-permute-done.1.down2_in
  66.3 2.4 %collective-permute-start.2 = (bf16[176,2048]{1,0:T(8,128)(2,1)}, bf16[176,2048]{1,0:T(8,128)(2,1)S(1)}, u32[]{:S(2)}, u32[]{:S(2)}) collective-permute-start(bf16[176,2048]{1,0:T(8,128)(2,1)} %collective-permute-done.1.down2_in), channel_id=1, source_target_pairs={{0,2},{1,7},{2,4},{3,1},{4,6},{5,3},{6,0},{7,5},{8,10},{9,15},{10,... | collective-permute-start | bytes 2162696 | tf_op jit(solution)/shard_map/ppermute | solution.py:226
  68.7 2.5 %collective-permute-start.5 = (bf16[192,1408]{1,0:T(8,128)(2,1)}, bf16[192,1408]{1,0:T(8,128)(2,1)S(1)}, u32[]{:S(2)}, u32[]{:S(2)}) collective-permute-start(bf16[192,1408]{1,0:T(8,128)(2,1)} %bitcast.21), channel_id=1, source_target_pairs={{0,1},{1,0},{2,3},{3,2},{4,5},{5,4},{6,7},{7,6},{8,9},{9,8},{10,11... | collective-permute-start | bytes 1622024 | tf_op jit(solution)/shard_map/ppermute | solution.py:229
  71.2 0.0 collective-permute-done.7.g2_in
  71.2 4.3 %collective-permute-start.10 = (bf16[176,2048]{1,0:T(8,128)(2,1)S(1)}, bf16[176,2048]{1,0:T(8,128)(2,1)S(1)}, u32[]{:S(2)}, u32[]{:S(2)}) collective-permute-start(bf16[176,2048]{1,0:T(8,128)(2,1)S(1)} %collective-permute-done.7.g2_in), channel_id=1, source_target_pairs={{0,2},{1,7},{2,4},{3,1},{4,6},{5,3},{6,0},{7,5},{8,10},{9,15},{10,... | collective-permute-start | bytes 2162696 | tf_op jit(solution)/shard_map/ppermute | solution.py:226
  75.5 0.0 collective-permute-done.9.u2_in
  75.5 2.1 %collective-permute-start.11 = (bf16[176,2048]{1,0:T(8,128)(2,1)S(1)}, bf16[176,2048]{1,0:T(8,128)(2,1)S(1)}, u32[]{:S(2)}, u32[]{:S(2)}) collective-permute-start(bf16[176,2048]{1,0:T(8,128)(2,1)S(1)} %collective-permute-done.9.u2_in), channel_id=1, source_target_pairs={{0,2},{1,7},{2,4},{3,1},{4,6},{5,3},{6,0},{7,5},{8,10},{9,15},{10,... | collective-permute-start | bytes 2162696 | tf_op jit(solution)/shard_map/ppermute | solution.py:226
  77.6 0.0 copy-start.6
  77.7 1.0 copy-done.6
  78.7 1.0 copy-done.7
  79.7 2.3 %shard_map.84 = (f32[192,704]{1,0:T(8,128)S(1)}, f32[192,704]{1,0:T(8,128)S(1)}) custom-call(bf16[192,1408]{1,0:T(8,128)(2,1)S(1)} %bitcast.20, bf16[192,1408]{1,0:T(8,128)(2,1)S(1)} %bitcast.22), custom_call_target="tpu_custom_call" | custom-call | bytes 2162688 | tf_op jit(solution)/shard_map/pallas_call | solution.py:20
  82.1 0.8 copy-done.4
  82.9 0.8 copy-done.5
  83.7 2.3 %shard_map.86 = (f32[192,704]{1,0:T(8,128)S(1)}, f32[192,704]{1,0:T(8,128)S(1)}) custom-call(bf16[192,1408]{1,0:T(8,128)(2,1)S(1)} %collective-permute-done.4.gate_ref, bf16[192,1408]{1,0:T(8,128)(2,1)S(1)} %collective-permute-done.5.up_ref), custom_call_target="tpu_custom_call" | custom-call | bytes 2162688 | tf_op jit(solution)/shard_map/pallas_call | solution.py:20
  86.0 0.8 copy-done.2
  86.9 0.8 copy-done.3
  87.7 0.0 collective-permute-done.2.down3_in
  87.7 0.9 copy-done.9
  88.5 3.5 %shard_map.85 = (bf16[192,1056]{1,0:T(8,128)(2,1)S(1)}, bf16[192,352]{1,0:T(8,128)(2,1)S(1)}) custom-call(bf16[64,48,128]{2,1,0:T(8,128)(2,1)} %all-to-all-done.packed_in, bf16[176,2048]{1,0:T(8,128)(2,1)} %bitcast.26, bf16[176,2048]{1,0:T(8,128)(2,1)} %collective-permute-done.down1_in, bf16[176,2048]{1,0:T(8,128)(2,1)} %collective-permute-done.1.down2_in, ...), custom_call_target="tpu_custom_call" | custom-call | flops 553648128 | bytes 5292032 | tf_op jit(solution)/shard_map/pallas_call | solution.py:20
  92.0 0.0 copy-start
  92.0 0.0 copy-start.1
  92.1 0.9 copy-done.10
  92.9 3.5 %shard_map.87 = (bf16[192,1056]{1,0:T(8,128)(2,1)S(1)}, bf16[192,352]{1,0:T(8,128)(2,1)S(1)}) custom-call(bf16[64,48,128]{2,1,0:T(8,128)(2,1)} %copy-done.10, bf16[176,2048]{1,0:T(8,128)(2,1)} %bitcast.27, bf16[176,2048]{1,0:T(8,128)(2,1)} %collective-permute-done.down1_in, bf16[176,2048]{1,0:T(8,128)(2,1)} %collective-permute-done.1.down2_in, ...), custom_call_target="tpu_custom_call" | custom-call | flops 553648128 | bytes 5292032 | tf_op jit(solution)/shard_map/pallas_call | solution.py:20
  96.4 3.4 %shard_map.88.sum_ref = f32[384,2048]{1,0:T(8,128)S(1)} custom-call(bf16[192,1056]{1,0:T(8,128)(2,1)S(1)} %get-tuple-element.17.own_in, bf16[192,1056]{1,0:T(8,128)(2,1)S(1)} %get-tuple-element.20.other_in, bf16[176,2048]{1,0:T(8,128)(2,1)S(1)} %bitcast.16, bf16[176,2048]{1,0:T(8,128)(2,1)S(1)} %collective-permute-done.6.g1_in, ...), custom_call_target="tpu_custom_call" | custom-call | flops 1660944384 | bytes 8282112 | tf_op jit(solution)/shard_map/pallas_call | solution.py:20
  99.9 0.0 collective-permute-done.10.gate_in
  99.9 1.7 %shard_map.89 = (bf16[192,2048]{1,0:T(8,128)(2,1)S(1)}, bf16[192,2048]{1,0:T(8,128)(2,1)S(1)}) custom-call(f32[384,2048]{1,0:T(8,128)S(1)} %shard_map.88.sum_ref, bf16[192,352]{1,0:T(8,128)(2,1)S(1)} %get-tuple-element.21.own_in, bf16[192,352]{1,0:T(8,128)(2,1)S(1)} %get-tuple-element.22.other_in, bf16[176,2048]{1,0:T(8,128)(2,1)S(1)} %collective-permute-done.10.gate_in, ...), custom_call_target="tpu_custom_call" | custom-call | flops 553648128 | bytes 6430720 | tf_op jit(solution)/shard_map/pallas_call | solution.py:20
  101.6 0.0 copy-start.8
  101.7 1.9 %collective-permute-start.12 = (bf16[192,2048]{1,0:T(8,128)(2,1)S(1)}, bf16[192,2048]{1,0:T(8,128)(2,1)S(1)}, u32[]{:S(2)}, u32[]{:S(2)}) collective-permute-start(bf16[192,2048]{1,0:T(8,128)(2,1)S(1)} %get-tuple-element.24), channel_id=1, source_target_pairs={{0,1},{1,0},{2,3},{3,2},{4,5},{5,4},{6,7},{7,6},{8,9},{9,8},{10,11... | collective-permute-start | bytes 2359304 | tf_op jit(solution)/shard_map/ppermute | solution.py:229
  103.6 2.3 %collective-permute-done.12.back_ref = bf16[192,2048]{1,0:T(8,128)(2,1)S(1)} collective-permute-done((bf16[192,2048]{1,0:T(8,128)(2,1)S(1)}, bf16[192,2048]{1,0:T(8,128)(2,1)S(1)}, u32[]{:S(2)}, u32[]{:S(2)}) %collective-permute-start.12) | collective-permute-done | bytes 786464 | tf_op jit(solution)/shard_map/ppermute | solution.py:229
  105.8 1.3 shard_map.90
  107.1 14.8 %all-to-all-start.1 = ((bf16[64,48,128]{2,1,0:T(8,128)(2,1)}), bf16[64,48,128]{2,1,0:T(8,128)(2,1)S(1)}, u32[]{:S(2)}, u32[]{:S(2)}) async-start(bf16[64,48,128]{2,1,0:T(8,128)(2,1)} %shard_map.90), calls=%async_computation.1 | async-start | bytes 1572864 | tf_op jit(solution)/shard_map/all_to_all | solution.py:232
  121.9 0.3 shard_map.82.hot_ref
  122.2 43.0 %all-to-all-done.1.back_ref = bf16[64,48,128]{2,1,0:T(8,128)(2,1)S(1)} async-done(((bf16[64,48,128]{2,1,0:T(8,128)(2,1)}), bf16[64,48,128]{2,1,0:T(8,128)(2,1)S(1)}, u32[]{:S(2)}, u32[]{:S(2)}) %all-to-all-start.1) | async-done | bytes 786464 | tf_op jit(solution)/shard_map/all_to_all | solution.py:232
  165.2 1.1 shard_map.91
  (14 shorter events, 0.0 us)
Async XLA Ops:
  2.6 61.8 %all-to-all-start = ((bf16[64,48,128]{2,1,0:T(8,128)(2,1)}), bf16[64,48,128]{2,1,0:T(8,128)(2,1)}, u32[]{:S(2)}, u32[]{:S(2)}) async-start(bf16[64,48,128]{2,1,0:T(8,128)(2,1)} %shard_map.83), calls=%async_computation | async-start | bytes 1572864 | tf_op jit(solution)/shard_map/all_to_all | solution.py:232
  21.6 13.5 %collective-permute-start = (bf16[176,2048]{1,0:T(8,128)(2,1)}, bf16[176,2048]{1,0:T(8,128)(2,1)}, u32[]{:S(2)}, u32[]{:S(2)}) collective-permute-start(bf16[176,2048]{1,0:T(8,128)(2,1)} %bitcast.25), channel_id=1, source_target_pairs={{0,2},{1,7},{2,4},{3,1},{4,6},{5,3},{6,0},{7,5},{8,10},{9,15},{10,... | collective-permute-start | bytes 2162696 | tf_op jit(solution)/shard_map/ppermute | solution.py:226
  24.0 18.7 %collective-permute-start.6 = (bf16[176,2048]{1,0:T(8,128)(2,1)}, bf16[176,2048]{1,0:T(8,128)(2,1)S(1)}, u32[]{:S(2)}, u32[]{:S(2)}) collective-permute-start(bf16[176,2048]{1,0:T(8,128)(2,1)} %bitcast.15), channel_id=1, source_target_pairs={{0,2},{1,7},{2,4},{3,1},{4,6},{5,3},{6,0},{7,5},{8,10},{9,15},{10,... | collective-permute-start | bytes 2162696 | tf_op jit(solution)/shard_map/ppermute | solution.py:226
  27.4 23.0 %collective-permute-start.8 = (bf16[176,2048]{1,0:T(8,128)(2,1)}, bf16[176,2048]{1,0:T(8,128)(2,1)S(1)}, u32[]{:S(2)}, u32[]{:S(2)}) collective-permute-start(bf16[176,2048]{1,0:T(8,128)(2,1)} %bitcast.17), channel_id=1, source_target_pairs={{0,2},{1,7},{2,4},{3,1},{4,6},{5,3},{6,0},{7,5},{8,10},{9,15},{10,... | collective-permute-start | bytes 2162696 | tf_op jit(solution)/shard_map/ppermute | solution.py:226
  35.1 31.2 %collective-permute-start.1 = (bf16[176,2048]{1,0:T(8,128)(2,1)}, bf16[176,2048]{1,0:T(8,128)(2,1)}, u32[]{:S(2)}, u32[]{:S(2)}) collective-permute-start(bf16[176,2048]{1,0:T(8,128)(2,1)} %collective-permute-done.down1_in), channel_id=1, source_target_pairs={{0,2},{1,7},{2,4},{3,1},{4,6},{5,3},{6,0},{7,5},{8,10},{9,15},{10,... | collective-permute-start | bytes 2162696 | tf_op jit(solution)/shard_map/ppermute | solution.py:226
  42.7 28.5 %collective-permute-start.7 = (bf16[176,2048]{1,0:T(8,128)(2,1)S(1)}, bf16[176,2048]{1,0:T(8,128)(2,1)S(1)}, u32[]{:S(2)}, u32[]{:S(2)}) collective-permute-start(bf16[176,2048]{1,0:T(8,128)(2,1)S(1)} %collective-permute-done.6.g1_in), channel_id=1, source_target_pairs={{0,2},{1,7},{2,4},{3,1},{4,6},{5,3},{6,0},{7,5},{8,10},{9,15},{10,... | collective-permute-start | bytes 2162696 | tf_op jit(solution)/shard_map/ppermute | solution.py:226
  50.4 25.1 %collective-permute-start.9 = (bf16[176,2048]{1,0:T(8,128)(2,1)S(1)}, bf16[176,2048]{1,0:T(8,128)(2,1)S(1)}, u32[]{:S(2)}, u32[]{:S(2)}) collective-permute-start(bf16[176,2048]{1,0:T(8,128)(2,1)S(1)} %collective-permute-done.8.u1_in), channel_id=1, source_target_pairs={{0,2},{1,7},{2,4},{3,1},{4,6},{5,3},{6,0},{7,5},{8,10},{9,15},{10,... | collective-permute-start | bytes 2162696 | tf_op jit(solution)/shard_map/ppermute | solution.py:226
  54.0 14.7 %collective-permute-start.4 = (bf16[192,1408]{1,0:T(8,128)(2,1)}, bf16[192,1408]{1,0:T(8,128)(2,1)S(1)}, u32[]{:S(2)}, u32[]{:S(2)}) collective-permute-start(bf16[192,1408]{1,0:T(8,128)(2,1)} %bitcast.19), channel_id=1, source_target_pairs={{0,1},{1,0},{2,3},{3,2},{4,5},{5,4},{6,7},{7,6},{8,9},{9,8},{10,11... | collective-permute-start | bytes 1622024 | tf_op jit(solution)/shard_map/ppermute | solution.py:229
  64.4 27.7 %collective-permute-start.3 = (bf16[64,48,128]{2,1,0:T(8,128)(2,1)}, bf16[64,48,128]{2,1,0:T(8,128)(2,1)S(1)}, u32[]{:S(2)}, u32[]{:S(2)}) collective-permute-start(bf16[64,48,128]{2,1,0:T(8,128)(2,1)} %all-to-all-done.packed_in), channel_id=1, source_target_pairs={{0,1},{1,0},{2,3},{3,2},{4,5},{5,4},{6,7},{7,6},{8,9},{9,8},{10,11... | collective-permute-start | bytes 2359304 | tf_op jit(solution)/shard_map/ppermute | solution.py:229
  66.3 21.4 %collective-permute-start.2 = (bf16[176,2048]{1,0:T(8,128)(2,1)}, bf16[176,2048]{1,0:T(8,128)(2,1)S(1)}, u32[]{:S(2)}, u32[]{:S(2)}) collective-permute-start(bf16[176,2048]{1,0:T(8,128)(2,1)} %collective-permute-done.1.down2_in), channel_id=1, source_target_pairs={{0,2},{1,7},{2,4},{3,1},{4,6},{5,3},{6,0},{7,5},{8,10},{9,15},{10,... | collective-permute-start | bytes 2162696 | tf_op jit(solution)/shard_map/ppermute | solution.py:226
  68.7 15.0 %collective-permute-start.5 = (bf16[192,1408]{1,0:T(8,128)(2,1)}, bf16[192,1408]{1,0:T(8,128)(2,1)S(1)}, u32[]{:S(2)}, u32[]{:S(2)}) collective-permute-start(bf16[192,1408]{1,0:T(8,128)(2,1)} %bitcast.21), channel_id=1, source_target_pairs={{0,1},{1,0},{2,3},{3,2},{4,5},{5,4},{6,7},{7,6},{8,9},{9,8},{10,11... | collective-permute-start | bytes 1622024 | tf_op jit(solution)/shard_map/ppermute | solution.py:229
  71.2 28.7 %collective-permute-start.10 = (bf16[176,2048]{1,0:T(8,128)(2,1)S(1)}, bf16[176,2048]{1,0:T(8,128)(2,1)S(1)}, u32[]{:S(2)}, u32[]{:S(2)}) collective-permute-start(bf16[176,2048]{1,0:T(8,128)(2,1)S(1)} %collective-permute-done.7.g2_in), channel_id=1, source_target_pairs={{0,2},{1,7},{2,4},{3,1},{4,6},{5,3},{6,0},{7,5},{8,10},{9,15},{10,... | collective-permute-start | bytes 2162696 | tf_op jit(solution)/shard_map/ppermute | solution.py:226
  75.5 24.4 %collective-permute-start.11 = (bf16[176,2048]{1,0:T(8,128)(2,1)S(1)}, bf16[176,2048]{1,0:T(8,128)(2,1)S(1)}, u32[]{:S(2)}, u32[]{:S(2)}) collective-permute-start(bf16[176,2048]{1,0:T(8,128)(2,1)S(1)} %collective-permute-done.9.u2_in), channel_id=1, source_target_pairs={{0,2},{1,7},{2,4},{3,1},{4,6},{5,3},{6,0},{7,5},{8,10},{9,15},{10,... | collective-permute-start | bytes 2162696 | tf_op jit(solution)/shard_map/ppermute | solution.py:226
  77.6 1.1 copy-start.6
  78.7 1.0 copy-start.7
  82.1 0.8 copy-start.4
  82.9 0.8 copy-start.5
  86.0 0.8 copy-start.2
  86.9 0.8 copy-start.3
  87.7 0.9 copy-start.9
  92.0 4.4 %copy-start = (bf16[1,176,2048]{2,1,0:T(8,128)(2,1)S(1)}, bf16[1,176,2048]{2,1,0:T(8,128)(2,1)}, u32[]{:S(2)}) copy-start(bf16[1,176,2048]{2,1,0:T(8,128)(2,1)} %param.11) | copy-start | bytes 2162692
  92.0 4.4 %copy-start.1 = (bf16[1,176,2048]{2,1,0:T(8,128)(2,1)S(1)}, bf16[1,176,2048]{2,1,0:T(8,128)(2,1)}, u32[]{:S(2)}) copy-start(bf16[1,176,2048]{2,1,0:T(8,128)(2,1)} %param.12) | copy-start | bytes 2162692
  92.0 0.9 copy-start.10
  101.6 20.3 %copy-start.8 = (s32[32,6]{0,1:T(8,128)S(1)}, s32[32,6]{0,1:T(8,128)}, u32[]{:S(2)}) copy-start(s32[32,6]{0,1:T(8,128)} %param.9) | copy-start | bytes 2308
  101.7 4.2 %collective-permute-start.12 = (bf16[192,2048]{1,0:T(8,128)(2,1)S(1)}, bf16[192,2048]{1,0:T(8,128)(2,1)S(1)}, u32[]{:S(2)}, u32[]{:S(2)}) collective-permute-start(bf16[192,2048]{1,0:T(8,128)(2,1)S(1)} %get-tuple-element.24), channel_id=1, source_target_pairs={{0,1},{1,0},{2,3},{3,2},{4,5},{5,4},{6,7},{7,6},{8,9},{9,8},{10,11... | collective-permute-start | bytes 2359304 | tf_op jit(solution)/shard_map/ppermute | solution.py:229
  107.1 58.0 %all-to-all-start.1 = ((bf16[64,48,128]{2,1,0:T(8,128)(2,1)}), bf16[64,48,128]{2,1,0:T(8,128)(2,1)S(1)}, u32[]{:S(2)}, u32[]{:S(2)}) async-start(bf16[64,48,128]{2,1,0:T(8,128)(2,1)} %shard_map.90), calls=%async_computation.1 | async-start | bytes 1572864 | tf_op jit(solution)/shard_map/all_to_all | solution.py:232
